TPU v7x, 128 devices: a whole 4x4x4 slice. The times are simulated.
128 devices in a mesh: row: 16 (over z, y), col: 8 (over x, core).
Axes of the slice: x: 4, y: 4, z: 4, core: 2. Of those that a mesh axis runs over, the one named last changes fastest.
Arguments:
- features: float32 [65536, 512], P(('row', 'col')), may hold values from -6 to 6
- tiles: float32 [16, 8, 128, 128, 128], P('row', 'col'), may hold values from -0.4 to 0.4
- tile_rows: int32 [16, 8, 128], P('row', 'col'), may hold values from 0 to 31
- tile_cols: int32 [16, 8, 128], P('row', 'col'), may hold values from 0 to 31
- tile_count: int32 [16, 8], P('row', 'col'), may hold values from 16 to 128, as said below
- needed: int32 [16, 8, 16, 2], P('row', 'col'), may hold values from 0 to 3, as said below
- w_in: bfloat16 [512, 2048], replicated, may hold values from -0.25 to 0.25
- bias_in: float32 [2048], replicated, may hold values from -5 to 5
- w_out: bfloat16 [2048, 512], replicated, may hold values from -0.125 to 0.125
- bias_out: float32 [512], replicated, may hold values from -5 to 5
Outputs:
- updated: bfloat16 [65536, 512], P(('row', 'col'))
Inputs may be any that keep to these rules, and one draw needn't show every extreme that they name: tile_count of every grid cell lies between 16 and 64, except one cell of each draw that has all 128 tiles live. Each list needed[r, c, q] holds 2 different block numbers.
All inputs are finite; a program needn't handle non-finite values.
Results may differ from a plain program's by a relative error of at most 0.0054.
Values sent between devices are 32-bit elements; how exact they have to be, the bound alone decides.
No kernel may reach another device: no remote copies, remote signals or barrier semaphores. Data moves between devices by JAX's collectives and lax.ppermute only.
A program may use at most 128 MiB of HBM per device.

v0:
```python
import math

import jax
import jax.numpy as jnp
from jax import lax
from jax.sharding import PartitionSpec as P

gin_epsilon = 0.25
precise_mode = lax.Precision.HIGHEST


def on_device(
    features, tiles, tile_rows, tile_cols, tile_count, needed, w_in, bias_in, w_out, bias_out
):
    tile_edge = tiles.shape[-1]
    width = features.shape[1]
    blocks_dev = features.shape[0] // tile_edge
    grid_cols = lax.axis_size("col")
    slot_count = needed.shape[-1]
    own_blocks = features.reshape(blocks_dev, tile_edge, width)
    my_tiles = tiles[0, 0]
    tile_row = tile_rows[0, 0]
    tile_col = tile_cols[0, 0]
    wanted = needed[0, 0]
    column_pool = lax.all_gather(own_blocks, "row", axis=0, tiled=True)
    source = tile_col // slot_count
    position = source * blocks_dev + jnp.take(wanted.reshape(-1), tile_col)
    tile_total = my_tiles.shape[0]
    group = math.gcd(32, tile_total)
    row_blocks = grid_cols * blocks_dev
    live = (jnp.arange(tile_total) < tile_count[0, 0]).astype(jnp.float32)
    block_ids = jnp.arange(row_blocks, dtype=jnp.int32)

    def add_group(turn, partial_value):
        start = turn * group
        group_tiles = lax.dynamic_slice_in_dim(my_tiles, start, group, 0)
        group_pos = lax.dynamic_slice_in_dim(position, start, group, 0)
        group_row = lax.dynamic_slice_in_dim(tile_row, start, group, 0)
        group_live = lax.dynamic_slice_in_dim(live, start, group, 0)
        inputs = jnp.take(column_pool, group_pos, axis=0)
        product = jnp.einsum("tpq,tqf->tpf", group_tiles, inputs, precision=precise_mode)
        selector = (group_row[None, :] == block_ids[:, None]).astype(jnp.float32) * group_live[
            None, :
        ]
        return partial_value + jnp.dot(
            selector, product.reshape(group, tile_edge * width), precision=precise_mode
        )

    partial_value = lax.fori_loop(
        0, tile_total // group, add_group, jnp.zeros((row_blocks, tile_edge * width), jnp.float32)
    )
    summed = lax.psum_scatter(
        partial_value.reshape(row_blocks * tile_edge, width), "col", scatter_dimension=0, tiled=True
    )
    mixed = ((1.0 + gin_epsilon) * features + summed).astype(jnp.bfloat16)
    hidden = jax.nn.relu(jnp.dot(mixed, w_in, preferred_element_type=jnp.float32) + bias_in).astype(
        jnp.bfloat16
    )
    return (jnp.dot(hidden, w_out, preferred_element_type=jnp.float32) + bias_out).astype(
        jnp.bfloat16
    )


def solution(mesh):
    placed = (
        P(("row", "col"), None),
        P("row", "col", None, None, None),
        P("row", "col", None),
        P("row", "col", None),
        P("row", "col"),
        P("row", "col", None, None),
        P(),
        P(),
        P(),
        P(),
    )
    return jax.shard_map(
        on_device, mesh=mesh, in_specs=placed, out_specs=P(("row", "col"), None), check_vma=False
    )
```

profile of v0, /device:TPU:1, one launch (start us, length us, event | category | flops | bytes accessed | tf_op | source)
XLA Modules:
  0.0 363.8 jit_solution(9578048227056878667)
XLA Ops:
  6.5 0.0 copy-start
  6.5 0.7 all-gather.2.cloned.1.call-update
  7.3 0.0 reduce-scatter.2.cloned.1.call-start
  7.3 0.8 copy.13
  8.1 0.1 reshape_squeeze.3
  8.8 0.7 fusion.18
  9.5 1.2 gather_fusion.1
  10.7 0.7 fusion.17
  11.4 112.5 %all-gather.2.cloned.1.call-done = f32[64,128,512]{2,1,0:T(8,128)} async-done(((f32[4,128,512]{2,1,0:T(8,128)}), f32[64,128,512]{2,1,0:T(8,128)}) %all-gather.2.cloned.1.call-update) | async-done | bytes 16777232 | tf_op jit(solution)/shard_map/all_gather | solution.py:25
  123.9 168.7 %while.14 = (s32[]{:T(128)}, f32[32,65536]{1,0:T(8,128)}, s32[128]{0:T(128)}, f32[128]{0:T(128)S(1)}, f32[128,128,128]{2,1,0:T(8,128)}, /*index=5*/s32[128]{0:T(...) while((s32[]{:T(128)}, f32[32,65536]{1,0:T(8,128)}, ...), condition=%wide.region_1.2_spmd.clone, body=%wide.region_0.1_spmd.clone.sunk | while | flops 4032826624 | bytes 77602320 | solution.py:49
  123.9 0.1 compare_and_fusion.2
  124.0 10.1 %gather_fusion = f32[32,128,512]{2,1,0:T(8,128)} fusion(f32[64,128,512]{2,1,0:T(8,128)} %get-tuple-element.262, s32[1024]{0:T(1024)S(1)} %pad_clamp_fusion.3), kind=kCustom, calls=%fused_computation.clone.clone.1 | custom fusion | bytes 16777344 | tf_op jit(solution)/shard_map/while/body/eval_jaxpr/jit(_take)/gather | solution.py:40
  134.0 10.9 %fusion.34 = f32[32,128,512]{2,1,0:T(8,128)S(1)} fusion(f32[32,128,512]{2,1,0:T(8,128)} %gather_fusion, pred[32]{0:T(512)(128)(4,1)S(1)} %get-tuple-element.233, f32[128,128,128]{2,1,0:T(8,128)} %get-tuple-element.260, s32[]{:T(128)S(6)} %select_n.79), kind=kOutput, calls=%fused_computation.4.clone.1 | convolution fusion | flops 3223322624 | bytes 18874404 | tf_op jit(solution)/shard_map/while/body/eval_jaxpr/tpq,tqf->tpf/dot_general | solution.py:41
  145.0 0.0 copy-start.4
  145.0 8.1 %copy.16 = f32[4,8,128,512]{3,1,2,0:T(8,128)} copy(f32[4,8,128,512]{3,2,1,0:T(8,128)S(1)} %bitcast.33) | data formatting | bytes 16777216 | tf_op jit(solution)/shard_map/while
  153.1 0.1 dynamic_slice.40
  153.1 0.0 copy-done.4
  153.1 0.1 dynamic_slice.41
  153.2 11.9 %convolution_add_fusion.3 = f32[32,65536]{1,0:T(8,128)} fusion(f32[32,65536]{1,0:T(8,128)} %bitcast.34, f32[32,65536]{1,0:T(8,128)} %get-tuple-element.246, pred[]{:T(512)S(6)} %compare.5, f32[32]{0:T(128)S(1)} %dynamic_slice.40, s32[32]{0:T(128)S(1)} %dynamic_slice.41), kind=kOutput, calls=%fused_computation.3.clone.1 | convolution fusion | flops 809502720 | bytes 25166080 | tf_op jit(solution)/shard_map/while/body/eval_jaxpr/dot_general | solution.py:45
  165.1 0.1 compare_and_fusion.2
  165.2 10.1 %gather_fusion = f32[32,128,512]{2,1,0:T(8,128)} fusion(f32[64,128,512]{2,1,0:T(8,128)} %get-tuple-element.262, s32[1024]{0:T(1024)S(1)} %pad_clamp_fusion.3), kind=kCustom, calls=%fused_computation.clone.clone.1 | custom fusion | bytes 16777344 | tf_op jit(solution)/shard_map/while/body/eval_jaxpr/jit(_take)/gather | solution.py:40
  175.3 10.9 %fusion.34 = f32[32,128,512]{2,1,0:T(8,128)S(1)} fusion(f32[32,128,512]{2,1,0:T(8,128)} %gather_fusion, pred[32]{0:T(512)(128)(4,1)S(1)} %get-tuple-element.233, f32[128,128,128]{2,1,0:T(8,128)} %get-tuple-element.260, s32[]{:T(128)S(6)} %select_n.79), kind=kOutput, calls=%fused_computation.4.clone.1 | convolution fusion | flops 3223322624 | bytes 18874404 | tf_op jit(solution)/shard_map/while/body/eval_jaxpr/tpq,tqf->tpf/dot_general | solution.py:41
  186.2 0.0 copy-start.4
  186.2 8.1 %copy.16 = f32[4,8,128,512]{3,1,2,0:T(8,128)} copy(f32[4,8,128,512]{3,2,1,0:T(8,128)S(1)} %bitcast.33) | data formatting | bytes 16777216 | tf_op jit(solution)/shard_map/while
  194.3 0.1 dynamic_slice.40
  194.3 0.1 dynamic_slice.41
  194.4 13.2 %convolution_add_fusion.3 = f32[32,65536]{1,0:T(8,128)} fusion(f32[32,65536]{1,0:T(8,128)} %bitcast.34, f32[32,65536]{1,0:T(8,128)} %get-tuple-element.246, pred[]{:T(512)S(6)} %compare.5, f32[32]{0:T(128)S(1)} %dynamic_slice.40, s32[32]{0:T(128)S(1)} %dynamic_slice.41), kind=kOutput, calls=%fused_computation.3.clone.1 | convolution fusion | flops 809502720 | bytes 25166080 | tf_op jit(solution)/shard_map/while/body/eval_jaxpr/dot_general | solution.py:45
  207.6 0.1 compare_and_fusion.2
  207.7 10.1 %gather_fusion = f32[32,128,512]{2,1,0:T(8,128)} fusion(f32[64,128,512]{2,1,0:T(8,128)} %get-tuple-element.262, s32[1024]{0:T(1024)S(1)} %pad_clamp_fusion.3), kind=kCustom, calls=%fused_computation.clone.clone.1 | custom fusion | bytes 16777344 | tf_op jit(solution)/shard_map/while/body/eval_jaxpr/jit(_take)/gather | solution.py:40
  217.8 10.9 %fusion.34 = f32[32,128,512]{2,1,0:T(8,128)S(1)} fusion(f32[32,128,512]{2,1,0:T(8,128)} %gather_fusion, pred[32]{0:T(512)(128)(4,1)S(1)} %get-tuple-element.233, f32[128,128,128]{2,1,0:T(8,128)} %get-tuple-element.260, s32[]{:T(128)S(6)} %select_n.79), kind=kOutput, calls=%fused_computation.4.clone.1 | convolution fusion | flops 3223322624 | bytes 18874404 | tf_op jit(solution)/shard_map/while/body/eval_jaxpr/tpq,tqf->tpf/dot_general | solution.py:41
  228.7 0.0 copy-start.4
  228.7 8.1 %copy.16 = f32[4,8,128,512]{3,1,2,0:T(8,128)} copy(f32[4,8,128,512]{3,2,1,0:T(8,128)S(1)} %bitcast.33) | data formatting | bytes 16777216 | tf_op jit(solution)/shard_map/while
  236.8 0.1 dynamic_slice.40
  236.8 0.1 dynamic_slice.41
  236.9 13.2 %convolution_add_fusion.3 = f32[32,65536]{1,0:T(8,128)} fusion(f32[32,65536]{1,0:T(8,128)} %bitcast.34, f32[32,65536]{1,0:T(8,128)} %get-tuple-element.246, pred[]{:T(512)S(6)} %compare.5, f32[32]{0:T(128)S(1)} %dynamic_slice.40, s32[32]{0:T(128)S(1)} %dynamic_slice.41), kind=kOutput, calls=%fused_computation.3.clone.1 | convolution fusion | flops 809502720 | bytes 25166080 | tf_op jit(solution)/shard_map/while/body/eval_jaxpr/dot_general | solution.py:45
  250.1 0.1 compare_and_fusion.2
  250.2 10.1 %gather_fusion = f32[32,128,512]{2,1,0:T(8,128)} fusion(f32[64,128,512]{2,1,0:T(8,128)} %get-tuple-element.262, s32[1024]{0:T(1024)S(1)} %pad_clamp_fusion.3), kind=kCustom, calls=%fused_computation.clone.clone.1 | custom fusion | bytes 16777344 | tf_op jit(solution)/shard_map/while/body/eval_jaxpr/jit(_take)/gather | solution.py:40
  260.2 10.9 %fusion.34 = f32[32,128,512]{2,1,0:T(8,128)S(1)} fusion(f32[32,128,512]{2,1,0:T(8,128)} %gather_fusion, pred[32]{0:T(512)(128)(4,1)S(1)} %get-tuple-element.233, f32[128,128,128]{2,1,0:T(8,128)} %get-tuple-element.260, s32[]{:T(128)S(6)} %select_n.79), kind=kOutput, calls=%fused_computation.4.clone.1 | convolution fusion | flops 3223322624 | bytes 18874404 | tf_op jit(solution)/shard_map/while/body/eval_jaxpr/tpq,tqf->tpf/dot_general | solution.py:41
  271.2 0.0 copy-start.4
  271.2 8.1 %copy.16 = f32[4,8,128,512]{3,1,2,0:T(8,128)} copy(f32[4,8,128,512]{3,2,1,0:T(8,128)S(1)} %bitcast.33) | data formatting | bytes 16777216 | tf_op jit(solution)/shard_map/while
  279.3 0.1 dynamic_slice.40
  279.3 0.1 dynamic_slice.41
  279.4 13.2 %convolution_add_fusion.3 = f32[32,65536]{1,0:T(8,128)} fusion(f32[32,65536]{1,0:T(8,128)} %bitcast.34, f32[32,65536]{1,0:T(8,128)} %get-tuple-element.246, pred[]{:T(512)S(6)} %compare.5, f32[32]{0:T(128)S(1)} %dynamic_slice.40, s32[32]{0:T(128)S(1)} %dynamic_slice.41), kind=kOutput, calls=%fused_computation.3.clone.1 | convolution fusion | flops 809502720 | bytes 25166080 | tf_op jit(solution)/shard_map/while/body/eval_jaxpr/dot_general | solution.py:45
  292.6 7.5 %reshape.58 = f32[4096,512]{1,0:T(8,128)} reshape(f32[32,65536]{1,0:T(8,128)} %get-tuple-element.144) | data formatting | bytes 16777216 | tf_op jit(solution)/shard_map/reshape | solution.py:53
  300.1 0.0 reduce-scatter.2.cloned.1.call-update
  300.1 51.8 %reduce-scatter.2.cloned.1.call-done = f32[512,512]{1,0:T(8,128)} async-done(((f32[4096,512]{1,0:T(8,128)}), f32[512,512]{1,0:T(8,128)}) %reduce-scatter.2.cloned.1.call-update) | async-done | bytes 1048592 | tf_op jit(solution)/shard_map/reduce_scatter | solution.py:52
  351.9 0.0 copy-done.1
  351.9 5.1 %fusion.14 = bf16[512,512]{1,0:T(8,128)(2,1)} fusion(bf16[2048,512]{1,0:T(8,128)(2,1)S(1)} %copy-done, bf16[512,2048]{1,0:T(8,128)(2,1)} %param.18, f32[2048]{0:T(1024)S(1)} %copy-done.2, f32[512,512]{1,0:T(8,128)} %reduce-scatter.2.cloned.1.call-done, f32[512,512]{1,0:T(8,128)S(1)} %copy-done.1, f32[512]{0:T(512)S(1)} %copy-done.3), kind=kOutput, calls=%fused_computation.22 | convolution fusion | flops 2151940096 | bytes 6825984 | tf_op jit(solution)/shard_map/dot_general | solution.py:59
  (17 shorter events, 0.1 us)
Async XLA Ops:
  6.5 345.4 %copy-start = (bf16[2048,512]{1,0:T(8,128)(2,1)S(1)}, bf16[2048,512]{1,0:T(8,128)(2,1)}, u32[]{:S(2)}) copy-start(bf16[2048,512]{1,0:T(8,128)(2,1)} %param.20) | copy-start | bytes 6291460
  6.5 117.3 %all-gather.2.cloned.1.call-start = ((), (), s32[]{:S(2)}) async-start(), calls=%async_computation.1 | async-start | bytes 17825792 | tf_op jit(solution)/shard_map/all_gather | solution.py:25
  7.3 344.6 %reduce-scatter.2.cloned.1.call-start = ((), (), s32[]{:S(2)}) async-start(), calls=%async_computation.2 | async-start | bytes 9437184 | tf_op jit(solution)/shard_map/reduce_scatter | solution.py:52
  145.0 8.2 %copy-start.4 = (s32[128]{0:T(128)S(1)}, s32[128]{0:T(128)}, u32[]{:S(2)}) copy-start(s32[128]{0:T(128)} %get-tuple-element.258) | copy-start | bytes 1540 | tf_op jit(solution)/shard_map/while
  186.2 8.2 %copy-start.4 = (s32[128]{0:T(128)S(1)}, s32[128]{0:T(128)}, u32[]{:S(2)}) copy-start(s32[128]{0:T(128)} %get-tuple-element.258) | copy-start | bytes 1540 | tf_op jit(solution)/shard_map/while
  228.7 8.2 %copy-start.4 = (s32[128]{0:T(128)S(1)}, s32[128]{0:T(128)}, u32[]{:S(2)}) copy-start(s32[128]{0:T(128)} %get-tuple-element.258) | copy-start | bytes 1540 | tf_op jit(solution)/shard_map/while
  271.2 8.2 %copy-start.4 = (s32[128]{0:T(128)S(1)}, s32[128]{0:T(128)}, u32[]{:S(2)}) copy-start(s32[128]{0:T(128)} %get-tuple-element.258) | copy-start | bytes 1540 | tf_op jit(solution)/shard_map/while
  300.1 51.8 %copy-start.1 = (f32[512,512]{1,0:T(8,128)S(1)}, f32[512,512]{1,0:T(8,128)}, u32[]{:S(2)}) copy-start(f32[512,512]{1,0:T(8,128)} %param.12) | copy-start | bytes 3145732
  300.1 51.8 %copy-start.2 = (f32[2048]{0:T(1024)S(1)}, f32[2048]{0:T(1024)}, u32[]{:S(2)}) copy-start(f32[2048]{0:T(1024)} %param.19) | copy-start | bytes 24580
  300.1 51.8 %copy-start.3 = (f32[512]{0:T(512)S(1)}, f32[512]{0:T(512)}, u32[]{:S(2)}) copy-start(f32[512]{0:T(512)} %param.21) | copy-start | bytes 6148
Sparse Core Ops, SparseCore 0:
  9.5 114.3 all-gather.1
  300.2 51.6 reduce-scatter.1
where the time goes:
time: 364 us
  waiting for transfers between devices  165 us (45%)
  matrix products  100 us (27%)
  local copies, waits for them, and re-layouts  82.8 us (23%)
  between operations  14.1 us (4%)
    all_gather x1, waiting for transfers between devices, on_device(): column_pool = lax.all_gather(own_blocks, 'row', axis=0, tiled=True)  112 us
    reduce_scatter x1, waiting for transfers between devices, on_device(): lax.psum_scatter(partial_value.reshape(row_blocks * tile_edge, width), 'c...  51.8 us
    dot_general x4, matrix products, add_group(): jnp.dot(selector, product.reshape(group, tile_edge * width), precision=pr...  51.4 us
    dot_general x4, matrix products, add_group(): jnp.einsum('tpq,tqf->tpf', group_tiles, inputs, precision=precise_mode)  43.6 us
    gather x4, local copies, waits for them, and re-layouts, add_group(): inputs = jnp.take(column_pool, group_pos, axis=0)  40.3 us
    while x12, local copies, waits for them, and re-layouts  32.4 us
    reshape x1, local copies, waits for them, and re-layouts, on_device(): partial_value.reshape(row_blocks * tile_edge, width)  7.49 us
  transfers between devices with their start and end apart: 2, of which 2 were waited for; matrix products, arithmetic and copies ran while one was open for 1% of the time, Pallas kernels for 0%

commit v1 on v0

v1 whole, which is shorter than its diff:
```python
import jax
import jax.numpy as jnp
from jax import lax
from jax.experimental import pallas as pl
from jax.experimental.pallas import tpu as pltpu
from jax.sharding import PartitionSpec as P

gin_epsilon = 0.25
unroll = 4
span = 256


def add_tiles(count_ref, row_ref, pos_ref, tile_ref, pool_ref, out_ref):
    out_ref[...] = jnp.zeros_like(out_ref)
    count = count_ref[0]

    def turn(step, carry):
        products = []
        for lane in range(unroll):
            slot = step * unroll + lane
            source = pool_ref[pos_ref[slot]].astype(jnp.bfloat16)
            product = jnp.dot(tile_ref[slot], source, preferred_element_type=jnp.float32)
            live = (slot < count).astype(jnp.float32)
            products.append((row_ref[slot], product * live))
        for target, product in products:
            out_ref[target] += product
        return carry

    lax.fori_loop(0, (count + unroll - 1) // unroll, turn, 0)


def aggregate(count, row, pos, tiles, pool, row_blocks):
    tile_total, edge, _ = tiles.shape
    pool_blocks, _, width = pool.shape
    return pl.pallas_call(
        add_tiles,
        grid_spec=pltpu.PrefetchScalarGridSpec(
            num_scalar_prefetch=3,
            grid=(width // span,),
            in_specs=[
                pl.BlockSpec((tile_total, edge, edge), lambda i, *_: (0, 0, 0)),
                pl.BlockSpec((pool_blocks, edge, span), lambda i, *_: (0, 0, i)),
            ],
            out_specs=pl.BlockSpec((row_blocks, edge, span), lambda i, *_: (0, 0, i)),
        ),
        out_shape=jax.ShapeDtypeStruct((row_blocks, edge, width), jnp.float32),
        compiler_params=pltpu.CompilerParams(vmem_limit_bytes=56 << 20),
    )(count, row, pos, tiles, pool)


def on_device(
    features, tiles, tile_rows, tile_cols, tile_count, needed, w_in, bias_in, w_out, bias_out
):
    tile_edge = tiles.shape[-1]
    width = features.shape[1]
    blocks_dev = features.shape[0] // tile_edge
    grid_cols = lax.axis_size("col")
    slot_count = needed.shape[-1]
    row_blocks = grid_cols * blocks_dev
    own_blocks = features.reshape(blocks_dev, tile_edge, width)
    tile_col = tile_cols[0, 0]
    column_pool = lax.all_gather(own_blocks, "row", axis=0, tiled=True)
    position = tile_col // slot_count * blocks_dev + jnp.take(needed[0, 0].reshape(-1), tile_col)
    partial_value = aggregate(
        tile_count[0],
        tile_rows[0, 0],
        position,
        tiles[0, 0].astype(jnp.bfloat16),
        column_pool,
        row_blocks,
    )
    summed = lax.psum_scatter(
        partial_value.reshape(row_blocks * tile_edge, width), "col", scatter_dimension=0, tiled=True
    )
    mixed = ((1.0 + gin_epsilon) * features + summed).astype(jnp.bfloat16)
    hidden = jax.nn.relu(jnp.dot(mixed, w_in, preferred_element_type=jnp.float32) + bias_in).astype(
        jnp.bfloat16
    )
    return (jnp.dot(hidden, w_out, preferred_element_type=jnp.float32) + bias_out).astype(
        jnp.bfloat16
    )


def solution(mesh):
    placed = (
        P(("row", "col"), None),
        P("row", "col", None, None, None),
        P("row", "col", None),
        P("row", "col", None),
        P("row", "col"),
        P("row", "col", None, None),
        P(),
        P(),
        P(),
        P(),
    )
    return jax.shard_map(
        on_device, mesh=mesh, in_specs=placed, out_specs=P(("row", "col"), None), check_vma=False
    )
```

time: 364 us -> 209 us (0.57)
  matrix products: 100 us -> 5.06 us
  local copies, waits for them, and re-layouts: 82.8 us -> 2.08 us
  Pallas kernels: 0 us -> 12.6 us
  other arithmetic: 1.68 us -> 8.16 us
    dot_general x8 -> x0, matrix products: 95 us -> none  [the longest x4 51.4 us: add_group(): jnp.dot(selector, product.reshape(group, tile_edge * width), precision=pr...]
    gather x5 -> x1, local copies, waits for them, and re-layouts: 41.5 us -> 1.22 us  [on_device(): jnp.take(needed[0, 0].reshape(-1), tile_col)]
    while x12 -> x0, local copies, waits for them, and re-layouts: 32.4 us -> none
    pallas_call x0 -> x1, Pallas kernels: none -> 12.6 us  [aggregate(): pl.pallas_call(add_tiles, grid_spec=pltpu.PrefetchScalarGridSpec(num_scal...]
    reduce_scatter x1, waiting for transfers between devices: 51.8 us -> 61 us  [on_device(): lax.psum_scatter(partial_value.reshape(row_blocks * tile_edge, width), 'c...]
    reshape x1 -> x0, local copies, waits for them, and re-layouts: 7.49 us -> none  [on_device(): partial_value.reshape(row_blocks * tile_edge, width)]
    all_gather x1, waiting for transfers between devices: 112 us -> 106 us  [on_device(): column_pool = lax.all_gather(own_blocks, 'row', axis=0, tiled=True)]
    convert_element_type x1, other arithmetic: 0.01 us -> 6.34 us  [on_device(): tiles[0, 0].astype(jnp.bfloat16)]
  transfers between devices with their start and end apart: 2 -> 2, of which waited for: 2 -> 2; matrix products, arithmetic and copies ran while one was open for 1% -> 5% of each run, Pallas kernels for 0% -> 0%
where the time goes in v1:
time: 209 us
  waiting for transfers between devices  167 us (80%)
  between operations  14.1 us (7%)
  Pallas kernels  12.6 us (6%)
  other arithmetic  8.16 us (4%)
  matrix products  5.06 us (2%)
    all_gather x1, waiting for transfers between devices, on_device(): column_pool = lax.all_gather(own_blocks, 'row', axis=0, tiled=True)  106 us
    reduce_scatter x1, waiting for transfers between devices, on_device(): lax.psum_scatter(partial_value.reshape(row_blocks * tile_edge, width), 'c...  61 us
    pallas_call x1, Pallas kernels, aggregate(): pl.pallas_call(add_tiles, grid_spec=pltpu.PrefetchScalarGridSpec(num_scal...  12.6 us
    convert_element_type x1, other arithmetic, on_device(): tiles[0, 0].astype(jnp.bfloat16)  6.34 us
    dot_general x1, matrix products, on_device(): jnp.dot(hidden, w_out, preferred_element_type=jnp.float32) + bias_out  5.06 us
  transfers between devices with their start and end apart: 2, of which 2 were waited for; matrix products, arithmetic and copies ran while one was open for 5% of the time, Pallas kernels for 0%

profile of v1, /device:TPU:1, one launch (start us, length us, event | category | flops | bytes accessed | tf_op | source)
XLA Modules:
  0.0 209.4 jit_solution(613955594002221310)
XLA Ops:
  6.5 0.0 copy-start
  6.5 0.0 all-gather.2.cloned.1.call-start
  6.5 0.7 all-gather.2.cloned.1.call-update
  7.3 0.0 reduce-scatter.2.cloned.1.call-start
  8.0 0.8 copy.13
  8.7 0.1 reshape_squeeze.3
  8.8 0.7 fusion.4
  9.5 1.2 gather_fusion
  10.7 1.1 fusion.3.pos_ref
  11.8 6.3 %convert_bitcast_fusion.tile_ref = bf16[128,128,128]{2,1,0:T(8,128)(2,1)} fusion(f32[1,1,128,128,128]{4,3,2,1,0:T(8,128)} %param.11), kind=kLoop, calls=%fused_computation.2 | loop fusion | flops 2097152 | bytes 12582912 | tf_op jit(solution)/shard_map/convert_element_type | solution.py:68
  18.2 105.7 %all-gather.2.cloned.1.call-done.pool_ref = f32[64,128,512]{2,1,0:T(8,128)} async-done(((f32[4,128,512]{2,1,0:T(8,128)}), f32[64,128,512]{2,1,0:T(8,128)}) %all-gather.2.cloned.1.call-update) | async-done | bytes 16777232 | tf_op jit(solution)/shard_map/all_gather | solution.py:62
  123.9 12.6 %shard_map.100 = f32[32,128,512]{2,1,0:T(8,128)} custom-call(s32[1]{0:T(128)} %bitcast.25.count_ref, s32[128]{0:T(128)} %bitcast.28, s32[128]{0:T(128)} %fusion.3.pos_ref, bf16[128,128,128]{2,1,0:T(8,128)(2,1)} %convert_bitcast_fusion.tile_ref, f32[64,128,512]{2,1,0:T(8,128)} %all-gather.2.cloned.1.call-done.pool_ref), custom_call_target="tpu_custom_call" | custom-call | tf_op jit(solution)/shard_map/pallas_call | solution.py:35
  136.5 0.0 copy-start.1
  136.5 0.0 copy-start.2
  136.5 0.0 copy-start.3
  136.5 0.0 reduce-scatter.2.cloned.1.call-update
  136.5 61.0 %reduce-scatter.2.cloned.1.call-done = f32[512,512]{1,0:T(8,128)} async-done(((f32[4096,512]{1,0:T(8,128)}), f32[512,512]{1,0:T(8,128)}) %reduce-scatter.2.cloned.1.call-update) | async-done | bytes 1048592 | tf_op jit(solution)/shard_map/reduce_scatter | solution.py:72
  197.5 0.0 copy-done
  197.5 0.0 copy-done.1
  197.5 0.0 copy-done.2
  197.5 0.0 copy-done.3
  197.5 5.1 %fusion = bf16[512,512]{1,0:T(8,128)(2,1)} fusion(bf16[2048,512]{1,0:T(8,128)(2,1)S(1)} %copy-done, bf16[512,2048]{1,0:T(8,128)(2,1)} %param.16, f32[2048]{0:T(1024)S(1)} %copy-done.2, f32[512,512]{1,0:T(8,128)} %reduce-scatter.2.cloned.1.call-done, f32[512,512]{1,0:T(8,128)S(1)} %copy-done.1, f32[512]{0:T(512)S(1)} %copy-done.3), kind=kOutput, calls=%fused_computation.4 | convolution fusion | flops 2151940096 | bytes 6825984 | tf_op jit(solution)/shard_map/dot_general | solution.py:79
  (1 shorter events, 0.0 us)
Async XLA Ops:
  6.5 190.9 %copy-start = (bf16[2048,512]{1,0:T(8,128)(2,1)S(1)}, bf16[2048,512]{1,0:T(8,128)(2,1)}, u32[]{:S(2)}) copy-start(bf16[2048,512]{1,0:T(8,128)(2,1)} %param.18) | copy-start | bytes 6291460
  6.5 117.3 %all-gather.2.cloned.1.call-start = ((), (), s32[]{:S(2)}) async-start(), calls=%async_computation.1 | async-start | bytes 17825792 | tf_op jit(solution)/shard_map/all_gather | solution.py:62
  7.3 190.2 %reduce-scatter.2.cloned.1.call-start = ((), (), s32[]{:S(2)}) async-start(), calls=%async_computation.2 | async-start | bytes 9437184 | tf_op jit(solution)/shard_map/reduce_scatter | solution.py:72
  136.5 61.0 %copy-start.1 = (f32[512,512]{1,0:T(8,128)S(1)}, f32[512,512]{1,0:T(8,128)}, u32[]{:S(2)}) copy-start(f32[512,512]{1,0:T(8,128)} %param.10) | copy-start | bytes 3145732
  136.5 61.0 %copy-start.2 = (f32[2048]{0:T(1024)S(1)}, f32[2048]{0:T(1024)}, u32[]{:S(2)}) copy-start(f32[2048]{0:T(1024)} %param.17) | copy-start | bytes 24580
  136.5 61.0 %copy-start.3 = (f32[512]{0:T(512)S(1)}, f32[512]{0:T(512)}, u32[]{:S(2)}) copy-start(f32[512]{0:T(512)} %param.19) | copy-start | bytes 6148
Sparse Core Ops, SparseCore 0:
  9.5 114.3 all-gather.1
  136.6 60.7 reduce-scatter.1

commit v2 on v1

v2 whole, which is shorter than its diff:
```python
import jax
import jax.numpy as jnp
from jax import lax
from jax.experimental import pallas as pl
from jax.experimental.pallas import tpu as pltpu
from jax.sharding import PartitionSpec as P


gin_epsilon = 0.25
unroll = 8
span = 256
side = 4
cores = 2
picks = 2
note_rows = 8
lanes = 128
chunk = 512

in_vmem = pl.BlockSpec(memory_space=pltpu.VMEM)
in_smem = pl.BlockSpec(memory_space=pltpu.SMEM)


def row_shift(step_z, step_y):
    return [
        (z * side + y, (z + step_z) % side * side + (y + step_y) % side)
        for z in range(side)
        for y in range(side)
    ]


def col_shift(step_x, step_core):
    return [
        (x * cores + k, (x + step_x) % side * cores + (k + step_core) % cores)
        for x in range(side)
        for k in range(cores)
    ]


def from_z(value, step):
    return lax.ppermute(value, "row", row_shift(-step, 0))


def from_y(value, step):
    return lax.ppermute(value, "row", row_shift(0, -step))


def back(step):
    return (side - step) % side


def half_at(number, half):
    return pl.ds(pl.multiple_of(number * half, half), half)


def spot_of(d, j, half):
    return slice((d * picks + j) * half, (d * picks + j + 1) * half)


def split(feature_ref, need_ref, *outs):
    half = lanes // 2
    rows = feature_ref.shape[0] // 2
    need = need_ref[...].astype(jnp.float32)
    for group in range(len(outs) // 2):
        part = slice(group * span, (group + 1) * span)
        for place, out in enumerate(outs[2 * group : 2 * group + 2]):
            for block in range(rows // half):
                start = (2 * block + place) * half
                out[block * half : (block + 1) * half, :] = feature_ref[start : start + half, part]
            if group == 0:
                out[rows:, :] = jnp.zeros((note_rows, span), jnp.float32)
                out[rows : rows + need.shape[0], : need.shape[1]] = need


def plan(row_ref, col_ref, count_ref, plan_ref, blocks_dev, entries):
    my_z = lax.axis_index("row") // side
    my_y = lax.axis_index("row") % side
    my_x = lax.axis_index("col") // cores
    my_core = lax.axis_index("col") % cores

    def write(at, slot, row, pos):
        plan_ref[at] = slot
        plan_ref[at + entries] = row
        plan_ref[at + 2 * entries] = pos

    def turn(slot, ends):
        target = row_ref[slot]
        column = target // blocks_dev
        row = lax.rem(column // cores - my_x + side, side) * blocks_dev + target % blocks_dev
        other = (column % cores != my_core).astype(jnp.int32)
        owner = col_ref[slot] // picks
        away_z = lax.rem(owner // side - my_z + side, side)
        away_y = lax.rem(owner % side - my_y + side, side)
        pos = (away_z * side + away_y) * picks + col_ref[slot] % picks
        for which, end in enumerate(ends):
            write(which * 3 * entries + end, slot, row, pos)
        return ends[0] + other, ends[1] + 1 - other

    ends = lax.fori_loop(0, count_ref[0, 0], turn, (0, 0))
    for which, end in enumerate(ends):
        plan_ref[6 * entries + which] = end
        for extra in range(unroll):
            write(which * 3 * entries + end + extra, 0, 0, 0)


def pack(half, *refs):
    first, second = refs[:side], refs[side : 2 * side]
    notes_from = refs[2 * side : 4 * side - 2]
    outs = refs[4 * side - 2 : 6 * side - 4]
    notes, sems = refs[6 * side - 4 :]
    rows = side * half
    copies = [
        pltpu.make_async_copy(
            source.at[rows : rows + note_rows, :lanes], notes.at[at], sems.at[at]
        )
        for at, source in enumerate(notes_from)
    ]
    for copy in copies:
        copy.start()
    for copy in copies:
        copy.wait()
    my_z = lax.axis_index("row") // side
    my_y = lax.axis_index("row") % side
    for away in range(1, side):
        for d in range(side):
            next_y = lax.rem(my_y + d, side)
            next_z = lax.rem(my_z + d, side)
            for j in range(picks):
                spot = spot_of(d, j, half)
                along_z = notes[away - 1, j, my_z * side + next_y].astype(jnp.int32)
                outs[away - 1][spot, :] = first[d][half_at(along_z, half), :]
                along_y = notes[side + away - 2, j, next_z * side + my_y].astype(jnp.int32)
                outs[side + away - 2][spot, :] = second[d][half_at(along_y, half), :]


def pack_group(first, second, notes, half):
    packed = jax.ShapeDtypeStruct((side * picks * half, span), jnp.float32)
    number = 2 * (side - 1)
    return pl.pallas_call(
        lambda *refs: pack(half, *refs),
        in_specs=[in_vmem] * (2 * side + number),
        out_specs=[in_vmem] * number,
        scratch_shapes=[
            pltpu.SMEM((number, note_rows, lanes), jnp.float32),
            pltpu.SemaphoreType.DMA((number,)),
        ],
        out_shape=[packed] * number,
        compiler_params=pltpu.CompilerParams(vmem_limit_bytes=16 << 20),
        cost_estimate=pl.CostEstimate(flops=0, bytes_accessed=5 << 20, transcendentals=0),
        name="pack",
    )(*first, *second, *notes)


def add_tiles(which, plan_ref, tile_ref, pool, total):
    entries = tile_ref.shape[0] + unroll
    base = which * 3 * entries
    total[...] = jnp.zeros_like(total)
    count = plan_ref[6 * entries + which]

    def turn(step, carry):
        products = []
        for lane in range(unroll):
            at = base + step * unroll + lane
            product = jnp.dot(
                tile_ref[plan_ref[at]],
                pool[plan_ref[at + 2 * entries]],
                preferred_element_type=jnp.float32,
            )
            live = (step * unroll + lane < count).astype(jnp.float32)
            products.append((plan_ref[at + entries], product * live))
        for target, product in products:
            total[target] += product
        return carry

    lax.fori_loop(0, (count + unroll - 1) // unroll, turn, 0)


def combine(plan_ref, need_ref, tile_ref, *refs):
    first, second = refs[:side], refs[side : 2 * side]
    along_z = refs[2 * side : 3 * side - 1]
    along_y = refs[3 * side - 1 : 4 * side - 2]
    total, pool = refs[4 * side - 2 :]
    half = pool.shape[1] // 2
    top, low = slice(0, half), slice(half, 2 * half)
    my_z = lax.axis_index("row") // side
    my_y = lax.axis_index("row") % side
    for d in range(side):
        next_y = lax.rem(my_y + d, side)
        next_z = lax.rem(my_z + d, side)
        for j in range(picks):
            mine = need_ref[j, my_z * side + next_y]
            pool[d * picks + j, top, :] = first[d][half_at(mine, half), :].astype(pool.dtype)
            mine = need_ref[j, next_z * side + my_y]
            pool[d * side * picks + j, low, :] = second[d][half_at(mine, half), :].astype(
                pool.dtype
            )
            spot = spot_of(d, j, half)
            for away in range(1, side):
                pool[(back(away) * side + d) * picks + j, top, :] = along_z[away - 1][
                    spot, :
                ].astype(pool.dtype)
                pool[(d * side + back(away)) * picks + j, low, :] = along_y[away - 1][
                    spot, :
                ].astype(pool.dtype)
    add_tiles(0, plan_ref, tile_ref, pool, total)


def combine_sent(listed, need, tiles, first, second, along_z, along_y, blocks):
    edge = tiles.shape[1]
    return pl.pallas_call(
        combine,
        in_specs=[in_smem] * 2 + [in_vmem] * (4 * side - 1),
        out_specs=[in_vmem] * 2,
        out_shape=[
            jax.ShapeDtypeStruct((blocks, edge, span), jnp.float32),
            jax.ShapeDtypeStruct((side * side * picks, edge, span), jnp.bfloat16),
        ],
        compiler_params=pltpu.CompilerParams(vmem_limit_bytes=24 << 20),
        cost_estimate=pl.CostEstimate(flops=2 << 30, bytes_accessed=10 << 20, transcendentals=0),
        name="combine",
    )(listed, need, tiles, *first, *second, *along_z, *along_y)


def combine_kept(listed, tiles, pool, blocks):
    edge = tiles.shape[1]
    return pl.pallas_call(
        lambda plan_ref, tile_ref, pool, total: add_tiles(1, plan_ref, tile_ref, pool, total),
        in_specs=[in_smem] + [in_vmem] * 2,
        out_specs=in_vmem,
        out_shape=jax.ShapeDtypeStruct((blocks, edge, span), jnp.float32),
        compiler_params=pltpu.CompilerParams(vmem_limit_bytes=24 << 20),
        cost_estimate=pl.CostEstimate(flops=2 << 30, bytes_accessed=8 << 20, transcendentals=0),
        name="keep",
    )(listed, tiles, pool)


def mixed_of(group, feature_ref, totals):
    part = slice(group * span, (group + 1) * span)
    summed = totals[0][...]
    for other in totals[1:]:
        summed = summed + other[...]
    return ((1.0 + gin_epsilon) * feature_ref[:, part] + summed).astype(jnp.bfloat16)


def begin_mlp(feature_ref, w_ref, bias_ref, *refs):
    totals, out_ref, mixed = refs[:side], refs[side], refs[side + 1]
    mixed[...] = mixed_of(0, feature_ref, totals)

    def turn(step, carry):
        part = pl.ds(pl.multiple_of(step * chunk, chunk), chunk)
        out_ref[:, part] = (
            jnp.dot(mixed[...], w_ref[:span, part], preferred_element_type=jnp.float32)
            + bias_ref[:, part]
        )
        return carry

    lax.fori_loop(0, w_ref.shape[1] // chunk, turn, 0)


def end_mlp(feature_ref, w_ref, before_ref, w_out_ref, bias_ref, *refs):
    totals, out_ref, mixed, total = refs[:side], refs[side], refs[side + 1], refs[side + 2]
    mixed[...] = mixed_of(1, feature_ref, totals)
    total[...] = jnp.broadcast_to(bias_ref[...], total.shape)

    def turn(step, carry):
        part = pl.ds(pl.multiple_of(step * chunk, chunk), chunk)
        hidden = before_ref[:, part] + jnp.dot(
            mixed[...], w_ref[span:, part], preferred_element_type=jnp.float32
        )
        hidden = jnp.maximum(hidden, 0.0).astype(jnp.bfloat16)
        total[...] += jnp.dot(hidden, w_out_ref[part, :], preferred_element_type=jnp.float32)
        return carry

    lax.fori_loop(0, w_ref.shape[1] // chunk, turn, 0)
    out_ref[...] = total[...].astype(out_ref.dtype)


def on_device(
    features, tiles, tile_rows, tile_cols, tile_count, needed, w_in, bias_in, w_out, bias_out
):
    tile_total, edge = tiles.shape[2], tiles.shape[-1]
    half = edge // 2
    nodes, width = features.shape
    blocks_dev = nodes // edge
    hidden_size = w_in.shape[1]
    blocks = side * blocks_dev
    groups = width // span
    rows = nodes // 2

    need = needed[0, 0].T
    payload = [
        jax.ShapeDtypeStruct((rows + (note_rows if group == 0 else 0), span), jnp.float32)
        for group in range(groups)
        for _ in range(2)
    ]
    own = pl.pallas_call(
        split,
        in_specs=[in_vmem] * 2,
        out_specs=[in_vmem] * len(payload),
        out_shape=payload,
        compiler_params=pltpu.CompilerParams(vmem_limit_bytes=8 << 20),
        cost_estimate=pl.CostEstimate(flops=0, bytes_accessed=2 << 20, transcendentals=0),
        name="split",
    )(features, need)
    firsts, seconds = [], []
    for group in range(groups):
        first = [own[2 * group]] + [None] * (side - 1)
        second = [own[2 * group + 1]] + [None] * (side - 1)
        for away in (1, 3, 2):
            first[away] = from_y(first[0], away)
            second[away] = from_z(second[0], away)
        firsts.append(first)
        seconds.append(second)
    notes = seconds[0][1:] + firsts[0][1:]

    entries = tile_total + unroll
    listed = pl.pallas_call(
        lambda *refs: plan(*refs, blocks_dev, entries),
        in_specs=[in_smem] * 3,
        out_specs=in_smem,
        out_shape=jax.ShapeDtypeStruct((1024,), jnp.int32),
        cost_estimate=pl.CostEstimate(flops=0, bytes_accessed=1 << 20, transcendentals=0),
        name="plan",
    )(tile_rows[0, 0], tile_cols[0, 0], tile_count)
    tiles_low = tiles[0, 0].astype(jnp.bfloat16)

    sums = []
    for group in range(groups):
        first, second = firsts[group], seconds[group]
        packed = pack_group(first, second, notes, half)
        along_z, along_y = [None] * (side - 1), [None] * (side - 1)
        for away in (1, 3, 2):
            along_z[away - 1] = from_z(packed[away - 1], -away)
            along_y[away - 1] = from_y(packed[side + away - 2], -away)
        send, pool = combine_sent(listed, need, tiles_low, first, second, along_z, along_y, blocks)
        arrived = lax.ppermute(send, "col", col_shift(0, 1))
        keep = combine_kept(listed, tiles_low, pool, blocks)
        parts = [
            (
                keep[k * blocks_dev : (k + 1) * blocks_dev]
                + arrived[k * blocks_dev : (k + 1) * blocks_dev]
            ).reshape(nodes, span)
            for k in range(side)
        ]
        total = [parts[0]]
        for k in (1, 3, 2):
            total.append(lax.ppermute(parts[k], "col", col_shift(k, 0)))
        sums.append(total)

    before = pl.pallas_call(
        begin_mlp,
        in_specs=[in_vmem] * (3 + side),
        out_specs=in_vmem,
        out_shape=jax.ShapeDtypeStruct((nodes, hidden_size), jnp.float32),
        scratch_shapes=[pltpu.VMEM((nodes, span), jnp.bfloat16)],
        compiler_params=pltpu.CompilerParams(vmem_limit_bytes=24 << 20),
        cost_estimate=pl.CostEstimate(
            flops=1 << 29, bytes_accessed=8 << 20, transcendentals=0
        ),
        name="begin",
    )(features, w_in, bias_in.reshape(1, -1), *sums[0])
    return pl.pallas_call(
        end_mlp,
        in_specs=[in_vmem] * (5 + side),
        out_specs=in_vmem,
        out_shape=jax.ShapeDtypeStruct((nodes, width), jnp.bfloat16),
        scratch_shapes=[
            pltpu.VMEM((nodes, span), jnp.bfloat16),
            pltpu.VMEM((nodes, width), jnp.float32),
        ],
        compiler_params=pltpu.CompilerParams(vmem_limit_bytes=24 << 20),
        cost_estimate=pl.CostEstimate(
            flops=3 << 29, bytes_accessed=8 << 20, transcendentals=0
        ),
        name="end",
    )(features, w_in, before, w_out, bias_out.reshape(1, -1), *sums[1])


def solution(mesh):
    placed = (
        P(("row", "col"), None),
        P("row", "col", None, None, None),
        P("row", "col", None),
        P("row", "col", None),
        P("row", "col"),
        P("row", "col", None, None),
        P(),
        P(),
        P(),
        P(),
    )

    return jax.shard_map(
        on_device, mesh=mesh, in_specs=placed, out_specs=P(("row", "col"), None), check_vma=False
    )
```

time: 209 us -> 184 us (0.88); the launches traced: 209 us -> 181 us
  waiting for transfers between devices: 167 us -> 82.1 us
  starting transfers between devices: 0.04 us -> 56.8 us
  local copies, waits for them, and re-layouts: 2.08 us -> 16.7 us
  between operations: 14.1 us -> 0.89 us
  Pallas kernels: 12.6 us -> 20.7 us
  matrix products: 5.06 us -> 0 us
  other arithmetic: 8.16 us -> 3.53 us
    all_gather x1 -> x0, waiting for transfers between devices: 106 us -> none  [on_device(): column_pool = lax.all_gather(own_blocks, 'row', axis=0, tiled=True)]
    ppermute x0 -> x32, waiting for transfers between devices: none -> 82.1 us  [the longest x6 38.3 us: on_device(): total.append(lax.ppermute(parts[k], 'col', col_shift(k, 0)))]
    reduce_scatter x1 -> x0, waiting for transfers between devices: 61 us -> none  [on_device(): lax.psum_scatter(partial_value.reshape(row_blocks * tile_edge, width), 'c...]
    ppermute x0 -> x32, starting transfers between devices: none -> 56.8 us  [the longest x12 30 us: from_y(): return lax.ppermute(value, 'row', row_shift(0, -step))]
    unnamed x9 -> x64, local copies, waits for them, and re-layouts: 0.77 us -> 16.7 us
    pallas_call x1 -> x10, Pallas kernels: 12.6 us -> 20.7 us  [the longest x2 5.36 us: combine_sent(): pl.pallas_call(combine, in_specs=[in_smem] * 2 + [in_vmem] * (4 * side -...]
    dot_general x1 -> x0, matrix products: 5.06 us -> none  [on_device(): jnp.dot(hidden, w_out, preferred_element_type=jnp.float32) + bias_out]
    convert_element_type x1, other arithmetic: 6.34 us -> 2.98 us  [on_device(): tiles_low = tiles[0, 0].astype(jnp.bfloat16)]
  transfers between devices with their start and end apart: 2 -> 32, of which waited for: 2 -> 16; matrix products, arithmetic and copies ran while one was open for 5% -> 2% of each run, Pallas kernels for 0% -> 8%
where the time goes in v2:
time: 184 us; the launch traced here: 181 us
  waiting for transfers between devices  82.1 us (45%)
  starting transfers between devices  56.8 us (31%)
  Pallas kernels  20.7 us (11%)
  local copies, waits for them, and re-layouts  16.7 us (9%)
  other arithmetic  3.53 us (2%)
    ppermute x6, waiting for transfers between devices, on_device(): total.append(lax.ppermute(parts[k], 'col', col_shift(k, 0)))  38.3 us
    ppermute x12, waiting for transfers between devices, from_y(): return lax.ppermute(value, 'row', row_shift(0, -step))  36.7 us
    ppermute x12, starting transfers between devices, from_y(): return lax.ppermute(value, 'row', row_shift(0, -step))  30 us
    unnamed x64, local copies, waits for them, and re-layouts  16.7 us
    ppermute x12, starting transfers between devices, from_z(): return lax.ppermute(value, 'row', row_shift(-step, 0))  14.8 us
    ppermute x6, starting transfers between devices, on_device(): total.append(lax.ppermute(parts[k], 'col', col_shift(k, 0)))  8.43 us
    ppermute x12, waiting for transfers between devices, from_z(): return lax.ppermute(value, 'row', row_shift(-step, 0))  7.21 us
    pallas_call x2, Pallas kernels, combine_sent(): pl.pallas_call(combine, in_specs=[in_smem] * 2 + [in_vmem] * (4 * side -...  5.36 us
  transfers between devices with their start and end apart: 32, of which 16 were waited for; matrix products, arithmetic and copies ran while one was open for 2% of the time, Pallas kernels for 8%

profile of v2, /device:TPU:1, one launch (start us, length us, event | category | flops | bytes accessed | tf_op | source)
XLA Modules:
  0.0 180.7 jit_solution(2167545120776008619)
XLA Ops:
  0.0 1.2 copy-done.2
  2.0 3.6 %collective-permute-start.16 = (f32[256,256]{1,0:T(8,128)S(1)}, f32[256,256]{1,0:T(8,128)S(1)}, u32[]{:S(2)}, u32[]{:S(2)}) collective-permute-start(f32[256,256]{1,0:T(8,128)S(1)} %get-tuple-element.35.refs_0_), channel_id=1, source_target_pairs={{0,24},{8,0},{16,8},{24,16},{32,56},{40,32},{48,40},{56,48},{64,88... | collective-permute-start | bytes 786440 | tf_op jit(solution)/shard_map/ppermute | solution.py:44
  7.4 3.8 %collective-permute-start.19 = (f32[256,256]{1,0:T(8,128)S(1)}, f32[256,256]{1,0:T(8,128)S(1)}, u32[]{:S(2)}, u32[]{:S(2)}) collective-permute-start(f32[256,256]{1,0:T(8,128)S(1)} %get-tuple-element.36.refs_4_), channel_id=1, source_target_pairs={{0,96},{8,104},{16,112},{24,120},{32,0},{40,8},{48,16},{56,24},{64... | collective-permute-start | bytes 786440 | tf_op jit(solution)/shard_map/ppermute | solution.py:40
  11.2 3.9 %collective-permute-done.16.refs_1_ = f32[256,256]{1,0:T(8,128)S(1)} collective-permute-done((f32[256,256]{1,0:T(8,128)S(1)}, f32[256,256]{1,0:T(8,128)S(1)}, u32[]{:S(2)}, u32[]{:S(2)}) %collective-permute-start.16) | collective-permute-done | bytes 262176 | tf_op jit(solution)/shard_map/ppermute | solution.py:44
  15.9 5.0 %collective-permute-done.18.refs_3_ = f32[256,256]{1,0:T(8,128)S(1)} collective-permute-done((f32[256,256]{1,0:T(8,128)S(1)}, f32[256,256]{1,0:T(8,128)S(1)}, u32[]{:S(2)}, u32[]{:S(2)}) %collective-permute-start.18) | collective-permute-done | bytes 262176 | tf_op jit(solution)/shard_map/ppermute | solution.py:44
  21.3 2.5 %collective-permute-start.2 = (f32[264,256]{1,0:T(8,128)S(1)}, f32[264,256]{1,0:T(8,128)S(1)}, u32[]{:S(2)}, u32[]{:S(2)}) collective-permute-start(f32[264,256]{1,0:T(8,128)S(1)} %get-tuple-element.25.refs_0_), channel_id=1, source_target_pairs={{0,8},{8,16},{16,24},{24,0},{32,40},{40,48},{48,56},{56,32},{64,72... | collective-permute-start | bytes 811016 | tf_op jit(solution)/shard_map/ppermute | solution.py:44
  23.8 1.9 %collective-permute-start.3 = (f32[264,256]{1,0:T(8,128)S(1)}, f32[264,256]{1,0:T(8,128)S(1)}, u32[]{:S(2)}, u32[]{:S(2)}) collective-permute-start(f32[264,256]{1,0:T(8,128)S(1)} %get-tuple-element.26.refs_4_), channel_id=1, source_target_pairs={{0,96},{8,104},{16,112},{24,120},{32,0},{40,8},{48,16},{56,24},{64... | collective-permute-start | bytes 811016 | tf_op jit(solution)/shard_map/ppermute | solution.py:40
  25.7 1.1 collective-permute-start.5
  27.9 8.4 %collective-permute-done.2.refs_3_.refs_13_ = f32[264,256]{1,0:T(8,128)S(1)} collective-permute-done((f32[264,256]{1,0:T(8,128)S(1)}, f32[264,256]{1,0:T(8,128)S(1)}, u32[]{:S(2)}, u32[]{:S(2)}) %collective-permute-start.2) | collective-permute-done | bytes 270368 | tf_op jit(solution)/shard_map/ppermute | solution.py:44
  36.3 2.7 %pack.3 = (f32[512,256]{1,0:T(8,128)S(1)}, f32[512,256]{1,0:T(8,128)}, f32[512,256]{1,0:T(8,128)}, f32[512,256]{1,0:T(8,128)}, f32[512,256]{1,0:T(8,128)}, /*index=5*/f32[512,256]{1,0:T(8,128)}) custom-call(f32[256,256]{1,0:T(8,128)S(1)} %get-tuple-element.35.refs_0_, f32[256,256]{1,0:T(8,128)S(1)} %collective-permute-done.16.refs_1_, ...), custom_call_target="tpu_custom_call" | custom-call | bytes 5242880 | tf_op jit(solution)/shard_map/pack/pallas_call | solution.py:138
  39.1 2.0 %collective-permute-start.22 = (f32[512,256]{1,0:T(8,128)S(1)}, f32[512,256]{1,0:T(8,128)S(1)}, u32[]{:S(2)}, u32[]{:S(2)}) collective-permute-start(f32[512,256]{1,0:T(8,128)S(1)} %get-tuple-element.37), channel_id=1, source_target_pairs={{0,32},{8,40},{16,48},{24,56},{32,64},{40,72},{48,80},{56,88},{64,... | collective-permute-start | bytes 1572872 | tf_op jit(solution)/shard_map/ppermute | solution.py:40
  41.1 1.2 pack.2
  42.4 6.0 %collective-permute-start.10 = (f32[512,256]{1,0:T(8,128)S(1)}, f32[512,256]{1,0:T(8,128)S(1)}, u32[]{:S(2)}, u32[]{:S(2)}) collective-permute-start(f32[512,256]{1,0:T(8,128)S(1)} %get-tuple-element.31), channel_id=1, source_target_pairs={{0,16},{8,24},{16,0},{24,8},{32,48},{40,56},{48,32},{56,40},{64,80... | collective-permute-start | bytes 1572872 | tf_op jit(solution)/shard_map/ppermute | solution.py:44
  48.3 4.7 %collective-permute-start.11 = (f32[512,256]{1,0:T(8,128)S(1)}, f32[512,256]{1,0:T(8,128)S(1)}, u32[]{:S(2)}, u32[]{:S(2)}) collective-permute-start(f32[512,256]{1,0:T(8,128)S(1)} %get-tuple-element.32), channel_id=1, source_target_pairs={{0,24},{8,0},{16,8},{24,16},{32,56},{40,32},{48,40},{56,48},{64,88... | collective-permute-start | bytes 1572872 | tf_op jit(solution)/shard_map/ppermute | solution.py:44
  54.2 1.9 %collective-permute-start.6 = (f32[512,256]{1,0:T(8,128)S(1)}, f32[512,256]{1,0:T(8,128)S(1)}, u32[]{:S(2)}, u32[]{:S(2)}) collective-permute-start(f32[512,256]{1,0:T(8,128)S(1)} %get-tuple-element.27), channel_id=1, source_target_pairs={{0,32},{8,40},{16,48},{24,56},{32,64},{40,72},{48,80},{56,88},{64,... | collective-permute-start | bytes 1572872 | tf_op jit(solution)/shard_map/ppermute | solution.py:40
  56.9 1.3 collective-permute-start.7
  59.0 1.4 collective-permute-start.8
  60.4 15.3 %collective-permute-done.11.refs_13_ = f32[512,256]{1,0:T(8,128)S(1)} collective-permute-done((f32[512,256]{1,0:T(8,128)S(1)}, f32[512,256]{1,0:T(8,128)S(1)}, u32[]{:S(2)}, u32[]{:S(2)}) %collective-permute-start.11) | collective-permute-done | bytes 524320 | tf_op jit(solution)/shard_map/ppermute | solution.py:44
  76.5 1.4 collective-permute-start.9
  77.9 3.0 %convert_bitcast_fusion.tile_ref = bf16[128,128,128]{2,1,0:T(8,128)(2,1)} fusion(f32[1,1,128,128,128]{4,3,2,1,0:T(8,128)S(1)} %copy-done.31), kind=kLoop, calls=%fused_computation | loop fusion | flops 2097152 | bytes 12582912 | tf_op jit(solution)/shard_map/convert_element_type | solution.py:324
  80.9 2.7 %collective-permute-done.6.refs_8_ = f32[512,256]{1,0:T(8,128)S(1)} collective-permute-done((f32[512,256]{1,0:T(8,128)S(1)}, f32[512,256]{1,0:T(8,128)S(1)}, u32[]{:S(2)}, u32[]{:S(2)}) %collective-permute-start.6) | collective-permute-done | bytes 524320 | tf_op jit(solution)/shard_map/ppermute | solution.py:40
  84.4 4.3 %collective-permute-done.7.refs_9_ = f32[512,256]{1,0:T(8,128)S(1)} collective-permute-done((f32[512,256]{1,0:T(8,128)S(1)}, f32[512,256]{1,0:T(8,128)S(1)}, u32[]{:S(2)}, u32[]{:S(2)}) %collective-permute-start.7) | collective-permute-done | bytes 524320 | tf_op jit(solution)/shard_map/ppermute | solution.py:40
  89.6 7.3 %collective-permute-start.25 = (f32[512,256]{1,0:T(8,128)}, f32[512,256]{1,0:T(8,128)}, u32[]{:S(2)}, u32[]{:S(2)}) collective-permute-start(f32[512,256]{1,0:T(8,128)} %get-tuple-element.40), channel_id=1, source_target_pairs={{0,8},{8,16},{16,24},{24,0},{32,40},{40,48},{48,56},{56,32},{64,72... | collective-permute-start | bytes 1572872 | tf_op jit(solution)/shard_map/ppermute | solution.py:44
  97.7 1.1 collective-permute-start.26
  99.6 1.3 collective-permute-start.27
  100.9 3.2 %plan.1.plan_ref = s32[1024]{0:T(1024)} custom-call(s32[128]{0:T(128)} %bitcast.30, s32[128]{0:T(128)} %bitcast.31, s32[1,1]{1,0:T(1,128)S(6)} %copy.11.refs_2_), custom_call_target="tpu_custom_call" | custom-call | bytes 1048576 | tf_op jit(solution)/shard_map/plan/pallas_call | solution.py:316
  104.1 2.2 %copy-done = bf16[128,128,128]{2,1,0:T(8,128)(2,1)S(1)} copy-done((bf16[128,128,128]{2,1,0:T(8,128)(2,1)S(1)}, bf16[128,128,128]{2,1,0:T(8,128)(2,1)}, u32[]{:S(2)}) %copy-start) | copy-done | bytes 4194328
  106.3 1.0 copy-done.15
  107.4 1.0 copy-done.17
  113.3 2.1 %combine.2 = (f32[16,128,256]{2,1,0:T(8,128)S(1)}, bf16[32,128,256]{2,1,0:T(8,128)(2,1)S(1)}) custom-call(s32[1024]{0:T(1024)S(1)} %copy-done.26, s32[2,16]{1,0:T(2,128)S(1)} %bitcast.20, bf16[128,128,128]{2,1,0:T(8,128)(2,1)S(1)} %copy-done, f32[264,256]{1,0:T(8,128)S(1)} %get-tuple-element.25.refs_0_, ...), custom_call_target="tpu_custom_call" | custom-call | flops 2147483648 | bytes 10485760 | tf_op jit(solution)/shard_map/combine/pallas_call | solution.py:209
  115.4 2.0 %collective-permute-start.12 = (f32[16,128,256]{2,1,0:T(8,128)S(1)}, f32[16,128,256]{2,1,0:T(8,128)S(1)}, u32[]{:S(2)}, u32[]{:S(2)}) collective-permute-start(f32[16,128,256]{2,1,0:T(8,128)S(1)} %get-tuple-element.34), channel_id=1, source_target_pairs={{0,1},{1,0},{2,3},{3,2},{4,5},{5,4},{6,7},{7,6},{8,9},{9,8},{10,11... | collective-permute-start | bytes 6291464 | tf_op jit(solution)/shard_map/ppermute | solution.py:335
  118.0 2.6 %collective-permute-done.27.refs_13_ = f32[512,256]{1,0:T(8,128)} collective-permute-done((f32[512,256]{1,0:T(8,128)}, f32[512,256]{1,0:T(8,128)}, u32[]{:S(2)}, u32[]{:S(2)}) %collective-permute-start.27) | collective-permute-done | bytes 524320 | tf_op jit(solution)/shard_map/ppermute | solution.py:44
  120.6 3.2 %combine.3 = (f32[16,128,256]{2,1,0:T(8,128)S(1)}, bf16[32,128,256]{2,1,0:T(8,128)(2,1)S(1)}) custom-call(s32[1024]{0:T(1024)S(1)} %copy-done.26, s32[2,16]{1,0:T(2,128)S(1)} %bitcast.21, bf16[128,128,128]{2,1,0:T(8,128)(2,1)S(1)} %copy-done.1, f32[256,256]{1,0:T(8,128)S(1)} %get-tuple-element.35.refs_0_, f32[256,256]{1,0:T(8,128)S(1)} %collective-permute-done.16.refs_1_, ...), custom_call_target="tpu_custom_call" | custom-call | flops 2147483648 | bytes 10485760 | tf_op jit(solution)/shard_map/combine/pallas_call | solution.py:209
  123.8 1.5 collective-permute-start.28
  125.3 1.6 keep.2
  127.2 1.6 collective-permute-start.13
  128.8 1.6 keep.3
  130.4 1.4 collective-permute-start.14
  131.8 1.4 collective-permute-start.15
  133.9 2.4 %collective-permute-start.30 = (f32[512,256]{1,0:T(8,128)S(1)}, f32[512,256]{1,0:T(8,128)S(1)}, u32[]{:S(2)}, u32[]{:S(2)}) collective-permute-start(f32[512,256]{1,0:T(8,128)S(1)} %bitcast.28), channel_id=1, source_target_pairs={{0,6},{1,7},{2,0},{3,1},{4,2},{5,3},{6,4},{7,5},{8,14},{9,15},{10,... | collective-permute-start | bytes 1572872 | tf_op jit(solution)/shard_map/ppermute | solution.py:346
  136.2 6.2 %collective-permute-done.13.refs_1_ = f32[512,256]{1,0:T(8,128)S(1)} collective-permute-done((f32[512,256]{1,0:T(8,128)S(1)}, f32[512,256]{1,0:T(8,128)S(1)}, u32[]{:S(2)}, u32[]{:S(2)}) %collective-permute-start.13) | collective-permute-done | bytes 524320 | tf_op jit(solution)/shard_map/ppermute | solution.py:346
  142.5 1.3 collective-permute-start.31
  144.2 10.6 %collective-permute-done.15.refs_3_ = f32[512,256]{1,0:T(8,128)S(1)} collective-permute-done((f32[512,256]{1,0:T(8,128)S(1)}, f32[512,256]{1,0:T(8,128)S(1)}, u32[]{:S(2)}, u32[]{:S(2)}) %collective-permute-start.15) | collective-permute-done | bytes 524320 | tf_op jit(solution)/shard_map/ppermute | solution.py:346
  154.8 1.4 begin.1.before_ref
  156.2 8.8 %collective-permute-done.29.refs_1_ = f32[512,256]{1,0:T(8,128)S(1)} collective-permute-done((f32[512,256]{1,0:T(8,128)S(1)}, f32[512,256]{1,0:T(8,128)S(1)}, u32[]{:S(2)}, u32[]{:S(2)}) %collective-permute-start.29) | collective-permute-done | bytes 524320 | tf_op jit(solution)/shard_map/ppermute | solution.py:346
  164.9 1.5 collective-permute-done.30.refs_2_
  166.4 10.8 %collective-permute-done.31.refs_3_ = f32[512,256]{1,0:T(8,128)S(1)} collective-permute-done((f32[512,256]{1,0:T(8,128)S(1)}, f32[512,256]{1,0:T(8,128)S(1)}, u32[]{:S(2)}, u32[]{:S(2)}) %collective-permute-start.31) | collective-permute-done | bytes 524320 | tf_op jit(solution)/shard_map/ppermute | solution.py:346
  177.2 3.5 %end.1 = bf16[512,512]{1,0:T(8,128)(2,1)} custom-call(f32[512,512]{1,0:T(8,128)S(1)} %copy-done.3, bf16[512,2048]{1,0:T(8,128)(2,1)S(1)} %copy-done.4, f32[512,2048]{1,0:T(8,128)S(1)} %begin.1.before_ref, bf16[2048,512]{1,0:T(8,128)(2,1)S(1)} %copy-done.5, f32[1,512]{1,0:T(1,128)S(1)} %bitcast.23, f32[512,256]{1,0:T(8,128)S(1)} %bitcast.17, ...), custom_call_target="tpu_custom_call" | custom-call | flops 1610612736 | bytes 8388608 | tf_op jit(solution)/shard_map/end/pallas_call | solution.py:361
  (93 shorter events, 17.7 us)
Async XLA Ops:
  1.9 76.0 %copy-start.31 = (f32[1,1,128,128,128]{4,3,2,1,0:T(8,128)S(1)}, f32[1,1,128,128,128]{4,3,2,1,0:T(8,128)}, u32[]{:S(2)}) copy-start(f32[1,1,128,128,128]{4,3,2,1,0:T(8,128)} %param.11) | copy-start | bytes 25165828
  2.0 13.1 %collective-permute-start.16 = (f32[256,256]{1,0:T(8,128)S(1)}, f32[256,256]{1,0:T(8,128)S(1)}, u32[]{:S(2)}, u32[]{:S(2)}) collective-permute-start(f32[256,256]{1,0:T(8,128)S(1)} %get-tuple-element.35.refs_0_), channel_id=1, source_target_pairs={{0,24},{8,0},{16,8},{24,16},{32,56},{40,32},{48,40},{56,48},{64,88... | collective-permute-start | bytes 786440 | tf_op jit(solution)/shard_map/ppermute | solution.py:44
  5.6 9.6 %collective-permute-start.17 = (f32[256,256]{1,0:T(8,128)S(1)}, f32[256,256]{1,0:T(8,128)S(1)}, u32[]{:S(2)}, u32[]{:S(2)}) collective-permute-start(f32[256,256]{1,0:T(8,128)S(1)} %get-tuple-element.35.refs_0_), channel_id=1, source_target_pairs={{0,16},{8,24},{16,0},{24,8},{32,48},{40,56},{48,32},{56,40},{64,80... | collective-permute-start | bytes 786440 | tf_op jit(solution)/shard_map/ppermute | solution.py:44
  6.0 19.8 %collective-permute-start = (f32[264,256]{1,0:T(8,128)S(1)}, f32[264,256]{1,0:T(8,128)S(1)}, u32[]{:S(2)}, u32[]{:S(2)}) collective-permute-start(f32[264,256]{1,0:T(8,128)S(1)} %get-tuple-element.25.refs_0_), channel_id=1, source_target_pairs={{0,24},{8,0},{16,8},{24,16},{32,56},{40,32},{48,40},{56,48},{64,88... | collective-permute-start | bytes 811016 | tf_op jit(solution)/shard_map/ppermute | solution.py:44
  6.7 14.3 %collective-permute-start.18 = (f32[256,256]{1,0:T(8,128)S(1)}, f32[256,256]{1,0:T(8,128)S(1)}, u32[]{:S(2)}, u32[]{:S(2)}) collective-permute-start(f32[256,256]{1,0:T(8,128)S(1)} %get-tuple-element.35.refs_0_), channel_id=1, source_target_pairs={{0,8},{8,16},{16,24},{24,0},{32,40},{40,48},{48,56},{56,32},{64,72... | collective-permute-start | bytes 786440 | tf_op jit(solution)/shard_map/ppermute | solution.py:44
  7.4 13.9 %collective-permute-start.19 = (f32[256,256]{1,0:T(8,128)S(1)}, f32[256,256]{1,0:T(8,128)S(1)}, u32[]{:S(2)}, u32[]{:S(2)}) collective-permute-start(f32[256,256]{1,0:T(8,128)S(1)} %get-tuple-element.36.refs_4_), channel_id=1, source_target_pairs={{0,96},{8,104},{16,112},{24,120},{32,0},{40,8},{48,16},{56,24},{64... | collective-permute-start | bytes 786440 | tf_op jit(solution)/shard_map/ppermute | solution.py:40
  15.1 8.7 %collective-permute-start.20 = (f32[256,256]{1,0:T(8,128)S(1)}, f32[256,256]{1,0:T(8,128)S(1)}, u32[]{:S(2)}, u32[]{:S(2)}) collective-permute-start(f32[256,256]{1,0:T(8,128)S(1)} %get-tuple-element.36.refs_4_), channel_id=1, source_target_pairs={{0,64},{8,72},{16,80},{24,88},{32,96},{40,104},{48,112},{56,120},{... | collective-permute-start | bytes 786440 | tf_op jit(solution)/shard_map/ppermute | solution.py:40
  15.2 10.5 %collective-permute-start.21 = (f32[256,256]{1,0:T(8,128)S(1)}, f32[256,256]{1,0:T(8,128)S(1)}, u32[]{:S(2)}, u32[]{:S(2)}) collective-permute-start(f32[256,256]{1,0:T(8,128)S(1)} %get-tuple-element.36.refs_4_), channel_id=1, source_target_pairs={{0,32},{8,40},{16,48},{24,56},{32,64},{40,72},{48,80},{56,88},{64,... | collective-permute-start | bytes 786440 | tf_op jit(solution)/shard_map/ppermute | solution.py:40
  21.0 6.9 %collective-permute-start.1 = (f32[264,256]{1,0:T(8,128)S(1)}, f32[264,256]{1,0:T(8,128)S(1)}, u32[]{:S(2)}, u32[]{:S(2)}) collective-permute-start(f32[264,256]{1,0:T(8,128)S(1)} %get-tuple-element.25.refs_0_), channel_id=1, source_target_pairs={{0,16},{8,24},{16,0},{24,8},{32,48},{40,56},{48,32},{56,40},{64,80... | collective-permute-start | bytes 811016 | tf_op jit(solution)/shard_map/ppermute | solution.py:44
  21.3 21.0 %copy-start.6 = (f32[256,256]{1,0:T(8,128)}, f32[256,256]{1,0:T(8,128)S(1)}, u32[]{:S(2)}) copy-start(f32[256,256]{1,0:T(8,128)S(1)} %collective-permute-done.19.refs_5_) | copy-start | bytes 786436
  21.3 14.9 %collective-permute-start.2 = (f32[264,256]{1,0:T(8,128)S(1)}, f32[264,256]{1,0:T(8,128)S(1)}, u32[]{:S(2)}, u32[]{:S(2)}) collective-permute-start(f32[264,256]{1,0:T(8,128)S(1)} %get-tuple-element.25.refs_0_), channel_id=1, source_target_pairs={{0,8},{8,16},{16,24},{24,0},{32,40},{40,48},{48,56},{56,32},{64,72... | collective-permute-start | bytes 811016 | tf_op jit(solution)/shard_map/ppermute | solution.py:44
  23.8 18.6 %copy-start.8 = (f32[256,256]{1,0:T(8,128)}, f32[256,256]{1,0:T(8,128)S(1)}, u32[]{:S(2)}) copy-start(f32[256,256]{1,0:T(8,128)S(1)} %collective-permute-done.20.refs_6_) | copy-start | bytes 786436
  23.8 12.5 %collective-permute-start.3 = (f32[264,256]{1,0:T(8,128)S(1)}, f32[264,256]{1,0:T(8,128)S(1)}, u32[]{:S(2)}, u32[]{:S(2)}) collective-permute-start(f32[264,256]{1,0:T(8,128)S(1)} %get-tuple-element.26.refs_4_), channel_id=1, source_target_pairs={{0,96},{8,104},{16,112},{24,120},{32,0},{40,8},{48,16},{56,24},{64... | collective-permute-start | bytes 811016 | tf_op jit(solution)/shard_map/ppermute | solution.py:40
  25.7 16.6 %copy-start.10 = (f32[256,256]{1,0:T(8,128)}, f32[256,256]{1,0:T(8,128)S(1)}, u32[]{:S(2)}) copy-start(f32[256,256]{1,0:T(8,128)S(1)} %collective-permute-done.21.refs_7_) | copy-start | bytes 786436
  25.7 10.5 %collective-permute-start.4 = (f32[264,256]{1,0:T(8,128)S(1)}, f32[264,256]{1,0:T(8,128)S(1)}, u32[]{:S(2)}, u32[]{:S(2)}) collective-permute-start(f32[264,256]{1,0:T(8,128)S(1)} %get-tuple-element.26.refs_4_), channel_id=1, source_target_pairs={{0,64},{8,72},{16,80},{24,88},{32,96},{40,104},{48,112},{56,120},{... | collective-permute-start | bytes 811016 | tf_op jit(solution)/shard_map/ppermute | solution.py:40
  25.7 10.6 %collective-permute-start.5 = (f32[264,256]{1,0:T(8,128)S(1)}, f32[264,256]{1,0:T(8,128)S(1)}, u32[]{:S(2)}, u32[]{:S(2)}) collective-permute-start(f32[264,256]{1,0:T(8,128)S(1)} %get-tuple-element.26.refs_4_), channel_id=1, source_target_pairs={{0,32},{8,40},{16,48},{24,56},{32,64},{40,72},{48,80},{56,88},{64,... | collective-permute-start | bytes 811016 | tf_op jit(solution)/shard_map/ppermute | solution.py:40
  39.1 17.1 %collective-permute-start.22 = (f32[512,256]{1,0:T(8,128)S(1)}, f32[512,256]{1,0:T(8,128)S(1)}, u32[]{:S(2)}, u32[]{:S(2)}) collective-permute-start(f32[512,256]{1,0:T(8,128)S(1)} %get-tuple-element.37), channel_id=1, source_target_pairs={{0,32},{8,40},{16,48},{24,56},{32,64},{40,72},{48,80},{56,88},{64,... | collective-permute-start | bytes 1572872 | tf_op jit(solution)/shard_map/ppermute | solution.py:40
  42.4 15.9 %collective-permute-start.10 = (f32[512,256]{1,0:T(8,128)S(1)}, f32[512,256]{1,0:T(8,128)S(1)}, u32[]{:S(2)}, u32[]{:S(2)}) collective-permute-start(f32[512,256]{1,0:T(8,128)S(1)} %get-tuple-element.31), channel_id=1, source_target_pairs={{0,16},{8,24},{16,0},{24,8},{32,48},{40,56},{48,32},{56,40},{64,80... | collective-permute-start | bytes 1572872 | tf_op jit(solution)/shard_map/ppermute | solution.py:44
  48.3 27.4 %collective-permute-start.11 = (f32[512,256]{1,0:T(8,128)S(1)}, f32[512,256]{1,0:T(8,128)S(1)}, u32[]{:S(2)}, u32[]{:S(2)}) collective-permute-start(f32[512,256]{1,0:T(8,128)S(1)} %get-tuple-element.32), channel_id=1, source_target_pairs={{0,24},{8,0},{16,8},{24,16},{32,56},{40,32},{48,40},{56,48},{64,88... | collective-permute-start | bytes 1572872 | tf_op jit(solution)/shard_map/ppermute | solution.py:44
  53.7 61.7 %collective-permute-start.23 = (f32[512,256]{1,0:T(8,128)}, f32[512,256]{1,0:T(8,128)}, u32[]{:S(2)}, u32[]{:S(2)}) collective-permute-start(f32[512,256]{1,0:T(8,128)} %get-tuple-element.38), channel_id=1, source_target_pairs={{0,64},{8,72},{16,80},{24,88},{32,96},{40,104},{48,112},{56,120},{... | collective-permute-start | bytes 1572872 | tf_op jit(solution)/shard_map/ppermute | solution.py:40
  54.2 29.5 %collective-permute-start.6 = (f32[512,256]{1,0:T(8,128)S(1)}, f32[512,256]{1,0:T(8,128)S(1)}, u32[]{:S(2)}, u32[]{:S(2)}) collective-permute-start(f32[512,256]{1,0:T(8,128)S(1)} %get-tuple-element.27), channel_id=1, source_target_pairs={{0,32},{8,40},{16,48},{24,56},{32,64},{40,72},{48,80},{56,88},{64,... | collective-permute-start | bytes 1572872 | tf_op jit(solution)/shard_map/ppermute | solution.py:40
  56.9 31.9 %collective-permute-start.7 = (f32[512,256]{1,0:T(8,128)S(1)}, f32[512,256]{1,0:T(8,128)S(1)}, u32[]{:S(2)}, u32[]{:S(2)}) collective-permute-start(f32[512,256]{1,0:T(8,128)S(1)} %get-tuple-element.28), channel_id=1, source_target_pairs={{0,64},{8,72},{16,80},{24,88},{32,96},{40,104},{48,112},{56,120},{... | collective-permute-start | bytes 1572872 | tf_op jit(solution)/shard_map/ppermute | solution.py:40
  59.0 37.8 %collective-permute-start.8 = (f32[512,256]{1,0:T(8,128)S(1)}, f32[512,256]{1,0:T(8,128)S(1)}, u32[]{:S(2)}, u32[]{:S(2)}) collective-permute-start(f32[512,256]{1,0:T(8,128)S(1)} %get-tuple-element.29), channel_id=1, source_target_pairs={{0,96},{8,104},{16,112},{24,120},{32,0},{40,8},{48,16},{56,24},{64... | collective-permute-start | bytes 1572872 | tf_op jit(solution)/shard_map/ppermute | solution.py:40
  76.5 27.7 %copy-start.28 = (s32[1,1,16,2]{2,3,1,0:T(2,128)S(1)}, s32[1,1,16,2]{2,3,1,0:T(2,128)}, u32[]{:S(2)}) copy-start(s32[1,1,16,2]{2,3,1,0:T(2,128)} %param.15) | copy-start | bytes 388
  76.5 22.3 %collective-permute-start.9 = (f32[512,256]{1,0:T(8,128)S(1)}, f32[512,256]{1,0:T(8,128)S(1)}, u32[]{:S(2)}, u32[]{:S(2)}) collective-permute-start(f32[512,256]{1,0:T(8,128)S(1)} %get-tuple-element.30), channel_id=1, source_target_pairs={{0,8},{8,16},{16,24},{24,0},{32,40},{40,48},{48,56},{56,32},{64,72... | collective-permute-start | bytes 1572872 | tf_op jit(solution)/shard_map/ppermute | solution.py:44
  84.4 33.0 %collective-permute-start.24 = (f32[512,256]{1,0:T(8,128)}, f32[512,256]{1,0:T(8,128)}, u32[]{:S(2)}, u32[]{:S(2)}) collective-permute-start(f32[512,256]{1,0:T(8,128)} %get-tuple-element.39), channel_id=1, source_target_pairs={{0,96},{8,104},{16,112},{24,120},{32,0},{40,8},{48,16},{56,24},{64... | collective-permute-start | bytes 1572872 | tf_op jit(solution)/shard_map/ppermute | solution.py:40
  89.6 27.9 %collective-permute-start.25 = (f32[512,256]{1,0:T(8,128)}, f32[512,256]{1,0:T(8,128)}, u32[]{:S(2)}, u32[]{:S(2)}) collective-permute-start(f32[512,256]{1,0:T(8,128)} %get-tuple-element.40), channel_id=1, source_target_pairs={{0,8},{8,16},{16,24},{24,0},{32,40},{40,48},{48,56},{56,32},{64,72... | collective-permute-start | bytes 1572872 | tf_op jit(solution)/shard_map/ppermute | solution.py:44
  97.7 20.3 %collective-permute-start.26 = (f32[512,256]{1,0:T(8,128)}, f32[512,256]{1,0:T(8,128)}, u32[]{:S(2)}, u32[]{:S(2)}) collective-permute-start(f32[512,256]{1,0:T(8,128)} %get-tuple-element.41), channel_id=1, source_target_pairs={{0,16},{8,24},{16,0},{24,8},{32,48},{40,56},{48,32},{56,40},{64,80... | collective-permute-start | bytes 1572872 | tf_op jit(solution)/shard_map/ppermute | solution.py:44
  99.6 21.0 %collective-permute-start.27 = (f32[512,256]{1,0:T(8,128)}, f32[512,256]{1,0:T(8,128)}, u32[]{:S(2)}, u32[]{:S(2)}) collective-permute-start(f32[512,256]{1,0:T(8,128)} %get-tuple-element.42), channel_id=1, source_target_pairs={{0,24},{8,0},{16,8},{24,16},{32,56},{40,32},{48,40},{56,48},{64,88... | collective-permute-start | bytes 1572872 | tf_op jit(solution)/shard_map/ppermute | solution.py:44
  104.1 2.2 %copy-start = (bf16[128,128,128]{2,1,0:T(8,128)(2,1)S(1)}, bf16[128,128,128]{2,1,0:T(8,128)(2,1)}, u32[]{:S(2)}) copy-start(bf16[128,128,128]{2,1,0:T(8,128)(2,1)} %convert_bitcast_fusion.tile_ref) | copy-start | bytes 12582916
  113.2 7.3 %copy-start.1 = (bf16[128,128,128]{2,1,0:T(8,128)(2,1)S(1)}, bf16[128,128,128]{2,1,0:T(8,128)(2,1)}, u32[]{:S(2)}) copy-start(bf16[128,128,128]{2,1,0:T(8,128)(2,1)} %convert_bitcast_fusion.tile_ref) | copy-start | bytes 12582916
  113.3 7.3 %copy-start.7 = (f32[256,256]{1,0:T(8,128)S(1)}, f32[256,256]{1,0:T(8,128)}, u32[]{:S(2)}) copy-start(f32[256,256]{1,0:T(8,128)} %copy-done.6) | copy-start | bytes 786436
  113.3 7.3 %copy-start.9 = (f32[256,256]{1,0:T(8,128)S(1)}, f32[256,256]{1,0:T(8,128)}, u32[]{:S(2)}) copy-start(f32[256,256]{1,0:T(8,128)} %copy-done.8) | copy-start | bytes 786436
  113.3 7.3 %copy-start.11 = (f32[256,256]{1,0:T(8,128)S(1)}, f32[256,256]{1,0:T(8,128)}, u32[]{:S(2)}) copy-start(f32[256,256]{1,0:T(8,128)} %copy-done.10) | copy-start | bytes 786436
  113.3 7.3 %copy-start.13 = (f32[512,256]{1,0:T(8,128)S(1)}, f32[512,256]{1,0:T(8,128)}, u32[]{:S(2)}) copy-start(f32[512,256]{1,0:T(8,128)} %copy-done.12) | copy-start | bytes 1572868
  115.4 11.5 %collective-permute-start.12 = (f32[16,128,256]{2,1,0:T(8,128)S(1)}, f32[16,128,256]{2,1,0:T(8,128)S(1)}, u32[]{:S(2)}, u32[]{:S(2)}) collective-permute-start(f32[16,128,256]{2,1,0:T(8,128)S(1)} %get-tuple-element.34), channel_id=1, source_target_pairs={{0,1},{1,0},{2,3},{3,2},{4,5},{5,4},{6,7},{7,6},{8,9},{9,8},{10,11... | collective-permute-start | bytes 6291464 | tf_op jit(solution)/shard_map/ppermute | solution.py:335
  123.8 9.4 %collective-permute-start.28 = (f32[16,128,256]{2,1,0:T(8,128)S(1)}, f32[16,128,256]{2,1,0:T(8,128)S(1)}, u32[]{:S(2)}, u32[]{:S(2)}) collective-permute-start(f32[16,128,256]{2,1,0:T(8,128)S(1)} %get-tuple-element.44), channel_id=1, source_target_pairs={{0,1},{1,0},{2,3},{3,2},{4,5},{5,4},{6,7},{7,6},{8,9},{9,8},{10,11... | collective-permute-start | bytes 6291464 | tf_op jit(solution)/shard_map/ppermute | solution.py:335
  127.2 15.3 %collective-permute-start.13 = (f32[512,256]{1,0:T(8,128)S(1)}, f32[512,256]{1,0:T(8,128)S(1)}, u32[]{:S(2)}, u32[]{:S(2)}) collective-permute-start(f32[512,256]{1,0:T(8,128)S(1)} %bitcast.26), channel_id=1, source_target_pairs={{0,2},{1,3},{2,4},{3,5},{4,6},{5,7},{6,0},{7,1},{8,10},{9,11},{10,... | collective-permute-start | bytes 1572872 | tf_op jit(solution)/shard_map/ppermute | solution.py:346
  130.4 13.7 %collective-permute-start.14 = (f32[512,256]{1,0:T(8,128)S(1)}, f32[512,256]{1,0:T(8,128)S(1)}, u32[]{:S(2)}, u32[]{:S(2)}) collective-permute-start(f32[512,256]{1,0:T(8,128)S(1)} %bitcast.25), channel_id=1, source_target_pairs={{0,6},{1,7},{2,0},{3,1},{4,2},{5,3},{6,4},{7,5},{8,14},{9,15},{10,... | collective-permute-start | bytes 1572872 | tf_op jit(solution)/shard_map/ppermute | solution.py:346
  131.8 23.0 %copy-start.3 = (f32[512,512]{1,0:T(8,128)S(1)}, f32[512,512]{1,0:T(8,128)}, u32[]{:S(2)}) copy-start(f32[512,512]{1,0:T(8,128)} %feature_ref.5) | copy-start | bytes 3145732
  131.8 23.0 %copy-start.4 = (bf16[512,2048]{1,0:T(8,128)(2,1)S(1)}, bf16[512,2048]{1,0:T(8,128)(2,1)}, u32[]{:S(2)}) copy-start(bf16[512,2048]{1,0:T(8,128)(2,1)} %w_ref.3) | copy-start | bytes 6291460
  131.8 23.0 %copy-start.29 = (f32[2048]{0:T(1024)S(1)}, f32[2048]{0:T(1024)}, u32[]{:S(2)}) copy-start(f32[2048]{0:T(1024)} %param.17) | copy-start | bytes 24580
  131.8 23.0 %collective-permute-start.15 = (f32[512,256]{1,0:T(8,128)S(1)}, f32[512,256]{1,0:T(8,128)S(1)}, u32[]{:S(2)}, u32[]{:S(2)}) collective-permute-start(f32[512,256]{1,0:T(8,128)S(1)} %bitcast.24), channel_id=1, source_target_pairs={{0,4},{1,5},{2,6},{3,7},{4,0},{5,1},{6,2},{7,3},{8,12},{9,13},{10,... | collective-permute-start | bytes 1572872 | tf_op jit(solution)/shard_map/ppermute | solution.py:346
  133.5 31.4 %collective-permute-start.29 = (f32[512,256]{1,0:T(8,128)S(1)}, f32[512,256]{1,0:T(8,128)S(1)}, u32[]{:S(2)}, u32[]{:S(2)}) collective-permute-start(f32[512,256]{1,0:T(8,128)S(1)} %bitcast.29), channel_id=1, source_target_pairs={{0,2},{1,3},{2,4},{3,5},{4,6},{5,7},{6,0},{7,1},{8,10},{9,11},{10,... | collective-permute-start | bytes 1572872 | tf_op jit(solution)/shard_map/ppermute | solution.py:346
  133.9 32.6 %collective-permute-start.30 = (f32[512,256]{1,0:T(8,128)S(1)}, f32[512,256]{1,0:T(8,128)S(1)}, u32[]{:S(2)}, u32[]{:S(2)}) collective-permute-start(f32[512,256]{1,0:T(8,128)S(1)} %bitcast.28), channel_id=1, source_target_pairs={{0,6},{1,7},{2,0},{3,1},{4,2},{5,3},{6,4},{7,5},{8,14},{9,15},{10,... | collective-permute-start | bytes 1572872 | tf_op jit(solution)/shard_map/ppermute | solution.py:346
  142.5 34.8 %collective-permute-start.31 = (f32[512,256]{1,0:T(8,128)S(1)}, f32[512,256]{1,0:T(8,128)S(1)}, u32[]{:S(2)}, u32[]{:S(2)}) collective-permute-start(f32[512,256]{1,0:T(8,128)S(1)} %bitcast.27), channel_id=1, source_target_pairs={{0,4},{1,5},{2,6},{3,7},{4,0},{5,1},{6,2},{7,3},{8,12},{9,13},{10,... | collective-permute-start | bytes 1572872 | tf_op jit(solution)/shard_map/ppermute | solution.py:346
  154.8 22.5 %copy-start.5 = (bf16[2048,512]{1,0:T(8,128)(2,1)S(1)}, bf16[2048,512]{1,0:T(8,128)(2,1)}, u32[]{:S(2)}) copy-start(bf16[2048,512]{1,0:T(8,128)(2,1)} %w_out_ref.1) | copy-start | bytes 6291460
  154.8 22.5 %copy-start.30 = (f32[512]{0:T(512)S(1)}, f32[512]{0:T(512)}, u32[]{:S(2)}) copy-start(f32[512]{0:T(512)} %param.19) | copy-start | bytes 6148
  (16 other events, 14.4 us)

commit v3 on v2

--- a/solution.py
+++ b/solution.py
@@ -12,6 +12,7 @@
 side = 4
 cores = 2
 picks = 2
+parts = 3
 note_rows = 8
 lanes = 128
 chunk = 512
@@ -56,50 +57,106 @@
     return slice((d * picks + j) * half, (d * picks + j + 1) * half)
 
 
-def split(feature_ref, need_ref, *outs):
+def split(feature_ref, need_ref, *refs):
+    outs, (need, sems) = refs[:-2], refs[-2:]
     half = lanes // 2
     rows = feature_ref.shape[0] // 2
-    need = need_ref[...].astype(jnp.float32)
-    for group in range(len(outs) // 2):
-        part = slice(group * span, (group + 1) * span)
-        for place, out in enumerate(outs[2 * group : 2 * group + 2]):
-            for block in range(rows // half):
-                start = (2 * block + place) * half
-                out[block * half : (block + 1) * half, :] = feature_ref[start : start + half, part]
-            if group == 0:
-                out[rows:, :] = jnp.zeros((note_rows, span), jnp.float32)
-                out[rows : rows + need.shape[0], : need.shape[1]] = need
-
-
-def plan(row_ref, col_ref, count_ref, plan_ref, blocks_dev, entries):
+    copies = [pltpu.make_async_copy(need_ref, need, sems.at[0])]
+    for at, out in enumerate(outs):
+        group, place = at // 2, at % 2
+        for block in range(rows // half):
+            start = (2 * block + place) * half
+            copies.append(
+                pltpu.make_async_copy(
+                    feature_ref.at[start : start + half, group * span : (group + 1) * span],
+                    out.at[block * half : (block + 1) * half, :],
+                    sems.at[len(copies)],
+                )
+            )
+    for copy in copies:
+        copy.start()
+    copies[0].wait()
+    note = need[...].astype(jnp.float32)
+    for out in outs[:2]:
+        out[rows:, :] = jnp.zeros((note_rows, span), jnp.float32)
+        out[rows : rows + note.shape[0], : note.shape[1]] = note
+    for copy in copies[1:]:
+        copy.wait()
+
+
+def join(keep_ref, arrived_ref, mine_ref, right_ref, left_ref, over_right_ref, over_left_ref):
+    size = mine_ref.shape[0]
+    cut = size // 2
+    for at, out in enumerate((mine_ref, right_ref, None, left_ref)):
+        spot = slice(at * size, (at + 1) * size)
+        if out is None:
+            first, last = slice(at * size, at * size + cut), slice(at * size + cut, spot.stop)
+            over_right_ref[...] = keep_ref[first] + arrived_ref[first]
+            over_left_ref[...] = keep_ref[last] + arrived_ref[last]
+        else:
+            out[...] = keep_ref[spot] + arrived_ref[spot]
+
+
+def relay(right_ref, left_ref, from_left_ref, from_right_ref, right_out, left_out):
+    cut = from_left_ref.shape[0]
+    right_out[:cut] = right_ref[:cut] + from_left_ref[...]
+    left_out[cut:] = left_ref[cut:] + from_right_ref[...]
+
+
+def log(value):
+    return value.bit_length() - 1
+
+
+def pairs_of(tile_total, blocks):
+    return (tile_total + blocks) // 2 + unroll
+
+
+def plan(row_ref, col_ref, count_ref, plan_ref, waiting, blocks_dev):
+    tile_total = row_ref.shape[0]
+    blocks = side * blocks_dev
+    entries = pairs_of(tile_total, blocks)
+    slot_bits = log(tile_total)
+    code_bits = slot_bits + log(side * side * picks) + 1
+    empty = (side * side * picks) << slot_bits
     my_z = lax.axis_index("row") // side
     my_y = lax.axis_index("row") % side
     my_x = lax.axis_index("col") // cores
     my_core = lax.axis_index("col") % cores
 
-    def write(at, slot, row, pos):
-        plan_ref[at] = slot
-        plan_ref[at + entries] = row
-        plan_ref[at + 2 * entries] = pos
+    def pair(place, first, second):
+        return first | (second << code_bits) | (place << (2 * code_bits))
+
+    for place in range(2 * blocks):
+        waiting[place] = -1
 
     def turn(slot, ends):
         target = row_ref[slot]
-        column = target // blocks_dev
-        row = lax.rem(column // cores - my_x + side, side) * blocks_dev + target % blocks_dev
-        other = (column % cores != my_core).astype(jnp.int32)
-        owner = col_ref[slot] // picks
-        away_z = lax.rem(owner // side - my_z + side, side)
-        away_y = lax.rem(owner % side - my_y + side, side)
-        pos = (away_z * side + away_y) * picks + col_ref[slot] % picks
-        for which, end in enumerate(ends):
-            write(which * 3 * entries + end, slot, row, pos)
-        return ends[0] + other, ends[1] + 1 - other
-
-    ends = lax.fori_loop(0, count_ref[0, 0], turn, (0, 0))
-    for which, end in enumerate(ends):
-        plan_ref[6 * entries + which] = end
+        source = col_ref[slot]
+        column = lax.shift_right_logical(target, log(blocks_dev))
+        away_x = (lax.shift_right_logical(column, log(cores)) - my_x) & (side - 1)
+        place = away_x * blocks_dev + (target & (blocks_dev - 1))
+        kept = 1 - ((column & (cores - 1)) ^ my_core)
+        owner = lax.shift_right_logical(source, log(picks))
+        away_z = (lax.shift_right_logical(owner, log(side)) - my_z) & (side - 1)
+        away_y = (owner - my_y) & (side - 1)
+        pos = (away_z * side + away_y) * picks + (source & (picks - 1))
+        code = slot | (pos << slot_bits)
+        before = waiting[kept * blocks + place]
+        full = (before >= 0).astype(jnp.int32)
+        end = jnp.where(kept == 1, ends[1], ends[0])
+        plan_ref[kept * entries + end] = pair(place, before, code)
+        waiting[kept * blocks + place] = jnp.where(before >= 0, -1, code)
+        return ends[0] + full * (1 - kept), ends[1] + full * kept
+
+    ends = list(lax.fori_loop(0, count_ref[0, 0], turn, (0, 0)))
+    for kept in range(2):
+        for place in range(blocks):
+            before = waiting[kept * blocks + place]
+            plan_ref[kept * entries + ends[kept]] = pair(place, before, empty)
+            ends[kept] = ends[kept] + (before >= 0).astype(jnp.int32)
         for extra in range(unroll):
-            write(which * 3 * entries + end + extra, 0, 0, 0)
+            plan_ref[kept * entries + ends[kept] + extra] = pair(0, empty, empty)
+        plan_ref[2 * entries + kept] = ends[kept]
 
 
 def pack(half, *refs):
@@ -144,33 +201,41 @@
             pltpu.SemaphoreType.DMA((number,)),
         ],
         out_shape=[packed] * number,
-        compiler_params=pltpu.CompilerParams(vmem_limit_bytes=16 << 20),
+        compiler_params=pltpu.CompilerParams(vmem_limit_bytes=5 << 20),
         cost_estimate=pl.CostEstimate(flops=0, bytes_accessed=5 << 20, transcendentals=0),
         name="pack",
     )(*first, *second, *notes)
 
 
-def add_tiles(which, plan_ref, tile_ref, pool, total):
-    entries = tile_ref.shape[0] + unroll
-    base = which * 3 * entries
+def add_tiles(kept, plan_ref, tile_ref, pool, total):
+    tile_total = tile_ref.shape[0]
+    sources = pool.shape[0] - 1
+    entries = pairs_of(tile_total, total.shape[0])
+    slot_bits = log(tile_total)
+    pos_bits = log(sources) + 1
     total[...] = jnp.zeros_like(total)
-    count = plan_ref[6 * entries + which]
 
     def turn(step, carry):
         products = []
         for lane in range(unroll):
-            at = base + step * unroll + lane
+            code = plan_ref[kept * entries + step * unroll + lane]
+            left, right = [], []
+            for _ in range(2):
+                left.append(tile_ref[code & (tile_total - 1)].astype(jnp.bfloat16))
+                code = lax.shift_right_logical(code, slot_bits)
+                right.append(pool[code & ((1 << pos_bits) - 1)])
+                code = lax.shift_right_logical(code, pos_bits)
             product = jnp.dot(
-                tile_ref[plan_ref[at]],
-                pool[plan_ref[at + 2 * entries]],
+                jnp.concatenate(left, axis=1),
+                jnp.concatenate(right, axis=0),
                 preferred_element_type=jnp.float32,
             )
-            live = (step * unroll + lane < count).astype(jnp.float32)
-            products.append((plan_ref[at + entries], product * live))
+            products.append((code, product))
         for target, product in products:
             total[target] += product
         return carry
 
+    count = plan_ref[2 * entries + kept]
     lax.fori_loop(0, (count + unroll - 1) // unroll, turn, 0)
 
 
@@ -201,6 +266,7 @@
                 pool[(d * side + back(away)) * picks + j, low, :] = along_y[away - 1][
                     spot, :
                 ].astype(pool.dtype)
+    pool[side * side * picks] = jnp.zeros(pool.shape[1:], pool.dtype)
     add_tiles(0, plan_ref, tile_ref, pool, total)
 
 
@@ -212,9 +278,9 @@
         out_specs=[in_vmem] * 2,
         out_shape=[
             jax.ShapeDtypeStruct((blocks, edge, span), jnp.float32),
-            jax.ShapeDtypeStruct((side * side * picks, edge, span), jnp.bfloat16),
+            jax.ShapeDtypeStruct((side * side * picks + 1, edge, span), jnp.bfloat16),
         ],
-        compiler_params=pltpu.CompilerParams(vmem_limit_bytes=24 << 20),
+        compiler_params=pltpu.CompilerParams(vmem_limit_bytes=10 << 20),
         cost_estimate=pl.CostEstimate(flops=2 << 30, bytes_accessed=10 << 20, transcendentals=0),
         name="combine",
     )(listed, need, tiles, *first, *second, *along_z, *along_y)
@@ -227,7 +293,7 @@
         in_specs=[in_smem] + [in_vmem] * 2,
         out_specs=in_vmem,
         out_shape=jax.ShapeDtypeStruct((blocks, edge, span), jnp.float32),
-        compiler_params=pltpu.CompilerParams(vmem_limit_bytes=24 << 20),
+        compiler_params=pltpu.CompilerParams(vmem_limit_bytes=6 << 20),
         cost_estimate=pl.CostEstimate(flops=2 << 30, bytes_accessed=8 << 20, transcendentals=0),
         name="keep",
     )(listed, tiles, pool)
@@ -242,7 +308,7 @@
 
 
 def begin_mlp(feature_ref, w_ref, bias_ref, *refs):
-    totals, out_ref, mixed = refs[:side], refs[side], refs[side + 1]
+    totals, out_ref, mixed = refs[:parts], refs[parts], refs[parts + 1]
     mixed[...] = mixed_of(0, feature_ref, totals)
 
     def turn(step, carry):
@@ -257,7 +323,7 @@
 
 
 def end_mlp(feature_ref, w_ref, before_ref, w_out_ref, bias_ref, *refs):
-    totals, out_ref, mixed, total = refs[:side], refs[side], refs[side + 1], refs[side + 2]
+    totals, out_ref, mixed, total = refs[:parts], refs[parts], refs[parts + 1], refs[parts + 2]
     mixed[...] = mixed_of(1, feature_ref, totals)
     total[...] = jnp.broadcast_to(bias_ref[...], total.shape)
 
@@ -277,7 +343,7 @@
 def on_device(
     features, tiles, tile_rows, tile_cols, tile_count, needed, w_in, bias_in, w_out, bias_out
 ):
-    tile_total, edge = tiles.shape[2], tiles.shape[-1]
+    edge = tiles.shape[-1]
     half = edge // 2
     nodes, width = features.shape
     blocks_dev = nodes // edge
@@ -294,10 +360,14 @@
     ]
     own = pl.pallas_call(
         split,
-        in_specs=[in_vmem] * 2,
+        in_specs=[pl.BlockSpec(memory_space=pltpu.HBM)] * 2,
         out_specs=[in_vmem] * len(payload),
+        scratch_shapes=[
+            pltpu.VMEM(need.shape, jnp.int32),
+            pltpu.SemaphoreType.DMA((1 + len(payload) * blocks_dev,)),
+        ],
         out_shape=payload,
-        compiler_params=pltpu.CompilerParams(vmem_limit_bytes=8 << 20),
+        compiler_params=pltpu.CompilerParams(vmem_limit_bytes=4 << 20),
         cost_estimate=pl.CostEstimate(flops=0, bytes_accessed=2 << 20, transcendentals=0),
         name="split",
     )(features, need)
@@ -312,16 +382,17 @@
         seconds.append(second)
     notes = seconds[0][1:] + firsts[0][1:]
 
-    entries = tile_total + unroll
     listed = pl.pallas_call(
-        lambda *refs: plan(*refs, blocks_dev, entries),
+        lambda *refs: plan(*refs, blocks_dev),
         in_specs=[in_smem] * 3,
         out_specs=in_smem,
-        out_shape=jax.ShapeDtypeStruct((1024,), jnp.int32),
+        out_shape=jax.ShapeDtypeStruct((256,), jnp.int32),
+        scratch_shapes=[pltpu.SMEM((2 * blocks,), jnp.int32)],
+        compiler_params=pltpu.CompilerParams(vmem_limit_bytes=1 << 20),
         cost_estimate=pl.CostEstimate(flops=0, bytes_accessed=1 << 20, transcendentals=0),
         name="plan",
     )(tile_rows[0, 0], tile_cols[0, 0], tile_count)
-    tiles_low = tiles[0, 0].astype(jnp.bfloat16)
+    cell_tiles = tiles[0, 0]
 
     sums = []
     for group in range(groups):
@@ -331,28 +402,43 @@
         for away in (1, 3, 2):
             along_z[away - 1] = from_z(packed[away - 1], -away)
             along_y[away - 1] = from_y(packed[side + away - 2], -away)
-        send, pool = combine_sent(listed, need, tiles_low, first, second, along_z, along_y, blocks)
+        send, pool = combine_sent(listed, need, cell_tiles, first, second, along_z, along_y, blocks)
         arrived = lax.ppermute(send, "col", col_shift(0, 1))
-        keep = combine_kept(listed, tiles_low, pool, blocks)
-        parts = [
-            (
-                keep[k * blocks_dev : (k + 1) * blocks_dev]
-                + arrived[k * blocks_dev : (k + 1) * blocks_dev]
-            ).reshape(nodes, span)
-            for k in range(side)
-        ]
-        total = [parts[0]]
-        for k in (1, 3, 2):
-            total.append(lax.ppermute(parts[k], "col", col_shift(k, 0)))
-        sums.append(total)
+        keep = combine_kept(listed, cell_tiles, pool, blocks)
+        full = jax.ShapeDtypeStruct((blocks_dev, edge, span), jnp.float32)
+        part = jax.ShapeDtypeStruct((blocks_dev // 2, edge, span), jnp.float32)
+        mine, right, left, over_right, over_left = pl.pallas_call(
+            join,
+            in_specs=[in_vmem] * 2,
+            out_specs=[in_vmem] * 5,
+            out_shape=[full] * 3 + [part] * 2,
+            compiler_params=pltpu.CompilerParams(vmem_limit_bytes=6 << 20),
+            cost_estimate=pl.CostEstimate(flops=0, bytes_accessed=4 << 20, transcendentals=0),
+            name="join",
+        )(keep, arrived)
+        relay_right = lax.ppermute(over_right, "col", col_shift(1, 0))
+        relay_left = lax.ppermute(over_left, "col", col_shift(-1, 0))
+        right, left = pl.pallas_call(
+            relay,
+            in_specs=[in_vmem] * 4,
+            out_specs=[in_vmem] * 2,
+            out_shape=[full] * 2,
+            input_output_aliases={0: 0, 1: 1},
+            compiler_params=pltpu.CompilerParams(vmem_limit_bytes=5 << 20),
+            cost_estimate=pl.CostEstimate(flops=0, bytes_accessed=2 << 20, transcendentals=0),
+            name="relay",
+        )(right, left, relay_right, relay_left)
+        from_left = lax.ppermute(right, "col", col_shift(1, 0))
+        from_right = lax.ppermute(left, "col", col_shift(-1, 0))
+        sums.append([v.reshape(nodes, span) for v in (mine, from_left, from_right)])
 
     before = pl.pallas_call(
         begin_mlp,
-        in_specs=[in_vmem] * (3 + side),
+        in_specs=[in_vmem] * (3 + parts),
         out_specs=in_vmem,
         out_shape=jax.ShapeDtypeStruct((nodes, hidden_size), jnp.float32),
         scratch_shapes=[pltpu.VMEM((nodes, span), jnp.bfloat16)],
-        compiler_params=pltpu.CompilerParams(vmem_limit_bytes=24 << 20),
+        compiler_params=pltpu.CompilerParams(vmem_limit_bytes=8 << 20),
         cost_estimate=pl.CostEstimate(
             flops=1 << 29, bytes_accessed=8 << 20, transcendentals=0
         ),
@@ -360,14 +446,14 @@
     )(features, w_in, bias_in.reshape(1, -1), *sums[0])
     return pl.pallas_call(
         end_mlp,
-        in_specs=[in_vmem] * (5 + side),
+        in_specs=[in_vmem] * (5 + parts),
         out_specs=in_vmem,
         out_shape=jax.ShapeDtypeStruct((nodes, width), jnp.bfloat16),
         scratch_shapes=[
             pltpu.VMEM((nodes, span), jnp.bfloat16),
             pltpu.VMEM((nodes, width), jnp.float32),
         ],
-        compiler_params=pltpu.CompilerParams(vmem_limit_bytes=24 << 20),
+        compiler_params=pltpu.CompilerParams(vmem_limit_bytes=6 << 20),
         cost_estimate=pl.CostEstimate(
             flops=3 << 29, bytes_accessed=8 << 20, transcendentals=0
         ),

time: 184 us -> 155 us (0.84); the launches traced: 181 us -> 154 us
  local copies, waits for them, and re-layouts: 16.7 us -> 1.95 us
  starting transfers between devices: 56.8 us -> 48 us
  waiting for transfers between devices: 82.1 us -> 86.8 us
  Pallas kernels: 20.7 us -> 16.3 us
  other arithmetic: 3.53 us -> 0 us
    ppermute x12, waiting for transfers between devices: 7.21 us -> 50.7 us  [from_z(): return lax.ppermute(value, 'row', row_shift(-step, 0))]
    ppermute x12, waiting for transfers between devices: 36.7 us -> 13.7 us  [from_y(): return lax.ppermute(value, 'row', row_shift(0, -step))]
    ppermute x12, starting transfers between devices: 30 us -> 12.6 us  [from_y(): return lax.ppermute(value, 'row', row_shift(0, -step))]
    ppermute x6 -> x8, waiting for transfers between devices: 38.3 us -> 22.5 us  [the longest x2 17.3 us: on_device(): from_left = lax.ppermute(right, 'col', col_shift(1, 0))]
    unnamed x64 -> x20, local copies, waits for them, and re-layouts: 16.7 us -> 1.95 us
    ppermute x12, starting transfers between devices: 14.8 us -> 19.3 us  [from_z(): return lax.ppermute(value, 'row', row_shift(-step, 0))]
    convert_element_type x1 -> x0, other arithmetic: 2.98 us -> none  [on_device(): tiles_low = tiles[0, 0].astype(jnp.bfloat16)]
    ppermute x6 -> x8, starting transfers between devices: 8.43 us -> 11.3 us  [the longest x2 5.33 us: on_device(): from_right = lax.ppermute(left, 'col', col_shift(-1, 0))]
  transfers between devices with their start and end apart: 32 -> 34, of which waited for: 16 -> 18; matrix products, arithmetic and copies ran while one was open for 2% -> 0% of each run, Pallas kernels for 8% -> 7%
where the time goes in v3:
time: 155 us; the launch traced here: 154 us
  waiting for transfers between devices  86.8 us (56%)
  starting transfers between devices  48 us (31%)
  Pallas kernels  16.3 us (11%)
  local copies, waits for them, and re-layouts  1.95 us (1%)
    ppermute x12, waiting for transfers between devices, from_z(): return lax.ppermute(value, 'row', row_shift(-step, 0))  50.7 us
    ppermute x12, starting transfers between devices, from_z(): return lax.ppermute(value, 'row', row_shift(-step, 0))  19.3 us
    ppermute x2, waiting for transfers between devices, on_device(): from_left = lax.ppermute(right, 'col', col_shift(1, 0))  17.3 us
    ppermute x12, waiting for transfers between devices, from_y(): return lax.ppermute(value, 'row', row_shift(0, -step))  13.7 us
    ppermute x12, starting transfers between devices, from_y(): return lax.ppermute(value, 'row', row_shift(0, -step))  12.6 us
    ppermute x2, starting transfers between devices, on_device(): from_right = lax.ppermute(left, 'col', col_shift(-1, 0))  5.33 us
    ppermute x2, waiting for transfers between devices, on_device(): relay_right = lax.ppermute(over_right, 'col', col_shift(1, 0))  5.19 us
    ppermute x2, starting transfers between devices, on_device(): arrived = lax.ppermute(send, 'col', col_shift(0, 1))  4.7 us
  transfers between devices with their start and end apart: 34, of which 18 were waited for; matrix products, arithmetic and copies ran while one was open for 0% of the time, Pallas kernels for 7%

profile of v3, /device:TPU:1, one launch (start us, length us, event | category | flops | bytes accessed | tf_op | source)
XLA Modules:
  0.0 154.0 jit_solution(8404550842807437632)
XLA Ops:
  0.0 1.2 copy-done.1
  1.2 0.7 copy-done.5
  2.3 2.2 %collective-permute-start.19 = (f32[256,256]{1,0:T(8,128)S(1)}, f32[256,256]{1,0:T(8,128)S(1)}, u32[]{:S(2)}, u32[]{:S(2)}) collective-permute-start(f32[256,256]{1,0:T(8,128)S(1)} %get-tuple-element.56.refs_0_), channel_id=1, source_target_pairs={{0,8},{8,16},{16,24},{24,0},{32,40},{40,48},{48,56},{56,32},{64,72... | collective-permute-start | bytes 786440 | tf_op jit(solution)/shard_map/ppermute | solution.py:45
  4.5 2.6 %collective-permute-start.18 = (f32[256,256]{1,0:T(8,128)S(1)}, f32[256,256]{1,0:T(8,128)S(1)}, u32[]{:S(2)}, u32[]{:S(2)}) collective-permute-start(f32[256,256]{1,0:T(8,128)S(1)} %get-tuple-element.56.refs_0_), channel_id=1, source_target_pairs={{0,16},{8,24},{16,0},{24,8},{32,48},{40,56},{48,32},{56,40},{64,80... | collective-permute-start | bytes 786440 | tf_op jit(solution)/shard_map/ppermute | solution.py:45
  7.1 2.7 %collective-permute-start.17 = (f32[256,256]{1,0:T(8,128)S(1)}, f32[256,256]{1,0:T(8,128)S(1)}, u32[]{:S(2)}, u32[]{:S(2)}) collective-permute-start(f32[256,256]{1,0:T(8,128)S(1)} %get-tuple-element.56.refs_0_), channel_id=1, source_target_pairs={{0,24},{8,0},{16,8},{24,16},{32,56},{40,32},{48,40},{56,48},{64,88... | collective-permute-start | bytes 786440 | tf_op jit(solution)/shard_map/ppermute | solution.py:45
  9.8 1.6 %collective-permute-start.22 = (f32[256,256]{1,0:T(8,128)S(1)}, f32[256,256]{1,0:T(8,128)S(1)}, u32[]{:S(2)}, u32[]{:S(2)}) collective-permute-start(f32[256,256]{1,0:T(8,128)S(1)} %get-tuple-element.57.refs_4_), channel_id=1, source_target_pairs={{0,32},{8,40},{16,48},{24,56},{32,64},{40,72},{48,80},{56,88},{64,... | collective-permute-start | bytes 786440 | tf_op jit(solution)/shard_map/ppermute | solution.py:41
  11.8 3.5 %collective-permute-start.21 = (f32[256,256]{1,0:T(8,128)S(1)}, f32[256,256]{1,0:T(8,128)S(1)}, u32[]{:S(2)}, u32[]{:S(2)}) collective-permute-start(f32[256,256]{1,0:T(8,128)S(1)} %get-tuple-element.57.refs_4_), channel_id=1, source_target_pairs={{0,64},{8,72},{16,80},{24,88},{32,96},{40,104},{48,112},{56,120},{... | collective-permute-start | bytes 786440 | tf_op jit(solution)/shard_map/ppermute | solution.py:41
  15.3 3.2 %collective-permute-done.18.refs_2_ = f32[256,256]{1,0:T(8,128)S(1)} collective-permute-done((f32[256,256]{1,0:T(8,128)S(1)}, f32[256,256]{1,0:T(8,128)S(1)}, u32[]{:S(2)}, u32[]{:S(2)}) %collective-permute-start.18) | collective-permute-done | bytes 262176 | tf_op jit(solution)/shard_map/ppermute | solution.py:45
  18.5 3.8 %collective-permute-start.20 = (f32[256,256]{1,0:T(8,128)S(1)}, f32[256,256]{1,0:T(8,128)S(1)}, u32[]{:S(2)}, u32[]{:S(2)}) collective-permute-start(f32[256,256]{1,0:T(8,128)S(1)} %get-tuple-element.57.refs_4_), channel_id=1, source_target_pairs={{0,96},{8,104},{16,112},{24,120},{32,0},{40,8},{48,16},{56,24},{64... | collective-permute-start | bytes 786440 | tf_op jit(solution)/shard_map/ppermute | solution.py:41
  22.6 0.9 collective-permute-start
  23.5 1.4 collective-permute-done.21.refs_6_
  25.1 3.2 %collective-permute-done.20.refs_5_ = f32[256,256]{1,0:T(8,128)S(1)} collective-permute-done((f32[256,256]{1,0:T(8,128)S(1)}, f32[256,256]{1,0:T(8,128)S(1)}, u32[]{:S(2)}, u32[]{:S(2)}) %collective-permute-start.20) | collective-permute-done | bytes 262176 | tf_op jit(solution)/shard_map/ppermute | solution.py:41
  28.5 3.3 %collective-permute-start.3 = (f32[264,256]{1,0:T(8,128)S(1)}, f32[264,256]{1,0:T(8,128)S(1)}, u32[]{:S(2)}, u32[]{:S(2)}) collective-permute-start(f32[264,256]{1,0:T(8,128)S(1)} %get-tuple-element.40.refs_4_), channel_id=1, source_target_pairs={{0,96},{8,104},{16,112},{24,120},{32,0},{40,8},{48,16},{56,24},{64... | collective-permute-start | bytes 811016 | tf_op jit(solution)/shard_map/ppermute | solution.py:41
  31.7 0.9 collective-permute-done.refs_1_.refs_11_
  32.6 5.8 %collective-permute-done.4.refs_6_.refs_9_ = f32[264,256]{1,0:T(8,128)S(1)} collective-permute-done((f32[264,256]{1,0:T(8,128)S(1)}, f32[264,256]{1,0:T(8,128)S(1)}, u32[]{:S(2)}, u32[]{:S(2)}) %collective-permute-start.4) | collective-permute-done | bytes 270368 | tf_op jit(solution)/shard_map/ppermute | solution.py:41
  38.5 5.0 %collective-permute-done.3.refs_5_.refs_8_ = f32[264,256]{1,0:T(8,128)S(1)} collective-permute-done((f32[264,256]{1,0:T(8,128)S(1)}, f32[264,256]{1,0:T(8,128)S(1)}, u32[]{:S(2)}, u32[]{:S(2)}) %collective-permute-start.3) | collective-permute-done | bytes 270368 | tf_op jit(solution)/shard_map/ppermute | solution.py:41
  43.4 1.2 pack.3
  44.7 1.5 collective-permute-start.23
  46.2 1.2 pack.2
  47.5 3.3 %collective-permute-start.7 = (f32[512,256]{1,0:T(8,128)S(1)}, f32[512,256]{1,0:T(8,128)S(1)}, u32[]{:S(2)}, u32[]{:S(2)}) collective-permute-start(f32[512,256]{1,0:T(8,128)S(1)} %get-tuple-element.42), channel_id=1, source_target_pairs={{0,64},{8,72},{16,80},{24,88},{32,96},{40,104},{48,112},{56,120},{... | collective-permute-start | bytes 1572872 | tf_op jit(solution)/shard_map/ppermute | solution.py:41
  50.8 2.0 %collective-permute-start.8 = (f32[512,256]{1,0:T(8,128)S(1)}, f32[512,256]{1,0:T(8,128)S(1)}, u32[]{:S(2)}, u32[]{:S(2)}) collective-permute-start(f32[512,256]{1,0:T(8,128)S(1)} %get-tuple-element.43), channel_id=1, source_target_pairs={{0,96},{8,104},{16,112},{24,120},{32,0},{40,8},{48,16},{56,24},{64... | collective-permute-start | bytes 1572872 | tf_op jit(solution)/shard_map/ppermute | solution.py:41
  52.7 6.1 %collective-permute-done.23.refs_8_ = f32[512,256]{1,0:T(8,128)S(1)} collective-permute-done((f32[512,256]{1,0:T(8,128)S(1)}, f32[512,256]{1,0:T(8,128)S(1)}, u32[]{:S(2)}, u32[]{:S(2)}) %collective-permute-start.23) | collective-permute-done | bytes 524320 | tf_op jit(solution)/shard_map/ppermute | solution.py:41
  58.8 11.2 %collective-permute-done.6.refs_8_ = f32[512,256]{1,0:T(8,128)S(1)} collective-permute-done((f32[512,256]{1,0:T(8,128)S(1)}, f32[512,256]{1,0:T(8,128)S(1)}, u32[]{:S(2)}, u32[]{:S(2)}) %collective-permute-start.6) | collective-permute-done | bytes 524320 | tf_op jit(solution)/shard_map/ppermute | solution.py:41
  70.6 12.5 %collective-permute-done.7.refs_9_ = f32[512,256]{1,0:T(8,128)S(1)} collective-permute-done((f32[512,256]{1,0:T(8,128)S(1)}, f32[512,256]{1,0:T(8,128)S(1)}, u32[]{:S(2)}, u32[]{:S(2)}) %collective-permute-start.7) | collective-permute-done | bytes 524320 | tf_op jit(solution)/shard_map/ppermute | solution.py:41
  83.2 1.4 collective-permute-start.27
  84.6 1.8 %collective-permute-start.28 = (f32[512,256]{1,0:T(8,128)S(1)}, f32[512,256]{1,0:T(8,128)S(1)}, u32[]{:S(2)}, u32[]{:S(2)}) collective-permute-start(f32[512,256]{1,0:T(8,128)S(1)} %get-tuple-element.63), channel_id=1, source_target_pairs={{0,24},{8,0},{16,8},{24,16},{32,56},{40,32},{48,40},{56,48},{64,88... | collective-permute-start | bytes 1572872 | tf_op jit(solution)/shard_map/ppermute | solution.py:45
  87.1 2.2 %plan.1.plan_ref = s32[256]{0:T(256)S(1)} custom-call(s32[128]{0:T(128)S(1)} %bitcast.29, s32[128]{0:T(128)S(1)} %bitcast.30, s32[1,1]{1,0:T(1,128)S(6)} %copy.19.refs_2_), custom_call_target="tpu_custom_call" | custom-call | bytes 1048576 | tf_op jit(solution)/shard_map/plan/pallas_call | solution.py:385
  89.3 1.6 %combine.2 = (f32[16,128,256]{2,1,0:T(8,128)S(1)}, bf16[33,128,256]{2,1,0:T(8,128)(2,1)S(1)}) custom-call(s32[256]{0:T(256)S(1)} %plan.1.plan_ref, s32[2,16]{1,0:T(2,128)S(1)} %bitcast.25, f32[128,128,128]{2,1,0:T(8,128)S(1)} %bitcast.14, f32[264,256]{1,0:T(8,128)S(1)} %get-tuple-element.39.refs_0_, f32[264,256]{1,0:T(8,128)S(1)} %collective-permute-done.refs_1_.refs_11_, ...), custom_call_target="tpu_custom_call" | custom-call | flops 2147483648 | bytes 10485760 | tf_op jit(solution)/shard_map/combine/pallas_call | solution.py:275
  91.0 5.4 %collective-permute-done.24.refs_9_ = f32[512,256]{1,0:T(8,128)S(1)} collective-permute-done((f32[512,256]{1,0:T(8,128)S(1)}, f32[512,256]{1,0:T(8,128)S(1)}, u32[]{:S(2)}, u32[]{:S(2)}) %collective-permute-start.24) | collective-permute-done | bytes 524320 | tf_op jit(solution)/shard_map/ppermute | solution.py:41
  96.4 2.5 %collective-permute-start.12 = (f32[16,128,256]{2,1,0:T(8,128)S(1)}, f32[16,128,256]{2,1,0:T(8,128)S(1)}, u32[]{:S(2)}, u32[]{:S(2)}) collective-permute-start(f32[16,128,256]{2,1,0:T(8,128)S(1)} %get-tuple-element.48), channel_id=1, source_target_pairs={{0,1},{1,0},{2,3},{3,2},{4,5},{5,4},{6,7},{7,6},{8,9},{9,8},{10,11... | collective-permute-start | bytes 6291464 | tf_op jit(solution)/shard_map/ppermute | solution.py:406
  98.9 2.9 %collective-permute-done.26.refs_11_ = f32[512,256]{1,0:T(8,128)S(1)} collective-permute-done((f32[512,256]{1,0:T(8,128)S(1)}, f32[512,256]{1,0:T(8,128)S(1)}, u32[]{:S(2)}, u32[]{:S(2)}) %collective-permute-start.26) | collective-permute-done | bytes 524320 | tf_op jit(solution)/shard_map/ppermute | solution.py:45
  101.8 2.5 %collective-permute-done.27.refs_12_ = f32[512,256]{1,0:T(8,128)S(1)} collective-permute-done((f32[512,256]{1,0:T(8,128)S(1)}, f32[512,256]{1,0:T(8,128)S(1)}, u32[]{:S(2)}, u32[]{:S(2)}) %collective-permute-start.27) | collective-permute-done | bytes 524320 | tf_op jit(solution)/shard_map/ppermute | solution.py:45
  104.3 3.8 %collective-permute-done.28.refs_13_ = f32[512,256]{1,0:T(8,128)S(1)} collective-permute-done((f32[512,256]{1,0:T(8,128)S(1)}, f32[512,256]{1,0:T(8,128)S(1)}, u32[]{:S(2)}, u32[]{:S(2)}) %collective-permute-start.28) | collective-permute-done | bytes 524320 | tf_op jit(solution)/shard_map/ppermute | solution.py:45
  108.1 1.5 combine.3
  109.7 2.2 %collective-permute-start.29 = (f32[16,128,256]{2,1,0:T(8,128)S(1)}, f32[16,128,256]{2,1,0:T(8,128)S(1)}, u32[]{:S(2)}, u32[]{:S(2)}) collective-permute-start(f32[16,128,256]{2,1,0:T(8,128)S(1)} %get-tuple-element.65), channel_id=1, source_target_pairs={{0,1},{1,0},{2,3},{3,2},{4,5},{5,4},{6,7},{7,6},{8,9},{9,8},{10,11... | collective-permute-start | bytes 6291464 | tf_op jit(solution)/shard_map/ppermute | solution.py:406
  111.9 1.4 keep.2.keep_ref
  113.5 1.8 %collective-permute-start.13 = (f32[2,128,256]{2,1,0:T(8,128)S(1)}, f32[2,128,256]{2,1,0:T(8,128)S(1)}, u32[]{:S(2)}, u32[]{:S(2)}) collective-permute-start(f32[2,128,256]{2,1,0:T(8,128)S(1)} %get-tuple-element.52), channel_id=1, source_target_pairs={{0,2},{1,3},{2,4},{3,5},{4,6},{5,7},{6,0},{7,1},{8,10},{9,11},{10,... | collective-permute-start | bytes 786440 | tf_op jit(solution)/shard_map/ppermute | solution.py:419
  115.3 1.4 collective-permute-start.14
  116.6 1.3 keep.3.keep_ref
  118.3 2.7 %collective-permute-start.31 = (f32[2,128,256]{2,1,0:T(8,128)S(1)}, f32[2,128,256]{2,1,0:T(8,128)S(1)}, u32[]{:S(2)}, u32[]{:S(2)}) collective-permute-start(f32[2,128,256]{2,1,0:T(8,128)S(1)} %get-tuple-element.70), channel_id=1, source_target_pairs={{0,6},{1,7},{2,0},{3,1},{4,2},{5,3},{6,4},{7,5},{8,14},{9,15},{10,... | collective-permute-start | bytes 786440 | tf_op jit(solution)/shard_map/ppermute | solution.py:420
  121.0 2.4 %collective-permute-done.13.from_left_ref = f32[2,128,256]{2,1,0:T(8,128)S(1)} collective-permute-done((f32[2,128,256]{2,1,0:T(8,128)S(1)}, f32[2,128,256]{2,1,0:T(8,128)S(1)}, u32[]{:S(2)}, u32[]{:S(2)}) %collective-permute-start.13) | collective-permute-done | bytes 262176 | tf_op jit(solution)/shard_map/ppermute | solution.py:419
  123.6 2.7 %collective-permute-start.16 = (f32[4,128,256]{2,1,0:T(8,128)S(1)}, f32[4,128,256]{2,1,0:T(8,128)S(1)}, u32[]{:S(2)}, u32[]{:S(2)}) collective-permute-start(f32[4,128,256]{2,1,0:T(8,128)S(1)} %get-tuple-element.55), channel_id=1, source_target_pairs={{0,6},{1,7},{2,0},{3,1},{4,2},{5,3},{6,4},{7,5},{8,14},{9,15},{10,... | collective-permute-start | bytes 1572872 | tf_op jit(solution)/shard_map/ppermute | solution.py:432
  126.3 2.8 %collective-permute-done.30.from_left_ref = f32[2,128,256]{2,1,0:T(8,128)S(1)} collective-permute-done((f32[2,128,256]{2,1,0:T(8,128)S(1)}, f32[2,128,256]{2,1,0:T(8,128)S(1)}, u32[]{:S(2)}, u32[]{:S(2)}) %collective-permute-start.30) | collective-permute-done | bytes 262176 | tf_op jit(solution)/shard_map/ppermute | solution.py:419
  129.2 2.7 %collective-permute-start.33 = (f32[4,128,256]{2,1,0:T(8,128)S(1)}, f32[4,128,256]{2,1,0:T(8,128)S(1)}, u32[]{:S(2)}, u32[]{:S(2)}) collective-permute-start(f32[4,128,256]{2,1,0:T(8,128)S(1)} %get-tuple-element.72), channel_id=1, source_target_pairs={{0,6},{1,7},{2,0},{3,1},{4,2},{5,3},{6,4},{7,5},{8,14},{9,15},{10,... | collective-permute-start | bytes 1572872 | tf_op jit(solution)/shard_map/ppermute | solution.py:432
  131.9 7.4 %collective-permute-done.15 = f32[4,128,256]{2,1,0:T(8,128)S(1)} collective-permute-done((f32[4,128,256]{2,1,0:T(8,128)S(1)}, f32[4,128,256]{2,1,0:T(8,128)S(1)}, u32[]{:S(2)}, u32[]{:S(2)}) %collective-permute-start.15) | collective-permute-done | bytes 524320 | tf_op jit(solution)/shard_map/ppermute | solution.py:431
  139.4 1.3 begin.1.before_ref
  140.7 9.9 %collective-permute-done.32 = f32[4,128,256]{2,1,0:T(8,128)S(1)} collective-permute-done((f32[4,128,256]{2,1,0:T(8,128)S(1)}, f32[4,128,256]{2,1,0:T(8,128)S(1)}, u32[]{:S(2)}, u32[]{:S(2)}) %collective-permute-start.32) | collective-permute-done | bytes 524320 | tf_op jit(solution)/shard_map/ppermute | solution.py:431
  150.6 3.4 %end.1 = bf16[512,512]{1,0:T(8,128)(2,1)} custom-call(f32[512,512]{1,0:T(8,128)S(1)} %copy-done.2, bf16[512,2048]{1,0:T(8,128)(2,1)S(1)} %copy-done.3, f32[512,2048]{1,0:T(8,128)S(1)} %begin.1.before_ref, bf16[2048,512]{1,0:T(8,128)(2,1)S(1)} %copy-done.4, f32[1,512]{1,0:T(1,128)S(1)} %bitcast.28, f32[512,256]{1,0:T(8,128)S(1)} %bitcast.19, ...), custom_call_target="tpu_custom_call" | custom-call | flops 1610612736 | bytes 8388608 | tf_op jit(solution)/shard_map/end/pallas_call | solution.py:447
  (54 shorter events, 3.1 us)
Async XLA Ops:
  0.0 1.2 copy-start.1
  1.2 0.7 copy-start.5
  1.9 87.4 %copy-start = (f32[1,1,128,128,128]{4,3,2,1,0:T(8,128)S(1)}, f32[1,1,128,128,128]{4,3,2,1,0:T(8,128)}, u32[]{:S(2)}) copy-start(f32[1,1,128,128,128]{4,3,2,1,0:T(8,128)} %param.11) | copy-start | bytes 25165828
  2.3 9.5 %collective-permute-start.19 = (f32[256,256]{1,0:T(8,128)S(1)}, f32[256,256]{1,0:T(8,128)S(1)}, u32[]{:S(2)}, u32[]{:S(2)}) collective-permute-start(f32[256,256]{1,0:T(8,128)S(1)} %get-tuple-element.56.refs_0_), channel_id=1, source_target_pairs={{0,8},{8,16},{16,24},{24,0},{32,40},{40,48},{48,56},{56,32},{64,72... | collective-permute-start | bytes 786440 | tf_op jit(solution)/shard_map/ppermute | solution.py:45
  4.5 14.0 %collective-permute-start.18 = (f32[256,256]{1,0:T(8,128)S(1)}, f32[256,256]{1,0:T(8,128)S(1)}, u32[]{:S(2)}, u32[]{:S(2)}) collective-permute-start(f32[256,256]{1,0:T(8,128)S(1)} %get-tuple-element.56.refs_0_), channel_id=1, source_target_pairs={{0,16},{8,24},{16,0},{24,8},{32,48},{40,56},{48,32},{56,40},{64,80... | collective-permute-start | bytes 786440 | tf_op jit(solution)/shard_map/ppermute | solution.py:45
  7.1 21.4 %collective-permute-start.2 = (f32[264,256]{1,0:T(8,128)S(1)}, f32[264,256]{1,0:T(8,128)S(1)}, u32[]{:S(2)}, u32[]{:S(2)}) collective-permute-start(f32[264,256]{1,0:T(8,128)S(1)} %get-tuple-element.39.refs_0_), channel_id=1, source_target_pairs={{0,8},{8,16},{16,24},{24,0},{32,40},{40,48},{48,56},{56,32},{64,72... | collective-permute-start | bytes 811016 | tf_op jit(solution)/shard_map/ppermute | solution.py:45
  7.1 15.1 %collective-permute-start.17 = (f32[256,256]{1,0:T(8,128)S(1)}, f32[256,256]{1,0:T(8,128)S(1)}, u32[]{:S(2)}, u32[]{:S(2)}) collective-permute-start(f32[256,256]{1,0:T(8,128)S(1)} %get-tuple-element.56.refs_0_), channel_id=1, source_target_pairs={{0,24},{8,0},{16,8},{24,16},{32,56},{40,32},{48,40},{56,48},{64,88... | collective-permute-start | bytes 786440 | tf_op jit(solution)/shard_map/ppermute | solution.py:45
  9.8 12.8 %collective-permute-start.22 = (f32[256,256]{1,0:T(8,128)S(1)}, f32[256,256]{1,0:T(8,128)S(1)}, u32[]{:S(2)}, u32[]{:S(2)}) collective-permute-start(f32[256,256]{1,0:T(8,128)S(1)} %get-tuple-element.57.refs_4_), channel_id=1, source_target_pairs={{0,32},{8,40},{16,48},{24,56},{32,64},{40,72},{48,80},{56,88},{64,... | collective-permute-start | bytes 786440 | tf_op jit(solution)/shard_map/ppermute | solution.py:41
  11.8 13.1 %collective-permute-start.21 = (f32[256,256]{1,0:T(8,128)S(1)}, f32[256,256]{1,0:T(8,128)S(1)}, u32[]{:S(2)}, u32[]{:S(2)}) collective-permute-start(f32[256,256]{1,0:T(8,128)S(1)} %get-tuple-element.57.refs_4_), channel_id=1, source_target_pairs={{0,64},{8,72},{16,80},{24,88},{32,96},{40,104},{48,112},{56,120},{... | collective-permute-start | bytes 786440 | tf_op jit(solution)/shard_map/ppermute | solution.py:41
  18.5 9.8 %collective-permute-start.20 = (f32[256,256]{1,0:T(8,128)S(1)}, f32[256,256]{1,0:T(8,128)S(1)}, u32[]{:S(2)}, u32[]{:S(2)}) collective-permute-start(f32[256,256]{1,0:T(8,128)S(1)} %get-tuple-element.57.refs_4_), channel_id=1, source_target_pairs={{0,96},{8,104},{16,112},{24,120},{32,0},{40,8},{48,16},{56,24},{64... | collective-permute-start | bytes 786440 | tf_op jit(solution)/shard_map/ppermute | solution.py:41
  22.2 9.5 %collective-permute-start.1 = (f32[264,256]{1,0:T(8,128)S(1)}, f32[264,256]{1,0:T(8,128)S(1)}, u32[]{:S(2)}, u32[]{:S(2)}) collective-permute-start(f32[264,256]{1,0:T(8,128)S(1)} %get-tuple-element.39.refs_0_), channel_id=1, source_target_pairs={{0,16},{8,24},{16,0},{24,8},{32,48},{40,56},{48,32},{56,40},{64,80... | collective-permute-start | bytes 811016 | tf_op jit(solution)/shard_map/ppermute | solution.py:45
  22.6 10.0 %collective-permute-start = (f32[264,256]{1,0:T(8,128)S(1)}, f32[264,256]{1,0:T(8,128)S(1)}, u32[]{:S(2)}, u32[]{:S(2)}) collective-permute-start(f32[264,256]{1,0:T(8,128)S(1)} %get-tuple-element.39.refs_0_), channel_id=1, source_target_pairs={{0,24},{8,0},{16,8},{24,16},{32,56},{40,32},{48,40},{56,48},{64,88... | collective-permute-start | bytes 811016 | tf_op jit(solution)/shard_map/ppermute | solution.py:45
  24.9 7.7 %collective-permute-start.5 = (f32[264,256]{1,0:T(8,128)S(1)}, f32[264,256]{1,0:T(8,128)S(1)}, u32[]{:S(2)}, u32[]{:S(2)}) collective-permute-start(f32[264,256]{1,0:T(8,128)S(1)} %get-tuple-element.40.refs_4_), channel_id=1, source_target_pairs={{0,32},{8,40},{16,48},{24,56},{32,64},{40,72},{48,80},{56,88},{64,... | collective-permute-start | bytes 811016 | tf_op jit(solution)/shard_map/ppermute | solution.py:41
  28.3 10.1 %collective-permute-start.4 = (f32[264,256]{1,0:T(8,128)S(1)}, f32[264,256]{1,0:T(8,128)S(1)}, u32[]{:S(2)}, u32[]{:S(2)}) collective-permute-start(f32[264,256]{1,0:T(8,128)S(1)} %get-tuple-element.40.refs_4_), channel_id=1, source_target_pairs={{0,64},{8,72},{16,80},{24,88},{32,96},{40,104},{48,112},{56,120},{... | collective-permute-start | bytes 811016 | tf_op jit(solution)/shard_map/ppermute | solution.py:41
  28.5 15.0 %collective-permute-start.3 = (f32[264,256]{1,0:T(8,128)S(1)}, f32[264,256]{1,0:T(8,128)S(1)}, u32[]{:S(2)}, u32[]{:S(2)}) collective-permute-start(f32[264,256]{1,0:T(8,128)S(1)} %get-tuple-element.40.refs_4_), channel_id=1, source_target_pairs={{0,96},{8,104},{16,112},{24,120},{32,0},{40,8},{48,16},{56,24},{64... | collective-permute-start | bytes 811016 | tf_op jit(solution)/shard_map/ppermute | solution.py:41
  44.7 42.4 %copy-start.8 = (s32[1,1,128]{2,1,0:T(1,128)S(1)}, s32[1,1,128]{2,1,0:T(1,128)}, u32[]{:S(2)}) copy-start(s32[1,1,128]{2,1,0:T(1,128)} %param.12) | copy-start | bytes 1540
  44.7 42.4 %copy-start.9 = (s32[1,1,128]{2,1,0:T(1,128)S(1)}, s32[1,1,128]{2,1,0:T(1,128)}, u32[]{:S(2)}) copy-start(s32[1,1,128]{2,1,0:T(1,128)} %param.13) | copy-start | bytes 1540
  44.7 14.1 %collective-permute-start.23 = (f32[512,256]{1,0:T(8,128)S(1)}, f32[512,256]{1,0:T(8,128)S(1)}, u32[]{:S(2)}, u32[]{:S(2)}) collective-permute-start(f32[512,256]{1,0:T(8,128)S(1)} %get-tuple-element.58), channel_id=1, source_target_pairs={{0,32},{8,40},{16,48},{24,56},{32,64},{40,72},{48,80},{56,88},{64,... | collective-permute-start | bytes 1572872 | tf_op jit(solution)/shard_map/ppermute | solution.py:41
  47.4 22.6 %collective-permute-start.6 = (f32[512,256]{1,0:T(8,128)S(1)}, f32[512,256]{1,0:T(8,128)S(1)}, u32[]{:S(2)}, u32[]{:S(2)}) collective-permute-start(f32[512,256]{1,0:T(8,128)S(1)} %get-tuple-element.41), channel_id=1, source_target_pairs={{0,32},{8,40},{16,48},{24,56},{32,64},{40,72},{48,80},{56,88},{64,... | collective-permute-start | bytes 1572872 | tf_op jit(solution)/shard_map/ppermute | solution.py:41
  47.5 35.6 %collective-permute-start.7 = (f32[512,256]{1,0:T(8,128)S(1)}, f32[512,256]{1,0:T(8,128)S(1)}, u32[]{:S(2)}, u32[]{:S(2)}) collective-permute-start(f32[512,256]{1,0:T(8,128)S(1)} %get-tuple-element.42), channel_id=1, source_target_pairs={{0,64},{8,72},{16,80},{24,88},{32,96},{40,104},{48,112},{56,120},{... | collective-permute-start | bytes 1572872 | tf_op jit(solution)/shard_map/ppermute | solution.py:41
  50.8 32.3 %collective-permute-start.8 = (f32[512,256]{1,0:T(8,128)S(1)}, f32[512,256]{1,0:T(8,128)S(1)}, u32[]{:S(2)}, u32[]{:S(2)}) collective-permute-start(f32[512,256]{1,0:T(8,128)S(1)} %get-tuple-element.43), channel_id=1, source_target_pairs={{0,96},{8,104},{16,112},{24,120},{32,0},{40,8},{48,16},{56,24},{64... | collective-permute-start | bytes 1572872 | tf_op jit(solution)/shard_map/ppermute | solution.py:41
  52.7 30.3 %collective-permute-start.9 = (f32[512,256]{1,0:T(8,128)S(1)}, f32[512,256]{1,0:T(8,128)S(1)}, u32[]{:S(2)}, u32[]{:S(2)}) collective-permute-start(f32[512,256]{1,0:T(8,128)S(1)} %get-tuple-element.44), channel_id=1, source_target_pairs={{0,8},{8,16},{16,24},{24,0},{32,40},{40,48},{48,56},{56,32},{64,72... | collective-permute-start | bytes 1572872 | tf_op jit(solution)/shard_map/ppermute | solution.py:45
  58.8 24.4 %collective-permute-start.10 = (f32[512,256]{1,0:T(8,128)S(1)}, f32[512,256]{1,0:T(8,128)S(1)}, u32[]{:S(2)}, u32[]{:S(2)}) collective-permute-start(f32[512,256]{1,0:T(8,128)S(1)} %get-tuple-element.45), channel_id=1, source_target_pairs={{0,16},{8,24},{16,0},{24,8},{32,48},{40,56},{48,32},{56,40},{64,80... | collective-permute-start | bytes 1572872 | tf_op jit(solution)/shard_map/ppermute | solution.py:45
  70.0 14.6 %collective-permute-start.11 = (f32[512,256]{1,0:T(8,128)S(1)}, f32[512,256]{1,0:T(8,128)S(1)}, u32[]{:S(2)}, u32[]{:S(2)}) collective-permute-start(f32[512,256]{1,0:T(8,128)S(1)} %get-tuple-element.46), channel_id=1, source_target_pairs={{0,24},{8,0},{16,8},{24,16},{32,56},{40,32},{48,40},{56,48},{64,88... | collective-permute-start | bytes 1572872 | tf_op jit(solution)/shard_map/ppermute | solution.py:45
  83.1 13.3 %collective-permute-start.24 = (f32[512,256]{1,0:T(8,128)S(1)}, f32[512,256]{1,0:T(8,128)S(1)}, u32[]{:S(2)}, u32[]{:S(2)}) collective-permute-start(f32[512,256]{1,0:T(8,128)S(1)} %get-tuple-element.59), channel_id=1, source_target_pairs={{0,64},{8,72},{16,80},{24,88},{32,96},{40,104},{48,112},{56,120},{... | collective-permute-start | bytes 1572872 | tf_op jit(solution)/shard_map/ppermute | solution.py:41
  83.1 15.8 %collective-permute-start.25 = (f32[512,256]{1,0:T(8,128)S(1)}, f32[512,256]{1,0:T(8,128)S(1)}, u32[]{:S(2)}, u32[]{:S(2)}) collective-permute-start(f32[512,256]{1,0:T(8,128)S(1)} %get-tuple-element.60), channel_id=1, source_target_pairs={{0,96},{8,104},{16,112},{24,120},{32,0},{40,8},{48,16},{56,24},{64... | collective-permute-start | bytes 1572872 | tf_op jit(solution)/shard_map/ppermute | solution.py:41
  83.1 18.7 %collective-permute-start.26 = (f32[512,256]{1,0:T(8,128)S(1)}, f32[512,256]{1,0:T(8,128)S(1)}, u32[]{:S(2)}, u32[]{:S(2)}) collective-permute-start(f32[512,256]{1,0:T(8,128)S(1)} %get-tuple-element.61), channel_id=1, source_target_pairs={{0,8},{8,16},{16,24},{24,0},{32,40},{40,48},{48,56},{56,32},{64,72... | collective-permute-start | bytes 1572872 | tf_op jit(solution)/shard_map/ppermute | solution.py:45
  83.2 21.1 %collective-permute-start.27 = (f32[512,256]{1,0:T(8,128)S(1)}, f32[512,256]{1,0:T(8,128)S(1)}, u32[]{:S(2)}, u32[]{:S(2)}) collective-permute-start(f32[512,256]{1,0:T(8,128)S(1)} %get-tuple-element.62), channel_id=1, source_target_pairs={{0,16},{8,24},{16,0},{24,8},{32,48},{40,56},{48,32},{56,40},{64,80... | collective-permute-start | bytes 1572872 | tf_op jit(solution)/shard_map/ppermute | solution.py:45
  84.6 23.5 %collective-permute-start.28 = (f32[512,256]{1,0:T(8,128)S(1)}, f32[512,256]{1,0:T(8,128)S(1)}, u32[]{:S(2)}, u32[]{:S(2)}) collective-permute-start(f32[512,256]{1,0:T(8,128)S(1)} %get-tuple-element.63), channel_id=1, source_target_pairs={{0,24},{8,0},{16,8},{24,16},{32,56},{40,32},{48,40},{56,48},{64,88... | collective-permute-start | bytes 1572872 | tf_op jit(solution)/shard_map/ppermute | solution.py:45
  96.4 16.9 %collective-permute-start.12 = (f32[16,128,256]{2,1,0:T(8,128)S(1)}, f32[16,128,256]{2,1,0:T(8,128)S(1)}, u32[]{:S(2)}, u32[]{:S(2)}) collective-permute-start(f32[16,128,256]{2,1,0:T(8,128)S(1)} %get-tuple-element.48), channel_id=1, source_target_pairs={{0,1},{1,0},{2,3},{3,2},{4,5},{5,4},{6,7},{7,6},{8,9},{9,8},{10,11... | collective-permute-start | bytes 6291464 | tf_op jit(solution)/shard_map/ppermute | solution.py:406
  109.7 8.3 %collective-permute-start.29 = (f32[16,128,256]{2,1,0:T(8,128)S(1)}, f32[16,128,256]{2,1,0:T(8,128)S(1)}, u32[]{:S(2)}, u32[]{:S(2)}) collective-permute-start(f32[16,128,256]{2,1,0:T(8,128)S(1)} %get-tuple-element.65), channel_id=1, source_target_pairs={{0,1},{1,0},{2,3},{3,2},{4,5},{5,4},{6,7},{7,6},{8,9},{9,8},{10,11... | collective-permute-start | bytes 6291464 | tf_op jit(solution)/shard_map/ppermute | solution.py:406
  113.5 9.9 %collective-permute-start.13 = (f32[2,128,256]{2,1,0:T(8,128)S(1)}, f32[2,128,256]{2,1,0:T(8,128)S(1)}, u32[]{:S(2)}, u32[]{:S(2)}) collective-permute-start(f32[2,128,256]{2,1,0:T(8,128)S(1)} %get-tuple-element.52), channel_id=1, source_target_pairs={{0,2},{1,3},{2,4},{3,5},{4,6},{5,7},{6,0},{7,1},{8,10},{9,11},{10,... | collective-permute-start | bytes 786440 | tf_op jit(solution)/shard_map/ppermute | solution.py:419
  115.3 8.2 %collective-permute-start.14 = (f32[2,128,256]{2,1,0:T(8,128)S(1)}, f32[2,128,256]{2,1,0:T(8,128)S(1)}, u32[]{:S(2)}, u32[]{:S(2)}) collective-permute-start(f32[2,128,256]{2,1,0:T(8,128)S(1)} %get-tuple-element.53), channel_id=1, source_target_pairs={{0,6},{1,7},{2,0},{3,1},{4,2},{5,3},{6,4},{7,5},{8,14},{9,15},{10,... | collective-permute-start | bytes 786440 | tf_op jit(solution)/shard_map/ppermute | solution.py:420
  118.2 21.1 %copy-start.2 = (f32[512,512]{1,0:T(8,128)S(1)}, f32[512,512]{1,0:T(8,128)}, u32[]{:S(2)}) copy-start(f32[512,512]{1,0:T(8,128)} %feature_ref.5) | copy-start | bytes 3145732
  118.2 21.1 %copy-start.3 = (bf16[512,2048]{1,0:T(8,128)(2,1)S(1)}, bf16[512,2048]{1,0:T(8,128)(2,1)}, u32[]{:S(2)}) copy-start(bf16[512,2048]{1,0:T(8,128)(2,1)} %w_ref.3) | copy-start | bytes 6291460
  118.2 21.1 %copy-start.6 = (f32[2048]{0:T(1024)S(1)}, f32[2048]{0:T(1024)}, u32[]{:S(2)}) copy-start(f32[2048]{0:T(1024)} %param.17) | copy-start | bytes 24580
  118.2 10.8 %collective-permute-start.30 = (f32[2,128,256]{2,1,0:T(8,128)S(1)}, f32[2,128,256]{2,1,0:T(8,128)S(1)}, u32[]{:S(2)}, u32[]{:S(2)}) collective-permute-start(f32[2,128,256]{2,1,0:T(8,128)S(1)} %get-tuple-element.69), channel_id=1, source_target_pairs={{0,2},{1,3},{2,4},{3,5},{4,6},{5,7},{6,0},{7,1},{8,10},{9,11},{10,... | collective-permute-start | bytes 786440 | tf_op jit(solution)/shard_map/ppermute | solution.py:419
  118.3 10.7 %collective-permute-start.31 = (f32[2,128,256]{2,1,0:T(8,128)S(1)}, f32[2,128,256]{2,1,0:T(8,128)S(1)}, u32[]{:S(2)}, u32[]{:S(2)}) collective-permute-start(f32[2,128,256]{2,1,0:T(8,128)S(1)} %get-tuple-element.70), channel_id=1, source_target_pairs={{0,6},{1,7},{2,0},{3,1},{4,2},{5,3},{6,4},{7,5},{8,14},{9,15},{10,... | collective-permute-start | bytes 786440 | tf_op jit(solution)/shard_map/ppermute | solution.py:420
  123.5 15.8 %collective-permute-start.15 = (f32[4,128,256]{2,1,0:T(8,128)S(1)}, f32[4,128,256]{2,1,0:T(8,128)S(1)}, u32[]{:S(2)}, u32[]{:S(2)}) collective-permute-start(f32[4,128,256]{2,1,0:T(8,128)S(1)} %get-tuple-element.54), channel_id=1, source_target_pairs={{0,2},{1,3},{2,4},{3,5},{4,6},{5,7},{6,0},{7,1},{8,10},{9,11},{10,... | collective-permute-start | bytes 1572872 | tf_op jit(solution)/shard_map/ppermute | solution.py:431
  123.6 15.7 %collective-permute-start.16 = (f32[4,128,256]{2,1,0:T(8,128)S(1)}, f32[4,128,256]{2,1,0:T(8,128)S(1)}, u32[]{:S(2)}, u32[]{:S(2)}) collective-permute-start(f32[4,128,256]{2,1,0:T(8,128)S(1)} %get-tuple-element.55), channel_id=1, source_target_pairs={{0,6},{1,7},{2,0},{3,1},{4,2},{5,3},{6,4},{7,5},{8,14},{9,15},{10,... | collective-permute-start | bytes 1572872 | tf_op jit(solution)/shard_map/ppermute | solution.py:432
  129.1 21.4 %collective-permute-start.32 = (f32[4,128,256]{2,1,0:T(8,128)S(1)}, f32[4,128,256]{2,1,0:T(8,128)S(1)}, u32[]{:S(2)}, u32[]{:S(2)}) collective-permute-start(f32[4,128,256]{2,1,0:T(8,128)S(1)} %get-tuple-element.71), channel_id=1, source_target_pairs={{0,2},{1,3},{2,4},{3,5},{4,6},{5,7},{6,0},{7,1},{8,10},{9,11},{10,... | collective-permute-start | bytes 1572872 | tf_op jit(solution)/shard_map/ppermute | solution.py:431
  129.2 21.3 %collective-permute-start.33 = (f32[4,128,256]{2,1,0:T(8,128)S(1)}, f32[4,128,256]{2,1,0:T(8,128)S(1)}, u32[]{:S(2)}, u32[]{:S(2)}) collective-permute-start(f32[4,128,256]{2,1,0:T(8,128)S(1)} %get-tuple-element.72), channel_id=1, source_target_pairs={{0,6},{1,7},{2,0},{3,1},{4,2},{5,3},{6,4},{7,5},{8,14},{9,15},{10,... | collective-permute-start | bytes 1572872 | tf_op jit(solution)/shard_map/ppermute | solution.py:432
  139.3 11.2 %copy-start.4 = (bf16[2048,512]{1,0:T(8,128)(2,1)S(1)}, bf16[2048,512]{1,0:T(8,128)(2,1)}, u32[]{:S(2)}) copy-start(bf16[2048,512]{1,0:T(8,128)(2,1)} %w_out_ref.1) | copy-start | bytes 6291460
  139.3 11.2 %copy-start.7 = (f32[512]{0:T(512)S(1)}, f32[512]{0:T(512)}, u32[]{:S(2)}) copy-start(f32[512]{0:T(512)} %param.19) | copy-start | bytes 6148

commit v4 on v3

--- a/solution.py
+++ b/solution.py
@@ -12,10 +12,11 @@
 side = 4
 cores = 2
 picks = 2
-parts = 3
+lists = 4
+across_x = side // 2
 note_rows = 8
 lanes = 128
-chunk = 512
+chunk = 256
 
 in_vmem = pl.BlockSpec(memory_space=pltpu.VMEM)
 in_smem = pl.BlockSpec(memory_space=pltpu.SMEM)
@@ -84,37 +85,41 @@
         copy.wait()
 
 
-def join(keep_ref, arrived_ref, mine_ref, right_ref, left_ref, over_right_ref, over_left_ref):
-    size = mine_ref.shape[0]
-    cut = size // 2
-    for at, out in enumerate((mine_ref, right_ref, None, left_ref)):
-        spot = slice(at * size, (at + 1) * size)
-        if out is None:
-            first, last = slice(at * size, at * size + cut), slice(at * size + cut, spot.stop)
-            over_right_ref[...] = keep_ref[first] + arrived_ref[first]
-            over_left_ref[...] = keep_ref[last] + arrived_ref[last]
-        else:
-            out[...] = keep_ref[spot] + arrived_ref[spot]
+def join_across(keep_ref, arrived_ref, over_right_ref, over_left_ref):
+    cut = over_right_ref.shape[0]
+    over_right_ref[...] = keep_ref[:cut] + arrived_ref[:cut]
+    over_left_ref[...] = keep_ref[cut:] + arrived_ref[cut:]
+
+
+def join_rest(keep_ref, arrived_ref, *outs):
+    start = 0
+    for out in outs:
+        spot = slice(start, start + out.shape[0])
+        out[...] = keep_ref[spot] + arrived_ref[spot]
+        start = spot.stop
 
 
 def relay(right_ref, left_ref, from_left_ref, from_right_ref, right_out, left_out):
-    cut = from_left_ref.shape[0]
-    right_out[:cut] = right_ref[:cut] + from_left_ref[...]
-    left_out[cut:] = left_ref[cut:] + from_right_ref[...]
+    right_out[...] = right_ref[...] + from_left_ref[...]
+    left_out[...] = left_ref[...] + from_right_ref[...]
 
 
 def log(value):
     return value.bit_length() - 1
 
 
-def pairs_of(tile_total, blocks):
-    return (tile_total + blocks) // 2 + unroll
+def places_of(which, blocks_dev):
+    return blocks_dev * (1 if which % 2 == 0 else side - 1)
+
+
+def pairs_of(tile_total, blocks_dev):
+    return (tile_total + places_of(1, blocks_dev)) // 2 + unroll
 
 
 def plan(row_ref, col_ref, count_ref, plan_ref, waiting, blocks_dev):
     tile_total = row_ref.shape[0]
-    blocks = side * blocks_dev
-    entries = pairs_of(tile_total, blocks)
+    blocks = places_of(1, blocks_dev)
+    entries = pairs_of(tile_total, blocks_dev)
     slot_bits = log(tile_total)
     code_bits = slot_bits + log(side * side * picks) + 1
     empty = (side * side * picks) << slot_bits
@@ -126,37 +131,42 @@
     def pair(place, first, second):
         return first | (second << code_bits) | (place << (2 * code_bits))
 
-    for place in range(2 * blocks):
+    for place in range(lists * blocks):
         waiting[place] = -1
-
-    def turn(slot, ends):
+    for which in range(lists):
+        waiting[lists * blocks + which] = 0
+
+    def turn(slot, carry):
         target = row_ref[slot]
         source = col_ref[slot]
         column = lax.shift_right_logical(target, log(blocks_dev))
         away_x = (lax.shift_right_logical(column, log(cores)) - my_x) & (side - 1)
-        place = away_x * blocks_dev + (target & (blocks_dev - 1))
-        kept = 1 - ((column & (cores - 1)) ^ my_core)
+        across = (away_x == across_x).astype(jnp.int32)
+        order_x = jnp.where(across == 1, 0, away_x - (away_x > across_x).astype(jnp.int32))
+        place = order_x * blocks_dev + (target & (blocks_dev - 1))
+        which = 2 * (1 - ((column & (cores - 1)) ^ my_core)) + 1 - across
         owner = lax.shift_right_logical(source, log(picks))
         away_z = (lax.shift_right_logical(owner, log(side)) - my_z) & (side - 1)
         away_y = (owner - my_y) & (side - 1)
         pos = (away_z * side + away_y) * picks + (source & (picks - 1))
         code = slot | (pos << slot_bits)
-        before = waiting[kept * blocks + place]
-        full = (before >= 0).astype(jnp.int32)
-        end = jnp.where(kept == 1, ends[1], ends[0])
-        plan_ref[kept * entries + end] = pair(place, before, code)
-        waiting[kept * blocks + place] = jnp.where(before >= 0, -1, code)
-        return ends[0] + full * (1 - kept), ends[1] + full * kept
-
-    ends = list(lax.fori_loop(0, count_ref[0, 0], turn, (0, 0)))
-    for kept in range(2):
-        for place in range(blocks):
-            before = waiting[kept * blocks + place]
-            plan_ref[kept * entries + ends[kept]] = pair(place, before, empty)
-            ends[kept] = ends[kept] + (before >= 0).astype(jnp.int32)
+        before = waiting[which * blocks + place]
+        end = waiting[lists * blocks + which]
+        plan_ref[which * entries + end] = pair(place, before, code)
+        waiting[which * blocks + place] = jnp.where(before >= 0, -1, code)
+        waiting[lists * blocks + which] = end + (before >= 0).astype(jnp.int32)
+        return carry
+
+    lax.fori_loop(0, count_ref[0, 0], turn, 0)
+    for which in range(lists):
+        end = waiting[lists * blocks + which]
+        for place in range(places_of(which, blocks_dev)):
+            before = waiting[which * blocks + place]
+            plan_ref[which * entries + end] = pair(place, before, empty)
+            end = end + (before >= 0).astype(jnp.int32)
         for extra in range(unroll):
-            plan_ref[kept * entries + ends[kept] + extra] = pair(0, empty, empty)
-        plan_ref[2 * entries + kept] = ends[kept]
+            plan_ref[which * entries + end + extra] = pair(0, empty, empty)
+        plan_ref[lists * entries + which] = end
 
 
 def pack(half, *refs):
@@ -207,10 +217,10 @@
     )(*first, *second, *notes)
 
 
-def add_tiles(kept, plan_ref, tile_ref, pool, total):
+def add_tiles(which, blocks_dev, plan_ref, tile_ref, pool, total):
     tile_total = tile_ref.shape[0]
     sources = pool.shape[0] - 1
-    entries = pairs_of(tile_total, total.shape[0])
+    entries = pairs_of(tile_total, blocks_dev)
     slot_bits = log(tile_total)
     pos_bits = log(sources) + 1
     total[...] = jnp.zeros_like(total)
@@ -218,7 +228,7 @@
     def turn(step, carry):
         products = []
         for lane in range(unroll):
-            code = plan_ref[kept * entries + step * unroll + lane]
+            code = plan_ref[which * entries + step * unroll + lane]
             left, right = [], []
             for _ in range(2):
                 left.append(tile_ref[code & (tile_total - 1)].astype(jnp.bfloat16))
@@ -235,11 +245,11 @@
             total[target] += product
         return carry
 
-    count = plan_ref[2 * entries + kept]
+    count = plan_ref[lists * entries + which]
     lax.fori_loop(0, (count + unroll - 1) // unroll, turn, 0)
 
 
-def combine(plan_ref, need_ref, tile_ref, *refs):
+def combine(blocks_dev, plan_ref, need_ref, tile_ref, *refs):
     first, second = refs[:side], refs[side : 2 * side]
     along_z = refs[2 * side : 3 * side - 1]
     along_y = refs[3 * side - 1 : 4 * side - 2]
@@ -267,17 +277,17 @@
                     spot, :
                 ].astype(pool.dtype)
     pool[side * side * picks] = jnp.zeros(pool.shape[1:], pool.dtype)
-    add_tiles(0, plan_ref, tile_ref, pool, total)
-
-
-def combine_sent(listed, need, tiles, first, second, along_z, along_y, blocks):
+    add_tiles(0, blocks_dev, plan_ref, tile_ref, pool, total)
+
+
+def combine_sent(listed, need, tiles, first, second, along_z, along_y, blocks_dev):
     edge = tiles.shape[1]
     return pl.pallas_call(
-        combine,
+        lambda *refs: combine(blocks_dev, *refs),
         in_specs=[in_smem] * 2 + [in_vmem] * (4 * side - 1),
         out_specs=[in_vmem] * 2,
         out_shape=[
-            jax.ShapeDtypeStruct((blocks, edge, span), jnp.float32),
+            jax.ShapeDtypeStruct((places_of(0, blocks_dev), edge, span), jnp.float32),
             jax.ShapeDtypeStruct((side * side * picks + 1, edge, span), jnp.bfloat16),
         ],
         compiler_params=pltpu.CompilerParams(vmem_limit_bytes=10 << 20),
@@ -286,58 +296,59 @@
     )(listed, need, tiles, *first, *second, *along_z, *along_y)
 
 
-def combine_kept(listed, tiles, pool, blocks):
+def combine_listed(which, listed, tiles, pool, blocks_dev):
     edge = tiles.shape[1]
     return pl.pallas_call(
-        lambda plan_ref, tile_ref, pool, total: add_tiles(1, plan_ref, tile_ref, pool, total),
+        lambda *refs: add_tiles(which, blocks_dev, *refs),
         in_specs=[in_smem] + [in_vmem] * 2,
         out_specs=in_vmem,
-        out_shape=jax.ShapeDtypeStruct((blocks, edge, span), jnp.float32),
+        out_shape=jax.ShapeDtypeStruct((places_of(which, blocks_dev), edge, span), jnp.float32),
         compiler_params=pltpu.CompilerParams(vmem_limit_bytes=6 << 20),
         cost_estimate=pl.CostEstimate(flops=2 << 30, bytes_accessed=8 << 20, transcendentals=0),
-        name="keep",
+        name="listed",
     )(listed, tiles, pool)
 
 
-def mixed_of(group, feature_ref, totals):
+def mix(group, feature_ref, totals, mixed):
     part = slice(group * span, (group + 1) * span)
-    summed = totals[0][...]
-    for other in totals[1:]:
-        summed = summed + other[...]
-    return ((1.0 + gin_epsilon) * feature_ref[:, part] + summed).astype(jnp.bfloat16)
+    mine, rest = totals[0], totals[1:]
+    rows = rest[0].shape[0]
+    for at in range(2):
+        spot = slice(at * rows, (at + 1) * rows)
+        summed = mine[spot, :] + rest[2 * at][...] + rest[2 * at + 1][...]
+        mixed[spot, :] = ((1.0 + gin_epsilon) * feature_ref[spot, part] + summed).astype(mixed.dtype)
 
 
 def begin_mlp(feature_ref, w_ref, bias_ref, *refs):
-    totals, out_ref, mixed = refs[:parts], refs[parts], refs[parts + 1]
-    mixed[...] = mixed_of(0, feature_ref, totals)
+    totals, (out_ref, mixed) = refs[:-2], refs[-2:]
+    mix(0, feature_ref, totals, mixed)
 
     def turn(step, carry):
         part = pl.ds(pl.multiple_of(step * chunk, chunk), chunk)
-        out_ref[:, part] = (
-            jnp.dot(mixed[...], w_ref[:span, part], preferred_element_type=jnp.float32)
-            + bias_ref[:, part]
+        out_ref[part, :] = (
+            jnp.dot(mixed[part, :], w_ref[:span, :], preferred_element_type=jnp.float32)
+            + bias_ref[...]
         )
         return carry
 
-    lax.fori_loop(0, w_ref.shape[1] // chunk, turn, 0)
+    lax.fori_loop(0, out_ref.shape[0] // chunk, turn, 0)
 
 
 def end_mlp(feature_ref, w_ref, before_ref, w_out_ref, bias_ref, *refs):
-    totals, out_ref, mixed, total = refs[:parts], refs[parts], refs[parts + 1], refs[parts + 2]
-    mixed[...] = mixed_of(1, feature_ref, totals)
-    total[...] = jnp.broadcast_to(bias_ref[...], total.shape)
+    totals, (out_ref, mixed) = refs[:-2], refs[-2:]
+    mix(1, feature_ref, totals, mixed)
 
     def turn(step, carry):
         part = pl.ds(pl.multiple_of(step * chunk, chunk), chunk)
-        hidden = before_ref[:, part] + jnp.dot(
-            mixed[...], w_ref[span:, part], preferred_element_type=jnp.float32
+        hidden = before_ref[part, :] + jnp.dot(
+            mixed[part, :], w_ref[span:, :], preferred_element_type=jnp.float32
         )
         hidden = jnp.maximum(hidden, 0.0).astype(jnp.bfloat16)
-        total[...] += jnp.dot(hidden, w_out_ref[part, :], preferred_element_type=jnp.float32)
+        updated = jnp.dot(hidden, w_out_ref[...], preferred_element_type=jnp.float32)
+        out_ref[part, :] = (updated + bias_ref[...]).astype(out_ref.dtype)
         return carry
 
-    lax.fori_loop(0, w_ref.shape[1] // chunk, turn, 0)
-    out_ref[...] = total[...].astype(out_ref.dtype)
+    lax.fori_loop(0, out_ref.shape[0] // chunk, turn, 0)
 
 
 def on_device(
@@ -348,7 +359,7 @@
     nodes, width = features.shape
     blocks_dev = nodes // edge
     hidden_size = w_in.shape[1]
-    blocks = side * blocks_dev
+    blocks = places_of(1, blocks_dev)
     groups = width // span
     rows = nodes // 2
 
@@ -386,8 +397,8 @@
         lambda *refs: plan(*refs, blocks_dev),
         in_specs=[in_smem] * 3,
         out_specs=in_smem,
-        out_shape=jax.ShapeDtypeStruct((256,), jnp.int32),
-        scratch_shapes=[pltpu.SMEM((2 * blocks,), jnp.int32)],
+        out_shape=jax.ShapeDtypeStruct((512,), jnp.int32),
+        scratch_shapes=[pltpu.SMEM((lists * (blocks + 1),), jnp.int32)],
         compiler_params=pltpu.CompilerParams(vmem_limit_bytes=1 << 20),
         cost_estimate=pl.CostEstimate(flops=0, bytes_accessed=1 << 20, transcendentals=0),
         name="plan",
@@ -402,39 +413,59 @@
         for away in (1, 3, 2):
             along_z[away - 1] = from_z(packed[away - 1], -away)
             along_y[away - 1] = from_y(packed[side + away - 2], -away)
-        send, pool = combine_sent(listed, need, cell_tiles, first, second, along_z, along_y, blocks)
+        send, pool = combine_sent(
+            listed, need, cell_tiles, first, second, along_z, along_y, blocks_dev
+        )
         arrived = lax.ppermute(send, "col", col_shift(0, 1))
-        keep = combine_kept(listed, cell_tiles, pool, blocks)
-        full = jax.ShapeDtypeStruct((blocks_dev, edge, span), jnp.float32)
-        part = jax.ShapeDtypeStruct((blocks_dev // 2, edge, span), jnp.float32)
-        mine, right, left, over_right, over_left = pl.pallas_call(
-            join,
+        keep = combine_listed(2, listed, cell_tiles, pool, blocks_dev)
+        over_right, over_left = pl.pallas_call(
+            join_across,
             in_specs=[in_vmem] * 2,
-            out_specs=[in_vmem] * 5,
-            out_shape=[full] * 3 + [part] * 2,
+            out_specs=[in_vmem] * 2,
+            out_shape=[jax.ShapeDtypeStruct((blocks_dev // 2, edge, span), jnp.float32)] * 2,
+            compiler_params=pltpu.CompilerParams(vmem_limit_bytes=4 << 20),
+            cost_estimate=pl.CostEstimate(flops=0, bytes_accessed=2 << 20, transcendentals=0),
+            name="join",
+        )(keep, arrived)
+        relay_right = lax.ppermute(over_right, "col", col_shift(1, 0))
+        relay_left = lax.ppermute(over_left, "col", col_shift(-1, 0))
+        send = combine_listed(1, listed, cell_tiles, pool, blocks_dev)
+        arrived = lax.ppermute(send, "col", col_shift(0, 1))
+        keep = combine_listed(3, listed, cell_tiles, pool, blocks_dev)
+        cut = blocks_dev // 2
+        sizes = (blocks_dev, cut, cut, cut, cut)
+        mine, right_held, right, left, left_held = pl.pallas_call(
+            join_rest,
+            in_specs=[in_vmem] * 2,
+            out_specs=[in_vmem] * len(sizes),
+            out_shape=[jax.ShapeDtypeStruct((n, edge, span), jnp.float32) for n in sizes],
             compiler_params=pltpu.CompilerParams(vmem_limit_bytes=6 << 20),
             cost_estimate=pl.CostEstimate(flops=0, bytes_accessed=4 << 20, transcendentals=0),
             name="join",
         )(keep, arrived)
-        relay_right = lax.ppermute(over_right, "col", col_shift(1, 0))
-        relay_left = lax.ppermute(over_left, "col", col_shift(-1, 0))
-        right, left = pl.pallas_call(
+        from_left = lax.ppermute(right, "col", col_shift(1, 0))
+        from_right = lax.ppermute(left, "col", col_shift(-1, 0))
+        right_held, left_held = pl.pallas_call(
             relay,
             in_specs=[in_vmem] * 4,
             out_specs=[in_vmem] * 2,
-            out_shape=[full] * 2,
-            input_output_aliases={0: 0, 1: 1},
-            compiler_params=pltpu.CompilerParams(vmem_limit_bytes=5 << 20),
+            out_shape=[jax.ShapeDtypeStruct((cut, edge, span), jnp.float32)] * 2,
+            compiler_params=pltpu.CompilerParams(vmem_limit_bytes=4 << 20),
             cost_estimate=pl.CostEstimate(flops=0, bytes_accessed=2 << 20, transcendentals=0),
             name="relay",
-        )(right, left, relay_right, relay_left)
-        from_left = lax.ppermute(right, "col", col_shift(1, 0))
-        from_right = lax.ppermute(left, "col", col_shift(-1, 0))
-        sums.append([v.reshape(nodes, span) for v in (mine, from_left, from_right)])
+        )(right_held, left_held, relay_right, relay_left)
+        from_left_held = lax.ppermute(right_held, "col", col_shift(1, 0))
+        from_right_held = lax.ppermute(left_held, "col", col_shift(-1, 0))
+        sums.append(
+            [
+                v.reshape(-1, span)
+                for v in (mine, from_left_held, from_right, from_left, from_right_held)
+            ]
+        )
 
     before = pl.pallas_call(
         begin_mlp,
-        in_specs=[in_vmem] * (3 + parts),
+        in_specs=[in_vmem] * (3 + len(sums[0])),
         out_specs=in_vmem,
         out_shape=jax.ShapeDtypeStruct((nodes, hidden_size), jnp.float32),
         scratch_shapes=[pltpu.VMEM((nodes, span), jnp.bfloat16)],
@@ -446,14 +477,11 @@
     )(features, w_in, bias_in.reshape(1, -1), *sums[0])
     return pl.pallas_call(
         end_mlp,
-        in_specs=[in_vmem] * (5 + parts),
+        in_specs=[in_vmem] * (5 + len(sums[1])),
         out_specs=in_vmem,
         out_shape=jax.ShapeDtypeStruct((nodes, width), jnp.bfloat16),
-        scratch_shapes=[
-            pltpu.VMEM((nodes, span), jnp.bfloat16),
-            pltpu.VMEM((nodes, width), jnp.float32),
-        ],
-        compiler_params=pltpu.CompilerParams(vmem_limit_bytes=6 << 20),
+        scratch_shapes=[pltpu.VMEM((nodes, span), jnp.bfloat16)],
+        compiler_params=pltpu.CompilerParams(vmem_limit_bytes=8 << 20),
         cost_estimate=pl.CostEstimate(
             flops=3 << 29, bytes_accessed=8 << 20, transcendentals=0
         ),

time: 155 us -> 157 us (1.013)
  starting transfers between devices: 48 us -> 51.1 us
  waiting for transfers between devices: 86.8 us -> 84 us
  Pallas kernels: 16.3 us -> 18.5 us
    ppermute x2, waiting for transfers between devices: 17.3 us -> 0.01 us  [on_device(): from_left = lax.ppermute(right, 'col', col_shift(1, 0))]
    ppermute x2, waiting for transfers between devices: 0.01 us -> 8.37 us  [on_device(): from_right = lax.ppermute(left, 'col', col_shift(-1, 0))]
    ppermute x0 -> x4, waiting for transfers between devices: none -> 6.34 us  [the longest x2 5.52 us: on_device(): from_left_held = lax.ppermute(right_held, 'col', col_shift(1, 0))]
    ppermute x0 -> x4, starting transfers between devices: none -> 4.26 us  [the longest x2 3.33 us: on_device(): from_right_held = lax.ppermute(left_held, 'col', col_shift(-1, 0))]
    ppermute x2, starting transfers between devices: 5.33 us -> 2.66 us  [on_device(): from_right = lax.ppermute(left, 'col', col_shift(-1, 0))]
    ppermute x2 -> x4, waiting for transfers between devices: 0.01 us -> 2.35 us  [on_device(): arrived = lax.ppermute(send, 'col', col_shift(0, 1))]
    pallas_call x8 -> x14, Pallas kernels: 11.1 us -> 13.2 us  [the longest x6 6.46 us: combine_listed(): pl.pallas_call(lambda *refs: add_tiles(which, blocks_dev, *refs), in_spec...]
    ppermute x2, waiting for transfers between devices: 5.19 us -> 3.55 us  [on_device(): relay_right = lax.ppermute(over_right, 'col', col_shift(1, 0))]
  transfers between devices with their start and end apart: 34 -> 40, of which waited for: 18 -> 22; matrix products, arithmetic and copies ran while one was open for 0% -> 0% of each run, Pallas kernels for 7% -> 9%
where the time goes in v4:
time: 157 us
  waiting for transfers between devices  84 us (54%)
  starting transfers between devices  51.1 us (33%)
  Pallas kernels  18.5 us (12%)
  local copies, waits for them, and re-layouts  1.96 us (1%)
    ppermute x12, waiting for transfers between devices, from_z(): return lax.ppermute(value, 'row', row_shift(-step, 0))  49.7 us
    ppermute x12, starting transfers between devices, from_z(): return lax.ppermute(value, 'row', row_shift(-step, 0))  19.3 us
    ppermute x12, waiting for transfers between devices, from_y(): return lax.ppermute(value, 'row', row_shift(0, -step))  13.7 us
    ppermute x12, starting transfers between devices, from_y(): return lax.ppermute(value, 'row', row_shift(0, -step))  12.6 us
    ppermute x2, waiting for transfers between devices, on_device(): from_right = lax.ppermute(left, 'col', col_shift(-1, 0))  8.37 us
    pallas_call x6, Pallas kernels, combine_listed(): pl.pallas_call(lambda *refs: add_tiles(which, blocks_dev, *refs), in_spec...  6.46 us
    ppermute x2, waiting for transfers between devices, on_device(): from_left_held = lax.ppermute(right_held, 'col', col_shift(1, 0))  5.52 us
    ppermute x4, starting transfers between devices, on_device(): arrived = lax.ppermute(send, 'col', col_shift(0, 1))  5.21 us
  transfers between devices with their start and end apart: 40, of which 22 were waited for; matrix products, arithmetic and copies ran while one was open for 0% of the time, Pallas kernels for 9%

profile of v4, /device:TPU:1, one launch (start us, length us, event | category | flops | bytes accessed | tf_op | source)
XLA Modules:
  0.0 156.6 jit_solution(6580421499183072406)
XLA Ops:
  0.0 1.2 copy-done.1
  2.3 2.2 %collective-permute-start.22 = (f32[256,256]{1,0:T(8,128)S(1)}, f32[256,256]{1,0:T(8,128)S(1)}, u32[]{:S(2)}, u32[]{:S(2)}) collective-permute-start(f32[256,256]{1,0:T(8,128)S(1)} %get-tuple-element.62.refs_0_.refs_3_), channel_id=1, source_target_pairs={{0,8},{8,16},{16,24},{24,0},{32,40},{40,48},{48,56},{56,32},{64,72... | collective-permute-start | bytes 786440 | tf_op jit(solution)/shard_map/ppermute | solution.py:46
  4.5 2.6 %collective-permute-start.21 = (f32[256,256]{1,0:T(8,128)S(1)}, f32[256,256]{1,0:T(8,128)S(1)}, u32[]{:S(2)}, u32[]{:S(2)}) collective-permute-start(f32[256,256]{1,0:T(8,128)S(1)} %get-tuple-element.62.refs_0_.refs_3_), channel_id=1, source_target_pairs={{0,16},{8,24},{16,0},{24,8},{32,48},{40,56},{48,32},{56,40},{64,80... | collective-permute-start | bytes 786440 | tf_op jit(solution)/shard_map/ppermute | solution.py:46
  7.1 2.7 %collective-permute-start.20 = (f32[256,256]{1,0:T(8,128)S(1)}, f32[256,256]{1,0:T(8,128)S(1)}, u32[]{:S(2)}, u32[]{:S(2)}) collective-permute-start(f32[256,256]{1,0:T(8,128)S(1)} %get-tuple-element.62.refs_0_.refs_3_), channel_id=1, source_target_pairs={{0,24},{8,0},{16,8},{24,16},{32,56},{40,32},{48,40},{56,48},{64,88... | collective-permute-start | bytes 786440 | tf_op jit(solution)/shard_map/ppermute | solution.py:46
  9.8 1.6 %collective-permute-start.25 = (f32[256,256]{1,0:T(8,128)S(1)}, f32[256,256]{1,0:T(8,128)S(1)}, u32[]{:S(2)}, u32[]{:S(2)}) collective-permute-start(f32[256,256]{1,0:T(8,128)S(1)} %get-tuple-element.63.refs_4_.refs_7_), channel_id=1, source_target_pairs={{0,32},{8,40},{16,48},{24,56},{32,64},{40,72},{48,80},{56,88},{64,... | collective-permute-start | bytes 786440 | tf_op jit(solution)/shard_map/ppermute | solution.py:42
  11.8 3.5 %collective-permute-start.24 = (f32[256,256]{1,0:T(8,128)S(1)}, f32[256,256]{1,0:T(8,128)S(1)}, u32[]{:S(2)}, u32[]{:S(2)}) collective-permute-start(f32[256,256]{1,0:T(8,128)S(1)} %get-tuple-element.63.refs_4_.refs_7_), channel_id=1, source_target_pairs={{0,64},{8,72},{16,80},{24,88},{32,96},{40,104},{48,112},{56,120},{... | collective-permute-start | bytes 786440 | tf_op jit(solution)/shard_map/ppermute | solution.py:42
  15.3 3.2 %collective-permute-done.21.refs_2_.refs_5_ = f32[256,256]{1,0:T(8,128)S(1)} collective-permute-done((f32[256,256]{1,0:T(8,128)S(1)}, f32[256,256]{1,0:T(8,128)S(1)}, u32[]{:S(2)}, u32[]{:S(2)}) %collective-permute-start.21) | collective-permute-done | bytes 262176 | tf_op jit(solution)/shard_map/ppermute | solution.py:46
  18.5 3.8 %collective-permute-start.23 = (f32[256,256]{1,0:T(8,128)S(1)}, f32[256,256]{1,0:T(8,128)S(1)}, u32[]{:S(2)}, u32[]{:S(2)}) collective-permute-start(f32[256,256]{1,0:T(8,128)S(1)} %get-tuple-element.63.refs_4_.refs_7_), channel_id=1, source_target_pairs={{0,96},{8,104},{16,112},{24,120},{32,0},{40,8},{48,16},{56,24},{64... | collective-permute-start | bytes 786440 | tf_op jit(solution)/shard_map/ppermute | solution.py:42
  23.5 1.4 collective-permute-done.24.refs_6_.refs_9_
  25.1 3.2 %collective-permute-done.23.refs_5_.refs_8_ = f32[256,256]{1,0:T(8,128)S(1)} collective-permute-done((f32[256,256]{1,0:T(8,128)S(1)}, f32[256,256]{1,0:T(8,128)S(1)}, u32[]{:S(2)}, u32[]{:S(2)}) %collective-permute-start.23) | collective-permute-done | bytes 262176 | tf_op jit(solution)/shard_map/ppermute | solution.py:42
  28.5 3.3 %collective-permute-start.3 = (f32[264,256]{1,0:T(8,128)S(1)}, f32[264,256]{1,0:T(8,128)S(1)}, u32[]{:S(2)}, u32[]{:S(2)}) collective-permute-start(f32[264,256]{1,0:T(8,128)S(1)} %get-tuple-element.44.refs_4_.refs_7_), channel_id=1, source_target_pairs={{0,96},{8,104},{16,112},{24,120},{32,0},{40,8},{48,16},{56,24},{64... | collective-permute-start | bytes 811016 | tf_op jit(solution)/shard_map/ppermute | solution.py:42
  32.6 5.8 %collective-permute-done.4.refs_6_.refs_9_ = f32[264,256]{1,0:T(8,128)S(1)} collective-permute-done((f32[264,256]{1,0:T(8,128)S(1)}, f32[264,256]{1,0:T(8,128)S(1)}, u32[]{:S(2)}, u32[]{:S(2)}) %collective-permute-start.4) | collective-permute-done | bytes 270368 | tf_op jit(solution)/shard_map/ppermute | solution.py:42
  38.5 5.0 %collective-permute-done.3.refs_5_.refs_8_ = f32[264,256]{1,0:T(8,128)S(1)} collective-permute-done((f32[264,256]{1,0:T(8,128)S(1)}, f32[264,256]{1,0:T(8,128)S(1)}, u32[]{:S(2)}, u32[]{:S(2)}) %collective-permute-start.3) | collective-permute-done | bytes 270368 | tf_op jit(solution)/shard_map/ppermute | solution.py:42
  43.4 1.2 pack.3
  44.7 1.5 collective-permute-start.26
  46.2 1.2 pack.2
  47.5 3.3 %collective-permute-start.7 = (f32[512,256]{1,0:T(8,128)S(1)}, f32[512,256]{1,0:T(8,128)S(1)}, u32[]{:S(2)}, u32[]{:S(2)}) collective-permute-start(f32[512,256]{1,0:T(8,128)S(1)} %get-tuple-element.46), channel_id=1, source_target_pairs={{0,64},{8,72},{16,80},{24,88},{32,96},{40,104},{48,112},{56,120},{... | collective-permute-start | bytes 1572872 | tf_op jit(solution)/shard_map/ppermute | solution.py:42
  50.8 2.0 %collective-permute-start.8 = (f32[512,256]{1,0:T(8,128)S(1)}, f32[512,256]{1,0:T(8,128)S(1)}, u32[]{:S(2)}, u32[]{:S(2)}) collective-permute-start(f32[512,256]{1,0:T(8,128)S(1)} %get-tuple-element.47), channel_id=1, source_target_pairs={{0,96},{8,104},{16,112},{24,120},{32,0},{40,8},{48,16},{56,24},{64... | collective-permute-start | bytes 1572872 | tf_op jit(solution)/shard_map/ppermute | solution.py:42
  52.8 6.1 %collective-permute-done.26.refs_11_ = f32[512,256]{1,0:T(8,128)S(1)} collective-permute-done((f32[512,256]{1,0:T(8,128)S(1)}, f32[512,256]{1,0:T(8,128)S(1)}, u32[]{:S(2)}, u32[]{:S(2)}) %collective-permute-start.26) | collective-permute-done | bytes 524320 | tf_op jit(solution)/shard_map/ppermute | solution.py:42
  58.8 11.2 %collective-permute-done.6.refs_11_ = f32[512,256]{1,0:T(8,128)S(1)} collective-permute-done((f32[512,256]{1,0:T(8,128)S(1)}, f32[512,256]{1,0:T(8,128)S(1)}, u32[]{:S(2)}, u32[]{:S(2)}) %collective-permute-start.6) | collective-permute-done | bytes 524320 | tf_op jit(solution)/shard_map/ppermute | solution.py:42
  70.6 12.5 %collective-permute-done.7.refs_12_ = f32[512,256]{1,0:T(8,128)S(1)} collective-permute-done((f32[512,256]{1,0:T(8,128)S(1)}, f32[512,256]{1,0:T(8,128)S(1)}, u32[]{:S(2)}, u32[]{:S(2)}) %collective-permute-start.7) | collective-permute-done | bytes 524320 | tf_op jit(solution)/shard_map/ppermute | solution.py:42
  83.2 1.4 collective-permute-start.30
  84.6 1.8 %collective-permute-start.31 = (f32[512,256]{1,0:T(8,128)S(1)}, f32[512,256]{1,0:T(8,128)S(1)}, u32[]{:S(2)}, u32[]{:S(2)}) collective-permute-start(f32[512,256]{1,0:T(8,128)S(1)} %get-tuple-element.69), channel_id=1, source_target_pairs={{0,24},{8,0},{16,8},{24,16},{32,56},{40,32},{48,40},{56,48},{64,88... | collective-permute-start | bytes 1572872 | tf_op jit(solution)/shard_map/ppermute | solution.py:46
  87.1 2.3 %plan.1.refs_0_ = s32[512]{0:T(512)S(1)} custom-call(s32[128]{0:T(128)S(1)} %bitcast.41, s32[128]{0:T(128)S(1)} %bitcast.42, s32[1,1]{1,0:T(1,128)S(6)} %copy.11.refs_2_), custom_call_target="tpu_custom_call" | custom-call | bytes 1048576 | tf_op jit(solution)/shard_map/plan/pallas_call | solution.py:396
  89.5 1.2 combine.2
  90.6 1.3 listed.7
  91.9 4.5 %collective-permute-done.27.refs_12_ = f32[512,256]{1,0:T(8,128)S(1)} collective-permute-done((f32[512,256]{1,0:T(8,128)S(1)}, f32[512,256]{1,0:T(8,128)S(1)}, u32[]{:S(2)}, u32[]{:S(2)}) %collective-permute-start.27) | collective-permute-done | bytes 524320 | tf_op jit(solution)/shard_map/ppermute | solution.py:42
  96.4 2.5 %collective-permute-start.12 = (f32[12,128,256]{2,1,0:T(8,128)S(1)}, f32[12,128,256]{2,1,0:T(8,128)S(1)}, u32[]{:S(2)}, u32[]{:S(2)}) collective-permute-start(f32[12,128,256]{2,1,0:T(8,128)S(1)} %listed.7), channel_id=1, source_target_pairs={{0,1},{1,0},{2,3},{3,2},{4,5},{5,4},{6,7},{7,6},{8,9},{9,8},{10,11... | collective-permute-start | bytes 4718600 | tf_op jit(solution)/shard_map/ppermute | solution.py:433
  98.9 2.9 %collective-permute-done.29.refs_14_ = f32[512,256]{1,0:T(8,128)S(1)} collective-permute-done((f32[512,256]{1,0:T(8,128)S(1)}, f32[512,256]{1,0:T(8,128)S(1)}, u32[]{:S(2)}, u32[]{:S(2)}) %collective-permute-start.29) | collective-permute-done | bytes 524320 | tf_op jit(solution)/shard_map/ppermute | solution.py:46
  101.8 2.5 %collective-permute-done.30.refs_15_ = f32[512,256]{1,0:T(8,128)S(1)} collective-permute-done((f32[512,256]{1,0:T(8,128)S(1)}, f32[512,256]{1,0:T(8,128)S(1)}, u32[]{:S(2)}, u32[]{:S(2)}) %collective-permute-start.30) | collective-permute-done | bytes 524320 | tf_op jit(solution)/shard_map/ppermute | solution.py:46
  104.3 3.8 %collective-permute-done.31.refs_16_ = f32[512,256]{1,0:T(8,128)S(1)} collective-permute-done((f32[512,256]{1,0:T(8,128)S(1)}, f32[512,256]{1,0:T(8,128)S(1)}, u32[]{:S(2)}, u32[]{:S(2)}) %collective-permute-start.31) | collective-permute-done | bytes 524320 | tf_op jit(solution)/shard_map/ppermute | solution.py:46
  108.1 1.1 combine.3
  109.3 1.3 listed.10
  110.6 2.2 %collective-permute-start.32 = (f32[12,128,256]{2,1,0:T(8,128)S(1)}, f32[12,128,256]{2,1,0:T(8,128)S(1)}, u32[]{:S(2)}, u32[]{:S(2)}) collective-permute-start(f32[12,128,256]{2,1,0:T(8,128)S(1)} %listed.10), channel_id=1, source_target_pairs={{0,1},{1,0},{2,3},{3,2},{4,5},{5,4},{6,7},{7,6},{8,9},{9,8},{10,11... | collective-permute-start | bytes 4718600 | tf_op jit(solution)/shard_map/ppermute | solution.py:433
  114.3 2.3 %collective-permute-done.13.arrived_ref = f32[4,128,256]{2,1,0:T(8,128)S(1)} collective-permute-done((f32[4,128,256]{2,1,0:T(8,128)S(1)}, f32[4,128,256]{2,1,0:T(8,128)S(1)}, u32[]{:S(2)}, u32[]{:S(2)}) %collective-permute-start.13) | collective-permute-done | bytes 524320 | tf_op jit(solution)/shard_map/ppermute | solution.py:419
  116.7 1.6 %collective-permute-start.14 = (f32[2,128,256]{2,1,0:T(8,128)S(1)}, f32[2,128,256]{2,1,0:T(8,128)S(1)}, u32[]{:S(2)}, u32[]{:S(2)}) collective-permute-start(f32[2,128,256]{2,1,0:T(8,128)S(1)} %get-tuple-element.56), channel_id=1, source_target_pairs={{0,2},{1,3},{2,4},{3,5},{4,6},{5,7},{6,0},{7,1},{8,10},{9,11},{10,... | collective-permute-start | bytes 786440 | tf_op jit(solution)/shard_map/ppermute | solution.py:430
  118.3 1.3 collective-permute-start.15
  121.8 2.9 %collective-permute-start.35 = (f32[2,128,256]{2,1,0:T(8,128)S(1)}, f32[2,128,256]{2,1,0:T(8,128)S(1)}, u32[]{:S(2)}, u32[]{:S(2)}) collective-permute-start(f32[2,128,256]{2,1,0:T(8,128)S(1)} %get-tuple-element.76), channel_id=1, source_target_pairs={{0,6},{1,7},{2,0},{3,1},{4,2},{5,3},{6,4},{7,5},{8,14},{9,15},{10,... | collective-permute-start | bytes 786440 | tf_op jit(solution)/shard_map/ppermute | solution.py:431
  126.5 2.0 %collective-permute-start.19 = (f32[2,128,256]{2,1,0:T(8,128)S(1)}, f32[2,128,256]{2,1,0:T(8,128)S(1)}, u32[]{:S(2)}, u32[]{:S(2)}) collective-permute-start(f32[2,128,256]{2,1,0:T(8,128)S(1)} %get-tuple-element.61), channel_id=1, source_target_pairs={{0,6},{1,7},{2,0},{3,1},{4,2},{5,3},{6,4},{7,5},{8,14},{9,15},{10,... | collective-permute-start | bytes 786440 | tf_op jit(solution)/shard_map/ppermute | solution.py:458
  128.5 2.8 %collective-permute-done.34.from_left_ref = f32[2,128,256]{2,1,0:T(8,128)S(1)} collective-permute-done((f32[2,128,256]{2,1,0:T(8,128)S(1)}, f32[2,128,256]{2,1,0:T(8,128)S(1)}, u32[]{:S(2)}, u32[]{:S(2)}) %collective-permute-start.34) | collective-permute-done | bytes 262176 | tf_op jit(solution)/shard_map/ppermute | solution.py:430
  131.3 1.4 collective-permute-start.17
  134.2 2.7 %collective-permute-done.16 = f32[2,128,256]{2,1,0:T(8,128)S(1)} collective-permute-done((f32[2,128,256]{2,1,0:T(8,128)S(1)}, f32[2,128,256]{2,1,0:T(8,128)S(1)}, u32[]{:S(2)}, u32[]{:S(2)}) %collective-permute-start.16) | collective-permute-done | bytes 262176 | tf_op jit(solution)/shard_map/ppermute | solution.py:457
  136.9 1.4 collective-permute-start.39
  138.3 1.3 collective-permute-start.37
  139.6 2.8 %collective-permute-done.17 = f32[2,128,256]{2,1,0:T(8,128)S(1)} collective-permute-done((f32[2,128,256]{2,1,0:T(8,128)S(1)}, f32[2,128,256]{2,1,0:T(8,128)S(1)}, u32[]{:S(2)}, u32[]{:S(2)}) %collective-permute-start.17) | collective-permute-done | bytes 262176 | tf_op jit(solution)/shard_map/ppermute | solution.py:447
  144.3 2.8 %collective-permute-done.36 = f32[2,128,256]{2,1,0:T(8,128)S(1)} collective-permute-done((f32[2,128,256]{2,1,0:T(8,128)S(1)}, f32[2,128,256]{2,1,0:T(8,128)S(1)}, u32[]{:S(2)}, u32[]{:S(2)}) %collective-permute-start.36) | collective-permute-done | bytes 262176 | tf_op jit(solution)/shard_map/ppermute | solution.py:457
  147.9 5.6 %collective-permute-done.37 = f32[2,128,256]{2,1,0:T(8,128)S(1)} collective-permute-done((f32[2,128,256]{2,1,0:T(8,128)S(1)}, f32[2,128,256]{2,1,0:T(8,128)S(1)}, u32[]{:S(2)}, u32[]{:S(2)}) %collective-permute-start.37) | collective-permute-done | bytes 262176 | tf_op jit(solution)/shard_map/ppermute | solution.py:447
  153.6 3.0 %end.1 = bf16[512,512]{1,0:T(8,128)(2,1)} custom-call(f32[512,512]{1,0:T(8,128)S(1)} %copy-done.2, bf16[512,2048]{1,0:T(8,128)(2,1)S(1)} %copy-done.3, f32[512,2048]{1,0:T(8,128)S(1)} %begin.1.before_ref, bf16[2048,512]{1,0:T(8,128)(2,1)S(1)} %copy-done.4, f32[1,512]{1,0:T(1,128)S(1)} %bitcast.40, f32[512,256]{1,0:T(8,128)S(1)} %bitcast.27, ...), custom_call_target="tpu_custom_call" | custom-call | flops 1610612736 | bytes 8388608 | tf_op jit(solution)/shard_map/end/pallas_call | solution.py:478
  (74 shorter events, 14.4 us)
Async XLA Ops:
  1.9 87.5 %copy-start = (f32[1,1,128,128,128]{4,3,2,1,0:T(8,128)S(1)}, f32[1,1,128,128,128]{4,3,2,1,0:T(8,128)}, u32[]{:S(2)}) copy-start(f32[1,1,128,128,128]{4,3,2,1,0:T(8,128)} %param.11) | copy-start | bytes 25165828
  2.3 9.5 %collective-permute-start.22 = (f32[256,256]{1,0:T(8,128)S(1)}, f32[256,256]{1,0:T(8,128)S(1)}, u32[]{:S(2)}, u32[]{:S(2)}) collective-permute-start(f32[256,256]{1,0:T(8,128)S(1)} %get-tuple-element.62.refs_0_.refs_3_), channel_id=1, source_target_pairs={{0,8},{8,16},{16,24},{24,0},{32,40},{40,48},{48,56},{56,32},{64,72... | collective-permute-start | bytes 786440 | tf_op jit(solution)/shard_map/ppermute | solution.py:46
  4.5 14.0 %collective-permute-start.21 = (f32[256,256]{1,0:T(8,128)S(1)}, f32[256,256]{1,0:T(8,128)S(1)}, u32[]{:S(2)}, u32[]{:S(2)}) collective-permute-start(f32[256,256]{1,0:T(8,128)S(1)} %get-tuple-element.62.refs_0_.refs_3_), channel_id=1, source_target_pairs={{0,16},{8,24},{16,0},{24,8},{32,48},{40,56},{48,32},{56,40},{64,80... | collective-permute-start | bytes 786440 | tf_op jit(solution)/shard_map/ppermute | solution.py:46
  7.1 21.4 %collective-permute-start.2 = (f32[264,256]{1,0:T(8,128)S(1)}, f32[264,256]{1,0:T(8,128)S(1)}, u32[]{:S(2)}, u32[]{:S(2)}) collective-permute-start(f32[264,256]{1,0:T(8,128)S(1)} %get-tuple-element.43.refs_0_.refs_3_), channel_id=1, source_target_pairs={{0,8},{8,16},{16,24},{24,0},{32,40},{40,48},{48,56},{56,32},{64,72... | collective-permute-start | bytes 811016 | tf_op jit(solution)/shard_map/ppermute | solution.py:46
  7.1 15.1 %collective-permute-start.20 = (f32[256,256]{1,0:T(8,128)S(1)}, f32[256,256]{1,0:T(8,128)S(1)}, u32[]{:S(2)}, u32[]{:S(2)}) collective-permute-start(f32[256,256]{1,0:T(8,128)S(1)} %get-tuple-element.62.refs_0_.refs_3_), channel_id=1, source_target_pairs={{0,24},{8,0},{16,8},{24,16},{32,56},{40,32},{48,40},{56,48},{64,88... | collective-permute-start | bytes 786440 | tf_op jit(solution)/shard_map/ppermute | solution.py:46
  9.8 12.8 %collective-permute-start.25 = (f32[256,256]{1,0:T(8,128)S(1)}, f32[256,256]{1,0:T(8,128)S(1)}, u32[]{:S(2)}, u32[]{:S(2)}) collective-permute-start(f32[256,256]{1,0:T(8,128)S(1)} %get-tuple-element.63.refs_4_.refs_7_), channel_id=1, source_target_pairs={{0,32},{8,40},{16,48},{24,56},{32,64},{40,72},{48,80},{56,88},{64,... | collective-permute-start | bytes 786440 | tf_op jit(solution)/shard_map/ppermute | solution.py:42
  11.8 13.1 %collective-permute-start.24 = (f32[256,256]{1,0:T(8,128)S(1)}, f32[256,256]{1,0:T(8,128)S(1)}, u32[]{:S(2)}, u32[]{:S(2)}) collective-permute-start(f32[256,256]{1,0:T(8,128)S(1)} %get-tuple-element.63.refs_4_.refs_7_), channel_id=1, source_target_pairs={{0,64},{8,72},{16,80},{24,88},{32,96},{40,104},{48,112},{56,120},{... | collective-permute-start | bytes 786440 | tf_op jit(solution)/shard_map/ppermute | solution.py:42
  18.5 9.8 %collective-permute-start.23 = (f32[256,256]{1,0:T(8,128)S(1)}, f32[256,256]{1,0:T(8,128)S(1)}, u32[]{:S(2)}, u32[]{:S(2)}) collective-permute-start(f32[256,256]{1,0:T(8,128)S(1)} %get-tuple-element.63.refs_4_.refs_7_), channel_id=1, source_target_pairs={{0,96},{8,104},{16,112},{24,120},{32,0},{40,8},{48,16},{56,24},{64... | collective-permute-start | bytes 786440 | tf_op jit(solution)/shard_map/ppermute | solution.py:42
  22.2 9.5 %collective-permute-start.1 = (f32[264,256]{1,0:T(8,128)S(1)}, f32[264,256]{1,0:T(8,128)S(1)}, u32[]{:S(2)}, u32[]{:S(2)}) collective-permute-start(f32[264,256]{1,0:T(8,128)S(1)} %get-tuple-element.43.refs_0_.refs_3_), channel_id=1, source_target_pairs={{0,16},{8,24},{16,0},{24,8},{32,48},{40,56},{48,32},{56,40},{64,80... | collective-permute-start | bytes 811016 | tf_op jit(solution)/shard_map/ppermute | solution.py:46
  22.6 10.0 %collective-permute-start = (f32[264,256]{1,0:T(8,128)S(1)}, f32[264,256]{1,0:T(8,128)S(1)}, u32[]{:S(2)}, u32[]{:S(2)}) collective-permute-start(f32[264,256]{1,0:T(8,128)S(1)} %get-tuple-element.43.refs_0_.refs_3_), channel_id=1, source_target_pairs={{0,24},{8,0},{16,8},{24,16},{32,56},{40,32},{48,40},{56,48},{64,88... | collective-permute-start | bytes 811016 | tf_op jit(solution)/shard_map/ppermute | solution.py:46
  24.9 7.7 %collective-permute-start.5 = (f32[264,256]{1,0:T(8,128)S(1)}, f32[264,256]{1,0:T(8,128)S(1)}, u32[]{:S(2)}, u32[]{:S(2)}) collective-permute-start(f32[264,256]{1,0:T(8,128)S(1)} %get-tuple-element.44.refs_4_.refs_7_), channel_id=1, source_target_pairs={{0,32},{8,40},{16,48},{24,56},{32,64},{40,72},{48,80},{56,88},{64,... | collective-permute-start | bytes 811016 | tf_op jit(solution)/shard_map/ppermute | solution.py:42
  28.3 10.1 %collective-permute-start.4 = (f32[264,256]{1,0:T(8,128)S(1)}, f32[264,256]{1,0:T(8,128)S(1)}, u32[]{:S(2)}, u32[]{:S(2)}) collective-permute-start(f32[264,256]{1,0:T(8,128)S(1)} %get-tuple-element.44.refs_4_.refs_7_), channel_id=1, source_target_pairs={{0,64},{8,72},{16,80},{24,88},{32,96},{40,104},{48,112},{56,120},{... | collective-permute-start | bytes 811016 | tf_op jit(solution)/shard_map/ppermute | solution.py:42
  28.5 15.0 %collective-permute-start.3 = (f32[264,256]{1,0:T(8,128)S(1)}, f32[264,256]{1,0:T(8,128)S(1)}, u32[]{:S(2)}, u32[]{:S(2)}) collective-permute-start(f32[264,256]{1,0:T(8,128)S(1)} %get-tuple-element.44.refs_4_.refs_7_), channel_id=1, source_target_pairs={{0,96},{8,104},{16,112},{24,120},{32,0},{40,8},{48,16},{56,24},{64... | collective-permute-start | bytes 811016 | tf_op jit(solution)/shard_map/ppermute | solution.py:42
  44.7 42.4 %copy-start.9 = (s32[1,1,128]{2,1,0:T(1,128)S(1)}, s32[1,1,128]{2,1,0:T(1,128)}, u32[]{:S(2)}) copy-start(s32[1,1,128]{2,1,0:T(1,128)} %param.12) | copy-start | bytes 1540
  44.7 42.4 %copy-start.10 = (s32[1,1,128]{2,1,0:T(1,128)S(1)}, s32[1,1,128]{2,1,0:T(1,128)}, u32[]{:S(2)}) copy-start(s32[1,1,128]{2,1,0:T(1,128)} %param.13) | copy-start | bytes 1540
  44.7 44.7 %copy-start.6 = (s32[1,1,16,2]{2,3,1,0:T(2,128)S(1)}, s32[1,1,16,2]{2,3,1,0:T(2,128)}, u32[]{:S(2)}) copy-start(s32[1,1,16,2]{2,3,1,0:T(2,128)} %param.15) | copy-start | bytes 388
  44.7 14.1 %collective-permute-start.26 = (f32[512,256]{1,0:T(8,128)S(1)}, f32[512,256]{1,0:T(8,128)S(1)}, u32[]{:S(2)}, u32[]{:S(2)}) collective-permute-start(f32[512,256]{1,0:T(8,128)S(1)} %get-tuple-element.64), channel_id=1, source_target_pairs={{0,32},{8,40},{16,48},{24,56},{32,64},{40,72},{48,80},{56,88},{64,... | collective-permute-start | bytes 1572872 | tf_op jit(solution)/shard_map/ppermute | solution.py:42
  47.4 22.6 %collective-permute-start.6 = (f32[512,256]{1,0:T(8,128)S(1)}, f32[512,256]{1,0:T(8,128)S(1)}, u32[]{:S(2)}, u32[]{:S(2)}) collective-permute-start(f32[512,256]{1,0:T(8,128)S(1)} %get-tuple-element.45), channel_id=1, source_target_pairs={{0,32},{8,40},{16,48},{24,56},{32,64},{40,72},{48,80},{56,88},{64,... | collective-permute-start | bytes 1572872 | tf_op jit(solution)/shard_map/ppermute | solution.py:42
  47.5 35.6 %collective-permute-start.7 = (f32[512,256]{1,0:T(8,128)S(1)}, f32[512,256]{1,0:T(8,128)S(1)}, u32[]{:S(2)}, u32[]{:S(2)}) collective-permute-start(f32[512,256]{1,0:T(8,128)S(1)} %get-tuple-element.46), channel_id=1, source_target_pairs={{0,64},{8,72},{16,80},{24,88},{32,96},{40,104},{48,112},{56,120},{... | collective-permute-start | bytes 1572872 | tf_op jit(solution)/shard_map/ppermute | solution.py:42
  50.8 32.3 %collective-permute-start.8 = (f32[512,256]{1,0:T(8,128)S(1)}, f32[512,256]{1,0:T(8,128)S(1)}, u32[]{:S(2)}, u32[]{:S(2)}) collective-permute-start(f32[512,256]{1,0:T(8,128)S(1)} %get-tuple-element.47), channel_id=1, source_target_pairs={{0,96},{8,104},{16,112},{24,120},{32,0},{40,8},{48,16},{56,24},{64... | collective-permute-start | bytes 1572872 | tf_op jit(solution)/shard_map/ppermute | solution.py:42
  52.8 30.3 %collective-permute-start.9 = (f32[512,256]{1,0:T(8,128)S(1)}, f32[512,256]{1,0:T(8,128)S(1)}, u32[]{:S(2)}, u32[]{:S(2)}) collective-permute-start(f32[512,256]{1,0:T(8,128)S(1)} %get-tuple-element.48), channel_id=1, source_target_pairs={{0,8},{8,16},{16,24},{24,0},{32,40},{40,48},{48,56},{56,32},{64,72... | collective-permute-start | bytes 1572872 | tf_op jit(solution)/shard_map/ppermute | solution.py:46
  58.8 24.4 %collective-permute-start.10 = (f32[512,256]{1,0:T(8,128)S(1)}, f32[512,256]{1,0:T(8,128)S(1)}, u32[]{:S(2)}, u32[]{:S(2)}) collective-permute-start(f32[512,256]{1,0:T(8,128)S(1)} %get-tuple-element.49), channel_id=1, source_target_pairs={{0,16},{8,24},{16,0},{24,8},{32,48},{40,56},{48,32},{56,40},{64,80... | collective-permute-start | bytes 1572872 | tf_op jit(solution)/shard_map/ppermute | solution.py:46
  70.1 14.6 %collective-permute-start.11 = (f32[512,256]{1,0:T(8,128)S(1)}, f32[512,256]{1,0:T(8,128)S(1)}, u32[]{:S(2)}, u32[]{:S(2)}) collective-permute-start(f32[512,256]{1,0:T(8,128)S(1)} %get-tuple-element.50), channel_id=1, source_target_pairs={{0,24},{8,0},{16,8},{24,16},{32,56},{40,32},{48,40},{56,48},{64,88... | collective-permute-start | bytes 1572872 | tf_op jit(solution)/shard_map/ppermute | solution.py:46
  83.1 13.3 %collective-permute-start.27 = (f32[512,256]{1,0:T(8,128)S(1)}, f32[512,256]{1,0:T(8,128)S(1)}, u32[]{:S(2)}, u32[]{:S(2)}) collective-permute-start(f32[512,256]{1,0:T(8,128)S(1)} %get-tuple-element.65), channel_id=1, source_target_pairs={{0,64},{8,72},{16,80},{24,88},{32,96},{40,104},{48,112},{56,120},{... | collective-permute-start | bytes 1572872 | tf_op jit(solution)/shard_map/ppermute | solution.py:42
  83.1 15.8 %collective-permute-start.28 = (f32[512,256]{1,0:T(8,128)S(1)}, f32[512,256]{1,0:T(8,128)S(1)}, u32[]{:S(2)}, u32[]{:S(2)}) collective-permute-start(f32[512,256]{1,0:T(8,128)S(1)} %get-tuple-element.66), channel_id=1, source_target_pairs={{0,96},{8,104},{16,112},{24,120},{32,0},{40,8},{48,16},{56,24},{64... | collective-permute-start | bytes 1572872 | tf_op jit(solution)/shard_map/ppermute | solution.py:42
  83.1 18.7 %collective-permute-start.29 = (f32[512,256]{1,0:T(8,128)S(1)}, f32[512,256]{1,0:T(8,128)S(1)}, u32[]{:S(2)}, u32[]{:S(2)}) collective-permute-start(f32[512,256]{1,0:T(8,128)S(1)} %get-tuple-element.67), channel_id=1, source_target_pairs={{0,8},{8,16},{16,24},{24,0},{32,40},{40,48},{48,56},{56,32},{64,72... | collective-permute-start | bytes 1572872 | tf_op jit(solution)/shard_map/ppermute | solution.py:46
  83.2 21.1 %collective-permute-start.30 = (f32[512,256]{1,0:T(8,128)S(1)}, f32[512,256]{1,0:T(8,128)S(1)}, u32[]{:S(2)}, u32[]{:S(2)}) collective-permute-start(f32[512,256]{1,0:T(8,128)S(1)} %get-tuple-element.68), channel_id=1, source_target_pairs={{0,16},{8,24},{16,0},{24,8},{32,48},{40,56},{48,32},{56,40},{64,80... | collective-permute-start | bytes 1572872 | tf_op jit(solution)/shard_map/ppermute | solution.py:46
  84.6 23.5 %collective-permute-start.31 = (f32[512,256]{1,0:T(8,128)S(1)}, f32[512,256]{1,0:T(8,128)S(1)}, u32[]{:S(2)}, u32[]{:S(2)}) collective-permute-start(f32[512,256]{1,0:T(8,128)S(1)} %get-tuple-element.69), channel_id=1, source_target_pairs={{0,24},{8,0},{16,8},{24,16},{32,56},{40,32},{48,40},{56,48},{64,88... | collective-permute-start | bytes 1572872 | tf_op jit(solution)/shard_map/ppermute | solution.py:46
  96.4 25.4 %collective-permute-start.12 = (f32[12,128,256]{2,1,0:T(8,128)S(1)}, f32[12,128,256]{2,1,0:T(8,128)S(1)}, u32[]{:S(2)}, u32[]{:S(2)}) collective-permute-start(f32[12,128,256]{2,1,0:T(8,128)S(1)} %listed.7), channel_id=1, source_target_pairs={{0,1},{1,0},{2,3},{3,2},{4,5},{5,4},{6,7},{7,6},{8,9},{9,8},{10,11... | collective-permute-start | bytes 4718600 | tf_op jit(solution)/shard_map/ppermute | solution.py:433
  110.6 22.0 %collective-permute-start.32 = (f32[12,128,256]{2,1,0:T(8,128)S(1)}, f32[12,128,256]{2,1,0:T(8,128)S(1)}, u32[]{:S(2)}, u32[]{:S(2)}) collective-permute-start(f32[12,128,256]{2,1,0:T(8,128)S(1)} %listed.10), channel_id=1, source_target_pairs={{0,1},{1,0},{2,3},{3,2},{4,5},{5,4},{6,7},{7,6},{8,9},{9,8},{10,11... | collective-permute-start | bytes 4718600 | tf_op jit(solution)/shard_map/ppermute | solution.py:433
  112.8 3.8 %collective-permute-start.13 = (f32[4,128,256]{2,1,0:T(8,128)S(1)}, f32[4,128,256]{2,1,0:T(8,128)S(1)}, u32[]{:S(2)}, u32[]{:S(2)}) collective-permute-start(f32[4,128,256]{2,1,0:T(8,128)S(1)} %get-tuple-element.55), channel_id=1, source_target_pairs={{0,1},{1,0},{2,3},{3,2},{4,5},{5,4},{6,7},{7,6},{8,9},{9,8},{10,11... | collective-permute-start | bytes 1572872 | tf_op jit(solution)/shard_map/ppermute | solution.py:419
  113.1 7.4 %collective-permute-start.33 = (f32[4,128,256]{2,1,0:T(8,128)S(1)}, f32[4,128,256]{2,1,0:T(8,128)S(1)}, u32[]{:S(2)}, u32[]{:S(2)}) collective-permute-start(f32[4,128,256]{2,1,0:T(8,128)S(1)} %get-tuple-element.74), channel_id=1, source_target_pairs={{0,1},{1,0},{2,3},{3,2},{4,5},{5,4},{6,7},{7,6},{8,9},{9,8},{10,11... | collective-permute-start | bytes 1572872 | tf_op jit(solution)/shard_map/ppermute | solution.py:419
  116.7 9.0 %collective-permute-start.14 = (f32[2,128,256]{2,1,0:T(8,128)S(1)}, f32[2,128,256]{2,1,0:T(8,128)S(1)}, u32[]{:S(2)}, u32[]{:S(2)}) collective-permute-start(f32[2,128,256]{2,1,0:T(8,128)S(1)} %get-tuple-element.56), channel_id=1, source_target_pairs={{0,2},{1,3},{2,4},{3,5},{4,6},{5,7},{6,0},{7,1},{8,10},{9,11},{10,... | collective-permute-start | bytes 786440 | tf_op jit(solution)/shard_map/ppermute | solution.py:430
  118.3 7.4 %collective-permute-start.15 = (f32[2,128,256]{2,1,0:T(8,128)S(1)}, f32[2,128,256]{2,1,0:T(8,128)S(1)}, u32[]{:S(2)}, u32[]{:S(2)}) collective-permute-start(f32[2,128,256]{2,1,0:T(8,128)S(1)} %get-tuple-element.57), channel_id=1, source_target_pairs={{0,6},{1,7},{2,0},{3,1},{4,2},{5,3},{6,4},{7,5},{8,14},{9,15},{10,... | collective-permute-start | bytes 786440 | tf_op jit(solution)/shard_map/ppermute | solution.py:431
  120.6 10.7 %collective-permute-start.34 = (f32[2,128,256]{2,1,0:T(8,128)S(1)}, f32[2,128,256]{2,1,0:T(8,128)S(1)}, u32[]{:S(2)}, u32[]{:S(2)}) collective-permute-start(f32[2,128,256]{2,1,0:T(8,128)S(1)} %get-tuple-element.75), channel_id=1, source_target_pairs={{0,2},{1,3},{2,4},{3,5},{4,6},{5,7},{6,0},{7,1},{8,10},{9,11},{10,... | collective-permute-start | bytes 786440 | tf_op jit(solution)/shard_map/ppermute | solution.py:430
  121.8 12.1 %collective-permute-start.35 = (f32[2,128,256]{2,1,0:T(8,128)S(1)}, f32[2,128,256]{2,1,0:T(8,128)S(1)}, u32[]{:S(2)}, u32[]{:S(2)}) collective-permute-start(f32[2,128,256]{2,1,0:T(8,128)S(1)} %get-tuple-element.76), channel_id=1, source_target_pairs={{0,6},{1,7},{2,0},{3,1},{4,2},{5,3},{6,4},{7,5},{8,14},{9,15},{10,... | collective-permute-start | bytes 786440 | tf_op jit(solution)/shard_map/ppermute | solution.py:431
  125.7 11.2 %collective-permute-start.16 = (f32[2,128,256]{2,1,0:T(8,128)S(1)}, f32[2,128,256]{2,1,0:T(8,128)S(1)}, u32[]{:S(2)}, u32[]{:S(2)}) collective-permute-start(f32[2,128,256]{2,1,0:T(8,128)S(1)} %get-tuple-element.58), channel_id=1, source_target_pairs={{0,2},{1,3},{2,4},{3,5},{4,6},{5,7},{6,0},{7,1},{8,10},{9,11},{10,... | collective-permute-start | bytes 786440 | tf_op jit(solution)/shard_map/ppermute | solution.py:457
  126.5 11.8 %collective-permute-start.19 = (f32[2,128,256]{2,1,0:T(8,128)S(1)}, f32[2,128,256]{2,1,0:T(8,128)S(1)}, u32[]{:S(2)}, u32[]{:S(2)}) collective-permute-start(f32[2,128,256]{2,1,0:T(8,128)S(1)} %get-tuple-element.61), channel_id=1, source_target_pairs={{0,6},{1,7},{2,0},{3,1},{4,2},{5,3},{6,4},{7,5},{8,14},{9,15},{10,... | collective-permute-start | bytes 786440 | tf_op jit(solution)/shard_map/ppermute | solution.py:458
  131.3 11.0 %collective-permute-start.17 = (f32[2,128,256]{2,1,0:T(8,128)S(1)}, f32[2,128,256]{2,1,0:T(8,128)S(1)}, u32[]{:S(2)}, u32[]{:S(2)}) collective-permute-start(f32[2,128,256]{2,1,0:T(8,128)S(1)} %get-tuple-element.59), channel_id=1, source_target_pairs={{0,6},{1,7},{2,0},{3,1},{4,2},{5,3},{6,4},{7,5},{8,14},{9,15},{10,... | collective-permute-start | bytes 786440 | tf_op jit(solution)/shard_map/ppermute | solution.py:447
  132.6 10.6 %collective-permute-start.18 = (f32[2,128,256]{2,1,0:T(8,128)S(1)}, f32[2,128,256]{2,1,0:T(8,128)S(1)}, u32[]{:S(2)}, u32[]{:S(2)}) collective-permute-start(f32[2,128,256]{2,1,0:T(8,128)S(1)} %get-tuple-element.60), channel_id=1, source_target_pairs={{0,2},{1,3},{2,4},{3,5},{4,6},{5,7},{6,0},{7,1},{8,10},{9,11},{10,... | collective-permute-start | bytes 786440 | tf_op jit(solution)/shard_map/ppermute | solution.py:446
  133.7 9.5 %copy-start.2 = (f32[512,512]{1,0:T(8,128)S(1)}, f32[512,512]{1,0:T(8,128)}, u32[]{:S(2)}) copy-start(f32[512,512]{1,0:T(8,128)} %feature_ref.5) | copy-start | bytes 3145732
  133.8 9.5 %copy-start.3 = (bf16[512,2048]{1,0:T(8,128)(2,1)S(1)}, bf16[512,2048]{1,0:T(8,128)(2,1)}, u32[]{:S(2)}) copy-start(bf16[512,2048]{1,0:T(8,128)(2,1)} %w_ref.3) | copy-start | bytes 6291460
  134.0 13.1 %collective-permute-start.36 = (f32[2,128,256]{2,1,0:T(8,128)S(1)}, f32[2,128,256]{2,1,0:T(8,128)S(1)}, u32[]{:S(2)}, u32[]{:S(2)}) collective-permute-start(f32[2,128,256]{2,1,0:T(8,128)S(1)} %get-tuple-element.77), channel_id=1, source_target_pairs={{0,2},{1,3},{2,4},{3,5},{4,6},{5,7},{6,0},{7,1},{8,10},{9,11},{10,... | collective-permute-start | bytes 786440 | tf_op jit(solution)/shard_map/ppermute | solution.py:457
  136.9 11.0 %collective-permute-start.39 = (f32[2,128,256]{2,1,0:T(8,128)S(1)}, f32[2,128,256]{2,1,0:T(8,128)S(1)}, u32[]{:S(2)}, u32[]{:S(2)}) collective-permute-start(f32[2,128,256]{2,1,0:T(8,128)S(1)} %get-tuple-element.80), channel_id=1, source_target_pairs={{0,6},{1,7},{2,0},{3,1},{4,2},{5,3},{6,4},{7,5},{8,14},{9,15},{10,... | collective-permute-start | bytes 786440 | tf_op jit(solution)/shard_map/ppermute | solution.py:458
  138.3 15.3 %collective-permute-start.37 = (f32[2,128,256]{2,1,0:T(8,128)S(1)}, f32[2,128,256]{2,1,0:T(8,128)S(1)}, u32[]{:S(2)}, u32[]{:S(2)}) collective-permute-start(f32[2,128,256]{2,1,0:T(8,128)S(1)} %get-tuple-element.78), channel_id=1, source_target_pairs={{0,6},{1,7},{2,0},{3,1},{4,2},{5,3},{6,4},{7,5},{8,14},{9,15},{10,... | collective-permute-start | bytes 786440 | tf_op jit(solution)/shard_map/ppermute | solution.py:447
  142.3 11.2 %collective-permute-start.38 = (f32[2,128,256]{2,1,0:T(8,128)S(1)}, f32[2,128,256]{2,1,0:T(8,128)S(1)}, u32[]{:S(2)}, u32[]{:S(2)}) collective-permute-start(f32[2,128,256]{2,1,0:T(8,128)S(1)} %get-tuple-element.79), channel_id=1, source_target_pairs={{0,2},{1,3},{2,4},{3,5},{4,6},{5,7},{6,0},{7,1},{8,10},{9,11},{10,... | collective-permute-start | bytes 786440 | tf_op jit(solution)/shard_map/ppermute | solution.py:446
  143.2 10.3 %copy-start.4 = (bf16[2048,512]{1,0:T(8,128)(2,1)S(1)}, bf16[2048,512]{1,0:T(8,128)(2,1)}, u32[]{:S(2)}) copy-start(bf16[2048,512]{1,0:T(8,128)(2,1)} %w_out_ref.1) | copy-start | bytes 6291460
  143.2 10.3 %copy-start.8 = (f32[512]{0:T(512)S(1)}, f32[512]{0:T(512)}, u32[]{:S(2)}) copy-start(f32[512]{0:T(512)} %param.19) | copy-start | bytes 6148
  (3 other events, 11.4 us)

commit v5 on v4

--- a/solution.py
+++ b/solution.py
@@ -12,7 +12,7 @@
 side = 4
 cores = 2
 picks = 2
-lists = 4
+kinds = 3
 across_x = side // 2
 note_rows = 8
 lanes = 128
@@ -58,31 +58,57 @@
     return slice((d * picks + j) * half, (d * picks + j + 1) * half)
 
 
-def split(feature_ref, need_ref, *refs):
-    outs, (need, sems) = refs[:-2], refs[-2:]
+def split(group, feature_ref, *refs):
+    noted = group == 0
+    if noted:
+        need_ref, first_ref, second_ref, need, sems = refs
+    else:
+        first_ref, second_ref, sems = refs
     half = lanes // 2
     rows = feature_ref.shape[0] // 2
-    copies = [pltpu.make_async_copy(need_ref, need, sems.at[0])]
-    for at, out in enumerate(outs):
-        group, place = at // 2, at % 2
+    part = slice(group * span, (group + 1) * span)
+    copies = []
+    for place, out in enumerate((first_ref, second_ref)):
         for block in range(rows // half):
             start = (2 * block + place) * half
             copies.append(
                 pltpu.make_async_copy(
-                    feature_ref.at[start : start + half, group * span : (group + 1) * span],
+                    feature_ref.at[start : start + half, part],
                     out.at[block * half : (block + 1) * half, :],
                     sems.at[len(copies)],
                 )
             )
-    for copy in copies:
+    if noted:
+        copy = pltpu.make_async_copy(need_ref, need, sems.at[len(copies)])
         copy.start()
-    copies[0].wait()
-    note = need[...].astype(jnp.float32)
-    for out in outs[:2]:
-        out[rows:, :] = jnp.zeros((note_rows, span), jnp.float32)
-        out[rows : rows + note.shape[0], : note.shape[1]] = note
-    for copy in copies[1:]:
+    for each in copies:
+        each.start()
+    if noted:
         copy.wait()
+        note = need[...].astype(jnp.float32)
+        for out in (first_ref, second_ref):
+            out[rows:, :] = jnp.zeros((note_rows, span), jnp.float32)
+            out[rows : rows + note.shape[0], : note.shape[1]] = note
+    for each in copies:
+        each.wait()
+
+
+def split_group(group, features, need):
+    nodes = features.shape[0]
+    args = [features] + ([need] if group == 0 else [])
+    rows = nodes // 2 + (note_rows if group == 0 else 0)
+    copies = nodes // lanes * 2 + (1 if group == 0 else 0)
+    return pl.pallas_call(
+        lambda *refs: split(group, *refs),
+        in_specs=[pl.BlockSpec(memory_space=pltpu.HBM)] * len(args),
+        out_specs=[in_vmem] * 2,
+        scratch_shapes=([pltpu.VMEM(need.shape, jnp.int32)] if group == 0 else [])
+        + [pltpu.SemaphoreType.DMA((copies,))],
+        out_shape=[jax.ShapeDtypeStruct((rows, span), jnp.float32)] * 2,
+        compiler_params=pltpu.CompilerParams(vmem_limit_bytes=4 << 20),
+        cost_estimate=pl.CostEstimate(flops=0, bytes_accessed=1 << 20, transcendentals=0),
+        name="split",
+    )(*[pltpu.with_memory_space_constraint(v, pltpu.HBM) for v in args])
 
 
 def join_across(keep_ref, arrived_ref, over_right_ref, over_left_ref):
@@ -109,7 +135,7 @@
 
 
 def places_of(which, blocks_dev):
-    return blocks_dev * (1 if which % 2 == 0 else side - 1)
+    return blocks_dev * (2 if which % kinds == 1 else 1)
 
 
 def pairs_of(tile_total, blocks_dev):
@@ -131,42 +157,43 @@
     def pair(place, first, second):
         return first | (second << code_bits) | (place << (2 * code_bits))
 
-    for place in range(lists * blocks):
+    for place in range(2 * kinds * blocks):
         waiting[place] = -1
-    for which in range(lists):
-        waiting[lists * blocks + which] = 0
+    for which in range(2 * kinds):
+        waiting[2 * kinds * blocks + which] = 0
 
     def turn(slot, carry):
         target = row_ref[slot]
         source = col_ref[slot]
         column = lax.shift_right_logical(target, log(blocks_dev))
         away_x = (lax.shift_right_logical(column, log(cores)) - my_x) & (side - 1)
-        across = (away_x == across_x).astype(jnp.int32)
-        order_x = jnp.where(across == 1, 0, away_x - (away_x > across_x).astype(jnp.int32))
-        place = order_x * blocks_dev + (target & (blocks_dev - 1))
-        which = 2 * (1 - ((column & (cores - 1)) ^ my_core)) + 1 - across
+        beside = away_x & 1
+        kind = jnp.where(beside == 1, 1, jnp.where(away_x == across_x, 0, 2))
+        right = (away_x > across_x).astype(jnp.int32)
+        place = right * blocks_dev + (target & (blocks_dev - 1))
+        which = kinds * (1 - ((column & (cores - 1)) ^ my_core)) + kind
         owner = lax.shift_right_logical(source, log(picks))
         away_z = (lax.shift_right_logical(owner, log(side)) - my_z) & (side - 1)
         away_y = (owner - my_y) & (side - 1)
         pos = (away_z * side + away_y) * picks + (source & (picks - 1))
         code = slot | (pos << slot_bits)
         before = waiting[which * blocks + place]
-        end = waiting[lists * blocks + which]
+        end = waiting[2 * kinds * blocks + which]
         plan_ref[which * entries + end] = pair(place, before, code)
         waiting[which * blocks + place] = jnp.where(before >= 0, -1, code)
-        waiting[lists * blocks + which] = end + (before >= 0).astype(jnp.int32)
+        waiting[2 * kinds * blocks + which] = end + (before >= 0).astype(jnp.int32)
         return carry
 
     lax.fori_loop(0, count_ref[0, 0], turn, 0)
-    for which in range(lists):
-        end = waiting[lists * blocks + which]
+    for which in range(2 * kinds):
+        end = waiting[2 * kinds * blocks + which]
         for place in range(places_of(which, blocks_dev)):
             before = waiting[which * blocks + place]
             plan_ref[which * entries + end] = pair(place, before, empty)
             end = end + (before >= 0).astype(jnp.int32)
         for extra in range(unroll):
             plan_ref[which * entries + end + extra] = pair(0, empty, empty)
-        plan_ref[lists * entries + which] = end
+        plan_ref[2 * kinds * entries + which] = end
 
 
 def pack(half, *refs):
@@ -245,7 +272,7 @@
             total[target] += product
         return carry
 
-    count = plan_ref[lists * entries + which]
+    count = plan_ref[2 * kinds * entries + which]
     lax.fori_loop(0, (count + unroll - 1) // unroll, turn, 0)
 
 
@@ -311,11 +338,11 @@
 
 def mix(group, feature_ref, totals, mixed):
     part = slice(group * span, (group + 1) * span)
-    mine, rest = totals[0], totals[1:]
+    (mine, other), rest = totals[:2], totals[2:]
     rows = rest[0].shape[0]
     for at in range(2):
         spot = slice(at * rows, (at + 1) * rows)
-        summed = mine[spot, :] + rest[2 * at][...] + rest[2 * at + 1][...]
+        summed = mine[spot, :] + other[spot, :] + rest[2 * at][...] + rest[2 * at + 1][...]
         mixed[spot, :] = ((1.0 + gin_epsilon) * feature_ref[spot, part] + summed).astype(mixed.dtype)
 
 
@@ -361,31 +388,13 @@
     hidden_size = w_in.shape[1]
     blocks = places_of(1, blocks_dev)
     groups = width // span
-    rows = nodes // 2
 
     need = needed[0, 0].T
-    payload = [
-        jax.ShapeDtypeStruct((rows + (note_rows if group == 0 else 0), span), jnp.float32)
-        for group in range(groups)
-        for _ in range(2)
-    ]
-    own = pl.pallas_call(
-        split,
-        in_specs=[pl.BlockSpec(memory_space=pltpu.HBM)] * 2,
-        out_specs=[in_vmem] * len(payload),
-        scratch_shapes=[
-            pltpu.VMEM(need.shape, jnp.int32),
-            pltpu.SemaphoreType.DMA((1 + len(payload) * blocks_dev,)),
-        ],
-        out_shape=payload,
-        compiler_params=pltpu.CompilerParams(vmem_limit_bytes=4 << 20),
-        cost_estimate=pl.CostEstimate(flops=0, bytes_accessed=2 << 20, transcendentals=0),
-        name="split",
-    )(features, need)
     firsts, seconds = [], []
     for group in range(groups):
-        first = [own[2 * group]] + [None] * (side - 1)
-        second = [own[2 * group + 1]] + [None] * (side - 1)
+        top, low = split_group(group, features, need)
+        first = [top] + [None] * (side - 1)
+        second = [low] + [None] * (side - 1)
         for away in (1, 3, 2):
             first[away] = from_y(first[0], away)
             second[away] = from_z(second[0], away)
@@ -398,7 +407,7 @@
         in_specs=[in_smem] * 3,
         out_specs=in_smem,
         out_shape=jax.ShapeDtypeStruct((512,), jnp.int32),
-        scratch_shapes=[pltpu.SMEM((lists * (blocks + 1),), jnp.int32)],
+        scratch_shapes=[pltpu.SMEM((2 * kinds * (blocks + 1),), jnp.int32)],
         compiler_params=pltpu.CompilerParams(vmem_limit_bytes=1 << 20),
         cost_estimate=pl.CostEstimate(flops=0, bytes_accessed=1 << 20, transcendentals=0),
         name="plan",
@@ -417,7 +426,7 @@
             listed, need, cell_tiles, first, second, along_z, along_y, blocks_dev
         )
         arrived = lax.ppermute(send, "col", col_shift(0, 1))
-        keep = combine_listed(2, listed, cell_tiles, pool, blocks_dev)
+        keep = combine_listed(kinds, listed, cell_tiles, pool, blocks_dev)
         over_right, over_left = pl.pallas_call(
             join_across,
             in_specs=[in_vmem] * 2,
@@ -431,14 +440,13 @@
         relay_left = lax.ppermute(over_left, "col", col_shift(-1, 0))
         send = combine_listed(1, listed, cell_tiles, pool, blocks_dev)
         arrived = lax.ppermute(send, "col", col_shift(0, 1))
-        keep = combine_listed(3, listed, cell_tiles, pool, blocks_dev)
+        keep = combine_listed(kinds + 1, listed, cell_tiles, pool, blocks_dev)
         cut = blocks_dev // 2
-        sizes = (blocks_dev, cut, cut, cut, cut)
-        mine, right_held, right, left, left_held = pl.pallas_call(
+        right_held, right, left, left_held = pl.pallas_call(
             join_rest,
             in_specs=[in_vmem] * 2,
-            out_specs=[in_vmem] * len(sizes),
-            out_shape=[jax.ShapeDtypeStruct((n, edge, span), jnp.float32) for n in sizes],
+            out_specs=[in_vmem] * 4,
+            out_shape=[jax.ShapeDtypeStruct((cut, edge, span), jnp.float32)] * 4,
             compiler_params=pltpu.CompilerParams(vmem_limit_bytes=6 << 20),
             cost_estimate=pl.CostEstimate(flops=0, bytes_accessed=4 << 20, transcendentals=0),
             name="join",
@@ -456,10 +464,20 @@
         )(right_held, left_held, relay_right, relay_left)
         from_left_held = lax.ppermute(right_held, "col", col_shift(1, 0))
         from_right_held = lax.ppermute(left_held, "col", col_shift(-1, 0))
+        send = combine_listed(2, listed, cell_tiles, pool, blocks_dev)
+        arrived = lax.ppermute(send, "col", col_shift(0, 1))
+        keep = combine_listed(kinds + 2, listed, cell_tiles, pool, blocks_dev)
         sums.append(
             [
                 v.reshape(-1, span)
-                for v in (mine, from_left_held, from_right, from_left, from_right_held)
+                for v in (
+                    keep,
+                    arrived,
+                    from_left_held,
+                    from_right,
+                    from_left,
+                    from_right_held,
+                )
             ]
         )
 

time: 157 us -> 157 us (level)
  waiting for transfers between devices: 84 us -> 61.4 us
  starting transfers between devices: 51.1 us -> 67.7 us
  Pallas kernels: 18.5 us -> 24.3 us
    ppermute x12, waiting for transfers between devices: 49.7 us -> 39.3 us  [from_z(): return lax.ppermute(value, 'row', row_shift(-step, 0))]
    ppermute x4 -> x6, starting transfers between devices: 5.21 us -> 13.8 us  [on_device(): arrived = lax.ppermute(send, 'col', col_shift(0, 1))]
    ppermute x2, waiting for transfers between devices: 5.52 us -> 0.01 us  [on_device(): from_left_held = lax.ppermute(right_held, 'col', col_shift(1, 0))]
    ppermute x12, starting transfers between devices: 12.6 us -> 17.7 us  [from_y(): return lax.ppermute(value, 'row', row_shift(0, -step))]
    ppermute x2, waiting for transfers between devices: 8.37 us -> 4.5 us  [on_device(): from_right = lax.ppermute(left, 'col', col_shift(-1, 0))]
    pallas_call x6 -> x10, Pallas kernels: 6.46 us -> 10.2 us  [combine_listed(): pl.pallas_call(lambda *refs: add_tiles(which, blocks_dev, *refs), in_spec...]
    ppermute x2, waiting for transfers between devices: 3.55 us -> 6.84 us  [on_device(): relay_right = lax.ppermute(over_right, 'col', col_shift(1, 0))]
    ppermute x12, waiting for transfers between devices: 13.7 us -> 10.7 us  [from_y(): return lax.ppermute(value, 'row', row_shift(0, -step))]
  transfers between devices with their start and end apart: 40 -> 42, of which waited for: 22 -> 17; matrix products, arithmetic and copies ran while one was open for 0% -> 0% of each run, Pallas kernels for 9% -> 12%
where the time goes in v5:
time: 157 us; the launch traced here: 156 us
  starting transfers between devices  67.7 us (43%)
  waiting for transfers between devices  61.4 us (39%)
  Pallas kernels  24.3 us (15%)
    ppermute x12, waiting for transfers between devices, from_z(): return lax.ppermute(value, 'row', row_shift(-step, 0))  39.3 us
    ppermute x12, starting transfers between devices, from_z(): return lax.ppermute(value, 'row', row_shift(-step, 0))  20.5 us
    ppermute x12, starting transfers between devices, from_y(): return lax.ppermute(value, 'row', row_shift(0, -step))  17.7 us
    ppermute x6, starting transfers between devices, on_device(): arrived = lax.ppermute(send, 'col', col_shift(0, 1))  13.8 us
    ppermute x12, waiting for transfers between devices, from_y(): return lax.ppermute(value, 'row', row_shift(0, -step))  10.7 us
    pallas_call x10, Pallas kernels, combine_listed(): pl.pallas_call(lambda *refs: add_tiles(which, blocks_dev, *refs), in_spec...  10.2 us
    ppermute x2, waiting for transfers between devices, on_device(): relay_right = lax.ppermute(over_right, 'col', col_shift(1, 0))  6.84 us
    ppermute x2, starting transfers between devices, on_device(): from_right_held = lax.ppermute(left_held, 'col', col_shift(-1, 0))  5.31 us
  transfers between devices with their start and end apart: 42, of which 17 were waited for; matrix products, arithmetic and copies ran while one was open for 0% of the time, Pallas kernels for 12%

profile of v5, /device:TPU:1, one launch (start us, length us, event | category | flops | bytes accessed | tf_op | source)
XLA Modules:
  0.0 155.5 jit_solution(12562269294364813474)
XLA Ops:
  0.0 1.1 split.3
  1.1 2.2 %collective-permute-start.23 = (f32[256,256]{1,0:T(8,128)S(1)}, f32[256,256]{1,0:T(8,128)S(1)}, u32[]{:S(2)}, u32[]{:S(2)}) collective-permute-start(f32[256,256]{1,0:T(8,128)S(1)} %get-tuple-element.59.refs_0_.refs_3_), channel_id=1, source_target_pairs={{0,8},{8,16},{16,24},{24,0},{32,40},{40,48},{48,56},{56,32},{64,72... | collective-permute-start | bytes 786440 | tf_op jit(solution)/shard_map/ppermute | solution.py:46
  3.3 2.6 %collective-permute-start.22 = (f32[256,256]{1,0:T(8,128)S(1)}, f32[256,256]{1,0:T(8,128)S(1)}, u32[]{:S(2)}, u32[]{:S(2)}) collective-permute-start(f32[256,256]{1,0:T(8,128)S(1)} %get-tuple-element.59.refs_0_.refs_3_), channel_id=1, source_target_pairs={{0,16},{8,24},{16,0},{24,8},{32,48},{40,56},{48,32},{56,40},{64,80... | collective-permute-start | bytes 786440 | tf_op jit(solution)/shard_map/ppermute | solution.py:46
  5.9 1.3 split.2
  7.3 2.7 %collective-permute-start.21 = (f32[256,256]{1,0:T(8,128)S(1)}, f32[256,256]{1,0:T(8,128)S(1)}, u32[]{:S(2)}, u32[]{:S(2)}) collective-permute-start(f32[256,256]{1,0:T(8,128)S(1)} %get-tuple-element.59.refs_0_.refs_3_), channel_id=1, source_target_pairs={{0,24},{8,0},{16,8},{24,16},{32,56},{40,32},{48,40},{56,48},{64,88... | collective-permute-start | bytes 786440 | tf_op jit(solution)/shard_map/ppermute | solution.py:46
  10.0 1.6 %collective-permute-start.26 = (f32[256,256]{1,0:T(8,128)S(1)}, f32[256,256]{1,0:T(8,128)S(1)}, u32[]{:S(2)}, u32[]{:S(2)}) collective-permute-start(f32[256,256]{1,0:T(8,128)S(1)} %get-tuple-element.60.refs_4_.refs_7_), channel_id=1, source_target_pairs={{0,32},{8,40},{16,48},{24,56},{32,64},{40,72},{48,80},{56,88},{64,... | collective-permute-start | bytes 786440 | tf_op jit(solution)/shard_map/ppermute | solution.py:42
  11.6 3.3 %collective-permute-start.25 = (f32[256,256]{1,0:T(8,128)S(1)}, f32[256,256]{1,0:T(8,128)S(1)}, u32[]{:S(2)}, u32[]{:S(2)}) collective-permute-start(f32[256,256]{1,0:T(8,128)S(1)} %get-tuple-element.60.refs_4_.refs_7_), channel_id=1, source_target_pairs={{0,64},{8,72},{16,80},{24,88},{32,96},{40,104},{48,112},{56,120},{... | collective-permute-start | bytes 786440 | tf_op jit(solution)/shard_map/ppermute | solution.py:42
  14.9 2.4 %collective-permute-done.22.refs_2_.refs_5_ = f32[256,256]{1,0:T(8,128)S(1)} collective-permute-done((f32[256,256]{1,0:T(8,128)S(1)}, f32[256,256]{1,0:T(8,128)S(1)}, u32[]{:S(2)}, u32[]{:S(2)}) %collective-permute-start.22) | collective-permute-done | bytes 262176 | tf_op jit(solution)/shard_map/ppermute | solution.py:46
  17.3 3.8 %collective-permute-start.24 = (f32[256,256]{1,0:T(8,128)S(1)}, f32[256,256]{1,0:T(8,128)S(1)}, u32[]{:S(2)}, u32[]{:S(2)}) collective-permute-start(f32[256,256]{1,0:T(8,128)S(1)} %get-tuple-element.60.refs_4_.refs_7_), channel_id=1, source_target_pairs={{0,96},{8,104},{16,112},{24,120},{32,0},{40,8},{48,16},{56,24},{64... | collective-permute-start | bytes 786440 | tf_op jit(solution)/shard_map/ppermute | solution.py:42
  22.4 2.8 %collective-permute-done.25.refs_6_.refs_9_ = f32[256,256]{1,0:T(8,128)S(1)} collective-permute-done((f32[256,256]{1,0:T(8,128)S(1)}, f32[256,256]{1,0:T(8,128)S(1)}, u32[]{:S(2)}, u32[]{:S(2)}) %collective-permute-start.25) | collective-permute-done | bytes 262176 | tf_op jit(solution)/shard_map/ppermute | solution.py:42
  25.8 1.5 collective-permute-start.4
  27.3 2.1 %collective-permute-start.3 = (f32[264,256]{1,0:T(8,128)S(1)}, f32[264,256]{1,0:T(8,128)S(1)}, u32[]{:S(2)}, u32[]{:S(2)}) collective-permute-start(f32[264,256]{1,0:T(8,128)S(1)} %get-tuple-element.42.refs_4_.refs_7_), channel_id=1, source_target_pairs={{0,96},{8,104},{16,112},{24,120},{32,0},{40,8},{48,16},{56,24},{64... | collective-permute-start | bytes 811016 | tf_op jit(solution)/shard_map/ppermute | solution.py:42
  29.4 1.4 collective-permute-done.refs_1_.refs_11_.refs_4_
  31.7 7.0 %collective-permute-done.4.refs_6_.refs_9_ = f32[264,256]{1,0:T(8,128)S(1)} collective-permute-done((f32[264,256]{1,0:T(8,128)S(1)}, f32[264,256]{1,0:T(8,128)S(1)}, u32[]{:S(2)}, u32[]{:S(2)}) %collective-permute-start.4) | collective-permute-done | bytes 270368 | tf_op jit(solution)/shard_map/ppermute | solution.py:42
  38.7 1.1 collective-permute-done.3.refs_5_.refs_8_
  39.7 1.2 pack.3
  41.0 2.7 %collective-permute-start.27 = (f32[512,256]{1,0:T(8,128)S(1)}, f32[512,256]{1,0:T(8,128)S(1)}, u32[]{:S(2)}, u32[]{:S(2)}) collective-permute-start(f32[512,256]{1,0:T(8,128)S(1)} %get-tuple-element.61), channel_id=1, source_target_pairs={{0,32},{8,40},{16,48},{24,56},{32,64},{40,72},{48,80},{56,88},{64,... | collective-permute-start | bytes 1572872 | tf_op jit(solution)/shard_map/ppermute | solution.py:42
  43.7 1.2 pack.2
  45.1 2.0 %collective-permute-start.7 = (f32[512,256]{1,0:T(8,128)S(1)}, f32[512,256]{1,0:T(8,128)S(1)}, u32[]{:S(2)}, u32[]{:S(2)}) collective-permute-start(f32[512,256]{1,0:T(8,128)S(1)} %get-tuple-element.44), channel_id=1, source_target_pairs={{0,64},{8,72},{16,80},{24,88},{32,96},{40,104},{48,112},{56,120},{... | collective-permute-start | bytes 1572872 | tf_op jit(solution)/shard_map/ppermute | solution.py:42
  47.1 2.0 %collective-permute-start.8 = (f32[512,256]{1,0:T(8,128)S(1)}, f32[512,256]{1,0:T(8,128)S(1)}, u32[]{:S(2)}, u32[]{:S(2)}) collective-permute-start(f32[512,256]{1,0:T(8,128)S(1)} %get-tuple-element.45), channel_id=1, source_target_pairs={{0,96},{8,104},{16,112},{24,120},{32,0},{40,8},{48,16},{56,24},{64... | collective-permute-start | bytes 1572872 | tf_op jit(solution)/shard_map/ppermute | solution.py:42
  49.0 5.9 %collective-permute-done.27.refs_11_ = f32[512,256]{1,0:T(8,128)S(1)} collective-permute-done((f32[512,256]{1,0:T(8,128)S(1)}, f32[512,256]{1,0:T(8,128)S(1)}, u32[]{:S(2)}, u32[]{:S(2)}) %collective-permute-start.27) | collective-permute-done | bytes 524320 | tf_op jit(solution)/shard_map/ppermute | solution.py:42
  55.0 11.2 %collective-permute-done.6.refs_11_ = f32[512,256]{1,0:T(8,128)S(1)} collective-permute-done((f32[512,256]{1,0:T(8,128)S(1)}, f32[512,256]{1,0:T(8,128)S(1)}, u32[]{:S(2)}, u32[]{:S(2)}) %collective-permute-start.6) | collective-permute-done | bytes 524320 | tf_op jit(solution)/shard_map/ppermute | solution.py:42
  66.2 3.2 %collective-permute-start.11 = (f32[512,256]{1,0:T(8,128)S(1)}, f32[512,256]{1,0:T(8,128)S(1)}, u32[]{:S(2)}, u32[]{:S(2)}) collective-permute-start(f32[512,256]{1,0:T(8,128)S(1)} %get-tuple-element.48), channel_id=1, source_target_pairs={{0,24},{8,0},{16,8},{24,16},{32,56},{40,32},{48,40},{56,48},{64,88... | collective-permute-start | bytes 1572872 | tf_op jit(solution)/shard_map/ppermute | solution.py:46
  69.4 9.5 %collective-permute-done.7.refs_12_ = f32[512,256]{1,0:T(8,128)S(1)} collective-permute-done((f32[512,256]{1,0:T(8,128)S(1)}, f32[512,256]{1,0:T(8,128)S(1)}, u32[]{:S(2)}, u32[]{:S(2)}) %collective-permute-start.7) | collective-permute-done | bytes 524320 | tf_op jit(solution)/shard_map/ppermute | solution.py:42
  78.9 1.4 collective-permute-start.28
  80.5 3.0 %collective-permute-start.31 = (f32[512,256]{1,0:T(8,128)S(1)}, f32[512,256]{1,0:T(8,128)S(1)}, u32[]{:S(2)}, u32[]{:S(2)}) collective-permute-start(f32[512,256]{1,0:T(8,128)S(1)} %get-tuple-element.65), channel_id=1, source_target_pairs={{0,16},{8,24},{16,0},{24,8},{32,48},{40,56},{48,32},{56,40},{64,80... | collective-permute-start | bytes 1572872 | tf_op jit(solution)/shard_map/ppermute | solution.py:46
  83.5 2.5 %collective-permute-start.32 = (f32[512,256]{1,0:T(8,128)S(1)}, f32[512,256]{1,0:T(8,128)S(1)}, u32[]{:S(2)}, u32[]{:S(2)}) collective-permute-start(f32[512,256]{1,0:T(8,128)S(1)} %get-tuple-element.66), channel_id=1, source_target_pairs={{0,24},{8,0},{16,8},{24,16},{32,56},{40,32},{48,40},{56,48},{64,88... | collective-permute-start | bytes 1572872 | tf_op jit(solution)/shard_map/ppermute | solution.py:46
  86.7 2.4 %plan.1.refs_0_ = s32[512]{0:T(512)S(1)} custom-call(s32[128]{0:T(128)S(1)} %bitcast.49, s32[128]{0:T(128)S(1)} %bitcast.50, s32[1,1]{1,0:T(1,128)S(6)} %copy.11.refs_2_), custom_call_target="tpu_custom_call" | custom-call | bytes 1048576 | tf_op jit(solution)/shard_map/plan/pallas_call | solution.py:405
  89.1 1.2 combine.2
  90.3 1.3 listed.13
  91.8 5.4 %collective-permute-start.13 = (f32[8,128,256]{2,1,0:T(8,128)S(1)}, f32[8,128,256]{2,1,0:T(8,128)S(1)}, u32[]{:S(2)}, u32[]{:S(2)}) collective-permute-start(f32[8,128,256]{2,1,0:T(8,128)S(1)} %listed.13), channel_id=1, source_target_pairs={{0,1},{1,0},{2,3},{3,2},{4,5},{5,4},{6,7},{7,6},{8,9},{9,8},{10,11... | collective-permute-start | bytes 3145736 | tf_op jit(solution)/shard_map/ppermute | solution.py:442
  97.3 4.1 %collective-permute-done.31.refs_15_ = f32[512,256]{1,0:T(8,128)S(1)} collective-permute-done((f32[512,256]{1,0:T(8,128)S(1)}, f32[512,256]{1,0:T(8,128)S(1)}, u32[]{:S(2)}, u32[]{:S(2)}) %collective-permute-start.31) | collective-permute-done | bytes 524320 | tf_op jit(solution)/shard_map/ppermute | solution.py:46
  101.3 2.9 %collective-permute-done.32.refs_16_ = f32[512,256]{1,0:T(8,128)S(1)} collective-permute-done((f32[512,256]{1,0:T(8,128)S(1)}, f32[512,256]{1,0:T(8,128)S(1)}, u32[]{:S(2)}, u32[]{:S(2)}) %collective-permute-start.32) | collective-permute-done | bytes 524320 | tf_op jit(solution)/shard_map/ppermute | solution.py:46
  104.2 1.2 combine.3
  105.4 3.7 %collective-permute-start.35 = (f32[4,128,256]{2,1,0:T(8,128)S(1)}, f32[4,128,256]{2,1,0:T(8,128)S(1)}, u32[]{:S(2)}, u32[]{:S(2)}) collective-permute-start(f32[4,128,256]{2,1,0:T(8,128)S(1)} %get-tuple-element.70), channel_id=1, source_target_pairs={{0,1},{1,0},{2,3},{3,2},{4,5},{5,4},{6,7},{7,6},{8,9},{9,8},{10,11... | collective-permute-start | bytes 1572872 | tf_op jit(solution)/shard_map/ppermute | solution.py:428
  109.2 1.5 listed.18
  114.2 1.8 %collective-permute-start.16 = (f32[2,128,256]{2,1,0:T(8,128)S(1)}, f32[2,128,256]{2,1,0:T(8,128)S(1)}, u32[]{:S(2)}, u32[]{:S(2)}) collective-permute-start(f32[2,128,256]{2,1,0:T(8,128)S(1)} %get-tuple-element.54), channel_id=1, source_target_pairs={{0,6},{1,7},{2,0},{3,1},{4,2},{5,3},{6,4},{7,5},{8,14},{9,15},{10,... | collective-permute-start | bytes 786440 | tf_op jit(solution)/shard_map/ppermute | solution.py:440
  117.0 5.3 %collective-permute-done.15.from_left_ref = f32[2,128,256]{2,1,0:T(8,128)S(1)} collective-permute-done((f32[2,128,256]{2,1,0:T(8,128)S(1)}, f32[2,128,256]{2,1,0:T(8,128)S(1)}, u32[]{:S(2)}, u32[]{:S(2)}) %collective-permute-start.15) | collective-permute-done | bytes 262176 | tf_op jit(solution)/shard_map/ppermute | solution.py:439
  122.3 2.7 %collective-permute-start.37 = (f32[2,128,256]{2,1,0:T(8,128)S(1)}, f32[2,128,256]{2,1,0:T(8,128)S(1)}, u32[]{:S(2)}, u32[]{:S(2)}) collective-permute-start(f32[2,128,256]{2,1,0:T(8,128)S(1)} %get-tuple-element.72), channel_id=1, source_target_pairs={{0,6},{1,7},{2,0},{3,1},{4,2},{5,3},{6,4},{7,5},{8,14},{9,15},{10,... | collective-permute-start | bytes 786440 | tf_op jit(solution)/shard_map/ppermute | solution.py:440
  126.2 2.7 %collective-permute-start.20 = (f32[2,128,256]{2,1,0:T(8,128)S(1)}, f32[2,128,256]{2,1,0:T(8,128)S(1)}, u32[]{:S(2)}, u32[]{:S(2)}) collective-permute-start(f32[2,128,256]{2,1,0:T(8,128)S(1)} %get-tuple-element.58), channel_id=1, source_target_pairs={{0,6},{1,7},{2,0},{3,1},{4,2},{5,3},{6,4},{7,5},{8,14},{9,15},{10,... | collective-permute-start | bytes 786440 | tf_op jit(solution)/shard_map/ppermute | solution.py:466
  128.9 1.5 collective-permute-done.36.from_left_ref
  130.5 1.4 collective-permute-start.19
  132.8 3.8 %collective-permute-start.33 = (f32[4,128,256]{2,1,0:T(8,128)S(1)}, f32[4,128,256]{2,1,0:T(8,128)S(1)}, u32[]{:S(2)}, u32[]{:S(2)}) collective-permute-start(f32[4,128,256]{2,1,0:T(8,128)S(1)} %listed.16), channel_id=1, source_target_pairs={{0,1},{1,0},{2,3},{3,2},{4,5},{5,4},{6,7},{7,6},{8,9},{9,8},{10,11... | collective-permute-start | bytes 1572872 | tf_op jit(solution)/shard_map/ppermute | solution.py:468
  137.9 2.7 %collective-permute-start.41 = (f32[2,128,256]{2,1,0:T(8,128)S(1)}, f32[2,128,256]{2,1,0:T(8,128)S(1)}, u32[]{:S(2)}, u32[]{:S(2)}) collective-permute-start(f32[2,128,256]{2,1,0:T(8,128)S(1)} %get-tuple-element.76), channel_id=1, source_target_pairs={{0,6},{1,7},{2,0},{3,1},{4,2},{5,3},{6,4},{7,5},{8,14},{9,15},{10,... | collective-permute-start | bytes 786440 | tf_op jit(solution)/shard_map/ppermute | solution.py:466
  140.7 3.4 %collective-permute-start.39 = (f32[2,128,256]{2,1,0:T(8,128)S(1)}, f32[2,128,256]{2,1,0:T(8,128)S(1)}, u32[]{:S(2)}, u32[]{:S(2)}) collective-permute-start(f32[2,128,256]{2,1,0:T(8,128)S(1)} %get-tuple-element.74), channel_id=1, source_target_pairs={{0,6},{1,7},{2,0},{3,1},{4,2},{5,3},{6,4},{7,5},{8,14},{9,15},{10,... | collective-permute-start | bytes 786440 | tf_op jit(solution)/shard_map/ppermute | solution.py:455
  146.9 1.1 begin.1.before_ref
  148.0 4.4 %collective-permute-done.39 = f32[2,128,256]{2,1,0:T(8,128)S(1)} collective-permute-done((f32[2,128,256]{2,1,0:T(8,128)S(1)}, f32[2,128,256]{2,1,0:T(8,128)S(1)}, u32[]{:S(2)}, u32[]{:S(2)}) %collective-permute-start.39) | collective-permute-done | bytes 262176 | tf_op jit(solution)/shard_map/ppermute | solution.py:455
  152.5 3.0 %end.1 = bf16[512,512]{1,0:T(8,128)(2,1)} custom-call(f32[512,512]{1,0:T(8,128)S(1)} %copy-done.1, bf16[512,2048]{1,0:T(8,128)(2,1)S(1)} %copy-done.2, f32[512,2048]{1,0:T(8,128)S(1)} %begin.1.before_ref, bf16[2048,512]{1,0:T(8,128)(2,1)S(1)} %copy-done.3, f32[1,512]{1,0:T(1,128)S(1)} %bitcast.48, f32[512,256]{1,0:T(8,128)S(1)} %bitcast.32, ...), custom_call_target="tpu_custom_call" | custom-call | flops 1610612736 | bytes 8388608 | tf_op jit(solution)/shard_map/end/pallas_call | solution.py:496
  (79 shorter events, 14.3 us)
Async XLA Ops:
  1.1 10.5 %collective-permute-start.23 = (f32[256,256]{1,0:T(8,128)S(1)}, f32[256,256]{1,0:T(8,128)S(1)}, u32[]{:S(2)}, u32[]{:S(2)}) collective-permute-start(f32[256,256]{1,0:T(8,128)S(1)} %get-tuple-element.59.refs_0_.refs_3_), channel_id=1, source_target_pairs={{0,8},{8,16},{16,24},{24,0},{32,40},{40,48},{48,56},{56,32},{64,72... | collective-permute-start | bytes 786440 | tf_op jit(solution)/shard_map/ppermute | solution.py:46
  3.3 14.0 %collective-permute-start.22 = (f32[256,256]{1,0:T(8,128)S(1)}, f32[256,256]{1,0:T(8,128)S(1)}, u32[]{:S(2)}, u32[]{:S(2)}) collective-permute-start(f32[256,256]{1,0:T(8,128)S(1)} %get-tuple-element.59.refs_0_.refs_3_), channel_id=1, source_target_pairs={{0,16},{8,24},{16,0},{24,8},{32,48},{40,56},{48,32},{56,40},{64,80... | collective-permute-start | bytes 786440 | tf_op jit(solution)/shard_map/ppermute | solution.py:46
  5.9 83.2 %copy-start = (f32[1,1,128,128,128]{4,3,2,1,0:T(8,128)S(1)}, f32[1,1,128,128,128]{4,3,2,1,0:T(8,128)}, u32[]{:S(2)}) copy-start(f32[1,1,128,128,128]{4,3,2,1,0:T(8,128)} %param.11) | copy-start | bytes 25165828
  7.3 20.1 %collective-permute-start.2 = (f32[264,256]{1,0:T(8,128)S(1)}, f32[264,256]{1,0:T(8,128)S(1)}, u32[]{:S(2)}, u32[]{:S(2)}) collective-permute-start(f32[264,256]{1,0:T(8,128)S(1)} %get-tuple-element.41.refs_0_.refs_3_), channel_id=1, source_target_pairs={{0,8},{8,16},{16,24},{24,0},{32,40},{40,48},{48,56},{56,32},{64,72... | collective-permute-start | bytes 811016 | tf_op jit(solution)/shard_map/ppermute | solution.py:46
  7.3 13.8 %collective-permute-start.21 = (f32[256,256]{1,0:T(8,128)S(1)}, f32[256,256]{1,0:T(8,128)S(1)}, u32[]{:S(2)}, u32[]{:S(2)}) collective-permute-start(f32[256,256]{1,0:T(8,128)S(1)} %get-tuple-element.59.refs_0_.refs_3_), channel_id=1, source_target_pairs={{0,24},{8,0},{16,8},{24,16},{32,56},{40,32},{48,40},{56,48},{64,88... | collective-permute-start | bytes 786440 | tf_op jit(solution)/shard_map/ppermute | solution.py:46
  10.0 11.4 %collective-permute-start.26 = (f32[256,256]{1,0:T(8,128)S(1)}, f32[256,256]{1,0:T(8,128)S(1)}, u32[]{:S(2)}, u32[]{:S(2)}) collective-permute-start(f32[256,256]{1,0:T(8,128)S(1)} %get-tuple-element.60.refs_4_.refs_7_), channel_id=1, source_target_pairs={{0,32},{8,40},{16,48},{24,56},{32,64},{40,72},{48,80},{56,88},{64,... | collective-permute-start | bytes 786440 | tf_op jit(solution)/shard_map/ppermute | solution.py:42
  11.6 13.5 %collective-permute-start.25 = (f32[256,256]{1,0:T(8,128)S(1)}, f32[256,256]{1,0:T(8,128)S(1)}, u32[]{:S(2)}, u32[]{:S(2)}) collective-permute-start(f32[256,256]{1,0:T(8,128)S(1)} %get-tuple-element.60.refs_4_.refs_7_), channel_id=1, source_target_pairs={{0,64},{8,72},{16,80},{24,88},{32,96},{40,104},{48,112},{56,120},{... | collective-permute-start | bytes 786440 | tf_op jit(solution)/shard_map/ppermute | solution.py:42
  17.3 8.5 %collective-permute-start.24 = (f32[256,256]{1,0:T(8,128)S(1)}, f32[256,256]{1,0:T(8,128)S(1)}, u32[]{:S(2)}, u32[]{:S(2)}) collective-permute-start(f32[256,256]{1,0:T(8,128)S(1)} %get-tuple-element.60.refs_4_.refs_7_), channel_id=1, source_target_pairs={{0,96},{8,104},{16,112},{24,120},{32,0},{40,8},{48,16},{56,24},{64... | collective-permute-start | bytes 786440 | tf_op jit(solution)/shard_map/ppermute | solution.py:42
  21.1 8.3 %collective-permute-start.1 = (f32[264,256]{1,0:T(8,128)S(1)}, f32[264,256]{1,0:T(8,128)S(1)}, u32[]{:S(2)}, u32[]{:S(2)}) collective-permute-start(f32[264,256]{1,0:T(8,128)S(1)} %get-tuple-element.41.refs_0_.refs_3_), channel_id=1, source_target_pairs={{0,16},{8,24},{16,0},{24,8},{32,48},{40,56},{48,32},{56,40},{64,80... | collective-permute-start | bytes 811016 | tf_op jit(solution)/shard_map/ppermute | solution.py:46
  21.4 9.4 %collective-permute-start = (f32[264,256]{1,0:T(8,128)S(1)}, f32[264,256]{1,0:T(8,128)S(1)}, u32[]{:S(2)}, u32[]{:S(2)}) collective-permute-start(f32[264,256]{1,0:T(8,128)S(1)} %get-tuple-element.41.refs_0_.refs_3_), channel_id=1, source_target_pairs={{0,24},{8,0},{16,8},{24,16},{32,56},{40,32},{48,40},{56,48},{64,88... | collective-permute-start | bytes 811016 | tf_op jit(solution)/shard_map/ppermute | solution.py:46
  25.2 6.5 %collective-permute-start.5 = (f32[264,256]{1,0:T(8,128)S(1)}, f32[264,256]{1,0:T(8,128)S(1)}, u32[]{:S(2)}, u32[]{:S(2)}) collective-permute-start(f32[264,256]{1,0:T(8,128)S(1)} %get-tuple-element.42.refs_4_.refs_7_), channel_id=1, source_target_pairs={{0,32},{8,40},{16,48},{24,56},{32,64},{40,72},{48,80},{56,88},{64,... | collective-permute-start | bytes 811016 | tf_op jit(solution)/shard_map/ppermute | solution.py:42
  25.8 12.8 %collective-permute-start.4 = (f32[264,256]{1,0:T(8,128)S(1)}, f32[264,256]{1,0:T(8,128)S(1)}, u32[]{:S(2)}, u32[]{:S(2)}) collective-permute-start(f32[264,256]{1,0:T(8,128)S(1)} %get-tuple-element.42.refs_4_.refs_7_), channel_id=1, source_target_pairs={{0,64},{8,72},{16,80},{24,88},{32,96},{40,104},{48,112},{56,120},{... | collective-permute-start | bytes 811016 | tf_op jit(solution)/shard_map/ppermute | solution.py:42
  27.3 12.4 %collective-permute-start.3 = (f32[264,256]{1,0:T(8,128)S(1)}, f32[264,256]{1,0:T(8,128)S(1)}, u32[]{:S(2)}, u32[]{:S(2)}) collective-permute-start(f32[264,256]{1,0:T(8,128)S(1)} %get-tuple-element.42.refs_4_.refs_7_), channel_id=1, source_target_pairs={{0,96},{8,104},{16,112},{24,120},{32,0},{40,8},{48,16},{56,24},{64... | collective-permute-start | bytes 811016 | tf_op jit(solution)/shard_map/ppermute | solution.py:42
  41.0 45.7 %copy-start.7 = (s32[1,1,128]{2,1,0:T(1,128)S(1)}, s32[1,1,128]{2,1,0:T(1,128)}, u32[]{:S(2)}) copy-start(s32[1,1,128]{2,1,0:T(1,128)} %param.12) | copy-start | bytes 1540
  41.0 45.7 %copy-start.8 = (s32[1,1,128]{2,1,0:T(1,128)S(1)}, s32[1,1,128]{2,1,0:T(1,128)}, u32[]{:S(2)}) copy-start(s32[1,1,128]{2,1,0:T(1,128)} %param.13) | copy-start | bytes 1540
  41.0 48.1 %copy-start.4 = (s32[1,1,16,2]{2,3,1,0:T(2,128)S(1)}, s32[1,1,16,2]{2,3,1,0:T(2,128)}, u32[]{:S(2)}) copy-start(s32[1,1,16,2]{2,3,1,0:T(2,128)} %param.15) | copy-start | bytes 388
  41.0 14.0 %collective-permute-start.27 = (f32[512,256]{1,0:T(8,128)S(1)}, f32[512,256]{1,0:T(8,128)S(1)}, u32[]{:S(2)}, u32[]{:S(2)}) collective-permute-start(f32[512,256]{1,0:T(8,128)S(1)} %get-tuple-element.61), channel_id=1, source_target_pairs={{0,32},{8,40},{16,48},{24,56},{32,64},{40,72},{48,80},{56,88},{64,... | collective-permute-start | bytes 1572872 | tf_op jit(solution)/shard_map/ppermute | solution.py:42
  45.0 21.2 %collective-permute-start.6 = (f32[512,256]{1,0:T(8,128)S(1)}, f32[512,256]{1,0:T(8,128)S(1)}, u32[]{:S(2)}, u32[]{:S(2)}) collective-permute-start(f32[512,256]{1,0:T(8,128)S(1)} %get-tuple-element.43), channel_id=1, source_target_pairs={{0,32},{8,40},{16,48},{24,56},{32,64},{40,72},{48,80},{56,88},{64,... | collective-permute-start | bytes 1572872 | tf_op jit(solution)/shard_map/ppermute | solution.py:42
  45.1 33.9 %collective-permute-start.7 = (f32[512,256]{1,0:T(8,128)S(1)}, f32[512,256]{1,0:T(8,128)S(1)}, u32[]{:S(2)}, u32[]{:S(2)}) collective-permute-start(f32[512,256]{1,0:T(8,128)S(1)} %get-tuple-element.44), channel_id=1, source_target_pairs={{0,64},{8,72},{16,80},{24,88},{32,96},{40,104},{48,112},{56,120},{... | collective-permute-start | bytes 1572872 | tf_op jit(solution)/shard_map/ppermute | solution.py:42
  47.1 33.3 %collective-permute-start.8 = (f32[512,256]{1,0:T(8,128)S(1)}, f32[512,256]{1,0:T(8,128)S(1)}, u32[]{:S(2)}, u32[]{:S(2)}) collective-permute-start(f32[512,256]{1,0:T(8,128)S(1)} %get-tuple-element.45), channel_id=1, source_target_pairs={{0,96},{8,104},{16,112},{24,120},{32,0},{40,8},{48,16},{56,24},{64... | collective-permute-start | bytes 1572872 | tf_op jit(solution)/shard_map/ppermute | solution.py:42
  49.0 31.3 %collective-permute-start.9 = (f32[512,256]{1,0:T(8,128)S(1)}, f32[512,256]{1,0:T(8,128)S(1)}, u32[]{:S(2)}, u32[]{:S(2)}) collective-permute-start(f32[512,256]{1,0:T(8,128)S(1)} %get-tuple-element.46), channel_id=1, source_target_pairs={{0,8},{8,16},{16,24},{24,0},{32,40},{40,48},{48,56},{56,32},{64,72... | collective-permute-start | bytes 1572872 | tf_op jit(solution)/shard_map/ppermute | solution.py:46
  55.0 25.5 %collective-permute-start.10 = (f32[512,256]{1,0:T(8,128)S(1)}, f32[512,256]{1,0:T(8,128)S(1)}, u32[]{:S(2)}, u32[]{:S(2)}) collective-permute-start(f32[512,256]{1,0:T(8,128)S(1)} %get-tuple-element.47), channel_id=1, source_target_pairs={{0,16},{8,24},{16,0},{24,8},{32,48},{40,56},{48,32},{56,40},{64,80... | collective-permute-start | bytes 1572872 | tf_op jit(solution)/shard_map/ppermute | solution.py:46
  66.2 17.3 %collective-permute-start.11 = (f32[512,256]{1,0:T(8,128)S(1)}, f32[512,256]{1,0:T(8,128)S(1)}, u32[]{:S(2)}, u32[]{:S(2)}) collective-permute-start(f32[512,256]{1,0:T(8,128)S(1)} %get-tuple-element.48), channel_id=1, source_target_pairs={{0,24},{8,0},{16,8},{24,16},{32,56},{40,32},{48,40},{56,48},{64,88... | collective-permute-start | bytes 1572872 | tf_op jit(solution)/shard_map/ppermute | solution.py:46
  78.9 12.9 %collective-permute-start.28 = (f32[512,256]{1,0:T(8,128)S(1)}, f32[512,256]{1,0:T(8,128)S(1)}, u32[]{:S(2)}, u32[]{:S(2)}) collective-permute-start(f32[512,256]{1,0:T(8,128)S(1)} %get-tuple-element.62), channel_id=1, source_target_pairs={{0,64},{8,72},{16,80},{24,88},{32,96},{40,104},{48,112},{56,120},{... | collective-permute-start | bytes 1572872 | tf_op jit(solution)/shard_map/ppermute | solution.py:42
  80.4 16.9 %collective-permute-start.29 = (f32[512,256]{1,0:T(8,128)S(1)}, f32[512,256]{1,0:T(8,128)S(1)}, u32[]{:S(2)}, u32[]{:S(2)}) collective-permute-start(f32[512,256]{1,0:T(8,128)S(1)} %get-tuple-element.63), channel_id=1, source_target_pairs={{0,96},{8,104},{16,112},{24,120},{32,0},{40,8},{48,16},{56,24},{64... | collective-permute-start | bytes 1572872 | tf_op jit(solution)/shard_map/ppermute | solution.py:42
  80.4 16.9 %collective-permute-start.30 = (f32[512,256]{1,0:T(8,128)S(1)}, f32[512,256]{1,0:T(8,128)S(1)}, u32[]{:S(2)}, u32[]{:S(2)}) collective-permute-start(f32[512,256]{1,0:T(8,128)S(1)} %get-tuple-element.64), channel_id=1, source_target_pairs={{0,8},{8,16},{16,24},{24,0},{32,40},{40,48},{48,56},{56,32},{64,72... | collective-permute-start | bytes 1572872 | tf_op jit(solution)/shard_map/ppermute | solution.py:46
  80.5 20.9 %collective-permute-start.31 = (f32[512,256]{1,0:T(8,128)S(1)}, f32[512,256]{1,0:T(8,128)S(1)}, u32[]{:S(2)}, u32[]{:S(2)}) collective-permute-start(f32[512,256]{1,0:T(8,128)S(1)} %get-tuple-element.65), channel_id=1, source_target_pairs={{0,16},{8,24},{16,0},{24,8},{32,48},{40,56},{48,32},{56,40},{64,80... | collective-permute-start | bytes 1572872 | tf_op jit(solution)/shard_map/ppermute | solution.py:46
  83.5 20.7 %collective-permute-start.32 = (f32[512,256]{1,0:T(8,128)S(1)}, f32[512,256]{1,0:T(8,128)S(1)}, u32[]{:S(2)}, u32[]{:S(2)}) collective-permute-start(f32[512,256]{1,0:T(8,128)S(1)} %get-tuple-element.66), channel_id=1, source_target_pairs={{0,24},{8,0},{16,8},{24,16},{32,56},{40,32},{48,40},{56,48},{64,88... | collective-permute-start | bytes 1572872 | tf_op jit(solution)/shard_map/ppermute | solution.py:46
  91.8 30.5 %collective-permute-start.13 = (f32[8,128,256]{2,1,0:T(8,128)S(1)}, f32[8,128,256]{2,1,0:T(8,128)S(1)}, u32[]{:S(2)}, u32[]{:S(2)}) collective-permute-start(f32[8,128,256]{2,1,0:T(8,128)S(1)} %listed.13), channel_id=1, source_target_pairs={{0,1},{1,0},{2,3},{3,2},{4,5},{5,4},{6,7},{7,6},{8,9},{9,8},{10,11... | collective-permute-start | bytes 3145736 | tf_op jit(solution)/shard_map/ppermute | solution.py:442
  105.4 8.8 %collective-permute-start.35 = (f32[4,128,256]{2,1,0:T(8,128)S(1)}, f32[4,128,256]{2,1,0:T(8,128)S(1)}, u32[]{:S(2)}, u32[]{:S(2)}) collective-permute-start(f32[4,128,256]{2,1,0:T(8,128)S(1)} %get-tuple-element.70), channel_id=1, source_target_pairs={{0,1},{1,0},{2,3},{3,2},{4,5},{5,4},{6,7},{7,6},{8,9},{9,8},{10,11... | collective-permute-start | bytes 1572872 | tf_op jit(solution)/shard_map/ppermute | solution.py:428
  109.1 4.1 %collective-permute-start.14 = (f32[4,128,256]{2,1,0:T(8,128)S(1)}, f32[4,128,256]{2,1,0:T(8,128)S(1)}, u32[]{:S(2)}, u32[]{:S(2)}) collective-permute-start(f32[4,128,256]{2,1,0:T(8,128)S(1)} %get-tuple-element.52), channel_id=1, source_target_pairs={{0,1},{1,0},{2,3},{3,2},{4,5},{5,4},{6,7},{7,6},{8,9},{9,8},{10,11... | collective-permute-start | bytes 1572872 | tf_op jit(solution)/shard_map/ppermute | solution.py:428
  110.6 22.2 %collective-permute-start.34 = (f32[8,128,256]{2,1,0:T(8,128)S(1)}, f32[8,128,256]{2,1,0:T(8,128)S(1)}, u32[]{:S(2)}, u32[]{:S(2)}) collective-permute-start(f32[8,128,256]{2,1,0:T(8,128)S(1)} %listed.18), channel_id=1, source_target_pairs={{0,1},{1,0},{2,3},{3,2},{4,5},{5,4},{6,7},{7,6},{8,9},{9,8},{10,11... | collective-permute-start | bytes 3145736 | tf_op jit(solution)/shard_map/ppermute | solution.py:442
  111.7 14.5 %collective-permute-start.12 = (f32[4,128,256]{2,1,0:T(8,128)S(1)}, f32[4,128,256]{2,1,0:T(8,128)S(1)}, u32[]{:S(2)}, u32[]{:S(2)}) collective-permute-start(f32[4,128,256]{2,1,0:T(8,128)S(1)} %listed.11), channel_id=1, source_target_pairs={{0,1},{1,0},{2,3},{3,2},{4,5},{5,4},{6,7},{7,6},{8,9},{9,8},{10,11... | collective-permute-start | bytes 1572872 | tf_op jit(solution)/shard_map/ppermute | solution.py:468
  113.2 9.1 %collective-permute-start.15 = (f32[2,128,256]{2,1,0:T(8,128)S(1)}, f32[2,128,256]{2,1,0:T(8,128)S(1)}, u32[]{:S(2)}, u32[]{:S(2)}) collective-permute-start(f32[2,128,256]{2,1,0:T(8,128)S(1)} %get-tuple-element.53), channel_id=1, source_target_pairs={{0,2},{1,3},{2,4},{3,5},{4,6},{5,7},{6,0},{7,1},{8,10},{9,11},{10,... | collective-permute-start | bytes 786440 | tf_op jit(solution)/shard_map/ppermute | solution.py:439
  114.2 11.8 %collective-permute-start.16 = (f32[2,128,256]{2,1,0:T(8,128)S(1)}, f32[2,128,256]{2,1,0:T(8,128)S(1)}, u32[]{:S(2)}, u32[]{:S(2)}) collective-permute-start(f32[2,128,256]{2,1,0:T(8,128)S(1)} %get-tuple-element.54), channel_id=1, source_target_pairs={{0,6},{1,7},{2,0},{3,1},{4,2},{5,3},{6,4},{7,5},{8,14},{9,15},{10,... | collective-permute-start | bytes 786440 | tf_op jit(solution)/shard_map/ppermute | solution.py:440
  122.3 8.1 %collective-permute-start.36 = (f32[2,128,256]{2,1,0:T(8,128)S(1)}, f32[2,128,256]{2,1,0:T(8,128)S(1)}, u32[]{:S(2)}, u32[]{:S(2)}) collective-permute-start(f32[2,128,256]{2,1,0:T(8,128)S(1)} %get-tuple-element.71), channel_id=1, source_target_pairs={{0,2},{1,3},{2,4},{3,5},{4,6},{5,7},{6,0},{7,1},{8,10},{9,11},{10,... | collective-permute-start | bytes 786440 | tf_op jit(solution)/shard_map/ppermute | solution.py:439
  122.3 8.2 %collective-permute-start.37 = (f32[2,128,256]{2,1,0:T(8,128)S(1)}, f32[2,128,256]{2,1,0:T(8,128)S(1)}, u32[]{:S(2)}, u32[]{:S(2)}) collective-permute-start(f32[2,128,256]{2,1,0:T(8,128)S(1)} %get-tuple-element.72), channel_id=1, source_target_pairs={{0,6},{1,7},{2,0},{3,1},{4,2},{5,3},{6,4},{7,5},{8,14},{9,15},{10,... | collective-permute-start | bytes 786440 | tf_op jit(solution)/shard_map/ppermute | solution.py:440
  126.1 11.7 %collective-permute-start.17 = (f32[2,128,256]{2,1,0:T(8,128)S(1)}, f32[2,128,256]{2,1,0:T(8,128)S(1)}, u32[]{:S(2)}, u32[]{:S(2)}) collective-permute-start(f32[2,128,256]{2,1,0:T(8,128)S(1)} %get-tuple-element.55), channel_id=1, source_target_pairs={{0,2},{1,3},{2,4},{3,5},{4,6},{5,7},{6,0},{7,1},{8,10},{9,11},{10,... | collective-permute-start | bytes 786440 | tf_op jit(solution)/shard_map/ppermute | solution.py:465
  126.2 11.7 %collective-permute-start.20 = (f32[2,128,256]{2,1,0:T(8,128)S(1)}, f32[2,128,256]{2,1,0:T(8,128)S(1)}, u32[]{:S(2)}, u32[]{:S(2)}) collective-permute-start(f32[2,128,256]{2,1,0:T(8,128)S(1)} %get-tuple-element.58), channel_id=1, source_target_pairs={{0,6},{1,7},{2,0},{3,1},{4,2},{5,3},{6,4},{7,5},{8,14},{9,15},{10,... | collective-permute-start | bytes 786440 | tf_op jit(solution)/shard_map/ppermute | solution.py:466
  130.4 10.2 %collective-permute-start.18 = (f32[2,128,256]{2,1,0:T(8,128)S(1)}, f32[2,128,256]{2,1,0:T(8,128)S(1)}, u32[]{:S(2)}, u32[]{:S(2)}) collective-permute-start(f32[2,128,256]{2,1,0:T(8,128)S(1)} %get-tuple-element.56), channel_id=1, source_target_pairs={{0,6},{1,7},{2,0},{3,1},{4,2},{5,3},{6,4},{7,5},{8,14},{9,15},{10,... | collective-permute-start | bytes 786440 | tf_op jit(solution)/shard_map/ppermute | solution.py:455
  130.5 13.6 %collective-permute-start.19 = (f32[2,128,256]{2,1,0:T(8,128)S(1)}, f32[2,128,256]{2,1,0:T(8,128)S(1)}, u32[]{:S(2)}, u32[]{:S(2)}) collective-permute-start(f32[2,128,256]{2,1,0:T(8,128)S(1)} %get-tuple-element.57), channel_id=1, source_target_pairs={{0,2},{1,3},{2,4},{3,5},{4,6},{5,7},{6,0},{7,1},{8,10},{9,11},{10,... | collective-permute-start | bytes 786440 | tf_op jit(solution)/shard_map/ppermute | solution.py:454
  132.8 15.2 %collective-permute-start.33 = (f32[4,128,256]{2,1,0:T(8,128)S(1)}, f32[4,128,256]{2,1,0:T(8,128)S(1)}, u32[]{:S(2)}, u32[]{:S(2)}) collective-permute-start(f32[4,128,256]{2,1,0:T(8,128)S(1)} %listed.16), channel_id=1, source_target_pairs={{0,1},{1,0},{2,3},{3,2},{4,5},{5,4},{6,7},{7,6},{8,9},{9,8},{10,11... | collective-permute-start | bytes 1572872 | tf_op jit(solution)/shard_map/ppermute | solution.py:468
  137.8 10.2 %collective-permute-start.38 = (f32[2,128,256]{2,1,0:T(8,128)S(1)}, f32[2,128,256]{2,1,0:T(8,128)S(1)}, u32[]{:S(2)}, u32[]{:S(2)}) collective-permute-start(f32[2,128,256]{2,1,0:T(8,128)S(1)} %get-tuple-element.73), channel_id=1, source_target_pairs={{0,2},{1,3},{2,4},{3,5},{4,6},{5,7},{6,0},{7,1},{8,10},{9,11},{10,... | collective-permute-start | bytes 786440 | tf_op jit(solution)/shard_map/ppermute | solution.py:465
  137.9 10.1 %collective-permute-start.41 = (f32[2,128,256]{2,1,0:T(8,128)S(1)}, f32[2,128,256]{2,1,0:T(8,128)S(1)}, u32[]{:S(2)}, u32[]{:S(2)}) collective-permute-start(f32[2,128,256]{2,1,0:T(8,128)S(1)} %get-tuple-element.76), channel_id=1, source_target_pairs={{0,6},{1,7},{2,0},{3,1},{4,2},{5,3},{6,4},{7,5},{8,14},{9,15},{10,... | collective-permute-start | bytes 786440 | tf_op jit(solution)/shard_map/ppermute | solution.py:466
  140.7 11.8 %collective-permute-start.39 = (f32[2,128,256]{2,1,0:T(8,128)S(1)}, f32[2,128,256]{2,1,0:T(8,128)S(1)}, u32[]{:S(2)}, u32[]{:S(2)}) collective-permute-start(f32[2,128,256]{2,1,0:T(8,128)S(1)} %get-tuple-element.74), channel_id=1, source_target_pairs={{0,6},{1,7},{2,0},{3,1},{4,2},{5,3},{6,4},{7,5},{8,14},{9,15},{10,... | collective-permute-start | bytes 786440 | tf_op jit(solution)/shard_map/ppermute | solution.py:455
  144.1 8.4 %collective-permute-start.40 = (f32[2,128,256]{2,1,0:T(8,128)S(1)}, f32[2,128,256]{2,1,0:T(8,128)S(1)}, u32[]{:S(2)}, u32[]{:S(2)}) collective-permute-start(f32[2,128,256]{2,1,0:T(8,128)S(1)} %get-tuple-element.75), channel_id=1, source_target_pairs={{0,2},{1,3},{2,4},{3,5},{4,6},{5,7},{6,0},{7,1},{8,10},{9,11},{10,... | collective-permute-start | bytes 786440 | tf_op jit(solution)/shard_map/ppermute | solution.py:454
  146.9 5.5 %copy-start.3 = (bf16[2048,512]{1,0:T(8,128)(2,1)S(1)}, bf16[2048,512]{1,0:T(8,128)(2,1)}, u32[]{:S(2)}) copy-start(bf16[2048,512]{1,0:T(8,128)(2,1)} %w_out_ref.1) | copy-start | bytes 6291460
  146.9 5.5 %copy-start.6 = (f32[512]{0:T(512)S(1)}, f32[512]{0:T(512)}, u32[]{:S(2)}) copy-start(f32[512]{0:T(512)} %param.19) | copy-start | bytes 6148
  (3 other events, 5.0 us)

commit v6 on v5

--- a/solution.py
+++ b/solution.py
@@ -125,9 +125,14 @@
         start = spot.stop
 
 
-def relay(right_ref, left_ref, from_left_ref, from_right_ref, right_out, left_out):
-    right_out[...] = right_ref[...] + from_left_ref[...]
-    left_out[...] = left_ref[...] + from_right_ref[...]
+def relay(from_left_ref, from_right_ref, *refs):
+    helds, outs = refs[: len(refs) // 2], refs[len(refs) // 2 :]
+    pieces = len(outs) // 2
+    for at, (held, out) in enumerate(zip(helds, outs)):
+        size = out.shape[0]
+        source = from_left_ref if at < pieces else from_right_ref
+        start = at % pieces * size
+        out[...] = held[...] + source[start : start + size]
 
 
 def log(value):
@@ -323,32 +328,46 @@
     )(listed, need, tiles, *first, *second, *along_z, *along_y)
 
 
-def combine_listed(which, listed, tiles, pool, blocks_dev):
+def combine_listed(which_ones, listed, tiles, pool, blocks_dev):
     edge = tiles.shape[1]
+
+    def body(plan_ref, tile_ref, pool_ref, *totals):
+        for which, total in zip(which_ones, totals):
+            add_tiles(which, blocks_dev, plan_ref, tile_ref, pool_ref, total)
+
     return pl.pallas_call(
-        lambda *refs: add_tiles(which, blocks_dev, *refs),
+        body,
         in_specs=[in_smem] + [in_vmem] * 2,
-        out_specs=in_vmem,
-        out_shape=jax.ShapeDtypeStruct((places_of(which, blocks_dev), edge, span), jnp.float32),
+        out_specs=[in_vmem] * len(which_ones),
+        out_shape=[
+            jax.ShapeDtypeStruct((places_of(which, blocks_dev), edge, span), jnp.float32)
+            for which in which_ones
+        ],
         compiler_params=pltpu.CompilerParams(vmem_limit_bytes=6 << 20),
         cost_estimate=pl.CostEstimate(flops=2 << 30, bytes_accessed=8 << 20, transcendentals=0),
         name="listed",
     )(listed, tiles, pool)
 
 
-def mix(group, feature_ref, totals, mixed):
+def mix(group, feature_ref, keep, arrived, from_right, from_left, left_held, right_held, piece):
     part = slice(group * span, (group + 1) * span)
-    (mine, other), rest = totals[:2], totals[2:]
-    rows = rest[0].shape[0]
-    for at in range(2):
-        spot = slice(at * rows, (at + 1) * rows)
-        summed = mine[spot, :] + other[spot, :] + rest[2 * at][...] + rest[2 * at + 1][...]
-        mixed[spot, :] = ((1.0 + gin_epsilon) * feature_ref[spot, part] + summed).astype(mixed.dtype)
+    pieces = keep.shape[0] // lanes // 2
+    shift = 0 if left_held.shape[0] > lanes else piece
+    whole = slice(piece * lanes, (piece + 1) * lanes)
+    own = slice((piece - shift) * lanes, (piece - shift + 1) * lanes)
+    mixed = []
+    for low, ready, held in ((0, from_right, left_held), (1, from_left, right_held)):
+        spot = slice((low * pieces + piece) * lanes, (low * pieces + piece + 1) * lanes)
+        summed = keep[spot, :] + arrived[spot, :] + ready[whole, :] + held[own, :]
+        mixed.append(((1.0 + gin_epsilon) * feature_ref[spot, part] + summed).astype(jnp.bfloat16))
+    return mixed
 
 
 def begin_mlp(feature_ref, w_ref, bias_ref, *refs):
     totals, (out_ref, mixed) = refs[:-2], refs[-2:]
-    mix(0, feature_ref, totals, mixed)
+    for piece in range(mixed.shape[0] // lanes // 2):
+        for low, value in enumerate(mix(0, feature_ref, *totals, piece)):
+            mixed[(2 * piece + low) * lanes : (2 * piece + low + 1) * lanes, :] = value
 
     def turn(step, carry):
         part = pl.ds(pl.multiple_of(step * chunk, chunk), chunk)
@@ -361,21 +380,30 @@
     lax.fori_loop(0, out_ref.shape[0] // chunk, turn, 0)
 
 
-def end_mlp(feature_ref, w_ref, before_ref, w_out_ref, bias_ref, *refs):
-    totals, (out_ref, mixed) = refs[:-2], refs[-2:]
-    mix(1, feature_ref, totals, mixed)
-
-    def turn(step, carry):
-        part = pl.ds(pl.multiple_of(step * chunk, chunk), chunk)
-        hidden = before_ref[part, :] + jnp.dot(
-            mixed[part, :], w_ref[span:, :], preferred_element_type=jnp.float32
+def end_mlp(piece, feature_ref, w_ref, before_ref, w_out_ref, bias_ref, *refs):
+    totals, (out_ref, mixed, result, sems) = refs[:6], refs[-4:]
+    for low, value in enumerate(mix(1, feature_ref, *totals, piece)):
+        mixed[low * lanes : (low + 1) * lanes, :] = value
+    rows = mixed.shape[0]
+    hidden = before_ref[piece * rows : (piece + 1) * rows, :] + jnp.dot(
+        mixed[...], w_ref[span:, :], preferred_element_type=jnp.float32
+    )
+    hidden = jnp.maximum(hidden, 0.0).astype(jnp.bfloat16)
+    updated = jnp.dot(hidden, w_out_ref[...], preferred_element_type=jnp.float32)
+    result[...] = (updated + bias_ref[...]).astype(result.dtype)
+    pieces = out_ref.shape[0] // rows
+    copies = [
+        pltpu.make_async_copy(
+            result.at[low * lanes : (low + 1) * lanes, :],
+            out_ref.at[(low * pieces + piece) * lanes : (low * pieces + piece + 1) * lanes, :],
+            sems.at[low],
         )
-        hidden = jnp.maximum(hidden, 0.0).astype(jnp.bfloat16)
-        updated = jnp.dot(hidden, w_out_ref[...], preferred_element_type=jnp.float32)
-        out_ref[part, :] = (updated + bias_ref[...]).astype(out_ref.dtype)
-        return carry
-
-    lax.fori_loop(0, out_ref.shape[0] // chunk, turn, 0)
+        for low in range(2)
+    ]
+    for copy in copies:
+        copy.start()
+    for copy in copies:
+        copy.wait()
 
 
 def on_device(
@@ -426,7 +454,7 @@
             listed, need, cell_tiles, first, second, along_z, along_y, blocks_dev
         )
         arrived = lax.ppermute(send, "col", col_shift(0, 1))
-        keep = combine_listed(kinds, listed, cell_tiles, pool, blocks_dev)
+        keep, sides = combine_listed((kinds, 1), listed, cell_tiles, pool, blocks_dev)
         over_right, over_left = pl.pallas_call(
             join_across,
             in_specs=[in_vmem] * 2,
@@ -438,52 +466,51 @@
         )(keep, arrived)
         relay_right = lax.ppermute(over_right, "col", col_shift(1, 0))
         relay_left = lax.ppermute(over_left, "col", col_shift(-1, 0))
-        send = combine_listed(1, listed, cell_tiles, pool, blocks_dev)
-        arrived = lax.ppermute(send, "col", col_shift(0, 1))
-        keep = combine_listed(kinds + 1, listed, cell_tiles, pool, blocks_dev)
+        arrived = lax.ppermute(sides, "col", col_shift(0, 1))
+        keep, mine_sent, mine_kept = combine_listed(
+            (kinds + 1, 2, kinds + 2), listed, cell_tiles, pool, blocks_dev
+        )
         cut = blocks_dev // 2
-        right_held, right, left, left_held = pl.pallas_call(
+        held = [cut] if group < groups - 1 else [1] * cut
+        sizes = held + [cut, cut] + held
+        joined = pl.pallas_call(
             join_rest,
             in_specs=[in_vmem] * 2,
-            out_specs=[in_vmem] * 4,
-            out_shape=[jax.ShapeDtypeStruct((cut, edge, span), jnp.float32)] * 4,
+            out_specs=[in_vmem] * len(sizes),
+            out_shape=[jax.ShapeDtypeStruct((n, edge, span), jnp.float32) for n in sizes],
             compiler_params=pltpu.CompilerParams(vmem_limit_bytes=6 << 20),
             cost_estimate=pl.CostEstimate(flops=0, bytes_accessed=4 << 20, transcendentals=0),
             name="join",
         )(keep, arrived)
+        right_held, (right, left) = joined[: len(held)], joined[len(held) : len(held) + 2]
+        left_held = joined[len(held) + 2 :]
         from_left = lax.ppermute(right, "col", col_shift(1, 0))
         from_right = lax.ppermute(left, "col", col_shift(-1, 0))
-        right_held, left_held = pl.pallas_call(
+        relayed = pl.pallas_call(
             relay,
-            in_specs=[in_vmem] * 4,
-            out_specs=[in_vmem] * 2,
-            out_shape=[jax.ShapeDtypeStruct((cut, edge, span), jnp.float32)] * 2,
+            in_specs=[in_vmem] * (2 + 2 * len(held)),
+            out_specs=[in_vmem] * (2 * len(held)),
+            out_shape=[jax.ShapeDtypeStruct((n, edge, span), jnp.float32) for n in held * 2],
             compiler_params=pltpu.CompilerParams(vmem_limit_bytes=4 << 20),
             cost_estimate=pl.CostEstimate(flops=0, bytes_accessed=2 << 20, transcendentals=0),
             name="relay",
-        )(right_held, left_held, relay_right, relay_left)
-        from_left_held = lax.ppermute(right_held, "col", col_shift(1, 0))
-        from_right_held = lax.ppermute(left_held, "col", col_shift(-1, 0))
-        send = combine_listed(2, listed, cell_tiles, pool, blocks_dev)
-        arrived = lax.ppermute(send, "col", col_shift(0, 1))
-        keep = combine_listed(kinds + 2, listed, cell_tiles, pool, blocks_dev)
-        sums.append(
-            [
-                v.reshape(-1, span)
-                for v in (
-                    keep,
-                    arrived,
-                    from_left_held,
-                    from_right,
-                    from_left,
-                    from_right_held,
-                )
-            ]
-        )
-
+        )(relay_right, relay_left, *right_held, *left_held)
+        from_left_held, from_right_held = [], []
+        for piece in range(len(held)):
+            from_left_held.append(
+                lax.ppermute(relayed[piece], "col", col_shift(1, 0))
+            )
+            from_right_held.append(
+                lax.ppermute(relayed[len(held) + piece], "col", col_shift(-1, 0))
+            )
+        arrived = lax.ppermute(mine_sent, "col", col_shift(0, 1))
+        sums.append((mine_kept, arrived, from_right, from_left, from_left_held, from_right_held))
+
+    flat = [[jax.tree.map(lambda v: v.reshape(-1, span), part) for part in one] for one in sums]
+    *ready, (left_part,), (right_part,) = flat[0]
     before = pl.pallas_call(
         begin_mlp,
-        in_specs=[in_vmem] * (3 + len(sums[0])),
+        in_specs=[in_vmem] * 9,
         out_specs=in_vmem,
         out_shape=jax.ShapeDtypeStruct((nodes, hidden_size), jnp.float32),
         scratch_shapes=[pltpu.VMEM((nodes, span), jnp.bfloat16)],
@@ -492,19 +519,42 @@
             flops=1 << 29, bytes_accessed=8 << 20, transcendentals=0
         ),
         name="begin",
-    )(features, w_in, bias_in.reshape(1, -1), *sums[0])
-    return pl.pallas_call(
-        end_mlp,
-        in_specs=[in_vmem] * (5 + len(sums[1])),
-        out_specs=in_vmem,
-        out_shape=jax.ShapeDtypeStruct((nodes, width), jnp.bfloat16),
-        scratch_shapes=[pltpu.VMEM((nodes, span), jnp.bfloat16)],
-        compiler_params=pltpu.CompilerParams(vmem_limit_bytes=8 << 20),
-        cost_estimate=pl.CostEstimate(
-            flops=3 << 29, bytes_accessed=8 << 20, transcendentals=0
-        ),
-        name="end",
-    )(features, w_in, before, w_out, bias_out.reshape(1, -1), *sums[1])
+    )(features, w_in, bias_in.reshape(1, -1), *ready, left_part, right_part)
+    updated = []
+    *ready, left_parts, right_parts = flat[1]
+    for piece in range(len(left_parts)):
+        rows = nodes // len(left_parts)
+        hbm = pl.BlockSpec(memory_space=pltpu.HBM)
+        updated = [
+            pl.pallas_call(
+                lambda *refs: end_mlp(piece, *refs),
+                in_specs=[in_vmem] * 11 + [hbm] * len(updated),
+                out_specs=hbm,
+                out_shape=jax.ShapeDtypeStruct((nodes, width), jnp.bfloat16),
+                scratch_shapes=[
+                    pltpu.VMEM((rows, span), jnp.bfloat16),
+                    pltpu.VMEM((rows, width), jnp.bfloat16),
+                    pltpu.SemaphoreType.DMA((2,)),
+                ],
+                input_output_aliases={11: 0} if updated else {},
+                compiler_params=pltpu.CompilerParams(vmem_limit_bytes=8 << 20),
+                cost_estimate=pl.CostEstimate(
+                    flops=3 << 28, bytes_accessed=4 << 20, transcendentals=0
+                ),
+                name="end",
+            )(
+                features,
+                w_in,
+                before,
+                w_out,
+                bias_out.reshape(1, -1),
+                *ready,
+                left_parts[piece],
+                right_parts[piece],
+                *updated,
+            )
+        ]
+    return updated[0]
 
 
 def solution(mesh):

time: 157 us -> 158 us (level)
  the two profiles are of different devices: /device:TPU:1 before, /device:TPU:6 now
where the time goes in v6:
time: 158 us
  starting transfers between devices  73 us (46%)
  waiting for transfers between devices  63.2 us (40%)
  Pallas kernels  20.2 us (13%)
    ppermute x12, starting transfers between devices, from_y(): return lax.ppermute(value, 'row', row_shift(0, -step))  33.8 us
    ppermute x12, waiting for transfers between devices, from_z(): return lax.ppermute(value, 'row', row_shift(-step, 0))  26.5 us
    ppermute x12, starting transfers between devices, from_z(): return lax.ppermute(value, 'row', row_shift(-step, 0))  21.9 us
    ppermute x12, waiting for transfers between devices, from_y(): return lax.ppermute(value, 'row', row_shift(0, -step))  13.6 us
    ppermute x2, waiting for transfers between devices, on_device(): relay_right = lax.ppermute(over_right, 'col', col_shift(1, 0))  8.21 us
    ppermute x2, starting transfers between devices, on_device(): from_left = lax.ppermute(right, 'col', col_shift(1, 0))  6.38 us
    pallas_call x4, Pallas kernels, combine_listed(): pl.pallas_call(body, in_specs=[in_smem] + [in_vmem] * 2, out_specs=[in_vm...  6.15 us
    ppermute x2, waiting for transfers between devices, on_device(): from_right = lax.ppermute(left, 'col', col_shift(-1, 0))  5.62 us
  transfers between devices with their start and end apart: 44, of which 18 were waited for; matrix products, arithmetic and copies ran while one was open for 0% of the time, Pallas kernels for 10%

profile of v6, /device:TPU:6, one launch (start us, length us, event | category | flops | bytes accessed | tf_op | source)
XLA Modules:
  0.0 157.7 jit_solution(3180486057579325031)
XLA Ops:
  1.1 1.6 %collective-permute-start.23 = (f32[256,256]{1,0:T(8,128)S(1)}, f32[256,256]{1,0:T(8,128)S(1)}, u32[]{:S(2)}, u32[]{:S(2)}) collective-permute-start(f32[256,256]{1,0:T(8,128)S(1)} %get-tuple-element.78.refs_0_.refs_3_), channel_id=1, source_target_pairs={{0,8},{8,16},{16,24},{24,0},{32,40},{40,48},{48,56},{56,32},{64,72... | collective-permute-start | bytes 786440 | tf_op jit(solution)/shard_map/ppermute | solution.py:46
  2.8 2.9 %collective-permute-start.22 = (f32[256,256]{1,0:T(8,128)S(1)}, f32[256,256]{1,0:T(8,128)S(1)}, u32[]{:S(2)}, u32[]{:S(2)}) collective-permute-start(f32[256,256]{1,0:T(8,128)S(1)} %get-tuple-element.78.refs_0_.refs_3_), channel_id=1, source_target_pairs={{0,16},{8,24},{16,0},{24,8},{32,48},{40,56},{48,32},{56,40},{64,80... | collective-permute-start | bytes 786440 | tf_op jit(solution)/shard_map/ppermute | solution.py:46
  5.7 1.3 split.2
  7.1 3.2 %collective-permute-start.21 = (f32[256,256]{1,0:T(8,128)S(1)}, f32[256,256]{1,0:T(8,128)S(1)}, u32[]{:S(2)}, u32[]{:S(2)}) collective-permute-start(f32[256,256]{1,0:T(8,128)S(1)} %get-tuple-element.78.refs_0_.refs_3_), channel_id=1, source_target_pairs={{0,24},{8,0},{16,8},{24,16},{32,56},{40,32},{48,40},{56,48},{64,88... | collective-permute-start | bytes 786440 | tf_op jit(solution)/shard_map/ppermute | solution.py:46
  10.3 1.9 %collective-permute-start.26 = (f32[256,256]{1,0:T(8,128)S(1)}, f32[256,256]{1,0:T(8,128)S(1)}, u32[]{:S(2)}, u32[]{:S(2)}) collective-permute-start(f32[256,256]{1,0:T(8,128)S(1)} %get-tuple-element.79.refs_4_.refs_7_), channel_id=1, source_target_pairs={{0,32},{8,40},{16,48},{24,56},{32,64},{40,72},{48,80},{56,88},{64,... | collective-permute-start | bytes 786440 | tf_op jit(solution)/shard_map/ppermute | solution.py:42
  12.2 3.6 %collective-permute-start.25 = (f32[256,256]{1,0:T(8,128)S(1)}, f32[256,256]{1,0:T(8,128)S(1)}, u32[]{:S(2)}, u32[]{:S(2)}) collective-permute-start(f32[256,256]{1,0:T(8,128)S(1)} %get-tuple-element.79.refs_4_.refs_7_), channel_id=1, source_target_pairs={{0,64},{8,72},{16,80},{24,88},{32,96},{40,104},{48,112},{56,120},{... | collective-permute-start | bytes 786440 | tf_op jit(solution)/shard_map/ppermute | solution.py:42
  15.8 2.7 %collective-permute-done.22.refs_2_.refs_5_ = f32[256,256]{1,0:T(8,128)S(1)} collective-permute-done((f32[256,256]{1,0:T(8,128)S(1)}, f32[256,256]{1,0:T(8,128)S(1)}, u32[]{:S(2)}, u32[]{:S(2)}) %collective-permute-start.22) | collective-permute-done | bytes 262176 | tf_op jit(solution)/shard_map/ppermute | solution.py:46
  18.5 4.0 %collective-permute-start.24 = (f32[256,256]{1,0:T(8,128)S(1)}, f32[256,256]{1,0:T(8,128)S(1)}, u32[]{:S(2)}, u32[]{:S(2)}) collective-permute-start(f32[256,256]{1,0:T(8,128)S(1)} %get-tuple-element.79.refs_4_.refs_7_), channel_id=1, source_target_pairs={{0,96},{8,104},{16,112},{24,120},{32,0},{40,8},{48,16},{56,24},{64... | collective-permute-start | bytes 786440 | tf_op jit(solution)/shard_map/ppermute | solution.py:42
  22.5 1.3 collective-permute-start.1
  23.8 2.5 %collective-permute-done.25.refs_6_.refs_9_ = f32[256,256]{1,0:T(8,128)S(1)} collective-permute-done((f32[256,256]{1,0:T(8,128)S(1)}, f32[256,256]{1,0:T(8,128)S(1)}, u32[]{:S(2)}, u32[]{:S(2)}) %collective-permute-start.25) | collective-permute-done | bytes 262176 | tf_op jit(solution)/shard_map/ppermute | solution.py:42
  26.4 2.3 %collective-permute-start.4 = (f32[264,256]{1,0:T(8,128)S(1)}, f32[264,256]{1,0:T(8,128)S(1)}, u32[]{:S(2)}, u32[]{:S(2)}) collective-permute-start(f32[264,256]{1,0:T(8,128)S(1)} %get-tuple-element.56.refs_4_.refs_7_), channel_id=1, source_target_pairs={{0,64},{8,72},{16,80},{24,88},{32,96},{40,104},{48,112},{56,120},{... | collective-permute-start | bytes 811016 | tf_op jit(solution)/shard_map/ppermute | solution.py:42
  28.7 1.8 %collective-permute-start.3 = (f32[264,256]{1,0:T(8,128)S(1)}, f32[264,256]{1,0:T(8,128)S(1)}, u32[]{:S(2)}, u32[]{:S(2)}) collective-permute-start(f32[264,256]{1,0:T(8,128)S(1)} %get-tuple-element.56.refs_4_.refs_7_), channel_id=1, source_target_pairs={{0,96},{8,104},{16,112},{24,120},{32,0},{40,8},{48,16},{56,24},{64... | collective-permute-start | bytes 811016 | tf_op jit(solution)/shard_map/ppermute | solution.py:42
  30.6 1.3 collective-permute-done.refs_1_.refs_11_.refs_4_
  31.9 7.9 %collective-permute-done.5.refs_7_.refs_10_ = f32[264,256]{1,0:T(8,128)S(1)} collective-permute-done((f32[264,256]{1,0:T(8,128)S(1)}, f32[264,256]{1,0:T(8,128)S(1)}, u32[]{:S(2)}, u32[]{:S(2)}) %collective-permute-start.5) | collective-permute-done | bytes 270368 | tf_op jit(solution)/shard_map/ppermute | solution.py:42
  40.5 1.2 pack.3
  41.8 1.6 collective-permute-start.27
  45.3 2.6 %collective-permute-start.7 = (f32[512,256]{1,0:T(8,128)S(1)}, f32[512,256]{1,0:T(8,128)S(1)}, u32[]{:S(2)}, u32[]{:S(2)}) collective-permute-start(f32[512,256]{1,0:T(8,128)S(1)} %get-tuple-element.58), channel_id=1, source_target_pairs={{0,64},{8,72},{16,80},{24,88},{32,96},{40,104},{48,112},{56,120},{... | collective-permute-start | bytes 1572872 | tf_op jit(solution)/shard_map/ppermute | solution.py:42
  47.9 2.0 %collective-permute-start.8 = (f32[512,256]{1,0:T(8,128)S(1)}, f32[512,256]{1,0:T(8,128)S(1)}, u32[]{:S(2)}, u32[]{:S(2)}) collective-permute-start(f32[512,256]{1,0:T(8,128)S(1)} %get-tuple-element.59), channel_id=1, source_target_pairs={{0,96},{8,104},{16,112},{24,120},{32,0},{40,8},{48,16},{56,24},{64... | collective-permute-start | bytes 1572872 | tf_op jit(solution)/shard_map/ppermute | solution.py:42
  49.9 2.3 %collective-permute-start.9 = (f32[512,256]{1,0:T(8,128)S(1)}, f32[512,256]{1,0:T(8,128)S(1)}, u32[]{:S(2)}, u32[]{:S(2)}) collective-permute-start(f32[512,256]{1,0:T(8,128)S(1)} %get-tuple-element.60), channel_id=1, source_target_pairs={{0,8},{8,16},{16,24},{24,0},{32,40},{40,48},{48,56},{56,32},{64,72... | collective-permute-start | bytes 1572872 | tf_op jit(solution)/shard_map/ppermute | solution.py:46
  52.2 5.6 %collective-permute-done.27.refs_11_ = f32[512,256]{1,0:T(8,128)S(1)} collective-permute-done((f32[512,256]{1,0:T(8,128)S(1)}, f32[512,256]{1,0:T(8,128)S(1)}, u32[]{:S(2)}, u32[]{:S(2)}) %collective-permute-start.27) | collective-permute-done | bytes 524320 | tf_op jit(solution)/shard_map/ppermute | solution.py:42
  57.9 10.0 %collective-permute-start.10 = (f32[512,256]{1,0:T(8,128)S(1)}, f32[512,256]{1,0:T(8,128)S(1)}, u32[]{:S(2)}, u32[]{:S(2)}) collective-permute-start(f32[512,256]{1,0:T(8,128)S(1)} %get-tuple-element.61), channel_id=1, source_target_pairs={{0,16},{8,24},{16,0},{24,8},{32,48},{40,56},{48,32},{56,40},{64,80... | collective-permute-start | bytes 1572872 | tf_op jit(solution)/shard_map/ppermute | solution.py:46
  67.9 2.1 %collective-permute-start.11 = (f32[512,256]{1,0:T(8,128)S(1)}, f32[512,256]{1,0:T(8,128)S(1)}, u32[]{:S(2)}, u32[]{:S(2)}) collective-permute-start(f32[512,256]{1,0:T(8,128)S(1)} %get-tuple-element.62), channel_id=1, source_target_pairs={{0,24},{8,0},{16,8},{24,16},{32,56},{40,32},{48,40},{56,48},{64,88... | collective-permute-start | bytes 1572872 | tf_op jit(solution)/shard_map/ppermute | solution.py:46
  70.0 9.5 %collective-permute-done.7.refs_12_ = f32[512,256]{1,0:T(8,128)S(1)} collective-permute-done((f32[512,256]{1,0:T(8,128)S(1)}, f32[512,256]{1,0:T(8,128)S(1)}, u32[]{:S(2)}, u32[]{:S(2)}) %collective-permute-start.7) | collective-permute-done | bytes 524320 | tf_op jit(solution)/shard_map/ppermute | solution.py:42
  79.5 1.3 collective-permute-start.28
  80.9 7.6 %collective-permute-start.31 = (f32[512,256]{1,0:T(8,128)S(1)}, f32[512,256]{1,0:T(8,128)S(1)}, u32[]{:S(2)}, u32[]{:S(2)}) collective-permute-start(f32[512,256]{1,0:T(8,128)S(1)} %get-tuple-element.84), channel_id=1, source_target_pairs={{0,16},{8,24},{16,0},{24,8},{32,48},{40,56},{48,32},{56,40},{64,80... | collective-permute-start | bytes 1572872 | tf_op jit(solution)/shard_map/ppermute | solution.py:46
  88.6 2.5 %collective-permute-start.32 = (f32[512,256]{1,0:T(8,128)S(1)}, f32[512,256]{1,0:T(8,128)S(1)}, u32[]{:S(2)}, u32[]{:S(2)}) collective-permute-start(f32[512,256]{1,0:T(8,128)S(1)} %get-tuple-element.85), channel_id=1, source_target_pairs={{0,24},{8,0},{16,8},{24,16},{32,56},{40,32},{48,40},{56,48},{64,88... | collective-permute-start | bytes 1572872 | tf_op jit(solution)/shard_map/ppermute | solution.py:46
  91.8 1.8 %plan.1.refs_0_.plan_ref = s32[512]{0:T(512)S(1)} custom-call(s32[128]{0:T(128)S(1)} %bitcast.52, s32[128]{0:T(128)S(1)} %bitcast.53, s32[1,1]{1,0:T(1,128)S(6)} %copy.13.refs_2_), custom_call_target="tpu_custom_call" | custom-call | bytes 1048576 | tf_op jit(solution)/shard_map/plan/pallas_call | solution.py:433
  94.8 1.3 listed.5
  96.7 3.4 %collective-permute-done.30.refs_14_ = f32[512,256]{1,0:T(8,128)S(1)} collective-permute-done((f32[512,256]{1,0:T(8,128)S(1)}, f32[512,256]{1,0:T(8,128)S(1)}, u32[]{:S(2)}, u32[]{:S(2)}) %collective-permute-start.30) | collective-permute-done | bytes 524320 | tf_op jit(solution)/shard_map/ppermute | solution.py:46
  100.1 6.0 %collective-permute-done.31.refs_15_ = f32[512,256]{1,0:T(8,128)S(1)} collective-permute-done((f32[512,256]{1,0:T(8,128)S(1)}, f32[512,256]{1,0:T(8,128)S(1)}, u32[]{:S(2)}, u32[]{:S(2)}) %collective-permute-start.31) | collective-permute-done | bytes 524320 | tf_op jit(solution)/shard_map/ppermute | solution.py:46
  107.5 1.5 listed.7
  110.2 1.7 %listed.6 = (f32[8,128,256]{2,1,0:T(8,128)S(1)}, f32[4,128,256]{2,1,0:T(8,128)S(1)}, f32[4,128,256]{2,1,0:T(8,128)S(1)}) custom-call(s32[512]{0:T(512)S(1)} %plan.1.refs_0_.plan_ref, f32[128,128,128]{2,1,0:T(8,128)S(1)} %bitcast.26, bf16[33,128,256]{2,1,0:T(8,128)(2,1)S(1)} %get-tuple-element.86.pool_ref), custom_call_target="tpu_custom_call" | custom-call | flops 2147483648 | bytes 8388608 | tf_op jit(solution)/shard_map/listed/pallas_call | solution.py:338
  111.9 1.6 %collective-permute-start.18 = (f32[2,128,256]{2,1,0:T(8,128)S(1)}, f32[2,128,256]{2,1,0:T(8,128)S(1)}, u32[]{:S(2)}, u32[]{:S(2)}) collective-permute-start(f32[2,128,256]{2,1,0:T(8,128)S(1)} %get-tuple-element.73), channel_id=1, source_target_pairs={{0,6},{1,7},{2,0},{3,1},{4,2},{5,3},{6,4},{7,5},{8,14},{9,15},{10,... | collective-permute-start | bytes 786440 | tf_op jit(solution)/shard_map/ppermute | solution.py:468
  113.5 1.7 %listed.4 = (f32[8,128,256]{2,1,0:T(8,128)S(1)}, f32[4,128,256]{2,1,0:T(8,128)S(1)}, f32[4,128,256]{2,1,0:T(8,128)S(1)}) custom-call(s32[512]{0:T(512)S(1)} %plan.1.refs_0_.plan_ref, f32[128,128,128]{2,1,0:T(8,128)S(1)} %bitcast.27, bf16[33,128,256]{2,1,0:T(8,128)(2,1)S(1)} %get-tuple-element.63.pool_ref), custom_call_target="tpu_custom_call" | custom-call | flops 2147483648 | bytes 8388608 | tf_op jit(solution)/shard_map/listed/pallas_call | solution.py:338
  115.3 2.7 %collective-permute-done.17.from_left_ref = f32[2,128,256]{2,1,0:T(8,128)S(1)} collective-permute-done((f32[2,128,256]{2,1,0:T(8,128)S(1)}, f32[2,128,256]{2,1,0:T(8,128)S(1)}, u32[]{:S(2)}, u32[]{:S(2)}) %collective-permute-start.17) | collective-permute-done | bytes 262176 | tf_op jit(solution)/shard_map/ppermute | solution.py:467
  118.1 3.4 %collective-permute-done.18.from_right_ref = f32[2,128,256]{2,1,0:T(8,128)S(1)} collective-permute-done((f32[2,128,256]{2,1,0:T(8,128)S(1)}, f32[2,128,256]{2,1,0:T(8,128)S(1)}, u32[]{:S(2)}, u32[]{:S(2)}) %collective-permute-start.18) | collective-permute-done | bytes 262176 | tf_op jit(solution)/shard_map/ppermute | solution.py:468
  121.5 2.0 %collective-permute-start.39 = (f32[2,128,256]{2,1,0:T(8,128)S(1)}, f32[2,128,256]{2,1,0:T(8,128)S(1)}, u32[]{:S(2)}, u32[]{:S(2)}) collective-permute-start(f32[2,128,256]{2,1,0:T(8,128)S(1)} %get-tuple-element.96), channel_id=1, source_target_pairs={{0,6},{1,7},{2,0},{3,1},{4,2},{5,3},{6,4},{7,5},{8,14},{9,15},{10,... | collective-permute-start | bytes 786440 | tf_op jit(solution)/shard_map/ppermute | solution.py:468
  123.8 1.3 collective-permute-start.19
  125.2 5.5 %collective-permute-done.38.from_left_ref = f32[2,128,256]{2,1,0:T(8,128)S(1)} collective-permute-done((f32[2,128,256]{2,1,0:T(8,128)S(1)}, f32[2,128,256]{2,1,0:T(8,128)S(1)}, u32[]{:S(2)}, u32[]{:S(2)}) %collective-permute-start.38) | collective-permute-done | bytes 262176 | tf_op jit(solution)/shard_map/ppermute | solution.py:467
  130.8 1.3 collective-permute-start.42
  133.0 3.2 %collective-permute-start.15 = (f32[2,128,256]{2,1,0:T(8,128)S(1)}, f32[2,128,256]{2,1,0:T(8,128)S(1)}, u32[]{:S(2)}, u32[]{:S(2)}) collective-permute-start(f32[2,128,256]{2,1,0:T(8,128)S(1)} %get-tuple-element.69), channel_id=1, source_target_pairs={{0,2},{1,3},{2,4},{3,5},{4,6},{5,7},{6,0},{7,1},{8,10},{9,11},{10,... | collective-permute-start | bytes 786440 | tf_op jit(solution)/shard_map/ppermute | solution.py:487
  136.1 3.0 %collective-permute-done.42 = f32[1,128,256]{2,1,0:T(8,128)S(1)} collective-permute-done((f32[1,128,256]{2,1,0:T(8,128)S(1)}, f32[1,128,256]{2,1,0:T(8,128)S(1)}, u32[]{:S(2)}, u32[]{:S(2)}) %collective-permute-start.42) | collective-permute-done | bytes 131104 | tf_op jit(solution)/shard_map/ppermute | solution.py:501
  139.1 3.2 %collective-permute-start.36 = (f32[2,128,256]{2,1,0:T(8,128)S(1)}, f32[2,128,256]{2,1,0:T(8,128)S(1)}, u32[]{:S(2)}, u32[]{:S(2)}) collective-permute-start(f32[2,128,256]{2,1,0:T(8,128)S(1)} %get-tuple-element.92), channel_id=1, source_target_pairs={{0,2},{1,3},{2,4},{3,5},{4,6},{5,7},{6,0},{7,1},{8,10},{9,11},{10,... | collective-permute-start | bytes 786440 | tf_op jit(solution)/shard_map/ppermute | solution.py:487
  142.4 5.6 %collective-permute-done.14 = f32[2,128,256]{2,1,0:T(8,128)S(1)} collective-permute-done((f32[2,128,256]{2,1,0:T(8,128)S(1)}, f32[2,128,256]{2,1,0:T(8,128)S(1)}, u32[]{:S(2)}, u32[]{:S(2)}) %collective-permute-start.14) | collective-permute-done | bytes 262176 | tf_op jit(solution)/shard_map/ppermute | solution.py:488
  148.1 2.0 %collective-permute-start.41 = (f32[1,128,256]{2,1,0:T(8,128)S(1)}, f32[1,128,256]{2,1,0:T(8,128)S(1)}, u32[]{:S(2)}, u32[]{:S(2)}) collective-permute-start(f32[1,128,256]{2,1,0:T(8,128)S(1)} %get-tuple-element.102), channel_id=1, source_target_pairs={{0,6},{1,7},{2,0},{3,1},{4,2},{5,3},{6,4},{7,5},{8,14},{9,15},{10,... | collective-permute-start | bytes 393224 | tf_op jit(solution)/shard_map/ppermute | solution.py:504
  151.2 2.8 %collective-permute-done.43 = f32[1,128,256]{2,1,0:T(8,128)S(1)} collective-permute-done((f32[1,128,256]{2,1,0:T(8,128)S(1)}, f32[1,128,256]{2,1,0:T(8,128)S(1)}, u32[]{:S(2)}, u32[]{:S(2)}) %collective-permute-start.43) | collective-permute-done | bytes 131104 | tf_op jit(solution)/shard_map/ppermute | solution.py:504
  154.0 1.8 %end.2.refs_11_ = bf16[512,512]{1,0:T(8,128)(2,1)} custom-call(f32[512,512]{1,0:T(8,128)S(1)} %copy-done.1, bf16[512,2048]{1,0:T(8,128)(2,1)S(1)} %copy-done.2, f32[512,2048]{1,0:T(8,128)S(1)} %begin.1.refs_2_, bf16[2048,512]{1,0:T(8,128)(2,1)S(1)} %copy-done.3, f32[1,512]{1,0:T(1,128)S(1)} %bitcast.49, f32[512,256]{1,0:T(8,128)S(1)} %bitcast.28, ...), custom_call_target="tpu_custom_call" | custom-call | flops 805306368 | bytes 4194304 | tf_op jit(solution)/shard_map/end/pallas_call | solution.py:529
  155.8 1.8 %end.3 = bf16[512,512]{1,0:T(8,128)(2,1)} custom-call(f32[512,512]{1,0:T(8,128)S(1)} %copy-done.1, bf16[512,2048]{1,0:T(8,128)(2,1)S(1)} %copy-done.2, f32[512,2048]{1,0:T(8,128)S(1)} %begin.1.refs_2_, bf16[2048,512]{1,0:T(8,128)(2,1)S(1)} %copy-done.3, f32[1,512]{1,0:T(1,128)S(1)} %bitcast.50, ...), custom_call_target="tpu_custom_call", output_to_operand_aliasing={{}: (11, {})} | custom-call | flops 805306368 | bytes 4194304 | tf_op jit(solution)/shard_map/end/pallas_call | solution.py:529
  (78 shorter events, 11.0 us)
Async XLA Ops:
  1.1 11.1 %collective-permute-start.23 = (f32[256,256]{1,0:T(8,128)S(1)}, f32[256,256]{1,0:T(8,128)S(1)}, u32[]{:S(2)}, u32[]{:S(2)}) collective-permute-start(f32[256,256]{1,0:T(8,128)S(1)} %get-tuple-element.78.refs_0_.refs_3_), channel_id=1, source_target_pairs={{0,8},{8,16},{16,24},{24,0},{32,40},{40,48},{48,56},{56,32},{64,72... | collective-permute-start | bytes 786440 | tf_op jit(solution)/shard_map/ppermute | solution.py:46
  2.8 15.7 %collective-permute-start.22 = (f32[256,256]{1,0:T(8,128)S(1)}, f32[256,256]{1,0:T(8,128)S(1)}, u32[]{:S(2)}, u32[]{:S(2)}) collective-permute-start(f32[256,256]{1,0:T(8,128)S(1)} %get-tuple-element.78.refs_0_.refs_3_), channel_id=1, source_target_pairs={{0,16},{8,24},{16,0},{24,8},{32,48},{40,56},{48,32},{56,40},{64,80... | collective-permute-start | bytes 786440 | tf_op jit(solution)/shard_map/ppermute | solution.py:46
  5.7 88.0 %copy-start = (f32[1,1,128,128,128]{4,3,2,1,0:T(8,128)S(1)}, f32[1,1,128,128,128]{4,3,2,1,0:T(8,128)}, u32[]{:S(2)}) copy-start(f32[1,1,128,128,128]{4,3,2,1,0:T(8,128)} %param.11) | copy-start | bytes 25165828
  7.0 21.8 %collective-permute-start.2 = (f32[264,256]{1,0:T(8,128)S(1)}, f32[264,256]{1,0:T(8,128)S(1)}, u32[]{:S(2)}, u32[]{:S(2)}) collective-permute-start(f32[264,256]{1,0:T(8,128)S(1)} %get-tuple-element.55.refs_0_.refs_3_), channel_id=1, source_target_pairs={{0,8},{8,16},{16,24},{24,0},{32,40},{40,48},{48,56},{56,32},{64,72... | collective-permute-start | bytes 811016 | tf_op jit(solution)/shard_map/ppermute | solution.py:46
  7.1 15.5 %collective-permute-start.21 = (f32[256,256]{1,0:T(8,128)S(1)}, f32[256,256]{1,0:T(8,128)S(1)}, u32[]{:S(2)}, u32[]{:S(2)}) collective-permute-start(f32[256,256]{1,0:T(8,128)S(1)} %get-tuple-element.78.refs_0_.refs_3_), channel_id=1, source_target_pairs={{0,24},{8,0},{16,8},{24,16},{32,56},{40,32},{48,40},{56,48},{64,88... | collective-permute-start | bytes 786440 | tf_op jit(solution)/shard_map/ppermute | solution.py:46
  10.3 13.5 %collective-permute-start.26 = (f32[256,256]{1,0:T(8,128)S(1)}, f32[256,256]{1,0:T(8,128)S(1)}, u32[]{:S(2)}, u32[]{:S(2)}) collective-permute-start(f32[256,256]{1,0:T(8,128)S(1)} %get-tuple-element.79.refs_4_.refs_7_), channel_id=1, source_target_pairs={{0,32},{8,40},{16,48},{24,56},{32,64},{40,72},{48,80},{56,88},{64,... | collective-permute-start | bytes 786440 | tf_op jit(solution)/shard_map/ppermute | solution.py:42
  12.2 14.1 %collective-permute-start.25 = (f32[256,256]{1,0:T(8,128)S(1)}, f32[256,256]{1,0:T(8,128)S(1)}, u32[]{:S(2)}, u32[]{:S(2)}) collective-permute-start(f32[256,256]{1,0:T(8,128)S(1)} %get-tuple-element.79.refs_4_.refs_7_), channel_id=1, source_target_pairs={{0,64},{8,72},{16,80},{24,88},{32,96},{40,104},{48,112},{56,120},{... | collective-permute-start | bytes 786440 | tf_op jit(solution)/shard_map/ppermute | solution.py:42
  18.5 7.9 %collective-permute-start.24 = (f32[256,256]{1,0:T(8,128)S(1)}, f32[256,256]{1,0:T(8,128)S(1)}, u32[]{:S(2)}, u32[]{:S(2)}) collective-permute-start(f32[256,256]{1,0:T(8,128)S(1)} %get-tuple-element.79.refs_4_.refs_7_), channel_id=1, source_target_pairs={{0,96},{8,104},{16,112},{24,120},{32,0},{40,8},{48,16},{56,24},{64... | collective-permute-start | bytes 786440 | tf_op jit(solution)/shard_map/ppermute | solution.py:42
  22.5 8.1 %collective-permute-start.1 = (f32[264,256]{1,0:T(8,128)S(1)}, f32[264,256]{1,0:T(8,128)S(1)}, u32[]{:S(2)}, u32[]{:S(2)}) collective-permute-start(f32[264,256]{1,0:T(8,128)S(1)} %get-tuple-element.55.refs_0_.refs_3_), channel_id=1, source_target_pairs={{0,16},{8,24},{16,0},{24,8},{32,48},{40,56},{48,32},{56,40},{64,80... | collective-permute-start | bytes 811016 | tf_op jit(solution)/shard_map/ppermute | solution.py:46
  23.8 8.1 %collective-permute-start = (f32[264,256]{1,0:T(8,128)S(1)}, f32[264,256]{1,0:T(8,128)S(1)}, u32[]{:S(2)}, u32[]{:S(2)}) collective-permute-start(f32[264,256]{1,0:T(8,128)S(1)} %get-tuple-element.55.refs_0_.refs_3_), channel_id=1, source_target_pairs={{0,24},{8,0},{16,8},{24,16},{32,56},{40,32},{48,40},{56,48},{64,88... | collective-permute-start | bytes 811016 | tf_op jit(solution)/shard_map/ppermute | solution.py:46
  26.3 13.5 %collective-permute-start.5 = (f32[264,256]{1,0:T(8,128)S(1)}, f32[264,256]{1,0:T(8,128)S(1)}, u32[]{:S(2)}, u32[]{:S(2)}) collective-permute-start(f32[264,256]{1,0:T(8,128)S(1)} %get-tuple-element.56.refs_4_.refs_7_), channel_id=1, source_target_pairs={{0,32},{8,40},{16,48},{24,56},{32,64},{40,72},{48,80},{56,88},{64,... | collective-permute-start | bytes 811016 | tf_op jit(solution)/shard_map/ppermute | solution.py:42
  26.4 13.3 %collective-permute-start.4 = (f32[264,256]{1,0:T(8,128)S(1)}, f32[264,256]{1,0:T(8,128)S(1)}, u32[]{:S(2)}, u32[]{:S(2)}) collective-permute-start(f32[264,256]{1,0:T(8,128)S(1)} %get-tuple-element.56.refs_4_.refs_7_), channel_id=1, source_target_pairs={{0,64},{8,72},{16,80},{24,88},{32,96},{40,104},{48,112},{56,120},{... | collective-permute-start | bytes 811016 | tf_op jit(solution)/shard_map/ppermute | solution.py:42
  28.7 11.8 %collective-permute-start.3 = (f32[264,256]{1,0:T(8,128)S(1)}, f32[264,256]{1,0:T(8,128)S(1)}, u32[]{:S(2)}, u32[]{:S(2)}) collective-permute-start(f32[264,256]{1,0:T(8,128)S(1)} %get-tuple-element.56.refs_4_.refs_7_), channel_id=1, source_target_pairs={{0,96},{8,104},{16,112},{24,120},{32,0},{40,8},{48,16},{56,24},{64... | collective-permute-start | bytes 811016 | tf_op jit(solution)/shard_map/ppermute | solution.py:42
  41.7 50.0 %copy-start.7 = (s32[1,1,128]{2,1,0:T(1,128)S(1)}, s32[1,1,128]{2,1,0:T(1,128)}, u32[]{:S(2)}) copy-start(s32[1,1,128]{2,1,0:T(1,128)} %param.12) | copy-start | bytes 1540
  41.8 50.0 %copy-start.8 = (s32[1,1,128]{2,1,0:T(1,128)S(1)}, s32[1,1,128]{2,1,0:T(1,128)}, u32[]{:S(2)}) copy-start(s32[1,1,128]{2,1,0:T(1,128)} %param.13) | copy-start | bytes 1540
  41.8 51.9 %copy-start.4 = (s32[1,1,16,2]{2,3,1,0:T(2,128)S(1)}, s32[1,1,16,2]{2,3,1,0:T(2,128)}, u32[]{:S(2)}) copy-start(s32[1,1,16,2]{2,3,1,0:T(2,128)} %param.15) | copy-start | bytes 388
  41.8 16.1 %collective-permute-start.27 = (f32[512,256]{1,0:T(8,128)S(1)}, f32[512,256]{1,0:T(8,128)S(1)}, u32[]{:S(2)}, u32[]{:S(2)}) collective-permute-start(f32[512,256]{1,0:T(8,128)S(1)} %get-tuple-element.80), channel_id=1, source_target_pairs={{0,32},{8,40},{16,48},{24,56},{32,64},{40,72},{48,80},{56,88},{64,... | collective-permute-start | bytes 1572872 | tf_op jit(solution)/shard_map/ppermute | solution.py:42
  44.6 23.3 %collective-permute-start.6 = (f32[512,256]{1,0:T(8,128)S(1)}, f32[512,256]{1,0:T(8,128)S(1)}, u32[]{:S(2)}, u32[]{:S(2)}) collective-permute-start(f32[512,256]{1,0:T(8,128)S(1)} %get-tuple-element.57), channel_id=1, source_target_pairs={{0,32},{8,40},{16,48},{24,56},{32,64},{40,72},{48,80},{56,88},{64,... | collective-permute-start | bytes 1572872 | tf_op jit(solution)/shard_map/ppermute | solution.py:42
  45.3 34.2 %collective-permute-start.7 = (f32[512,256]{1,0:T(8,128)S(1)}, f32[512,256]{1,0:T(8,128)S(1)}, u32[]{:S(2)}, u32[]{:S(2)}) collective-permute-start(f32[512,256]{1,0:T(8,128)S(1)} %get-tuple-element.58), channel_id=1, source_target_pairs={{0,64},{8,72},{16,80},{24,88},{32,96},{40,104},{48,112},{56,120},{... | collective-permute-start | bytes 1572872 | tf_op jit(solution)/shard_map/ppermute | solution.py:42
  47.9 33.0 %collective-permute-start.8 = (f32[512,256]{1,0:T(8,128)S(1)}, f32[512,256]{1,0:T(8,128)S(1)}, u32[]{:S(2)}, u32[]{:S(2)}) collective-permute-start(f32[512,256]{1,0:T(8,128)S(1)} %get-tuple-element.59), channel_id=1, source_target_pairs={{0,96},{8,104},{16,112},{24,120},{32,0},{40,8},{48,16},{56,24},{64... | collective-permute-start | bytes 1572872 | tf_op jit(solution)/shard_map/ppermute | solution.py:42
  49.9 31.0 %collective-permute-start.9 = (f32[512,256]{1,0:T(8,128)S(1)}, f32[512,256]{1,0:T(8,128)S(1)}, u32[]{:S(2)}, u32[]{:S(2)}) collective-permute-start(f32[512,256]{1,0:T(8,128)S(1)} %get-tuple-element.60), channel_id=1, source_target_pairs={{0,8},{8,16},{16,24},{24,0},{32,40},{40,48},{48,56},{56,32},{64,72... | collective-permute-start | bytes 1572872 | tf_op jit(solution)/shard_map/ppermute | solution.py:46
  57.9 23.1 %collective-permute-start.10 = (f32[512,256]{1,0:T(8,128)S(1)}, f32[512,256]{1,0:T(8,128)S(1)}, u32[]{:S(2)}, u32[]{:S(2)}) collective-permute-start(f32[512,256]{1,0:T(8,128)S(1)} %get-tuple-element.61), channel_id=1, source_target_pairs={{0,16},{8,24},{16,0},{24,8},{32,48},{40,56},{48,32},{56,40},{64,80... | collective-permute-start | bytes 1572872 | tf_op jit(solution)/shard_map/ppermute | solution.py:46
  67.9 20.7 %collective-permute-start.11 = (f32[512,256]{1,0:T(8,128)S(1)}, f32[512,256]{1,0:T(8,128)S(1)}, u32[]{:S(2)}, u32[]{:S(2)}) collective-permute-start(f32[512,256]{1,0:T(8,128)S(1)} %get-tuple-element.62), channel_id=1, source_target_pairs={{0,24},{8,0},{16,8},{24,16},{32,56},{40,32},{48,40},{56,48},{64,88... | collective-permute-start | bytes 1572872 | tf_op jit(solution)/shard_map/ppermute | solution.py:46
  79.5 16.6 %collective-permute-start.28 = (f32[512,256]{1,0:T(8,128)S(1)}, f32[512,256]{1,0:T(8,128)S(1)}, u32[]{:S(2)}, u32[]{:S(2)}) collective-permute-start(f32[512,256]{1,0:T(8,128)S(1)} %get-tuple-element.81), channel_id=1, source_target_pairs={{0,64},{8,72},{16,80},{24,88},{32,96},{40,104},{48,112},{56,120},{... | collective-permute-start | bytes 1572872 | tf_op jit(solution)/shard_map/ppermute | solution.py:42
  80.8 15.4 %collective-permute-start.29 = (f32[512,256]{1,0:T(8,128)S(1)}, f32[512,256]{1,0:T(8,128)S(1)}, u32[]{:S(2)}, u32[]{:S(2)}) collective-permute-start(f32[512,256]{1,0:T(8,128)S(1)} %get-tuple-element.82), channel_id=1, source_target_pairs={{0,96},{8,104},{16,112},{24,120},{32,0},{40,8},{48,16},{56,24},{64... | collective-permute-start | bytes 1572872 | tf_op jit(solution)/shard_map/ppermute | solution.py:42
  80.8 19.3 %collective-permute-start.30 = (f32[512,256]{1,0:T(8,128)S(1)}, f32[512,256]{1,0:T(8,128)S(1)}, u32[]{:S(2)}, u32[]{:S(2)}) collective-permute-start(f32[512,256]{1,0:T(8,128)S(1)} %get-tuple-element.83), channel_id=1, source_target_pairs={{0,8},{8,16},{16,24},{24,0},{32,40},{40,48},{48,56},{56,32},{64,72... | collective-permute-start | bytes 1572872 | tf_op jit(solution)/shard_map/ppermute | solution.py:46
  80.9 25.2 %collective-permute-start.31 = (f32[512,256]{1,0:T(8,128)S(1)}, f32[512,256]{1,0:T(8,128)S(1)}, u32[]{:S(2)}, u32[]{:S(2)}) collective-permute-start(f32[512,256]{1,0:T(8,128)S(1)} %get-tuple-element.84), channel_id=1, source_target_pairs={{0,16},{8,24},{16,0},{24,8},{32,48},{40,56},{48,32},{56,40},{64,80... | collective-permute-start | bytes 1572872 | tf_op jit(solution)/shard_map/ppermute | solution.py:46
  88.6 17.8 %collective-permute-start.32 = (f32[512,256]{1,0:T(8,128)S(1)}, f32[512,256]{1,0:T(8,128)S(1)}, u32[]{:S(2)}, u32[]{:S(2)}) collective-permute-start(f32[512,256]{1,0:T(8,128)S(1)} %get-tuple-element.85), channel_id=1, source_target_pairs={{0,24},{8,0},{16,8},{24,16},{32,56},{40,32},{48,40},{56,48},{64,88... | collective-permute-start | bytes 1572872 | tf_op jit(solution)/shard_map/ppermute | solution.py:46
  96.1 13.4 %collective-permute-start.16 = (f32[4,128,256]{2,1,0:T(8,128)S(1)}, f32[4,128,256]{2,1,0:T(8,128)S(1)}, u32[]{:S(2)}, u32[]{:S(2)}) collective-permute-start(f32[4,128,256]{2,1,0:T(8,128)S(1)} %get-tuple-element.71), channel_id=1, source_target_pairs={{0,1},{1,0},{2,3},{3,2},{4,5},{5,4},{6,7},{7,6},{8,9},{9,8},{10,11... | collective-permute-start | bytes 1572872 | tf_op jit(solution)/shard_map/ppermute | solution.py:456
  96.2 25.3 %collective-permute-start.13 = (f32[8,128,256]{2,1,0:T(8,128)S(1)}, f32[8,128,256]{2,1,0:T(8,128)S(1)}, u32[]{:S(2)}, u32[]{:S(2)}) collective-permute-start(f32[8,128,256]{2,1,0:T(8,128)S(1)} %get-tuple-element.67), channel_id=1, source_target_pairs={{0,1},{1,0},{2,3},{3,2},{4,5},{5,4},{6,7},{7,6},{8,9},{9,8},{10,11... | collective-permute-start | bytes 3145736 | tf_op jit(solution)/shard_map/ppermute | solution.py:469
  109.0 14.8 %collective-permute-start.34 = (f32[8,128,256]{2,1,0:T(8,128)S(1)}, f32[8,128,256]{2,1,0:T(8,128)S(1)}, u32[]{:S(2)}, u32[]{:S(2)}) collective-permute-start(f32[8,128,256]{2,1,0:T(8,128)S(1)} %get-tuple-element.90), channel_id=1, source_target_pairs={{0,1},{1,0},{2,3},{3,2},{4,5},{5,4},{6,7},{7,6},{8,9},{9,8},{10,11... | collective-permute-start | bytes 3145736 | tf_op jit(solution)/shard_map/ppermute | solution.py:469
  109.1 6.1 %collective-permute-start.37 = (f32[4,128,256]{2,1,0:T(8,128)S(1)}, f32[4,128,256]{2,1,0:T(8,128)S(1)}, u32[]{:S(2)}, u32[]{:S(2)}) collective-permute-start(f32[4,128,256]{2,1,0:T(8,128)S(1)} %get-tuple-element.94), channel_id=1, source_target_pairs={{0,1},{1,0},{2,3},{3,2},{4,5},{5,4},{6,7},{7,6},{8,9},{9,8},{10,11... | collective-permute-start | bytes 1572872 | tf_op jit(solution)/shard_map/ppermute | solution.py:456
  109.7 8.4 %collective-permute-start.17 = (f32[2,128,256]{2,1,0:T(8,128)S(1)}, f32[2,128,256]{2,1,0:T(8,128)S(1)}, u32[]{:S(2)}, u32[]{:S(2)}) collective-permute-start(f32[2,128,256]{2,1,0:T(8,128)S(1)} %get-tuple-element.72), channel_id=1, source_target_pairs={{0,2},{1,3},{2,4},{3,5},{4,6},{5,7},{6,0},{7,1},{8,10},{9,11},{10,... | collective-permute-start | bytes 786440 | tf_op jit(solution)/shard_map/ppermute | solution.py:467
  111.9 9.6 %collective-permute-start.18 = (f32[2,128,256]{2,1,0:T(8,128)S(1)}, f32[2,128,256]{2,1,0:T(8,128)S(1)}, u32[]{:S(2)}, u32[]{:S(2)}) collective-permute-start(f32[2,128,256]{2,1,0:T(8,128)S(1)} %get-tuple-element.73), channel_id=1, source_target_pairs={{0,6},{1,7},{2,0},{3,1},{4,2},{5,3},{6,4},{7,5},{8,14},{9,15},{10,... | collective-permute-start | bytes 786440 | tf_op jit(solution)/shard_map/ppermute | solution.py:468
  115.2 17.7 %collective-permute-start.33 = (f32[4,128,256]{2,1,0:T(8,128)S(1)}, f32[4,128,256]{2,1,0:T(8,128)S(1)}, u32[]{:S(2)}, u32[]{:S(2)}) collective-permute-start(f32[4,128,256]{2,1,0:T(8,128)S(1)} %get-tuple-element.88), channel_id=1, source_target_pairs={{0,1},{1,0},{2,3},{3,2},{4,5},{5,4},{6,7},{7,6},{8,9},{9,8},{10,11... | collective-permute-start | bytes 1572872 | tf_op jit(solution)/shard_map/ppermute | solution.py:506
  118.0 14.9 %collective-permute-start.12 = (f32[4,128,256]{2,1,0:T(8,128)S(1)}, f32[4,128,256]{2,1,0:T(8,128)S(1)}, u32[]{:S(2)}, u32[]{:S(2)}) collective-permute-start(f32[4,128,256]{2,1,0:T(8,128)S(1)} %get-tuple-element.65), channel_id=1, source_target_pairs={{0,1},{1,0},{2,3},{3,2},{4,5},{5,4},{6,7},{7,6},{8,9},{9,8},{10,11... | collective-permute-start | bytes 1572872 | tf_op jit(solution)/shard_map/ppermute | solution.py:506
  121.5 9.2 %collective-permute-start.38 = (f32[2,128,256]{2,1,0:T(8,128)S(1)}, f32[2,128,256]{2,1,0:T(8,128)S(1)}, u32[]{:S(2)}, u32[]{:S(2)}) collective-permute-start(f32[2,128,256]{2,1,0:T(8,128)S(1)} %get-tuple-element.95), channel_id=1, source_target_pairs={{0,2},{1,3},{2,4},{3,5},{4,6},{5,7},{6,0},{7,1},{8,10},{9,11},{10,... | collective-permute-start | bytes 786440 | tf_op jit(solution)/shard_map/ppermute | solution.py:467
  121.5 9.2 %collective-permute-start.39 = (f32[2,128,256]{2,1,0:T(8,128)S(1)}, f32[2,128,256]{2,1,0:T(8,128)S(1)}, u32[]{:S(2)}, u32[]{:S(2)}) collective-permute-start(f32[2,128,256]{2,1,0:T(8,128)S(1)} %get-tuple-element.96), channel_id=1, source_target_pairs={{0,6},{1,7},{2,0},{3,1},{4,2},{5,3},{6,4},{7,5},{8,14},{9,15},{10,... | collective-permute-start | bytes 786440 | tf_op jit(solution)/shard_map/ppermute | solution.py:468
  123.8 15.3 %collective-permute-start.19 = (f32[2,128,256]{2,1,0:T(8,128)S(1)}, f32[2,128,256]{2,1,0:T(8,128)S(1)}, u32[]{:S(2)}, u32[]{:S(2)}) collective-permute-start(f32[2,128,256]{2,1,0:T(8,128)S(1)} %get-tuple-element.76), channel_id=1, source_target_pairs={{0,2},{1,3},{2,4},{3,5},{4,6},{5,7},{6,0},{7,1},{8,10},{9,11},{10,... | collective-permute-start | bytes 786440 | tf_op jit(solution)/shard_map/ppermute | solution.py:501
  130.8 8.4 %collective-permute-start.42 = (f32[1,128,256]{2,1,0:T(8,128)S(1)}, f32[1,128,256]{2,1,0:T(8,128)S(1)}, u32[]{:S(2)}, u32[]{:S(2)}) collective-permute-start(f32[1,128,256]{2,1,0:T(8,128)S(1)} %get-tuple-element.103), channel_id=1, source_target_pairs={{0,2},{1,3},{2,4},{3,5},{4,6},{5,7},{6,0},{7,1},{8,10},{9,11},{10,... | collective-permute-start | bytes 393224 | tf_op jit(solution)/shard_map/ppermute | solution.py:501
  132.1 10.4 %collective-permute-start.20 = (f32[2,128,256]{2,1,0:T(8,128)S(1)}, f32[2,128,256]{2,1,0:T(8,128)S(1)}, u32[]{:S(2)}, u32[]{:S(2)}) collective-permute-start(f32[2,128,256]{2,1,0:T(8,128)S(1)} %get-tuple-element.77), channel_id=1, source_target_pairs={{0,6},{1,7},{2,0},{3,1},{4,2},{5,3},{6,4},{7,5},{8,14},{9,15},{10,... | collective-permute-start | bytes 786440 | tf_op jit(solution)/shard_map/ppermute | solution.py:504
  132.9 15.2 %collective-permute-start.14 = (f32[2,128,256]{2,1,0:T(8,128)S(1)}, f32[2,128,256]{2,1,0:T(8,128)S(1)}, u32[]{:S(2)}, u32[]{:S(2)}) collective-permute-start(f32[2,128,256]{2,1,0:T(8,128)S(1)} %get-tuple-element.68), channel_id=1, source_target_pairs={{0,6},{1,7},{2,0},{3,1},{4,2},{5,3},{6,4},{7,5},{8,14},{9,15},{10,... | collective-permute-start | bytes 786440 | tf_op jit(solution)/shard_map/ppermute | solution.py:488
  133.0 15.1 %collective-permute-start.15 = (f32[2,128,256]{2,1,0:T(8,128)S(1)}, f32[2,128,256]{2,1,0:T(8,128)S(1)}, u32[]{:S(2)}, u32[]{:S(2)}) collective-permute-start(f32[2,128,256]{2,1,0:T(8,128)S(1)} %get-tuple-element.69), channel_id=1, source_target_pairs={{0,2},{1,3},{2,4},{3,5},{4,6},{5,7},{6,0},{7,1},{8,10},{9,11},{10,... | collective-permute-start | bytes 786440 | tf_op jit(solution)/shard_map/ppermute | solution.py:487
  139.1 14.9 %collective-permute-start.35 = (f32[2,128,256]{2,1,0:T(8,128)S(1)}, f32[2,128,256]{2,1,0:T(8,128)S(1)}, u32[]{:S(2)}, u32[]{:S(2)}) collective-permute-start(f32[2,128,256]{2,1,0:T(8,128)S(1)} %get-tuple-element.91), channel_id=1, source_target_pairs={{0,6},{1,7},{2,0},{3,1},{4,2},{5,3},{6,4},{7,5},{8,14},{9,15},{10,... | collective-permute-start | bytes 786440 | tf_op jit(solution)/shard_map/ppermute | solution.py:488
  139.1 14.8 %collective-permute-start.36 = (f32[2,128,256]{2,1,0:T(8,128)S(1)}, f32[2,128,256]{2,1,0:T(8,128)S(1)}, u32[]{:S(2)}, u32[]{:S(2)}) collective-permute-start(f32[2,128,256]{2,1,0:T(8,128)S(1)} %get-tuple-element.92), channel_id=1, source_target_pairs={{0,2},{1,3},{2,4},{3,5},{4,6},{5,7},{6,0},{7,1},{8,10},{9,11},{10,... | collective-permute-start | bytes 786440 | tf_op jit(solution)/shard_map/ppermute | solution.py:487
  142.4 11.5 %collective-permute-start.43 = (f32[1,128,256]{2,1,0:T(8,128)S(1)}, f32[1,128,256]{2,1,0:T(8,128)S(1)}, u32[]{:S(2)}, u32[]{:S(2)}) collective-permute-start(f32[1,128,256]{2,1,0:T(8,128)S(1)} %get-tuple-element.104), channel_id=1, source_target_pairs={{0,6},{1,7},{2,0},{3,1},{4,2},{5,3},{6,4},{7,5},{8,14},{9,15},{10,... | collective-permute-start | bytes 393224 | tf_op jit(solution)/shard_map/ppermute | solution.py:504
  148.1 7.7 %collective-permute-start.40 = (f32[1,128,256]{2,1,0:T(8,128)S(1)}, f32[1,128,256]{2,1,0:T(8,128)S(1)}, u32[]{:S(2)}, u32[]{:S(2)}) collective-permute-start(f32[1,128,256]{2,1,0:T(8,128)S(1)} %get-tuple-element.101), channel_id=1, source_target_pairs={{0,2},{1,3},{2,4},{3,5},{4,6},{5,7},{6,0},{7,1},{8,10},{9,11},{10,... | collective-permute-start | bytes 393224 | tf_op jit(solution)/shard_map/ppermute | solution.py:501
  148.1 7.7 %collective-permute-start.41 = (f32[1,128,256]{2,1,0:T(8,128)S(1)}, f32[1,128,256]{2,1,0:T(8,128)S(1)}, u32[]{:S(2)}, u32[]{:S(2)}) collective-permute-start(f32[1,128,256]{2,1,0:T(8,128)S(1)} %get-tuple-element.102), channel_id=1, source_target_pairs={{0,6},{1,7},{2,0},{3,1},{4,2},{5,3},{6,4},{7,5},{8,14},{9,15},{10,... | collective-permute-start | bytes 393224 | tf_op jit(solution)/shard_map/ppermute | solution.py:504
  (5 other events, 87.0 us)

commit v7 on v6

--- a/solution.py
+++ b/solution.py
@@ -14,6 +14,7 @@
 picks = 2
 kinds = 3
 across_x = side // 2
+near = (1, 3)
 note_rows = 8
 lanes = 128
 chunk = 256
@@ -255,7 +256,6 @@
     entries = pairs_of(tile_total, blocks_dev)
     slot_bits = log(tile_total)
     pos_bits = log(sources) + 1
-    total[...] = jnp.zeros_like(total)
 
     def turn(step, carry):
         products = []
@@ -281,11 +281,19 @@
     lax.fori_loop(0, (count + unroll - 1) // unroll, turn, 0)
 
 
-def combine(blocks_dev, plan_ref, need_ref, tile_ref, *refs):
+def put(pool, along_z, along_y, away):
+    half = pool.shape[1] // 2
+    top, low = slice(0, half), slice(half, 2 * half)
+    for d in range(side):
+        for j in range(picks):
+            spot = spot_of(d, j, half)
+            pool[(back(away) * side + d) * picks + j, top, :] = along_z[spot, :].astype(pool.dtype)
+            pool[(d * side + back(away)) * picks + j, low, :] = along_y[spot, :].astype(pool.dtype)
+
+
+def fill(need_ref, *refs):
     first, second = refs[:side], refs[side : 2 * side]
-    along_z = refs[2 * side : 3 * side - 1]
-    along_y = refs[3 * side - 1 : 4 * side - 2]
-    total, pool = refs[4 * side - 2 :]
+    early, pool = refs[2 * side : -1], refs[-1]
     half = pool.shape[1] // 2
     top, low = slice(0, half), slice(half, 2 * half)
     my_z = lax.axis_index("row") // side
@@ -300,45 +308,70 @@
             pool[d * side * picks + j, low, :] = second[d][half_at(mine, half), :].astype(
                 pool.dtype
             )
-            spot = spot_of(d, j, half)
-            for away in range(1, side):
-                pool[(back(away) * side + d) * picks + j, top, :] = along_z[away - 1][
-                    spot, :
-                ].astype(pool.dtype)
-                pool[(d * side + back(away)) * picks + j, low, :] = along_y[away - 1][
-                    spot, :
-                ].astype(pool.dtype)
+    for at, away in enumerate(near):
+        put(pool, early[2 * at], early[2 * at + 1], away)
     pool[side * side * picks] = jnp.zeros(pool.shape[1:], pool.dtype)
-    add_tiles(0, blocks_dev, plan_ref, tile_ref, pool, total)
-
-
-def combine_sent(listed, need, tiles, first, second, along_z, along_y, blocks_dev):
+
+
+def fill_early(need, first, second, along_z, along_y, edge):
+    early = [v for away in near for v in (along_z[away - 1], along_y[away - 1])]
+    return pl.pallas_call(
+        fill,
+        in_specs=[in_smem] + [in_vmem] * (2 * side + len(early)),
+        out_specs=in_vmem,
+        out_shape=jax.ShapeDtypeStruct((side * side * picks + 1, edge, span), jnp.bfloat16),
+        compiler_params=pltpu.CompilerParams(vmem_limit_bytes=8 << 20),
+        cost_estimate=pl.CostEstimate(flops=0, bytes_accessed=5 << 20, transcendentals=0),
+        name="fill",
+    )(need, *first, *second, *early)
+
+
+def combine(blocks_dev, plan_ref, tile_ref, along_z, along_y, _, total, pool, listed, sem):
+    copy = pltpu.make_async_copy(plan_ref, listed, sem)
+    copy.start()
+    total[...] = jnp.zeros_like(total)
+    put(pool, along_z, along_y, side // 2)
+    copy.wait()
+    add_tiles(0, blocks_dev, listed, tile_ref, pool, total)
+
+
+def combine_sent(listed, tiles, along_z, along_y, pool, blocks_dev):
     edge = tiles.shape[1]
+    far = side // 2 - 1
     return pl.pallas_call(
         lambda *refs: combine(blocks_dev, *refs),
-        in_specs=[in_smem] * 2 + [in_vmem] * (4 * side - 1),
+        in_specs=[in_vmem] * 5,
         out_specs=[in_vmem] * 2,
+        scratch_shapes=[pltpu.SMEM(listed.shape, jnp.int32), pltpu.SemaphoreType.DMA(())],
         out_shape=[
             jax.ShapeDtypeStruct((places_of(0, blocks_dev), edge, span), jnp.float32),
-            jax.ShapeDtypeStruct((side * side * picks + 1, edge, span), jnp.bfloat16),
+            jax.ShapeDtypeStruct(pool.shape, pool.dtype),
         ],
+        input_output_aliases={4: 1},
         compiler_params=pltpu.CompilerParams(vmem_limit_bytes=10 << 20),
-        cost_estimate=pl.CostEstimate(flops=2 << 30, bytes_accessed=10 << 20, transcendentals=0),
+        cost_estimate=pl.CostEstimate(flops=2 << 30, bytes_accessed=6 << 20, transcendentals=0),
         name="combine",
-    )(listed, need, tiles, *first, *second, *along_z, *along_y)
+    )(listed, tiles, along_z[far], along_y[far], pool)
 
 
 def combine_listed(which_ones, listed, tiles, pool, blocks_dev):
     edge = tiles.shape[1]
 
-    def body(plan_ref, tile_ref, pool_ref, *totals):
+    def body(plan_ref, tile_ref, pool_ref, *refs):
+        totals, (lists, sem) = refs[:-2], refs[-2:]
+        copy = pltpu.make_async_copy(plan_ref, lists, sem)
+        copy.start()
+        for total in totals:
+            total[...] = jnp.zeros_like(total)
+        copy.wait()
         for which, total in zip(which_ones, totals):
-            add_tiles(which, blocks_dev, plan_ref, tile_ref, pool_ref, total)
+            add_tiles(which, blocks_dev, lists, tile_ref, pool_ref, total)
 
     return pl.pallas_call(
         body,
-        in_specs=[in_smem] + [in_vmem] * 2,
+        in_specs=[in_vmem] * 3,
         out_specs=[in_vmem] * len(which_ones),
+        scratch_shapes=[pltpu.SMEM(listed.shape, jnp.int32), pltpu.SemaphoreType.DMA(())],
         out_shape=[
             jax.ShapeDtypeStruct((places_of(which, blocks_dev), edge, span), jnp.float32)
             for which in which_ones
@@ -381,7 +414,23 @@
 
 
 def end_mlp(piece, feature_ref, w_ref, before_ref, w_out_ref, bias_ref, *refs):
-    totals, (out_ref, mixed, result, sems) = refs[:6], refs[-4:]
+    totals = refs[:6]
+    if piece == 0:
+        result, mixed = refs[6:]
+    else:
+        before_result, out_ref, mixed, result, sems = refs[6:]
+
+        def move(source, at, low):
+            start = (low * out_ref.shape[0] // 2) + at * lanes
+            return pltpu.make_async_copy(
+                source.at[low * lanes : (low + 1) * lanes, :],
+                out_ref.at[start : start + lanes, :],
+                sems.at[2 * at + low],
+            )
+
+        copies = [move(before_result, 0, low) for low in range(2)]
+        for copy in copies:
+            copy.start()
     for low, value in enumerate(mix(1, feature_ref, *totals, piece)):
         mixed[low * lanes : (low + 1) * lanes, :] = value
     rows = mixed.shape[0]
@@ -391,17 +440,11 @@
     hidden = jnp.maximum(hidden, 0.0).astype(jnp.bfloat16)
     updated = jnp.dot(hidden, w_out_ref[...], preferred_element_type=jnp.float32)
     result[...] = (updated + bias_ref[...]).astype(result.dtype)
-    pieces = out_ref.shape[0] // rows
-    copies = [
-        pltpu.make_async_copy(
-            result.at[low * lanes : (low + 1) * lanes, :],
-            out_ref.at[(low * pieces + piece) * lanes : (low * pieces + piece + 1) * lanes, :],
-            sems.at[low],
-        )
-        for low in range(2)
-    ]
-    for copy in copies:
-        copy.start()
+    if piece == 0:
+        return
+    for low in range(2):
+        copies.append(move(result, piece, low))
+        copies[-1].start()
     for copy in copies:
         copy.wait()
 
@@ -450,9 +493,8 @@
         for away in (1, 3, 2):
             along_z[away - 1] = from_z(packed[away - 1], -away)
             along_y[away - 1] = from_y(packed[side + away - 2], -away)
-        send, pool = combine_sent(
-            listed, need, cell_tiles, first, second, along_z, along_y, blocks_dev
-        )
+        pool = fill_early(need, first, second, along_z, along_y, edge)
+        send, pool = combine_sent(listed, cell_tiles, along_z, along_y, pool, blocks_dev)
         arrived = lax.ppermute(send, "col", col_shift(0, 1))
         keep, sides = combine_listed((kinds, 1), listed, cell_tiles, pool, blocks_dev)
         over_right, over_left = pl.pallas_call(
@@ -524,19 +566,19 @@
     *ready, left_parts, right_parts = flat[1]
     for piece in range(len(left_parts)):
         rows = nodes // len(left_parts)
-        hbm = pl.BlockSpec(memory_space=pltpu.HBM)
+        last = piece == len(left_parts) - 1
         updated = [
             pl.pallas_call(
                 lambda *refs: end_mlp(piece, *refs),
-                in_specs=[in_vmem] * 11 + [hbm] * len(updated),
-                out_specs=hbm,
-                out_shape=jax.ShapeDtypeStruct((nodes, width), jnp.bfloat16),
-                scratch_shapes=[
-                    pltpu.VMEM((rows, span), jnp.bfloat16),
-                    pltpu.VMEM((rows, width), jnp.bfloat16),
-                    pltpu.SemaphoreType.DMA((2,)),
-                ],
-                input_output_aliases={11: 0} if updated else {},
+                in_specs=[in_vmem] * (11 + len(updated)),
+                out_specs=pl.BlockSpec(memory_space=pltpu.HBM) if last else in_vmem,
+                out_shape=jax.ShapeDtypeStruct((nodes if last else rows, width), jnp.bfloat16),
+                scratch_shapes=[pltpu.VMEM((rows, span), jnp.bfloat16)]
+                + (
+                    [pltpu.VMEM((rows, width), jnp.bfloat16), pltpu.SemaphoreType.DMA((4,))]
+                    if last
+                    else []
+                ),
                 compiler_params=pltpu.CompilerParams(vmem_limit_bytes=8 << 20),
                 cost_estimate=pl.CostEstimate(
                     flops=3 << 28, bytes_accessed=4 << 20, transcendentals=0

time: 158 us -> 157 us (level)
  the two profiles are of different devices: /device:TPU:6 before, /device:TPU:14 now
where the time goes in v7:
time: 157 us
  starting transfers between devices  68.5 us (44%)
  waiting for transfers between devices  67.2 us (43%)
  Pallas kernels  20.1 us (13%)
    ppermute x12, starting transfers between devices, from_y(): return lax.ppermute(value, 'row', row_shift(0, -step))  33.1 us
    ppermute x12, waiting for transfers between devices, from_y(): return lax.ppermute(value, 'row', row_shift(0, -step))  22.2 us
    ppermute x12, waiting for transfers between devices, from_z(): return lax.ppermute(value, 'row', row_shift(-step, 0))  22.1 us
    ppermute x12, starting transfers between devices, from_z(): return lax.ppermute(value, 'row', row_shift(-step, 0))  18.2 us
    ppermute x2, waiting for transfers between devices, on_device(): relay_right = lax.ppermute(over_right, 'col', col_shift(1, 0))  8.38 us
    ppermute x2, starting transfers between devices, on_device(): from_left = lax.ppermute(right, 'col', col_shift(1, 0))  6.43 us
    pallas_call x4, Pallas kernels, combine_listed(): pl.pallas_call(body, in_specs=[in_vmem] * 3, out_specs=[in_vmem] * len(wh...  5.85 us
    ppermute x2, waiting for transfers between devices, on_device(): from_right = lax.ppermute(left, 'col', col_shift(-1, 0))  5.62 us
  transfers between devices with their start and end apart: 44, of which 19 were waited for; matrix products, arithmetic and copies ran while one was open for 0% of the time, Pallas kernels for 10%

profile of v7, /device:TPU:14, one launch (start us, length us, event | category | flops | bytes accessed | tf_op | source)
XLA Modules:
  0.0 157.1 jit_solution(14778882636629157139)
XLA Ops:
  0.0 1.3 split.3
  1.3 1.6 %collective-permute-start.23 = (f32[256,256]{1,0:T(8,128)S(1)}, f32[256,256]{1,0:T(8,128)S(1)}, u32[]{:S(2)}, u32[]{:S(2)}) collective-permute-start(f32[256,256]{1,0:T(8,128)S(1)} %get-tuple-element.78.refs_0_), channel_id=1, source_target_pairs={{0,8},{8,16},{16,24},{24,0},{32,40},{40,48},{48,56},{56,32},{64,72... | collective-permute-start | bytes 786440 | tf_op jit(solution)/shard_map/ppermute | solution.py:47
  3.9 1.2 split.2
  6.1 1.5 collective-permute-start.21
  7.6 1.9 %collective-permute-start.26 = (f32[256,256]{1,0:T(8,128)S(1)}, f32[256,256]{1,0:T(8,128)S(1)}, u32[]{:S(2)}, u32[]{:S(2)}) collective-permute-start(f32[256,256]{1,0:T(8,128)S(1)} %get-tuple-element.79.refs_4_), channel_id=1, source_target_pairs={{0,32},{8,40},{16,48},{24,56},{32,64},{40,72},{48,80},{56,88},{64,... | collective-permute-start | bytes 786440 | tf_op jit(solution)/shard_map/ppermute | solution.py:43
  9.5 5.3 %collective-permute-done.23.refs_3_ = f32[256,256]{1,0:T(8,128)S(1)} collective-permute-done((f32[256,256]{1,0:T(8,128)S(1)}, f32[256,256]{1,0:T(8,128)S(1)}, u32[]{:S(2)}, u32[]{:S(2)}) %collective-permute-start.23) | collective-permute-done | bytes 262176 | tf_op jit(solution)/shard_map/ppermute | solution.py:47
  14.8 3.9 %collective-permute-start.25 = (f32[256,256]{1,0:T(8,128)S(1)}, f32[256,256]{1,0:T(8,128)S(1)}, u32[]{:S(2)}, u32[]{:S(2)}) collective-permute-start(f32[256,256]{1,0:T(8,128)S(1)} %get-tuple-element.79.refs_4_), channel_id=1, source_target_pairs={{0,64},{8,72},{16,80},{24,88},{32,96},{40,104},{48,112},{56,120},{... | collective-permute-start | bytes 786440 | tf_op jit(solution)/shard_map/ppermute | solution.py:43
  19.4 5.0 %collective-permute-start = (f32[264,256]{1,0:T(8,128)S(1)}, f32[264,256]{1,0:T(8,128)S(1)}, u32[]{:S(2)}, u32[]{:S(2)}) collective-permute-start(f32[264,256]{1,0:T(8,128)S(1)} %get-tuple-element.55.refs_0_), channel_id=1, source_target_pairs={{0,24},{8,0},{16,8},{24,16},{32,56},{40,32},{48,40},{56,48},{64,88... | collective-permute-start | bytes 811016 | tf_op jit(solution)/shard_map/ppermute | solution.py:47
  24.4 1.3 collective-permute-start.5
  25.7 3.5 %collective-permute-done.24.refs_5_ = f32[256,256]{1,0:T(8,128)S(1)} collective-permute-done((f32[256,256]{1,0:T(8,128)S(1)}, f32[256,256]{1,0:T(8,128)S(1)}, u32[]{:S(2)}, u32[]{:S(2)}) %collective-permute-start.24) | collective-permute-done | bytes 262176 | tf_op jit(solution)/shard_map/ppermute | solution.py:43
  29.3 3.8 %collective-permute-start.3 = (f32[264,256]{1,0:T(8,128)S(1)}, f32[264,256]{1,0:T(8,128)S(1)}, u32[]{:S(2)}, u32[]{:S(2)}) collective-permute-start(f32[264,256]{1,0:T(8,128)S(1)} %get-tuple-element.56.refs_4_), channel_id=1, source_target_pairs={{0,96},{8,104},{16,112},{24,120},{32,0},{40,8},{48,16},{56,24},{64... | collective-permute-start | bytes 811016 | tf_op jit(solution)/shard_map/ppermute | solution.py:43
  33.5 3.9 %collective-permute-done.5.refs_7_.refs_10_ = f32[264,256]{1,0:T(8,128)S(1)} collective-permute-done((f32[264,256]{1,0:T(8,128)S(1)}, f32[264,256]{1,0:T(8,128)S(1)}, u32[]{:S(2)}, u32[]{:S(2)}) %collective-permute-start.5) | collective-permute-done | bytes 270368 | tf_op jit(solution)/shard_map/ppermute | solution.py:43
  37.4 5.0 %collective-permute-done.3.refs_5_.refs_8_ = f32[264,256]{1,0:T(8,128)S(1)} collective-permute-done((f32[264,256]{1,0:T(8,128)S(1)}, f32[264,256]{1,0:T(8,128)S(1)}, u32[]{:S(2)}, u32[]{:S(2)}) %collective-permute-start.3) | collective-permute-done | bytes 270368 | tf_op jit(solution)/shard_map/ppermute | solution.py:43
  42.4 1.2 pack.3
  43.8 1.2 pack.2
  45.1 3.5 %collective-permute-start.6 = (f32[512,256]{1,0:T(8,128)S(1)}, f32[512,256]{1,0:T(8,128)S(1)}, u32[]{:S(2)}, u32[]{:S(2)}) collective-permute-start(f32[512,256]{1,0:T(8,128)S(1)} %get-tuple-element.57), channel_id=1, source_target_pairs={{0,64},{8,72},{16,80},{24,88},{32,96},{40,104},{48,112},{56,120},{... | collective-permute-start | bytes 1572872 | tf_op jit(solution)/shard_map/ppermute | solution.py:43
  49.2 7.3 %collective-permute-start.9 = (f32[512,256]{1,0:T(8,128)S(1)}, f32[512,256]{1,0:T(8,128)S(1)}, u32[]{:S(2)}, u32[]{:S(2)}) collective-permute-start(f32[512,256]{1,0:T(8,128)S(1)} %get-tuple-element.60), channel_id=1, source_target_pairs={{0,8},{8,16},{16,24},{24,0},{32,40},{40,48},{48,56},{56,32},{64,72... | collective-permute-start | bytes 1572872 | tf_op jit(solution)/shard_map/ppermute | solution.py:47
  56.5 2.5 %collective-permute-done.29.refs_8_ = f32[512,256]{1,0:T(8,128)S(1)} collective-permute-done((f32[512,256]{1,0:T(8,128)S(1)}, f32[512,256]{1,0:T(8,128)S(1)}, u32[]{:S(2)}, u32[]{:S(2)}) %collective-permute-start.29) | collective-permute-done | bytes 524320 | tf_op jit(solution)/shard_map/ppermute | solution.py:43
  58.9 1.7 %collective-permute-start.10 = (f32[512,256]{1,0:T(8,128)S(1)}, f32[512,256]{1,0:T(8,128)S(1)}, u32[]{:S(2)}, u32[]{:S(2)}) collective-permute-start(f32[512,256]{1,0:T(8,128)S(1)} %get-tuple-element.61), channel_id=1, source_target_pairs={{0,96},{8,104},{16,112},{24,120},{32,0},{40,8},{48,16},{56,24},{64... | collective-permute-start | bytes 1572872 | tf_op jit(solution)/shard_map/ppermute | solution.py:43
  60.6 6.1 %collective-permute-done.6.refs_2_ = f32[512,256]{1,0:T(8,128)S(1)} collective-permute-done((f32[512,256]{1,0:T(8,128)S(1)}, f32[512,256]{1,0:T(8,128)S(1)}, u32[]{:S(2)}, u32[]{:S(2)}) %collective-permute-start.6) | collective-permute-done | bytes 524320 | tf_op jit(solution)/shard_map/ppermute | solution.py:43
  66.7 4.2 %collective-permute-start.11 = (f32[512,256]{1,0:T(8,128)S(1)}, f32[512,256]{1,0:T(8,128)S(1)}, u32[]{:S(2)}, u32[]{:S(2)}) collective-permute-start(f32[512,256]{1,0:T(8,128)S(1)} %get-tuple-element.62), channel_id=1, source_target_pairs={{0,24},{8,0},{16,8},{24,16},{32,56},{40,32},{48,40},{56,48},{64,88... | collective-permute-start | bytes 1572872 | tf_op jit(solution)/shard_map/ppermute | solution.py:47
  71.3 1.1 collective-permute-done.8.refs_8_
  72.3 9.3 %collective-permute-start.30 = (f32[512,256]{1,0:T(8,128)S(1)}, f32[512,256]{1,0:T(8,128)S(1)}, u32[]{:S(2)}, u32[]{:S(2)}) collective-permute-start(f32[512,256]{1,0:T(8,128)S(1)} %get-tuple-element.83), channel_id=1, source_target_pairs={{0,8},{8,16},{16,24},{24,0},{32,40},{40,48},{48,56},{56,32},{64,72... | collective-permute-start | bytes 1572872 | tf_op jit(solution)/shard_map/ppermute | solution.py:47
  82.7 1.3 collective-permute-done.11.refs_11_
  84.0 1.4 collective-permute-start.28
  86.2 1.7 %plan.1.refs_0_.plan_ref = s32[512]{0:T(512)S(1)} custom-call(s32[128]{0:T(128)S(1)} %bitcast.54, s32[128]{0:T(128)S(1)} %bitcast.55, s32[1,1]{1,0:T(1,128)S(6)} %copy.15.refs_2_), custom_call_target="tpu_custom_call" | custom-call | bytes 1048576 | tf_op jit(solution)/shard_map/plan/pallas_call | solution.py:476
  89.6 1.3 listed.5
  90.8 1.6 %collective-permute-done.30.refs_9_ = f32[512,256]{1,0:T(8,128)S(1)} collective-permute-done((f32[512,256]{1,0:T(8,128)S(1)}, f32[512,256]{1,0:T(8,128)S(1)}, u32[]{:S(2)}, u32[]{:S(2)}) %collective-permute-start.30) | collective-permute-done | bytes 524320 | tf_op jit(solution)/shard_map/ppermute | solution.py:47
  93.0 2.4 %collective-permute-done.32.refs_11_ = f32[512,256]{1,0:T(8,128)S(1)} collective-permute-done((f32[512,256]{1,0:T(8,128)S(1)}, f32[512,256]{1,0:T(8,128)S(1)}, u32[]{:S(2)}, u32[]{:S(2)}) %collective-permute-start.32) | collective-permute-done | bytes 524320 | tf_op jit(solution)/shard_map/ppermute | solution.py:47
  96.1 11.1 %collective-permute-done.28.refs_3_ = f32[512,256]{1,0:T(8,128)S(1)} collective-permute-done((f32[512,256]{1,0:T(8,128)S(1)}, f32[512,256]{1,0:T(8,128)S(1)}, u32[]{:S(2)}, u32[]{:S(2)}) %collective-permute-start.28) | collective-permute-done | bytes 524320 | tf_op jit(solution)/shard_map/ppermute | solution.py:47
  108.1 1.4 listed.7
  111.1 1.6 %listed.6 = (f32[8,128,256]{2,1,0:T(8,128)S(1)}, f32[4,128,256]{2,1,0:T(8,128)S(1)}, f32[4,128,256]{2,1,0:T(8,128)S(1)}) custom-call(s32[512]{0:T(512)S(1)} %plan.1.refs_0_.plan_ref, f32[128,128,128]{2,1,0:T(8,128)S(1)} %bitcast.28, bf16[33,128,256]{2,1,0:T(8,128)(2,1)S(1)} %get-tuple-element.86.pool_ref), custom_call_target="tpu_custom_call" | custom-call | flops 2147483648 | bytes 8388608 | tf_op jit(solution)/shard_map/listed/pallas_call | solution.py:370
  112.6 1.3 collective-permute-start.18
  113.9 1.6 %listed.4 = (f32[8,128,256]{2,1,0:T(8,128)S(1)}, f32[4,128,256]{2,1,0:T(8,128)S(1)}, f32[4,128,256]{2,1,0:T(8,128)S(1)}) custom-call(s32[512]{0:T(512)S(1)} %plan.1.refs_0_.plan_ref, f32[128,128,128]{2,1,0:T(8,128)S(1)} %bitcast.29, bf16[33,128,256]{2,1,0:T(8,128)(2,1)S(1)} %get-tuple-element.63.pool_ref), custom_call_target="tpu_custom_call" | custom-call | flops 2147483648 | bytes 8388608 | tf_op jit(solution)/shard_map/listed/pallas_call | solution.py:370
  115.6 2.9 %collective-permute-done.17.from_left_ref = f32[2,128,256]{2,1,0:T(8,128)S(1)} collective-permute-done((f32[2,128,256]{2,1,0:T(8,128)S(1)}, f32[2,128,256]{2,1,0:T(8,128)S(1)}, u32[]{:S(2)}, u32[]{:S(2)}) %collective-permute-start.17) | collective-permute-done | bytes 262176 | tf_op jit(solution)/shard_map/ppermute | solution.py:509
  118.6 3.3 %collective-permute-done.18.from_right_ref = f32[2,128,256]{2,1,0:T(8,128)S(1)} collective-permute-done((f32[2,128,256]{2,1,0:T(8,128)S(1)}, f32[2,128,256]{2,1,0:T(8,128)S(1)}, u32[]{:S(2)}, u32[]{:S(2)}) %collective-permute-start.18) | collective-permute-done | bytes 262176 | tf_op jit(solution)/shard_map/ppermute | solution.py:510
  122.0 2.0 %collective-permute-start.39 = (f32[2,128,256]{2,1,0:T(8,128)S(1)}, f32[2,128,256]{2,1,0:T(8,128)S(1)}, u32[]{:S(2)}, u32[]{:S(2)}) collective-permute-start(f32[2,128,256]{2,1,0:T(8,128)S(1)} %get-tuple-element.96), channel_id=1, source_target_pairs={{0,6},{1,7},{2,0},{3,1},{4,2},{5,3},{6,4},{7,5},{8,14},{9,15},{10,... | collective-permute-start | bytes 786440 | tf_op jit(solution)/shard_map/ppermute | solution.py:510
  124.3 1.3 collective-permute-start.19
  125.7 5.5 %collective-permute-done.38.from_left_ref = f32[2,128,256]{2,1,0:T(8,128)S(1)} collective-permute-done((f32[2,128,256]{2,1,0:T(8,128)S(1)}, f32[2,128,256]{2,1,0:T(8,128)S(1)}, u32[]{:S(2)}, u32[]{:S(2)}) %collective-permute-start.38) | collective-permute-done | bytes 262176 | tf_op jit(solution)/shard_map/ppermute | solution.py:509
  131.2 1.3 collective-permute-start.42
  133.3 3.2 %collective-permute-start.15 = (f32[2,128,256]{2,1,0:T(8,128)S(1)}, f32[2,128,256]{2,1,0:T(8,128)S(1)}, u32[]{:S(2)}, u32[]{:S(2)}) collective-permute-start(f32[2,128,256]{2,1,0:T(8,128)S(1)} %get-tuple-element.69), channel_id=1, source_target_pairs={{0,2},{1,3},{2,4},{3,5},{4,6},{5,7},{6,0},{7,1},{8,10},{9,11},{10,... | collective-permute-start | bytes 786440 | tf_op jit(solution)/shard_map/ppermute | solution.py:529
  136.5 3.0 %collective-permute-done.42 = f32[1,128,256]{2,1,0:T(8,128)S(1)} collective-permute-done((f32[1,128,256]{2,1,0:T(8,128)S(1)}, f32[1,128,256]{2,1,0:T(8,128)S(1)}, u32[]{:S(2)}, u32[]{:S(2)}) %collective-permute-start.42) | collective-permute-done | bytes 131104 | tf_op jit(solution)/shard_map/ppermute | solution.py:543
  139.6 3.2 %collective-permute-start.36 = (f32[2,128,256]{2,1,0:T(8,128)S(1)}, f32[2,128,256]{2,1,0:T(8,128)S(1)}, u32[]{:S(2)}, u32[]{:S(2)}) collective-permute-start(f32[2,128,256]{2,1,0:T(8,128)S(1)} %get-tuple-element.92), channel_id=1, source_target_pairs={{0,2},{1,3},{2,4},{3,5},{4,6},{5,7},{6,0},{7,1},{8,10},{9,11},{10,... | collective-permute-start | bytes 786440 | tf_op jit(solution)/shard_map/ppermute | solution.py:529
  142.8 5.6 %collective-permute-done.14 = f32[2,128,256]{2,1,0:T(8,128)S(1)} collective-permute-done((f32[2,128,256]{2,1,0:T(8,128)S(1)}, f32[2,128,256]{2,1,0:T(8,128)S(1)}, u32[]{:S(2)}, u32[]{:S(2)}) %collective-permute-start.14) | collective-permute-done | bytes 262176 | tf_op jit(solution)/shard_map/ppermute | solution.py:530
  148.5 2.0 %collective-permute-start.41 = (f32[1,128,256]{2,1,0:T(8,128)S(1)}, f32[1,128,256]{2,1,0:T(8,128)S(1)}, u32[]{:S(2)}, u32[]{:S(2)}) collective-permute-start(f32[1,128,256]{2,1,0:T(8,128)S(1)} %get-tuple-element.102), channel_id=1, source_target_pairs={{0,6},{1,7},{2,0},{3,1},{4,2},{5,3},{6,4},{7,5},{8,14},{9,15},{10,... | collective-permute-start | bytes 393224 | tf_op jit(solution)/shard_map/ppermute | solution.py:546
  151.6 2.2 %collective-permute-done.43 = f32[1,128,256]{2,1,0:T(8,128)S(1)} collective-permute-done((f32[1,128,256]{2,1,0:T(8,128)S(1)}, f32[1,128,256]{2,1,0:T(8,128)S(1)}, u32[]{:S(2)}, u32[]{:S(2)}) %collective-permute-start.43) | collective-permute-done | bytes 131104 | tf_op jit(solution)/shard_map/ppermute | solution.py:546
  153.8 1.1 end.2.refs_11_
  155.2 1.8 %end.3 = bf16[512,512]{1,0:T(8,128)(2,1)} custom-call(f32[512,512]{1,0:T(8,128)S(1)} %copy-done, bf16[512,2048]{1,0:T(8,128)(2,1)S(1)} %copy-done.1, f32[512,2048]{1,0:T(8,128)S(1)} %begin.1.refs_2_, bf16[2048,512]{1,0:T(8,128)(2,1)S(1)} %copy-done.2, f32[1,512]{1,0:T(1,128)S(1)} %bitcast.52, f32[512,256]{1,0:T(8,128)S(1)} %bitcast.31, ...), custom_call_target="tpu_custom_call" | custom-call | flops 805306368 | bytes 4194304 | tf_op jit(solution)/shard_map/end/pallas_call | solution.py:571
  (83 shorter events, 13.5 us)
Async XLA Ops:
  0.0 88.6 %slice-start = ((s8[8388608]{0:T(1024)(128)(4,1)}), s8[4194304]{0:T(1024)(128)(4,1)S(1)}, s32[]{:S(2)}) async-start(s8[8388608]{0:T(1024)(128)(4,1)} %bitcast.22), calls=%async_computation | async-start | bytes 8388608
  1.3 13.5 %collective-permute-start.23 = (f32[256,256]{1,0:T(8,128)S(1)}, f32[256,256]{1,0:T(8,128)S(1)}, u32[]{:S(2)}, u32[]{:S(2)}) collective-permute-start(f32[256,256]{1,0:T(8,128)S(1)} %get-tuple-element.78.refs_0_), channel_id=1, source_target_pairs={{0,8},{8,16},{16,24},{24,0},{32,40},{40,48},{48,56},{56,32},{64,72... | collective-permute-start | bytes 786440 | tf_op jit(solution)/shard_map/ppermute | solution.py:47
  2.9 15.8 %collective-permute-start.22 = (f32[256,256]{1,0:T(8,128)S(1)}, f32[256,256]{1,0:T(8,128)S(1)}, u32[]{:S(2)}, u32[]{:S(2)}) collective-permute-start(f32[256,256]{1,0:T(8,128)S(1)} %get-tuple-element.78.refs_0_), channel_id=1, source_target_pairs={{0,16},{8,24},{16,0},{24,8},{32,48},{40,56},{48,32},{56,40},{64,80... | collective-permute-start | bytes 786440 | tf_op jit(solution)/shard_map/ppermute | solution.py:47
  5.0 24.2 %collective-permute-start.2 = (f32[264,256]{1,0:T(8,128)S(1)}, f32[264,256]{1,0:T(8,128)S(1)}, u32[]{:S(2)}, u32[]{:S(2)}) collective-permute-start(f32[264,256]{1,0:T(8,128)S(1)} %get-tuple-element.55.refs_0_), channel_id=1, source_target_pairs={{0,8},{8,16},{16,24},{24,0},{32,40},{40,48},{48,56},{56,32},{64,72... | collective-permute-start | bytes 811016 | tf_op jit(solution)/shard_map/ppermute | solution.py:47
  6.1 13.3 %collective-permute-start.21 = (f32[256,256]{1,0:T(8,128)S(1)}, f32[256,256]{1,0:T(8,128)S(1)}, u32[]{:S(2)}, u32[]{:S(2)}) collective-permute-start(f32[256,256]{1,0:T(8,128)S(1)} %get-tuple-element.78.refs_0_), channel_id=1, source_target_pairs={{0,24},{8,0},{16,8},{24,16},{32,56},{40,32},{48,40},{56,48},{64,88... | collective-permute-start | bytes 786440 | tf_op jit(solution)/shard_map/ppermute | solution.py:47
  7.6 11.8 %collective-permute-start.26 = (f32[256,256]{1,0:T(8,128)S(1)}, f32[256,256]{1,0:T(8,128)S(1)}, u32[]{:S(2)}, u32[]{:S(2)}) collective-permute-start(f32[256,256]{1,0:T(8,128)S(1)} %get-tuple-element.79.refs_4_), channel_id=1, source_target_pairs={{0,32},{8,40},{16,48},{24,56},{32,64},{40,72},{48,80},{56,88},{64,... | collective-permute-start | bytes 786440 | tf_op jit(solution)/shard_map/ppermute | solution.py:43
  14.8 9.6 %collective-permute-start.25 = (f32[256,256]{1,0:T(8,128)S(1)}, f32[256,256]{1,0:T(8,128)S(1)}, u32[]{:S(2)}, u32[]{:S(2)}) collective-permute-start(f32[256,256]{1,0:T(8,128)S(1)} %get-tuple-element.79.refs_4_), channel_id=1, source_target_pairs={{0,64},{8,72},{16,80},{24,88},{32,96},{40,104},{48,112},{56,120},{... | collective-permute-start | bytes 786440 | tf_op jit(solution)/shard_map/ppermute | solution.py:43
  18.7 10.6 %collective-permute-start.24 = (f32[256,256]{1,0:T(8,128)S(1)}, f32[256,256]{1,0:T(8,128)S(1)}, u32[]{:S(2)}, u32[]{:S(2)}) collective-permute-start(f32[256,256]{1,0:T(8,128)S(1)} %get-tuple-element.79.refs_4_), channel_id=1, source_target_pairs={{0,96},{8,104},{16,112},{24,120},{32,0},{40,8},{48,16},{56,24},{64... | collective-permute-start | bytes 786440 | tf_op jit(solution)/shard_map/ppermute | solution.py:43
  19.4 13.7 %collective-permute-start.1 = (f32[264,256]{1,0:T(8,128)S(1)}, f32[264,256]{1,0:T(8,128)S(1)}, u32[]{:S(2)}, u32[]{:S(2)}) collective-permute-start(f32[264,256]{1,0:T(8,128)S(1)} %get-tuple-element.55.refs_0_), channel_id=1, source_target_pairs={{0,16},{8,24},{16,0},{24,8},{32,48},{40,56},{48,32},{56,40},{64,80... | collective-permute-start | bytes 811016 | tf_op jit(solution)/shard_map/ppermute | solution.py:47
  19.4 14.1 %collective-permute-start = (f32[264,256]{1,0:T(8,128)S(1)}, f32[264,256]{1,0:T(8,128)S(1)}, u32[]{:S(2)}, u32[]{:S(2)}) collective-permute-start(f32[264,256]{1,0:T(8,128)S(1)} %get-tuple-element.55.refs_0_), channel_id=1, source_target_pairs={{0,24},{8,0},{16,8},{24,16},{32,56},{40,32},{48,40},{56,48},{64,88... | collective-permute-start | bytes 811016 | tf_op jit(solution)/shard_map/ppermute | solution.py:47
  24.4 13.0 %collective-permute-start.5 = (f32[264,256]{1,0:T(8,128)S(1)}, f32[264,256]{1,0:T(8,128)S(1)}, u32[]{:S(2)}, u32[]{:S(2)}) collective-permute-start(f32[264,256]{1,0:T(8,128)S(1)} %get-tuple-element.56.refs_4_), channel_id=1, source_target_pairs={{0,32},{8,40},{16,48},{24,56},{32,64},{40,72},{48,80},{56,88},{64,... | collective-permute-start | bytes 811016 | tf_op jit(solution)/shard_map/ppermute | solution.py:43
  29.3 8.2 %collective-permute-start.4 = (f32[264,256]{1,0:T(8,128)S(1)}, f32[264,256]{1,0:T(8,128)S(1)}, u32[]{:S(2)}, u32[]{:S(2)}) collective-permute-start(f32[264,256]{1,0:T(8,128)S(1)} %get-tuple-element.56.refs_4_), channel_id=1, source_target_pairs={{0,64},{8,72},{16,80},{24,88},{32,96},{40,104},{48,112},{56,120},{... | collective-permute-start | bytes 811016 | tf_op jit(solution)/shard_map/ppermute | solution.py:43
  29.3 13.2 %collective-permute-start.3 = (f32[264,256]{1,0:T(8,128)S(1)}, f32[264,256]{1,0:T(8,128)S(1)}, u32[]{:S(2)}, u32[]{:S(2)}) collective-permute-start(f32[264,256]{1,0:T(8,128)S(1)} %get-tuple-element.56.refs_4_), channel_id=1, source_target_pairs={{0,96},{8,104},{16,112},{24,120},{32,0},{40,8},{48,16},{56,24},{64... | collective-permute-start | bytes 811016 | tf_op jit(solution)/shard_map/ppermute | solution.py:43
  43.7 42.5 %copy-start.6 = (s32[1,1,128]{2,1,0:T(1,128)S(1)}, s32[1,1,128]{2,1,0:T(1,128)}, u32[]{:S(2)}) copy-start(s32[1,1,128]{2,1,0:T(1,128)} %param.12) | copy-start | bytes 1540
  43.7 44.2 %copy-start.3 = (s32[1,1,16,2]{2,3,1,0:T(2,128)S(1)}, s32[1,1,16,2]{2,3,1,0:T(2,128)}, u32[]{:S(2)}) copy-start(s32[1,1,16,2]{2,3,1,0:T(2,128)} %param.15) | copy-start | bytes 388
  43.7 44.9 %slice-start.1 = ((s8[8388608]{0:T(1024)(128)(4,1)}), s8[4194304]{0:T(1024)(128)(4,1)S(1)}, s32[]{:S(2)}) async-start(s8[8388608]{0:T(1024)(128)(4,1)} %bitcast.22), calls=%async_computation.1 | async-start | bytes 8388608
  43.7 15.2 %collective-permute-start.29 = (f32[512,256]{1,0:T(8,128)S(1)}, f32[512,256]{1,0:T(8,128)S(1)}, u32[]{:S(2)}, u32[]{:S(2)}) collective-permute-start(f32[512,256]{1,0:T(8,128)S(1)} %get-tuple-element.82), channel_id=1, source_target_pairs={{0,32},{8,40},{16,48},{24,56},{32,64},{40,72},{48,80},{56,88},{64,... | collective-permute-start | bytes 1572872 | tf_op jit(solution)/shard_map/ppermute | solution.py:43
  45.1 21.7 %collective-permute-start.6 = (f32[512,256]{1,0:T(8,128)S(1)}, f32[512,256]{1,0:T(8,128)S(1)}, u32[]{:S(2)}, u32[]{:S(2)}) collective-permute-start(f32[512,256]{1,0:T(8,128)S(1)} %get-tuple-element.57), channel_id=1, source_target_pairs={{0,64},{8,72},{16,80},{24,88},{32,96},{40,104},{48,112},{56,120},{... | collective-permute-start | bytes 1572872 | tf_op jit(solution)/shard_map/ppermute | solution.py:43
  48.6 22.3 %collective-permute-start.7 = (f32[512,256]{1,0:T(8,128)S(1)}, f32[512,256]{1,0:T(8,128)S(1)}, u32[]{:S(2)}, u32[]{:S(2)}) collective-permute-start(f32[512,256]{1,0:T(8,128)S(1)} %get-tuple-element.58), channel_id=1, source_target_pairs={{0,16},{8,24},{16,0},{24,8},{32,48},{40,56},{48,32},{56,40},{64,80... | collective-permute-start | bytes 1572872 | tf_op jit(solution)/shard_map/ppermute | solution.py:47
  48.9 23.4 %collective-permute-start.8 = (f32[512,256]{1,0:T(8,128)S(1)}, f32[512,256]{1,0:T(8,128)S(1)}, u32[]{:S(2)}, u32[]{:S(2)}) collective-permute-start(f32[512,256]{1,0:T(8,128)S(1)} %get-tuple-element.59), channel_id=1, source_target_pairs={{0,32},{8,40},{16,48},{24,56},{32,64},{40,72},{48,80},{56,88},{64,... | collective-permute-start | bytes 1572872 | tf_op jit(solution)/shard_map/ppermute | solution.py:43
  49.2 32.4 %collective-permute-start.9 = (f32[512,256]{1,0:T(8,128)S(1)}, f32[512,256]{1,0:T(8,128)S(1)}, u32[]{:S(2)}, u32[]{:S(2)}) collective-permute-start(f32[512,256]{1,0:T(8,128)S(1)} %get-tuple-element.60), channel_id=1, source_target_pairs={{0,8},{8,16},{16,24},{24,0},{32,40},{40,48},{48,56},{56,32},{64,72... | collective-permute-start | bytes 1572872 | tf_op jit(solution)/shard_map/ppermute | solution.py:47
  58.9 23.3 %collective-permute-start.10 = (f32[512,256]{1,0:T(8,128)S(1)}, f32[512,256]{1,0:T(8,128)S(1)}, u32[]{:S(2)}, u32[]{:S(2)}) collective-permute-start(f32[512,256]{1,0:T(8,128)S(1)} %get-tuple-element.61), channel_id=1, source_target_pairs={{0,96},{8,104},{16,112},{24,120},{32,0},{40,8},{48,16},{56,24},{64... | collective-permute-start | bytes 1572872 | tf_op jit(solution)/shard_map/ppermute | solution.py:43
  66.7 17.3 %collective-permute-start.11 = (f32[512,256]{1,0:T(8,128)S(1)}, f32[512,256]{1,0:T(8,128)S(1)}, u32[]{:S(2)}, u32[]{:S(2)}) collective-permute-start(f32[512,256]{1,0:T(8,128)S(1)} %get-tuple-element.62), channel_id=1, source_target_pairs={{0,24},{8,0},{16,8},{24,16},{32,56},{40,32},{48,40},{56,48},{64,88... | collective-permute-start | bytes 1572872 | tf_op jit(solution)/shard_map/ppermute | solution.py:47
  70.9 25.2 %collective-permute-start.27 = (f32[512,256]{1,0:T(8,128)S(1)}, f32[512,256]{1,0:T(8,128)S(1)}, u32[]{:S(2)}, u32[]{:S(2)}) collective-permute-start(f32[512,256]{1,0:T(8,128)S(1)} %get-tuple-element.80), channel_id=1, source_target_pairs={{0,64},{8,72},{16,80},{24,88},{32,96},{40,104},{48,112},{56,120},{... | collective-permute-start | bytes 1572872 | tf_op jit(solution)/shard_map/ppermute | solution.py:43
  72.3 20.1 %collective-permute-start.30 = (f32[512,256]{1,0:T(8,128)S(1)}, f32[512,256]{1,0:T(8,128)S(1)}, u32[]{:S(2)}, u32[]{:S(2)}) collective-permute-start(f32[512,256]{1,0:T(8,128)S(1)} %get-tuple-element.83), channel_id=1, source_target_pairs={{0,8},{8,16},{16,24},{24,0},{32,40},{40,48},{48,56},{56,32},{64,72... | collective-permute-start | bytes 1572872 | tf_op jit(solution)/shard_map/ppermute | solution.py:47
  81.6 10.8 %collective-permute-start.31 = (f32[512,256]{1,0:T(8,128)S(1)}, f32[512,256]{1,0:T(8,128)S(1)}, u32[]{:S(2)}, u32[]{:S(2)}) collective-permute-start(f32[512,256]{1,0:T(8,128)S(1)} %get-tuple-element.84), channel_id=1, source_target_pairs={{0,96},{8,104},{16,112},{24,120},{32,0},{40,8},{48,16},{56,24},{64... | collective-permute-start | bytes 1572872 | tf_op jit(solution)/shard_map/ppermute | solution.py:43
  82.2 13.1 %collective-permute-start.32 = (f32[512,256]{1,0:T(8,128)S(1)}, f32[512,256]{1,0:T(8,128)S(1)}, u32[]{:S(2)}, u32[]{:S(2)}) collective-permute-start(f32[512,256]{1,0:T(8,128)S(1)} %get-tuple-element.85), channel_id=1, source_target_pairs={{0,24},{8,0},{16,8},{24,16},{32,56},{40,32},{48,40},{56,48},{64,88... | collective-permute-start | bytes 1572872 | tf_op jit(solution)/shard_map/ppermute | solution.py:47
  84.0 23.1 %collective-permute-start.28 = (f32[512,256]{1,0:T(8,128)S(1)}, f32[512,256]{1,0:T(8,128)S(1)}, u32[]{:S(2)}, u32[]{:S(2)}) collective-permute-start(f32[512,256]{1,0:T(8,128)S(1)} %get-tuple-element.81), channel_id=1, source_target_pairs={{0,16},{8,24},{16,0},{24,8},{32,48},{40,56},{48,32},{56,40},{64,80... | collective-permute-start | bytes 1572872 | tf_op jit(solution)/shard_map/ppermute | solution.py:47
  92.4 17.7 %collective-permute-start.16 = (f32[4,128,256]{2,1,0:T(8,128)S(1)}, f32[4,128,256]{2,1,0:T(8,128)S(1)}, u32[]{:S(2)}, u32[]{:S(2)}) collective-permute-start(f32[4,128,256]{2,1,0:T(8,128)S(1)} %get-tuple-element.71), channel_id=1, source_target_pairs={{0,1},{1,0},{2,3},{3,2},{4,5},{5,4},{6,7},{7,6},{8,9},{9,8},{10,11... | collective-permute-start | bytes 1572872 | tf_op jit(solution)/shard_map/ppermute | solution.py:498
  92.5 29.5 %collective-permute-start.13 = (f32[8,128,256]{2,1,0:T(8,128)S(1)}, f32[8,128,256]{2,1,0:T(8,128)S(1)}, u32[]{:S(2)}, u32[]{:S(2)}) collective-permute-start(f32[8,128,256]{2,1,0:T(8,128)S(1)} %get-tuple-element.67), channel_id=1, source_target_pairs={{0,1},{1,0},{2,3},{3,2},{4,5},{5,4},{6,7},{7,6},{8,9},{9,8},{10,11... | collective-permute-start | bytes 3145736 | tf_op jit(solution)/shard_map/ppermute | solution.py:511
  109.5 14.7 %collective-permute-start.34 = (f32[8,128,256]{2,1,0:T(8,128)S(1)}, f32[8,128,256]{2,1,0:T(8,128)S(1)}, u32[]{:S(2)}, u32[]{:S(2)}) collective-permute-start(f32[8,128,256]{2,1,0:T(8,128)S(1)} %get-tuple-element.90), channel_id=1, source_target_pairs={{0,1},{1,0},{2,3},{3,2},{4,5},{5,4},{6,7},{7,6},{8,9},{9,8},{10,11... | collective-permute-start | bytes 3145736 | tf_op jit(solution)/shard_map/ppermute | solution.py:511
  109.6 5.9 %collective-permute-start.37 = (f32[4,128,256]{2,1,0:T(8,128)S(1)}, f32[4,128,256]{2,1,0:T(8,128)S(1)}, u32[]{:S(2)}, u32[]{:S(2)}) collective-permute-start(f32[4,128,256]{2,1,0:T(8,128)S(1)} %get-tuple-element.94), channel_id=1, source_target_pairs={{0,1},{1,0},{2,3},{3,2},{4,5},{5,4},{6,7},{7,6},{8,9},{9,8},{10,11... | collective-permute-start | bytes 1572872 | tf_op jit(solution)/shard_map/ppermute | solution.py:498
  110.2 8.4 %collective-permute-start.17 = (f32[2,128,256]{2,1,0:T(8,128)S(1)}, f32[2,128,256]{2,1,0:T(8,128)S(1)}, u32[]{:S(2)}, u32[]{:S(2)}) collective-permute-start(f32[2,128,256]{2,1,0:T(8,128)S(1)} %get-tuple-element.72), channel_id=1, source_target_pairs={{0,2},{1,3},{2,4},{3,5},{4,6},{5,7},{6,0},{7,1},{8,10},{9,11},{10,... | collective-permute-start | bytes 786440 | tf_op jit(solution)/shard_map/ppermute | solution.py:509
  112.6 9.3 %collective-permute-start.18 = (f32[2,128,256]{2,1,0:T(8,128)S(1)}, f32[2,128,256]{2,1,0:T(8,128)S(1)}, u32[]{:S(2)}, u32[]{:S(2)}) collective-permute-start(f32[2,128,256]{2,1,0:T(8,128)S(1)} %get-tuple-element.73), channel_id=1, source_target_pairs={{0,6},{1,7},{2,0},{3,1},{4,2},{5,3},{6,4},{7,5},{8,14},{9,15},{10,... | collective-permute-start | bytes 786440 | tf_op jit(solution)/shard_map/ppermute | solution.py:510
  115.5 17.8 %collective-permute-start.33 = (f32[4,128,256]{2,1,0:T(8,128)S(1)}, f32[4,128,256]{2,1,0:T(8,128)S(1)}, u32[]{:S(2)}, u32[]{:S(2)}) collective-permute-start(f32[4,128,256]{2,1,0:T(8,128)S(1)} %get-tuple-element.88), channel_id=1, source_target_pairs={{0,1},{1,0},{2,3},{3,2},{4,5},{5,4},{6,7},{7,6},{8,9},{9,8},{10,11... | collective-permute-start | bytes 1572872 | tf_op jit(solution)/shard_map/ppermute | solution.py:548
  118.6 14.8 %collective-permute-start.12 = (f32[4,128,256]{2,1,0:T(8,128)S(1)}, f32[4,128,256]{2,1,0:T(8,128)S(1)}, u32[]{:S(2)}, u32[]{:S(2)}) collective-permute-start(f32[4,128,256]{2,1,0:T(8,128)S(1)} %get-tuple-element.65), channel_id=1, source_target_pairs={{0,1},{1,0},{2,3},{3,2},{4,5},{5,4},{6,7},{7,6},{8,9},{9,8},{10,11... | collective-permute-start | bytes 1572872 | tf_op jit(solution)/shard_map/ppermute | solution.py:548
  121.9 9.2 %collective-permute-start.38 = (f32[2,128,256]{2,1,0:T(8,128)S(1)}, f32[2,128,256]{2,1,0:T(8,128)S(1)}, u32[]{:S(2)}, u32[]{:S(2)}) collective-permute-start(f32[2,128,256]{2,1,0:T(8,128)S(1)} %get-tuple-element.95), channel_id=1, source_target_pairs={{0,2},{1,3},{2,4},{3,5},{4,6},{5,7},{6,0},{7,1},{8,10},{9,11},{10,... | collective-permute-start | bytes 786440 | tf_op jit(solution)/shard_map/ppermute | solution.py:509
  122.0 9.2 %collective-permute-start.39 = (f32[2,128,256]{2,1,0:T(8,128)S(1)}, f32[2,128,256]{2,1,0:T(8,128)S(1)}, u32[]{:S(2)}, u32[]{:S(2)}) collective-permute-start(f32[2,128,256]{2,1,0:T(8,128)S(1)} %get-tuple-element.96), channel_id=1, source_target_pairs={{0,6},{1,7},{2,0},{3,1},{4,2},{5,3},{6,4},{7,5},{8,14},{9,15},{10,... | collective-permute-start | bytes 786440 | tf_op jit(solution)/shard_map/ppermute | solution.py:510
  124.3 15.3 %collective-permute-start.19 = (f32[2,128,256]{2,1,0:T(8,128)S(1)}, f32[2,128,256]{2,1,0:T(8,128)S(1)}, u32[]{:S(2)}, u32[]{:S(2)}) collective-permute-start(f32[2,128,256]{2,1,0:T(8,128)S(1)} %get-tuple-element.76), channel_id=1, source_target_pairs={{0,2},{1,3},{2,4},{3,5},{4,6},{5,7},{6,0},{7,1},{8,10},{9,11},{10,... | collective-permute-start | bytes 786440 | tf_op jit(solution)/shard_map/ppermute | solution.py:543
  131.2 8.4 %collective-permute-start.42 = (f32[1,128,256]{2,1,0:T(8,128)S(1)}, f32[1,128,256]{2,1,0:T(8,128)S(1)}, u32[]{:S(2)}, u32[]{:S(2)}) collective-permute-start(f32[1,128,256]{2,1,0:T(8,128)S(1)} %get-tuple-element.103), channel_id=1, source_target_pairs={{0,2},{1,3},{2,4},{3,5},{4,6},{5,7},{6,0},{7,1},{8,10},{9,11},{10,... | collective-permute-start | bytes 393224 | tf_op jit(solution)/shard_map/ppermute | solution.py:543
  132.5 10.3 %collective-permute-start.20 = (f32[2,128,256]{2,1,0:T(8,128)S(1)}, f32[2,128,256]{2,1,0:T(8,128)S(1)}, u32[]{:S(2)}, u32[]{:S(2)}) collective-permute-start(f32[2,128,256]{2,1,0:T(8,128)S(1)} %get-tuple-element.77), channel_id=1, source_target_pairs={{0,6},{1,7},{2,0},{3,1},{4,2},{5,3},{6,4},{7,5},{8,14},{9,15},{10,... | collective-permute-start | bytes 786440 | tf_op jit(solution)/shard_map/ppermute | solution.py:546
  133.3 15.2 %collective-permute-start.14 = (f32[2,128,256]{2,1,0:T(8,128)S(1)}, f32[2,128,256]{2,1,0:T(8,128)S(1)}, u32[]{:S(2)}, u32[]{:S(2)}) collective-permute-start(f32[2,128,256]{2,1,0:T(8,128)S(1)} %get-tuple-element.68), channel_id=1, source_target_pairs={{0,6},{1,7},{2,0},{3,1},{4,2},{5,3},{6,4},{7,5},{8,14},{9,15},{10,... | collective-permute-start | bytes 786440 | tf_op jit(solution)/shard_map/ppermute | solution.py:530
  133.3 15.1 %collective-permute-start.15 = (f32[2,128,256]{2,1,0:T(8,128)S(1)}, f32[2,128,256]{2,1,0:T(8,128)S(1)}, u32[]{:S(2)}, u32[]{:S(2)}) collective-permute-start(f32[2,128,256]{2,1,0:T(8,128)S(1)} %get-tuple-element.69), channel_id=1, source_target_pairs={{0,2},{1,3},{2,4},{3,5},{4,6},{5,7},{6,0},{7,1},{8,10},{9,11},{10,... | collective-permute-start | bytes 786440 | tf_op jit(solution)/shard_map/ppermute | solution.py:529
  139.6 14.2 %collective-permute-start.35 = (f32[2,128,256]{2,1,0:T(8,128)S(1)}, f32[2,128,256]{2,1,0:T(8,128)S(1)}, u32[]{:S(2)}, u32[]{:S(2)}) collective-permute-start(f32[2,128,256]{2,1,0:T(8,128)S(1)} %get-tuple-element.91), channel_id=1, source_target_pairs={{0,6},{1,7},{2,0},{3,1},{4,2},{5,3},{6,4},{7,5},{8,14},{9,15},{10,... | collective-permute-start | bytes 786440 | tf_op jit(solution)/shard_map/ppermute | solution.py:530
  139.6 14.2 %collective-permute-start.36 = (f32[2,128,256]{2,1,0:T(8,128)S(1)}, f32[2,128,256]{2,1,0:T(8,128)S(1)}, u32[]{:S(2)}, u32[]{:S(2)}) collective-permute-start(f32[2,128,256]{2,1,0:T(8,128)S(1)} %get-tuple-element.92), channel_id=1, source_target_pairs={{0,2},{1,3},{2,4},{3,5},{4,6},{5,7},{6,0},{7,1},{8,10},{9,11},{10,... | collective-permute-start | bytes 786440 | tf_op jit(solution)/shard_map/ppermute | solution.py:529
  142.8 10.9 %collective-permute-start.43 = (f32[1,128,256]{2,1,0:T(8,128)S(1)}, f32[1,128,256]{2,1,0:T(8,128)S(1)}, u32[]{:S(2)}, u32[]{:S(2)}) collective-permute-start(f32[1,128,256]{2,1,0:T(8,128)S(1)} %get-tuple-element.104), channel_id=1, source_target_pairs={{0,6},{1,7},{2,0},{3,1},{4,2},{5,3},{6,4},{7,5},{8,14},{9,15},{10,... | collective-permute-start | bytes 393224 | tf_op jit(solution)/shard_map/ppermute | solution.py:546
  148.5 6.4 %collective-permute-start.40 = (f32[1,128,256]{2,1,0:T(8,128)S(1)}, f32[1,128,256]{2,1,0:T(8,128)S(1)}, u32[]{:S(2)}, u32[]{:S(2)}) collective-permute-start(f32[1,128,256]{2,1,0:T(8,128)S(1)} %get-tuple-element.101), channel_id=1, source_target_pairs={{0,2},{1,3},{2,4},{3,5},{4,6},{5,7},{6,0},{7,1},{8,10},{9,11},{10,... | collective-permute-start | bytes 393224 | tf_op jit(solution)/shard_map/ppermute | solution.py:543
  148.5 6.7 %collective-permute-start.41 = (f32[1,128,256]{2,1,0:T(8,128)S(1)}, f32[1,128,256]{2,1,0:T(8,128)S(1)}, u32[]{:S(2)}, u32[]{:S(2)}) collective-permute-start(f32[1,128,256]{2,1,0:T(8,128)S(1)} %get-tuple-element.102), channel_id=1, source_target_pairs={{0,6},{1,7},{2,0},{3,1},{4,2},{5,3},{6,4},{7,5},{8,14},{9,15},{10,... | collective-permute-start | bytes 393224 | tf_op jit(solution)/shard_map/ppermute | solution.py:546
  (6 other events, 128.1 us)

commit v8 on v7

--- a/solution.py
+++ b/solution.py
@@ -420,15 +420,20 @@
     else:
         before_result, out_ref, mixed, result, sems = refs[6:]
 
-        def move(source, at, low):
+        def move(source, at, low, columns):
             start = (low * out_ref.shape[0] // 2) + at * lanes
-            return pltpu.make_async_copy(
-                source.at[low * lanes : (low + 1) * lanes, :],
-                out_ref.at[start : start + lanes, :],
-                sems.at[2 * at + low],
+            copies.append(
+                pltpu.make_async_copy(
+                    source.at[low * lanes : (low + 1) * lanes, columns],
+                    out_ref.at[start : start + lanes, columns],
+                    sems.at[len(copies)],
+                )
             )
-
-        copies = [move(before_result, 0, low) for low in range(2)]
+            return copies[-1]
+
+        copies = []
+        for low in range(2):
+            move(before_result, 0, low, slice(None))
         for copy in copies:
             copy.start()
     for low, value in enumerate(mix(1, feature_ref, *totals, piece)):
@@ -438,14 +443,13 @@
         mixed[...], w_ref[span:, :], preferred_element_type=jnp.float32
     )
     hidden = jnp.maximum(hidden, 0.0).astype(jnp.bfloat16)
-    updated = jnp.dot(hidden, w_out_ref[...], preferred_element_type=jnp.float32)
-    result[...] = (updated + bias_ref[...]).astype(result.dtype)
-    if piece == 0:
-        return
-    for low in range(2):
-        copies.append(move(result, piece, low))
-        copies[-1].start()
-    for copy in copies:
+    for start in range(0, result.shape[1], span):
+        columns = slice(start, start + span)
+        updated = jnp.dot(hidden, w_out_ref[:, columns], preferred_element_type=jnp.float32)
+        result[:, columns] = (updated + bias_ref[:, columns]).astype(result.dtype)
+        for low in range(2 if piece else 0):
+            move(result, 1, low, columns).start()
+    for copy in copies if piece else []:
         copy.wait()
 
 
@@ -575,7 +579,7 @@
                 out_shape=jax.ShapeDtypeStruct((nodes if last else rows, width), jnp.bfloat16),
                 scratch_shapes=[pltpu.VMEM((rows, span), jnp.bfloat16)]
                 + (
-                    [pltpu.VMEM((rows, width), jnp.bfloat16), pltpu.SemaphoreType.DMA((4,))]
+                    [pltpu.VMEM((rows, width), jnp.bfloat16), pltpu.SemaphoreType.DMA((6,))]
                     if last
                     else []
                 ),

time: 157 us -> 157 us (level)
  no operation moved by 1% of the time
where the time goes in v8:
time: 157 us
  starting transfers between devices  68.5 us (44%)
  waiting for transfers between devices  67.2 us (43%)
  Pallas kernels  20.1 us (13%)
    ppermute x12, starting transfers between devices, from_y(): return lax.ppermute(value, 'row', row_shift(0, -step))  33.1 us
    ppermute x12, waiting for transfers between devices, from_y(): return lax.ppermute(value, 'row', row_shift(0, -step))  22.2 us
    ppermute x12, waiting for transfers between devices, from_z(): return lax.ppermute(value, 'row', row_shift(-step, 0))  22.1 us
    ppermute x12, starting transfers between devices, from_z(): return lax.ppermute(value, 'row', row_shift(-step, 0))  18.2 us
    ppermute x2, waiting for transfers between devices, on_device(): relay_right = lax.ppermute(over_right, 'col', col_shift(1, 0))  8.38 us
    ppermute x2, starting transfers between devices, on_device(): from_left = lax.ppermute(right, 'col', col_shift(1, 0))  6.43 us
    pallas_call x4, Pallas kernels, combine_listed(): pl.pallas_call(body, in_specs=[in_vmem] * 3, out_specs=[in_vmem] * len(wh...  5.85 us
    ppermute x2, waiting for transfers between devices, on_device(): from_right = lax.ppermute(left, 'col', col_shift(-1, 0))  5.62 us
  transfers between devices with their start and end apart: 44, of which 19 were waited for; matrix products, arithmetic and copies ran while one was open for 0% of the time, Pallas kernels for 10%

profile of v8, /device:TPU:14, one launch (start us, length us, event | category | flops | bytes accessed | tf_op | source)
XLA Modules:
  0.0 157.2 jit_solution(15819576492799537752)
XLA Ops:
  0.0 1.3 split.3
  1.3 1.6 %collective-permute-start.23 = (f32[256,256]{1,0:T(8,128)S(1)}, f32[256,256]{1,0:T(8,128)S(1)}, u32[]{:S(2)}, u32[]{:S(2)}) collective-permute-start(f32[256,256]{1,0:T(8,128)S(1)} %get-tuple-element.78.refs_0_), channel_id=1, source_target_pairs={{0,8},{8,16},{16,24},{24,0},{32,40},{40,48},{48,56},{56,32},{64,72... | collective-permute-start | bytes 786440 | tf_op jit(solution)/shard_map/ppermute | solution.py:47
  3.9 1.2 split.2
  6.1 1.5 collective-permute-start.21
  7.6 1.9 %collective-permute-start.26 = (f32[256,256]{1,0:T(8,128)S(1)}, f32[256,256]{1,0:T(8,128)S(1)}, u32[]{:S(2)}, u32[]{:S(2)}) collective-permute-start(f32[256,256]{1,0:T(8,128)S(1)} %get-tuple-element.79.refs_4_), channel_id=1, source_target_pairs={{0,32},{8,40},{16,48},{24,56},{32,64},{40,72},{48,80},{56,88},{64,... | collective-permute-start | bytes 786440 | tf_op jit(solution)/shard_map/ppermute | solution.py:43
  9.5 5.3 %collective-permute-done.23.refs_3_ = f32[256,256]{1,0:T(8,128)S(1)} collective-permute-done((f32[256,256]{1,0:T(8,128)S(1)}, f32[256,256]{1,0:T(8,128)S(1)}, u32[]{:S(2)}, u32[]{:S(2)}) %collective-permute-start.23) | collective-permute-done | bytes 262176 | tf_op jit(solution)/shard_map/ppermute | solution.py:47
  14.8 3.9 %collective-permute-start.25 = (f32[256,256]{1,0:T(8,128)S(1)}, f32[256,256]{1,0:T(8,128)S(1)}, u32[]{:S(2)}, u32[]{:S(2)}) collective-permute-start(f32[256,256]{1,0:T(8,128)S(1)} %get-tuple-element.79.refs_4_), channel_id=1, source_target_pairs={{0,64},{8,72},{16,80},{24,88},{32,96},{40,104},{48,112},{56,120},{... | collective-permute-start | bytes 786440 | tf_op jit(solution)/shard_map/ppermute | solution.py:43
  19.4 5.0 %collective-permute-start = (f32[264,256]{1,0:T(8,128)S(1)}, f32[264,256]{1,0:T(8,128)S(1)}, u32[]{:S(2)}, u32[]{:S(2)}) collective-permute-start(f32[264,256]{1,0:T(8,128)S(1)} %get-tuple-element.55.refs_0_), channel_id=1, source_target_pairs={{0,24},{8,0},{16,8},{24,16},{32,56},{40,32},{48,40},{56,48},{64,88... | collective-permute-start | bytes 811016 | tf_op jit(solution)/shard_map/ppermute | solution.py:47
  24.4 1.3 collective-permute-start.5
  25.7 3.5 %collective-permute-done.24.refs_5_ = f32[256,256]{1,0:T(8,128)S(1)} collective-permute-done((f32[256,256]{1,0:T(8,128)S(1)}, f32[256,256]{1,0:T(8,128)S(1)}, u32[]{:S(2)}, u32[]{:S(2)}) %collective-permute-start.24) | collective-permute-done | bytes 262176 | tf_op jit(solution)/shard_map/ppermute | solution.py:43
  29.3 3.8 %collective-permute-start.3 = (f32[264,256]{1,0:T(8,128)S(1)}, f32[264,256]{1,0:T(8,128)S(1)}, u32[]{:S(2)}, u32[]{:S(2)}) collective-permute-start(f32[264,256]{1,0:T(8,128)S(1)} %get-tuple-element.56.refs_4_), channel_id=1, source_target_pairs={{0,96},{8,104},{16,112},{24,120},{32,0},{40,8},{48,16},{56,24},{64... | collective-permute-start | bytes 811016 | tf_op jit(solution)/shard_map/ppermute | solution.py:43
  33.5 3.9 %collective-permute-done.5.refs_7_.refs_10_ = f32[264,256]{1,0:T(8,128)S(1)} collective-permute-done((f32[264,256]{1,0:T(8,128)S(1)}, f32[264,256]{1,0:T(8,128)S(1)}, u32[]{:S(2)}, u32[]{:S(2)}) %collective-permute-start.5) | collective-permute-done | bytes 270368 | tf_op jit(solution)/shard_map/ppermute | solution.py:43
  37.4 5.0 %collective-permute-done.3.refs_5_.refs_8_ = f32[264,256]{1,0:T(8,128)S(1)} collective-permute-done((f32[264,256]{1,0:T(8,128)S(1)}, f32[264,256]{1,0:T(8,128)S(1)}, u32[]{:S(2)}, u32[]{:S(2)}) %collective-permute-start.3) | collective-permute-done | bytes 270368 | tf_op jit(solution)/shard_map/ppermute | solution.py:43
  42.4 1.2 pack.3
  43.8 1.2 pack.2
  45.1 3.5 %collective-permute-start.6 = (f32[512,256]{1,0:T(8,128)S(1)}, f32[512,256]{1,0:T(8,128)S(1)}, u32[]{:S(2)}, u32[]{:S(2)}) collective-permute-start(f32[512,256]{1,0:T(8,128)S(1)} %get-tuple-element.57), channel_id=1, source_target_pairs={{0,64},{8,72},{16,80},{24,88},{32,96},{40,104},{48,112},{56,120},{... | collective-permute-start | bytes 1572872 | tf_op jit(solution)/shard_map/ppermute | solution.py:43
  49.2 7.3 %collective-permute-start.9 = (f32[512,256]{1,0:T(8,128)S(1)}, f32[512,256]{1,0:T(8,128)S(1)}, u32[]{:S(2)}, u32[]{:S(2)}) collective-permute-start(f32[512,256]{1,0:T(8,128)S(1)} %get-tuple-element.60), channel_id=1, source_target_pairs={{0,8},{8,16},{16,24},{24,0},{32,40},{40,48},{48,56},{56,32},{64,72... | collective-permute-start | bytes 1572872 | tf_op jit(solution)/shard_map/ppermute | solution.py:47
  56.5 2.5 %collective-permute-done.29.refs_8_ = f32[512,256]{1,0:T(8,128)S(1)} collective-permute-done((f32[512,256]{1,0:T(8,128)S(1)}, f32[512,256]{1,0:T(8,128)S(1)}, u32[]{:S(2)}, u32[]{:S(2)}) %collective-permute-start.29) | collective-permute-done | bytes 524320 | tf_op jit(solution)/shard_map/ppermute | solution.py:43
  58.9 1.7 %collective-permute-start.10 = (f32[512,256]{1,0:T(8,128)S(1)}, f32[512,256]{1,0:T(8,128)S(1)}, u32[]{:S(2)}, u32[]{:S(2)}) collective-permute-start(f32[512,256]{1,0:T(8,128)S(1)} %get-tuple-element.61), channel_id=1, source_target_pairs={{0,96},{8,104},{16,112},{24,120},{32,0},{40,8},{48,16},{56,24},{64... | collective-permute-start | bytes 1572872 | tf_op jit(solution)/shard_map/ppermute | solution.py:43
  60.6 6.1 %collective-permute-done.6.refs_2_ = f32[512,256]{1,0:T(8,128)S(1)} collective-permute-done((f32[512,256]{1,0:T(8,128)S(1)}, f32[512,256]{1,0:T(8,128)S(1)}, u32[]{:S(2)}, u32[]{:S(2)}) %collective-permute-start.6) | collective-permute-done | bytes 524320 | tf_op jit(solution)/shard_map/ppermute | solution.py:43
  66.7 4.2 %collective-permute-start.11 = (f32[512,256]{1,0:T(8,128)S(1)}, f32[512,256]{1,0:T(8,128)S(1)}, u32[]{:S(2)}, u32[]{:S(2)}) collective-permute-start(f32[512,256]{1,0:T(8,128)S(1)} %get-tuple-element.62), channel_id=1, source_target_pairs={{0,24},{8,0},{16,8},{24,16},{32,56},{40,32},{48,40},{56,48},{64,88... | collective-permute-start | bytes 1572872 | tf_op jit(solution)/shard_map/ppermute | solution.py:47
  71.3 1.1 collective-permute-done.8.refs_8_
  72.3 9.3 %collective-permute-start.30 = (f32[512,256]{1,0:T(8,128)S(1)}, f32[512,256]{1,0:T(8,128)S(1)}, u32[]{:S(2)}, u32[]{:S(2)}) collective-permute-start(f32[512,256]{1,0:T(8,128)S(1)} %get-tuple-element.83), channel_id=1, source_target_pairs={{0,8},{8,16},{16,24},{24,0},{32,40},{40,48},{48,56},{56,32},{64,72... | collective-permute-start | bytes 1572872 | tf_op jit(solution)/shard_map/ppermute | solution.py:47
  82.7 1.3 collective-permute-done.11.refs_11_
  84.0 1.4 collective-permute-start.28
  86.2 1.7 %plan.1.refs_0_.plan_ref = s32[512]{0:T(512)S(1)} custom-call(s32[128]{0:T(128)S(1)} %bitcast.54, s32[128]{0:T(128)S(1)} %bitcast.55, s32[1,1]{1,0:T(1,128)S(6)} %copy.15.refs_2_), custom_call_target="tpu_custom_call" | custom-call | bytes 1048576 | tf_op jit(solution)/shard_map/plan/pallas_call | solution.py:480
  89.6 1.3 listed.5
  90.8 1.6 %collective-permute-done.30.refs_9_ = f32[512,256]{1,0:T(8,128)S(1)} collective-permute-done((f32[512,256]{1,0:T(8,128)S(1)}, f32[512,256]{1,0:T(8,128)S(1)}, u32[]{:S(2)}, u32[]{:S(2)}) %collective-permute-start.30) | collective-permute-done | bytes 524320 | tf_op jit(solution)/shard_map/ppermute | solution.py:47
  93.0 2.4 %collective-permute-done.32.refs_11_ = f32[512,256]{1,0:T(8,128)S(1)} collective-permute-done((f32[512,256]{1,0:T(8,128)S(1)}, f32[512,256]{1,0:T(8,128)S(1)}, u32[]{:S(2)}, u32[]{:S(2)}) %collective-permute-start.32) | collective-permute-done | bytes 524320 | tf_op jit(solution)/shard_map/ppermute | solution.py:47
  96.1 11.1 %collective-permute-done.28.refs_3_ = f32[512,256]{1,0:T(8,128)S(1)} collective-permute-done((f32[512,256]{1,0:T(8,128)S(1)}, f32[512,256]{1,0:T(8,128)S(1)}, u32[]{:S(2)}, u32[]{:S(2)}) %collective-permute-start.28) | collective-permute-done | bytes 524320 | tf_op jit(solution)/shard_map/ppermute | solution.py:47
  108.1 1.4 listed.7
  111.1 1.6 %listed.6 = (f32[8,128,256]{2,1,0:T(8,128)S(1)}, f32[4,128,256]{2,1,0:T(8,128)S(1)}, f32[4,128,256]{2,1,0:T(8,128)S(1)}) custom-call(s32[512]{0:T(512)S(1)} %plan.1.refs_0_.plan_ref, f32[128,128,128]{2,1,0:T(8,128)S(1)} %bitcast.28, bf16[33,128,256]{2,1,0:T(8,128)(2,1)S(1)} %get-tuple-element.86.pool_ref), custom_call_target="tpu_custom_call" | custom-call | flops 2147483648 | bytes 8388608 | tf_op jit(solution)/shard_map/listed/pallas_call | solution.py:370
  112.6 1.3 collective-permute-start.18
  113.9 1.6 %listed.4 = (f32[8,128,256]{2,1,0:T(8,128)S(1)}, f32[4,128,256]{2,1,0:T(8,128)S(1)}, f32[4,128,256]{2,1,0:T(8,128)S(1)}) custom-call(s32[512]{0:T(512)S(1)} %plan.1.refs_0_.plan_ref, f32[128,128,128]{2,1,0:T(8,128)S(1)} %bitcast.29, bf16[33,128,256]{2,1,0:T(8,128)(2,1)S(1)} %get-tuple-element.63.pool_ref), custom_call_target="tpu_custom_call" | custom-call | flops 2147483648 | bytes 8388608 | tf_op jit(solution)/shard_map/listed/pallas_call | solution.py:370
  115.6 2.9 %collective-permute-done.17.from_left_ref = f32[2,128,256]{2,1,0:T(8,128)S(1)} collective-permute-done((f32[2,128,256]{2,1,0:T(8,128)S(1)}, f32[2,128,256]{2,1,0:T(8,128)S(1)}, u32[]{:S(2)}, u32[]{:S(2)}) %collective-permute-start.17) | collective-permute-done | bytes 262176 | tf_op jit(solution)/shard_map/ppermute | solution.py:513
  118.6 3.3 %collective-permute-done.18.from_right_ref = f32[2,128,256]{2,1,0:T(8,128)S(1)} collective-permute-done((f32[2,128,256]{2,1,0:T(8,128)S(1)}, f32[2,128,256]{2,1,0:T(8,128)S(1)}, u32[]{:S(2)}, u32[]{:S(2)}) %collective-permute-start.18) | collective-permute-done | bytes 262176 | tf_op jit(solution)/shard_map/ppermute | solution.py:514
  122.0 2.0 %collective-permute-start.39 = (f32[2,128,256]{2,1,0:T(8,128)S(1)}, f32[2,128,256]{2,1,0:T(8,128)S(1)}, u32[]{:S(2)}, u32[]{:S(2)}) collective-permute-start(f32[2,128,256]{2,1,0:T(8,128)S(1)} %get-tuple-element.96), channel_id=1, source_target_pairs={{0,6},{1,7},{2,0},{3,1},{4,2},{5,3},{6,4},{7,5},{8,14},{9,15},{10,... | collective-permute-start | bytes 786440 | tf_op jit(solution)/shard_map/ppermute | solution.py:514
  124.3 1.3 collective-permute-start.19
  125.7 5.5 %collective-permute-done.38.from_left_ref = f32[2,128,256]{2,1,0:T(8,128)S(1)} collective-permute-done((f32[2,128,256]{2,1,0:T(8,128)S(1)}, f32[2,128,256]{2,1,0:T(8,128)S(1)}, u32[]{:S(2)}, u32[]{:S(2)}) %collective-permute-start.38) | collective-permute-done | bytes 262176 | tf_op jit(solution)/shard_map/ppermute | solution.py:513
  131.2 1.3 collective-permute-start.42
  133.3 3.2 %collective-permute-start.15 = (f32[2,128,256]{2,1,0:T(8,128)S(1)}, f32[2,128,256]{2,1,0:T(8,128)S(1)}, u32[]{:S(2)}, u32[]{:S(2)}) collective-permute-start(f32[2,128,256]{2,1,0:T(8,128)S(1)} %get-tuple-element.69), channel_id=1, source_target_pairs={{0,2},{1,3},{2,4},{3,5},{4,6},{5,7},{6,0},{7,1},{8,10},{9,11},{10,... | collective-permute-start | bytes 786440 | tf_op jit(solution)/shard_map/ppermute | solution.py:533
  136.5 3.0 %collective-permute-done.42 = f32[1,128,256]{2,1,0:T(8,128)S(1)} collective-permute-done((f32[1,128,256]{2,1,0:T(8,128)S(1)}, f32[1,128,256]{2,1,0:T(8,128)S(1)}, u32[]{:S(2)}, u32[]{:S(2)}) %collective-permute-start.42) | collective-permute-done | bytes 131104 | tf_op jit(solution)/shard_map/ppermute | solution.py:547
  139.6 3.2 %collective-permute-start.36 = (f32[2,128,256]{2,1,0:T(8,128)S(1)}, f32[2,128,256]{2,1,0:T(8,128)S(1)}, u32[]{:S(2)}, u32[]{:S(2)}) collective-permute-start(f32[2,128,256]{2,1,0:T(8,128)S(1)} %get-tuple-element.92), channel_id=1, source_target_pairs={{0,2},{1,3},{2,4},{3,5},{4,6},{5,7},{6,0},{7,1},{8,10},{9,11},{10,... | collective-permute-start | bytes 786440 | tf_op jit(solution)/shard_map/ppermute | solution.py:533
  142.8 5.6 %collective-permute-done.14 = f32[2,128,256]{2,1,0:T(8,128)S(1)} collective-permute-done((f32[2,128,256]{2,1,0:T(8,128)S(1)}, f32[2,128,256]{2,1,0:T(8,128)S(1)}, u32[]{:S(2)}, u32[]{:S(2)}) %collective-permute-start.14) | collective-permute-done | bytes 262176 | tf_op jit(solution)/shard_map/ppermute | solution.py:534
  148.5 2.0 %collective-permute-start.41 = (f32[1,128,256]{2,1,0:T(8,128)S(1)}, f32[1,128,256]{2,1,0:T(8,128)S(1)}, u32[]{:S(2)}, u32[]{:S(2)}) collective-permute-start(f32[1,128,256]{2,1,0:T(8,128)S(1)} %get-tuple-element.102), channel_id=1, source_target_pairs={{0,6},{1,7},{2,0},{3,1},{4,2},{5,3},{6,4},{7,5},{8,14},{9,15},{10,... | collective-permute-start | bytes 393224 | tf_op jit(solution)/shard_map/ppermute | solution.py:550
  151.6 2.2 %collective-permute-done.43 = f32[1,128,256]{2,1,0:T(8,128)S(1)} collective-permute-done((f32[1,128,256]{2,1,0:T(8,128)S(1)}, f32[1,128,256]{2,1,0:T(8,128)S(1)}, u32[]{:S(2)}, u32[]{:S(2)}) %collective-permute-start.43) | collective-permute-done | bytes 131104 | tf_op jit(solution)/shard_map/ppermute | solution.py:550
  153.8 1.1 end.2.refs_11_
  155.2 1.8 %end.3 = bf16[512,512]{1,0:T(8,128)(2,1)} custom-call(f32[512,512]{1,0:T(8,128)S(1)} %copy-done, bf16[512,2048]{1,0:T(8,128)(2,1)S(1)} %copy-done.1, f32[512,2048]{1,0:T(8,128)S(1)} %begin.1.refs_2_, bf16[2048,512]{1,0:T(8,128)(2,1)S(1)} %copy-done.2, f32[1,512]{1,0:T(1,128)S(1)} %bitcast.52, f32[512,256]{1,0:T(8,128)S(1)} %bitcast.31, ...), custom_call_target="tpu_custom_call" | custom-call | flops 805306368 | bytes 4194304 | tf_op jit(solution)/shard_map/end/pallas_call | solution.py:575
  (83 shorter events, 13.5 us)
Async XLA Ops:
  0.0 88.6 %slice-start = ((s8[8388608]{0:T(1024)(128)(4,1)}), s8[4194304]{0:T(1024)(128)(4,1)S(1)}, s32[]{:S(2)}) async-start(s8[8388608]{0:T(1024)(128)(4,1)} %bitcast.22), calls=%async_computation | async-start | bytes 8388608
  1.3 13.5 %collective-permute-start.23 = (f32[256,256]{1,0:T(8,128)S(1)}, f32[256,256]{1,0:T(8,128)S(1)}, u32[]{:S(2)}, u32[]{:S(2)}) collective-permute-start(f32[256,256]{1,0:T(8,128)S(1)} %get-tuple-element.78.refs_0_), channel_id=1, source_target_pairs={{0,8},{8,16},{16,24},{24,0},{32,40},{40,48},{48,56},{56,32},{64,72... | collective-permute-start | bytes 786440 | tf_op jit(solution)/shard_map/ppermute | solution.py:47
  2.9 15.8 %collective-permute-start.22 = (f32[256,256]{1,0:T(8,128)S(1)}, f32[256,256]{1,0:T(8,128)S(1)}, u32[]{:S(2)}, u32[]{:S(2)}) collective-permute-start(f32[256,256]{1,0:T(8,128)S(1)} %get-tuple-element.78.refs_0_), channel_id=1, source_target_pairs={{0,16},{8,24},{16,0},{24,8},{32,48},{40,56},{48,32},{56,40},{64,80... | collective-permute-start | bytes 786440 | tf_op jit(solution)/shard_map/ppermute | solution.py:47
  5.0 24.2 %collective-permute-start.2 = (f32[264,256]{1,0:T(8,128)S(1)}, f32[264,256]{1,0:T(8,128)S(1)}, u32[]{:S(2)}, u32[]{:S(2)}) collective-permute-start(f32[264,256]{1,0:T(8,128)S(1)} %get-tuple-element.55.refs_0_), channel_id=1, source_target_pairs={{0,8},{8,16},{16,24},{24,0},{32,40},{40,48},{48,56},{56,32},{64,72... | collective-permute-start | bytes 811016 | tf_op jit(solution)/shard_map/ppermute | solution.py:47
  6.1 13.3 %collective-permute-start.21 = (f32[256,256]{1,0:T(8,128)S(1)}, f32[256,256]{1,0:T(8,128)S(1)}, u32[]{:S(2)}, u32[]{:S(2)}) collective-permute-start(f32[256,256]{1,0:T(8,128)S(1)} %get-tuple-element.78.refs_0_), channel_id=1, source_target_pairs={{0,24},{8,0},{16,8},{24,16},{32,56},{40,32},{48,40},{56,48},{64,88... | collective-permute-start | bytes 786440 | tf_op jit(solution)/shard_map/ppermute | solution.py:47
  7.6 11.8 %collective-permute-start.26 = (f32[256,256]{1,0:T(8,128)S(1)}, f32[256,256]{1,0:T(8,128)S(1)}, u32[]{:S(2)}, u32[]{:S(2)}) collective-permute-start(f32[256,256]{1,0:T(8,128)S(1)} %get-tuple-element.79.refs_4_), channel_id=1, source_target_pairs={{0,32},{8,40},{16,48},{24,56},{32,64},{40,72},{48,80},{56,88},{64,... | collective-permute-start | bytes 786440 | tf_op jit(solution)/shard_map/ppermute | solution.py:43
  14.8 9.6 %collective-permute-start.25 = (f32[256,256]{1,0:T(8,128)S(1)}, f32[256,256]{1,0:T(8,128)S(1)}, u32[]{:S(2)}, u32[]{:S(2)}) collective-permute-start(f32[256,256]{1,0:T(8,128)S(1)} %get-tuple-element.79.refs_4_), channel_id=1, source_target_pairs={{0,64},{8,72},{16,80},{24,88},{32,96},{40,104},{48,112},{56,120},{... | collective-permute-start | bytes 786440 | tf_op jit(solution)/shard_map/ppermute | solution.py:43
  18.7 10.6 %collective-permute-start.24 = (f32[256,256]{1,0:T(8,128)S(1)}, f32[256,256]{1,0:T(8,128)S(1)}, u32[]{:S(2)}, u32[]{:S(2)}) collective-permute-start(f32[256,256]{1,0:T(8,128)S(1)} %get-tuple-element.79.refs_4_), channel_id=1, source_target_pairs={{0,96},{8,104},{16,112},{24,120},{32,0},{40,8},{48,16},{56,24},{64... | collective-permute-start | bytes 786440 | tf_op jit(solution)/shard_map/ppermute | solution.py:43
  19.4 13.7 %collective-permute-start.1 = (f32[264,256]{1,0:T(8,128)S(1)}, f32[264,256]{1,0:T(8,128)S(1)}, u32[]{:S(2)}, u32[]{:S(2)}) collective-permute-start(f32[264,256]{1,0:T(8,128)S(1)} %get-tuple-element.55.refs_0_), channel_id=1, source_target_pairs={{0,16},{8,24},{16,0},{24,8},{32,48},{40,56},{48,32},{56,40},{64,80... | collective-permute-start | bytes 811016 | tf_op jit(solution)/shard_map/ppermute | solution.py:47
  19.4 14.1 %collective-permute-start = (f32[264,256]{1,0:T(8,128)S(1)}, f32[264,256]{1,0:T(8,128)S(1)}, u32[]{:S(2)}, u32[]{:S(2)}) collective-permute-start(f32[264,256]{1,0:T(8,128)S(1)} %get-tuple-element.55.refs_0_), channel_id=1, source_target_pairs={{0,24},{8,0},{16,8},{24,16},{32,56},{40,32},{48,40},{56,48},{64,88... | collective-permute-start | bytes 811016 | tf_op jit(solution)/shard_map/ppermute | solution.py:47
  24.4 13.0 %collective-permute-start.5 = (f32[264,256]{1,0:T(8,128)S(1)}, f32[264,256]{1,0:T(8,128)S(1)}, u32[]{:S(2)}, u32[]{:S(2)}) collective-permute-start(f32[264,256]{1,0:T(8,128)S(1)} %get-tuple-element.56.refs_4_), channel_id=1, source_target_pairs={{0,32},{8,40},{16,48},{24,56},{32,64},{40,72},{48,80},{56,88},{64,... | collective-permute-start | bytes 811016 | tf_op jit(solution)/shard_map/ppermute | solution.py:43
  29.3 8.2 %collective-permute-start.4 = (f32[264,256]{1,0:T(8,128)S(1)}, f32[264,256]{1,0:T(8,128)S(1)}, u32[]{:S(2)}, u32[]{:S(2)}) collective-permute-start(f32[264,256]{1,0:T(8,128)S(1)} %get-tuple-element.56.refs_4_), channel_id=1, source_target_pairs={{0,64},{8,72},{16,80},{24,88},{32,96},{40,104},{48,112},{56,120},{... | collective-permute-start | bytes 811016 | tf_op jit(solution)/shard_map/ppermute | solution.py:43
  29.3 13.2 %collective-permute-start.3 = (f32[264,256]{1,0:T(8,128)S(1)}, f32[264,256]{1,0:T(8,128)S(1)}, u32[]{:S(2)}, u32[]{:S(2)}) collective-permute-start(f32[264,256]{1,0:T(8,128)S(1)} %get-tuple-element.56.refs_4_), channel_id=1, source_target_pairs={{0,96},{8,104},{16,112},{24,120},{32,0},{40,8},{48,16},{56,24},{64... | collective-permute-start | bytes 811016 | tf_op jit(solution)/shard_map/ppermute | solution.py:43
  43.7 42.5 %copy-start.6 = (s32[1,1,128]{2,1,0:T(1,128)S(1)}, s32[1,1,128]{2,1,0:T(1,128)}, u32[]{:S(2)}) copy-start(s32[1,1,128]{2,1,0:T(1,128)} %param.12) | copy-start | bytes 1540
  43.7 44.2 %copy-start.3 = (s32[1,1,16,2]{2,3,1,0:T(2,128)S(1)}, s32[1,1,16,2]{2,3,1,0:T(2,128)}, u32[]{:S(2)}) copy-start(s32[1,1,16,2]{2,3,1,0:T(2,128)} %param.15) | copy-start | bytes 388
  43.7 44.9 %slice-start.1 = ((s8[8388608]{0:T(1024)(128)(4,1)}), s8[4194304]{0:T(1024)(128)(4,1)S(1)}, s32[]{:S(2)}) async-start(s8[8388608]{0:T(1024)(128)(4,1)} %bitcast.22), calls=%async_computation.1 | async-start | bytes 8388608
  43.7 15.2 %collective-permute-start.29 = (f32[512,256]{1,0:T(8,128)S(1)}, f32[512,256]{1,0:T(8,128)S(1)}, u32[]{:S(2)}, u32[]{:S(2)}) collective-permute-start(f32[512,256]{1,0:T(8,128)S(1)} %get-tuple-element.82), channel_id=1, source_target_pairs={{0,32},{8,40},{16,48},{24,56},{32,64},{40,72},{48,80},{56,88},{64,... | collective-permute-start | bytes 1572872 | tf_op jit(solution)/shard_map/ppermute | solution.py:43
  45.1 21.7 %collective-permute-start.6 = (f32[512,256]{1,0:T(8,128)S(1)}, f32[512,256]{1,0:T(8,128)S(1)}, u32[]{:S(2)}, u32[]{:S(2)}) collective-permute-start(f32[512,256]{1,0:T(8,128)S(1)} %get-tuple-element.57), channel_id=1, source_target_pairs={{0,64},{8,72},{16,80},{24,88},{32,96},{40,104},{48,112},{56,120},{... | collective-permute-start | bytes 1572872 | tf_op jit(solution)/shard_map/ppermute | solution.py:43
  48.6 22.3 %collective-permute-start.7 = (f32[512,256]{1,0:T(8,128)S(1)}, f32[512,256]{1,0:T(8,128)S(1)}, u32[]{:S(2)}, u32[]{:S(2)}) collective-permute-start(f32[512,256]{1,0:T(8,128)S(1)} %get-tuple-element.58), channel_id=1, source_target_pairs={{0,16},{8,24},{16,0},{24,8},{32,48},{40,56},{48,32},{56,40},{64,80... | collective-permute-start | bytes 1572872 | tf_op jit(solution)/shard_map/ppermute | solution.py:47
  48.9 23.4 %collective-permute-start.8 = (f32[512,256]{1,0:T(8,128)S(1)}, f32[512,256]{1,0:T(8,128)S(1)}, u32[]{:S(2)}, u32[]{:S(2)}) collective-permute-start(f32[512,256]{1,0:T(8,128)S(1)} %get-tuple-element.59), channel_id=1, source_target_pairs={{0,32},{8,40},{16,48},{24,56},{32,64},{40,72},{48,80},{56,88},{64,... | collective-permute-start | bytes 1572872 | tf_op jit(solution)/shard_map/ppermute | solution.py:43
  49.2 32.4 %collective-permute-start.9 = (f32[512,256]{1,0:T(8,128)S(1)}, f32[512,256]{1,0:T(8,128)S(1)}, u32[]{:S(2)}, u32[]{:S(2)}) collective-permute-start(f32[512,256]{1,0:T(8,128)S(1)} %get-tuple-element.60), channel_id=1, source_target_pairs={{0,8},{8,16},{16,24},{24,0},{32,40},{40,48},{48,56},{56,32},{64,72... | collective-permute-start | bytes 1572872 | tf_op jit(solution)/shard_map/ppermute | solution.py:47
  58.9 23.3 %collective-permute-start.10 = (f32[512,256]{1,0:T(8,128)S(1)}, f32[512,256]{1,0:T(8,128)S(1)}, u32[]{:S(2)}, u32[]{:S(2)}) collective-permute-start(f32[512,256]{1,0:T(8,128)S(1)} %get-tuple-element.61), channel_id=1, source_target_pairs={{0,96},{8,104},{16,112},{24,120},{32,0},{40,8},{48,16},{56,24},{64... | collective-permute-start | bytes 1572872 | tf_op jit(solution)/shard_map/ppermute | solution.py:43
  66.7 17.3 %collective-permute-start.11 = (f32[512,256]{1,0:T(8,128)S(1)}, f32[512,256]{1,0:T(8,128)S(1)}, u32[]{:S(2)}, u32[]{:S(2)}) collective-permute-start(f32[512,256]{1,0:T(8,128)S(1)} %get-tuple-element.62), channel_id=1, source_target_pairs={{0,24},{8,0},{16,8},{24,16},{32,56},{40,32},{48,40},{56,48},{64,88... | collective-permute-start | bytes 1572872 | tf_op jit(solution)/shard_map/ppermute | solution.py:47
  70.9 25.2 %collective-permute-start.27 = (f32[512,256]{1,0:T(8,128)S(1)}, f32[512,256]{1,0:T(8,128)S(1)}, u32[]{:S(2)}, u32[]{:S(2)}) collective-permute-start(f32[512,256]{1,0:T(8,128)S(1)} %get-tuple-element.80), channel_id=1, source_target_pairs={{0,64},{8,72},{16,80},{24,88},{32,96},{40,104},{48,112},{56,120},{... | collective-permute-start | bytes 1572872 | tf_op jit(solution)/shard_map/ppermute | solution.py:43
  72.3 20.1 %collective-permute-start.30 = (f32[512,256]{1,0:T(8,128)S(1)}, f32[512,256]{1,0:T(8,128)S(1)}, u32[]{:S(2)}, u32[]{:S(2)}) collective-permute-start(f32[512,256]{1,0:T(8,128)S(1)} %get-tuple-element.83), channel_id=1, source_target_pairs={{0,8},{8,16},{16,24},{24,0},{32,40},{40,48},{48,56},{56,32},{64,72... | collective-permute-start | bytes 1572872 | tf_op jit(solution)/shard_map/ppermute | solution.py:47
  81.6 10.8 %collective-permute-start.31 = (f32[512,256]{1,0:T(8,128)S(1)}, f32[512,256]{1,0:T(8,128)S(1)}, u32[]{:S(2)}, u32[]{:S(2)}) collective-permute-start(f32[512,256]{1,0:T(8,128)S(1)} %get-tuple-element.84), channel_id=1, source_target_pairs={{0,96},{8,104},{16,112},{24,120},{32,0},{40,8},{48,16},{56,24},{64... | collective-permute-start | bytes 1572872 | tf_op jit(solution)/shard_map/ppermute | solution.py:43
  82.2 13.1 %collective-permute-start.32 = (f32[512,256]{1,0:T(8,128)S(1)}, f32[512,256]{1,0:T(8,128)S(1)}, u32[]{:S(2)}, u32[]{:S(2)}) collective-permute-start(f32[512,256]{1,0:T(8,128)S(1)} %get-tuple-element.85), channel_id=1, source_target_pairs={{0,24},{8,0},{16,8},{24,16},{32,56},{40,32},{48,40},{56,48},{64,88... | collective-permute-start | bytes 1572872 | tf_op jit(solution)/shard_map/ppermute | solution.py:47
  84.0 23.1 %collective-permute-start.28 = (f32[512,256]{1,0:T(8,128)S(1)}, f32[512,256]{1,0:T(8,128)S(1)}, u32[]{:S(2)}, u32[]{:S(2)}) collective-permute-start(f32[512,256]{1,0:T(8,128)S(1)} %get-tuple-element.81), channel_id=1, source_target_pairs={{0,16},{8,24},{16,0},{24,8},{32,48},{40,56},{48,32},{56,40},{64,80... | collective-permute-start | bytes 1572872 | tf_op jit(solution)/shard_map/ppermute | solution.py:47
  92.4 17.7 %collective-permute-start.16 = (f32[4,128,256]{2,1,0:T(8,128)S(1)}, f32[4,128,256]{2,1,0:T(8,128)S(1)}, u32[]{:S(2)}, u32[]{:S(2)}) collective-permute-start(f32[4,128,256]{2,1,0:T(8,128)S(1)} %get-tuple-element.71), channel_id=1, source_target_pairs={{0,1},{1,0},{2,3},{3,2},{4,5},{5,4},{6,7},{7,6},{8,9},{9,8},{10,11... | collective-permute-start | bytes 1572872 | tf_op jit(solution)/shard_map/ppermute | solution.py:502
  92.5 29.5 %collective-permute-start.13 = (f32[8,128,256]{2,1,0:T(8,128)S(1)}, f32[8,128,256]{2,1,0:T(8,128)S(1)}, u32[]{:S(2)}, u32[]{:S(2)}) collective-permute-start(f32[8,128,256]{2,1,0:T(8,128)S(1)} %get-tuple-element.67), channel_id=1, source_target_pairs={{0,1},{1,0},{2,3},{3,2},{4,5},{5,4},{6,7},{7,6},{8,9},{9,8},{10,11... | collective-permute-start | bytes 3145736 | tf_op jit(solution)/shard_map/ppermute | solution.py:515
  109.5 14.7 %collective-permute-start.34 = (f32[8,128,256]{2,1,0:T(8,128)S(1)}, f32[8,128,256]{2,1,0:T(8,128)S(1)}, u32[]{:S(2)}, u32[]{:S(2)}) collective-permute-start(f32[8,128,256]{2,1,0:T(8,128)S(1)} %get-tuple-element.90), channel_id=1, source_target_pairs={{0,1},{1,0},{2,3},{3,2},{4,5},{5,4},{6,7},{7,6},{8,9},{9,8},{10,11... | collective-permute-start | bytes 3145736 | tf_op jit(solution)/shard_map/ppermute | solution.py:515
  109.6 5.9 %collective-permute-start.37 = (f32[4,128,256]{2,1,0:T(8,128)S(1)}, f32[4,128,256]{2,1,0:T(8,128)S(1)}, u32[]{:S(2)}, u32[]{:S(2)}) collective-permute-start(f32[4,128,256]{2,1,0:T(8,128)S(1)} %get-tuple-element.94), channel_id=1, source_target_pairs={{0,1},{1,0},{2,3},{3,2},{4,5},{5,4},{6,7},{7,6},{8,9},{9,8},{10,11... | collective-permute-start | bytes 1572872 | tf_op jit(solution)/shard_map/ppermute | solution.py:502
  110.2 8.4 %collective-permute-start.17 = (f32[2,128,256]{2,1,0:T(8,128)S(1)}, f32[2,128,256]{2,1,0:T(8,128)S(1)}, u32[]{:S(2)}, u32[]{:S(2)}) collective-permute-start(f32[2,128,256]{2,1,0:T(8,128)S(1)} %get-tuple-element.72), channel_id=1, source_target_pairs={{0,2},{1,3},{2,4},{3,5},{4,6},{5,7},{6,0},{7,1},{8,10},{9,11},{10,... | collective-permute-start | bytes 786440 | tf_op jit(solution)/shard_map/ppermute | solution.py:513
  112.6 9.3 %collective-permute-start.18 = (f32[2,128,256]{2,1,0:T(8,128)S(1)}, f32[2,128,256]{2,1,0:T(8,128)S(1)}, u32[]{:S(2)}, u32[]{:S(2)}) collective-permute-start(f32[2,128,256]{2,1,0:T(8,128)S(1)} %get-tuple-element.73), channel_id=1, source_target_pairs={{0,6},{1,7},{2,0},{3,1},{4,2},{5,3},{6,4},{7,5},{8,14},{9,15},{10,... | collective-permute-start | bytes 786440 | tf_op jit(solution)/shard_map/ppermute | solution.py:514
  115.5 17.8 %collective-permute-start.33 = (f32[4,128,256]{2,1,0:T(8,128)S(1)}, f32[4,128,256]{2,1,0:T(8,128)S(1)}, u32[]{:S(2)}, u32[]{:S(2)}) collective-permute-start(f32[4,128,256]{2,1,0:T(8,128)S(1)} %get-tuple-element.88), channel_id=1, source_target_pairs={{0,1},{1,0},{2,3},{3,2},{4,5},{5,4},{6,7},{7,6},{8,9},{9,8},{10,11... | collective-permute-start | bytes 1572872 | tf_op jit(solution)/shard_map/ppermute | solution.py:552
  118.6 14.8 %collective-permute-start.12 = (f32[4,128,256]{2,1,0:T(8,128)S(1)}, f32[4,128,256]{2,1,0:T(8,128)S(1)}, u32[]{:S(2)}, u32[]{:S(2)}) collective-permute-start(f32[4,128,256]{2,1,0:T(8,128)S(1)} %get-tuple-element.65), channel_id=1, source_target_pairs={{0,1},{1,0},{2,3},{3,2},{4,5},{5,4},{6,7},{7,6},{8,9},{9,8},{10,11... | collective-permute-start | bytes 1572872 | tf_op jit(solution)/shard_map/ppermute | solution.py:552
  121.9 9.2 %collective-permute-start.38 = (f32[2,128,256]{2,1,0:T(8,128)S(1)}, f32[2,128,256]{2,1,0:T(8,128)S(1)}, u32[]{:S(2)}, u32[]{:S(2)}) collective-permute-start(f32[2,128,256]{2,1,0:T(8,128)S(1)} %get-tuple-element.95), channel_id=1, source_target_pairs={{0,2},{1,3},{2,4},{3,5},{4,6},{5,7},{6,0},{7,1},{8,10},{9,11},{10,... | collective-permute-start | bytes 786440 | tf_op jit(solution)/shard_map/ppermute | solution.py:513
  122.0 9.2 %collective-permute-start.39 = (f32[2,128,256]{2,1,0:T(8,128)S(1)}, f32[2,128,256]{2,1,0:T(8,128)S(1)}, u32[]{:S(2)}, u32[]{:S(2)}) collective-permute-start(f32[2,128,256]{2,1,0:T(8,128)S(1)} %get-tuple-element.96), channel_id=1, source_target_pairs={{0,6},{1,7},{2,0},{3,1},{4,2},{5,3},{6,4},{7,5},{8,14},{9,15},{10,... | collective-permute-start | bytes 786440 | tf_op jit(solution)/shard_map/ppermute | solution.py:514
  124.3 15.3 %collective-permute-start.19 = (f32[2,128,256]{2,1,0:T(8,128)S(1)}, f32[2,128,256]{2,1,0:T(8,128)S(1)}, u32[]{:S(2)}, u32[]{:S(2)}) collective-permute-start(f32[2,128,256]{2,1,0:T(8,128)S(1)} %get-tuple-element.76), channel_id=1, source_target_pairs={{0,2},{1,3},{2,4},{3,5},{4,6},{5,7},{6,0},{7,1},{8,10},{9,11},{10,... | collective-permute-start | bytes 786440 | tf_op jit(solution)/shard_map/ppermute | solution.py:547
  131.2 8.4 %collective-permute-start.42 = (f32[1,128,256]{2,1,0:T(8,128)S(1)}, f32[1,128,256]{2,1,0:T(8,128)S(1)}, u32[]{:S(2)}, u32[]{:S(2)}) collective-permute-start(f32[1,128,256]{2,1,0:T(8,128)S(1)} %get-tuple-element.103), channel_id=1, source_target_pairs={{0,2},{1,3},{2,4},{3,5},{4,6},{5,7},{6,0},{7,1},{8,10},{9,11},{10,... | collective-permute-start | bytes 393224 | tf_op jit(solution)/shard_map/ppermute | solution.py:547
  132.5 10.3 %collective-permute-start.20 = (f32[2,128,256]{2,1,0:T(8,128)S(1)}, f32[2,128,256]{2,1,0:T(8,128)S(1)}, u32[]{:S(2)}, u32[]{:S(2)}) collective-permute-start(f32[2,128,256]{2,1,0:T(8,128)S(1)} %get-tuple-element.77), channel_id=1, source_target_pairs={{0,6},{1,7},{2,0},{3,1},{4,2},{5,3},{6,4},{7,5},{8,14},{9,15},{10,... | collective-permute-start | bytes 786440 | tf_op jit(solution)/shard_map/ppermute | solution.py:550
  133.3 15.2 %collective-permute-start.14 = (f32[2,128,256]{2,1,0:T(8,128)S(1)}, f32[2,128,256]{2,1,0:T(8,128)S(1)}, u32[]{:S(2)}, u32[]{:S(2)}) collective-permute-start(f32[2,128,256]{2,1,0:T(8,128)S(1)} %get-tuple-element.68), channel_id=1, source_target_pairs={{0,6},{1,7},{2,0},{3,1},{4,2},{5,3},{6,4},{7,5},{8,14},{9,15},{10,... | collective-permute-start | bytes 786440 | tf_op jit(solution)/shard_map/ppermute | solution.py:534
  133.3 15.1 %collective-permute-start.15 = (f32[2,128,256]{2,1,0:T(8,128)S(1)}, f32[2,128,256]{2,1,0:T(8,128)S(1)}, u32[]{:S(2)}, u32[]{:S(2)}) collective-permute-start(f32[2,128,256]{2,1,0:T(8,128)S(1)} %get-tuple-element.69), channel_id=1, source_target_pairs={{0,2},{1,3},{2,4},{3,5},{4,6},{5,7},{6,0},{7,1},{8,10},{9,11},{10,... | collective-permute-start | bytes 786440 | tf_op jit(solution)/shard_map/ppermute | solution.py:533
  139.6 14.2 %collective-permute-start.35 = (f32[2,128,256]{2,1,0:T(8,128)S(1)}, f32[2,128,256]{2,1,0:T(8,128)S(1)}, u32[]{:S(2)}, u32[]{:S(2)}) collective-permute-start(f32[2,128,256]{2,1,0:T(8,128)S(1)} %get-tuple-element.91), channel_id=1, source_target_pairs={{0,6},{1,7},{2,0},{3,1},{4,2},{5,3},{6,4},{7,5},{8,14},{9,15},{10,... | collective-permute-start | bytes 786440 | tf_op jit(solution)/shard_map/ppermute | solution.py:534
  139.6 14.2 %collective-permute-start.36 = (f32[2,128,256]{2,1,0:T(8,128)S(1)}, f32[2,128,256]{2,1,0:T(8,128)S(1)}, u32[]{:S(2)}, u32[]{:S(2)}) collective-permute-start(f32[2,128,256]{2,1,0:T(8,128)S(1)} %get-tuple-element.92), channel_id=1, source_target_pairs={{0,2},{1,3},{2,4},{3,5},{4,6},{5,7},{6,0},{7,1},{8,10},{9,11},{10,... | collective-permute-start | bytes 786440 | tf_op jit(solution)/shard_map/ppermute | solution.py:533
  142.8 10.9 %collective-permute-start.43 = (f32[1,128,256]{2,1,0:T(8,128)S(1)}, f32[1,128,256]{2,1,0:T(8,128)S(1)}, u32[]{:S(2)}, u32[]{:S(2)}) collective-permute-start(f32[1,128,256]{2,1,0:T(8,128)S(1)} %get-tuple-element.104), channel_id=1, source_target_pairs={{0,6},{1,7},{2,0},{3,1},{4,2},{5,3},{6,4},{7,5},{8,14},{9,15},{10,... | collective-permute-start | bytes 393224 | tf_op jit(solution)/shard_map/ppermute | solution.py:550
  148.5 6.4 %collective-permute-start.40 = (f32[1,128,256]{2,1,0:T(8,128)S(1)}, f32[1,128,256]{2,1,0:T(8,128)S(1)}, u32[]{:S(2)}, u32[]{:S(2)}) collective-permute-start(f32[1,128,256]{2,1,0:T(8,128)S(1)} %get-tuple-element.101), channel_id=1, source_target_pairs={{0,2},{1,3},{2,4},{3,5},{4,6},{5,7},{6,0},{7,1},{8,10},{9,11},{10,... | collective-permute-start | bytes 393224 | tf_op jit(solution)/shard_map/ppermute | solution.py:547
  148.5 6.7 %collective-permute-start.41 = (f32[1,128,256]{2,1,0:T(8,128)S(1)}, f32[1,128,256]{2,1,0:T(8,128)S(1)}, u32[]{:S(2)}, u32[]{:S(2)}) collective-permute-start(f32[1,128,256]{2,1,0:T(8,128)S(1)} %get-tuple-element.102), channel_id=1, source_target_pairs={{0,6},{1,7},{2,0},{3,1},{4,2},{5,3},{6,4},{7,5},{8,14},{9,15},{10,... | collective-permute-start | bytes 393224 | tf_op jit(solution)/shard_map/ppermute | solution.py:550
  (6 other events, 128.1 us)

commit v9 on v8

--- a/solution.py
+++ b/solution.py
@@ -251,6 +251,7 @@
 
 
 def add_tiles(which, blocks_dev, plan_ref, tile_ref, pool, total):
+    at_once = unroll if which % kinds == 1 else unroll // 2
     tile_total = tile_ref.shape[0]
     sources = pool.shape[0] - 1
     entries = pairs_of(tile_total, blocks_dev)
@@ -259,8 +260,8 @@
 
     def turn(step, carry):
         products = []
-        for lane in range(unroll):
-            code = plan_ref[which * entries + step * unroll + lane]
+        for lane in range(at_once):
+            code = plan_ref[which * entries + step * at_once + lane]
             left, right = [], []
             for _ in range(2):
                 left.append(tile_ref[code & (tile_total - 1)].astype(jnp.bfloat16))
@@ -278,7 +279,7 @@
         return carry
 
     count = plan_ref[2 * kinds * entries + which]
-    lax.fori_loop(0, (count + unroll - 1) // unroll, turn, 0)
+    lax.fori_loop(0, (count + at_once - 1) // at_once, turn, 0)
 
 
 def put(pool, along_z, along_y, away):

time: 157 us -> 158 us (level)
  transfers between devices with their start and end apart: 44 -> 44, of which waited for: 19 -> 20; matrix products, arithmetic and copies ran while one was open for 0% -> 0% of each run, Pallas kernels for 10% -> 10%
where the time goes in v9:
time: 158 us
  starting transfers between devices  69 us (44%)
  waiting for transfers between devices  68 us (43%)
  Pallas kernels  19.4 us (12%)
    ppermute x12, starting transfers between devices, from_y(): return lax.ppermute(value, 'row', row_shift(0, -step))  33.1 us
    ppermute x12, waiting for transfers between devices, from_y(): return lax.ppermute(value, 'row', row_shift(0, -step))  22.3 us
    ppermute x12, waiting for transfers between devices, from_z(): return lax.ppermute(value, 'row', row_shift(-step, 0))  22.1 us
    ppermute x12, starting transfers between devices, from_z(): return lax.ppermute(value, 'row', row_shift(-step, 0))  18.2 us
    ppermute x2, waiting for transfers between devices, on_device(): relay_right = lax.ppermute(over_right, 'col', col_shift(1, 0))  8.39 us
    ppermute x2, starting transfers between devices, on_device(): from_left = lax.ppermute(right, 'col', col_shift(1, 0))  6.43 us
    ppermute x2, waiting for transfers between devices, on_device(): from_right = lax.ppermute(left, 'col', col_shift(-1, 0))  5.62 us
    pallas_call x4, Pallas kernels, combine_listed(): pl.pallas_call(body, in_specs=[in_vmem] * 3, out_specs=[in_vmem] * len(wh...  5.23 us
  transfers between devices with their start and end apart: 44, of which 20 were waited for; matrix products, arithmetic and copies ran while one was open for 0% of the time, Pallas kernels for 10%

profile of v9, /device:TPU:14, one launch (start us, length us, event | category | flops | bytes accessed | tf_op | source)
XLA Modules:
  0.0 157.6 jit_solution(3517096076570781626)
XLA Ops:
  0.0 1.3 split.3
  1.3 1.6 %collective-permute-start.23 = (f32[256,256]{1,0:T(8,128)S(1)}, f32[256,256]{1,0:T(8,128)S(1)}, u32[]{:S(2)}, u32[]{:S(2)}) collective-permute-start(f32[256,256]{1,0:T(8,128)S(1)} %get-tuple-element.78.refs_0_), channel_id=1, source_target_pairs={{0,8},{8,16},{16,24},{24,0},{32,40},{40,48},{48,56},{56,32},{64,72... | collective-permute-start | bytes 786440 | tf_op jit(solution)/shard_map/ppermute | solution.py:47
  3.9 1.2 split.2
  6.1 1.5 collective-permute-start.21
  7.6 1.9 %collective-permute-start.26 = (f32[256,256]{1,0:T(8,128)S(1)}, f32[256,256]{1,0:T(8,128)S(1)}, u32[]{:S(2)}, u32[]{:S(2)}) collective-permute-start(f32[256,256]{1,0:T(8,128)S(1)} %get-tuple-element.79.refs_4_), channel_id=1, source_target_pairs={{0,32},{8,40},{16,48},{24,56},{32,64},{40,72},{48,80},{56,88},{64,... | collective-permute-start | bytes 786440 | tf_op jit(solution)/shard_map/ppermute | solution.py:43
  9.5 5.3 %collective-permute-done.23.refs_3_ = f32[256,256]{1,0:T(8,128)S(1)} collective-permute-done((f32[256,256]{1,0:T(8,128)S(1)}, f32[256,256]{1,0:T(8,128)S(1)}, u32[]{:S(2)}, u32[]{:S(2)}) %collective-permute-start.23) | collective-permute-done | bytes 262176 | tf_op jit(solution)/shard_map/ppermute | solution.py:47
  14.8 3.9 %collective-permute-start.25 = (f32[256,256]{1,0:T(8,128)S(1)}, f32[256,256]{1,0:T(8,128)S(1)}, u32[]{:S(2)}, u32[]{:S(2)}) collective-permute-start(f32[256,256]{1,0:T(8,128)S(1)} %get-tuple-element.79.refs_4_), channel_id=1, source_target_pairs={{0,64},{8,72},{16,80},{24,88},{32,96},{40,104},{48,112},{56,120},{... | collective-permute-start | bytes 786440 | tf_op jit(solution)/shard_map/ppermute | solution.py:43
  19.4 5.0 %collective-permute-start = (f32[264,256]{1,0:T(8,128)S(1)}, f32[264,256]{1,0:T(8,128)S(1)}, u32[]{:S(2)}, u32[]{:S(2)}) collective-permute-start(f32[264,256]{1,0:T(8,128)S(1)} %get-tuple-element.55.refs_0_), channel_id=1, source_target_pairs={{0,24},{8,0},{16,8},{24,16},{32,56},{40,32},{48,40},{56,48},{64,88... | collective-permute-start | bytes 811016 | tf_op jit(solution)/shard_map/ppermute | solution.py:47
  24.4 1.3 collective-permute-start.5
  25.7 3.5 %collective-permute-done.24.refs_5_ = f32[256,256]{1,0:T(8,128)S(1)} collective-permute-done((f32[256,256]{1,0:T(8,128)S(1)}, f32[256,256]{1,0:T(8,128)S(1)}, u32[]{:S(2)}, u32[]{:S(2)}) %collective-permute-start.24) | collective-permute-done | bytes 262176 | tf_op jit(solution)/shard_map/ppermute | solution.py:43
  29.3 3.8 %collective-permute-start.3 = (f32[264,256]{1,0:T(8,128)S(1)}, f32[264,256]{1,0:T(8,128)S(1)}, u32[]{:S(2)}, u32[]{:S(2)}) collective-permute-start(f32[264,256]{1,0:T(8,128)S(1)} %get-tuple-element.56.refs_4_), channel_id=1, source_target_pairs={{0,96},{8,104},{16,112},{24,120},{32,0},{40,8},{48,16},{56,24},{64... | collective-permute-start | bytes 811016 | tf_op jit(solution)/shard_map/ppermute | solution.py:43
  33.5 3.9 %collective-permute-done.5.refs_7_.refs_10_ = f32[264,256]{1,0:T(8,128)S(1)} collective-permute-done((f32[264,256]{1,0:T(8,128)S(1)}, f32[264,256]{1,0:T(8,128)S(1)}, u32[]{:S(2)}, u32[]{:S(2)}) %collective-permute-start.5) | collective-permute-done | bytes 270368 | tf_op jit(solution)/shard_map/ppermute | solution.py:43
  37.4 5.0 %collective-permute-done.3.refs_5_.refs_8_ = f32[264,256]{1,0:T(8,128)S(1)} collective-permute-done((f32[264,256]{1,0:T(8,128)S(1)}, f32[264,256]{1,0:T(8,128)S(1)}, u32[]{:S(2)}, u32[]{:S(2)}) %collective-permute-start.3) | collective-permute-done | bytes 270368 | tf_op jit(solution)/shard_map/ppermute | solution.py:43
  42.4 1.2 pack.3
  43.8 1.2 pack.2
  45.1 3.5 %collective-permute-start.6 = (f32[512,256]{1,0:T(8,128)S(1)}, f32[512,256]{1,0:T(8,128)S(1)}, u32[]{:S(2)}, u32[]{:S(2)}) collective-permute-start(f32[512,256]{1,0:T(8,128)S(1)} %get-tuple-element.57), channel_id=1, source_target_pairs={{0,64},{8,72},{16,80},{24,88},{32,96},{40,104},{48,112},{56,120},{... | collective-permute-start | bytes 1572872 | tf_op jit(solution)/shard_map/ppermute | solution.py:43
  49.2 7.3 %collective-permute-start.9 = (f32[512,256]{1,0:T(8,128)S(1)}, f32[512,256]{1,0:T(8,128)S(1)}, u32[]{:S(2)}, u32[]{:S(2)}) collective-permute-start(f32[512,256]{1,0:T(8,128)S(1)} %get-tuple-element.60), channel_id=1, source_target_pairs={{0,8},{8,16},{16,24},{24,0},{32,40},{40,48},{48,56},{56,32},{64,72... | collective-permute-start | bytes 1572872 | tf_op jit(solution)/shard_map/ppermute | solution.py:47
  56.5 2.5 %collective-permute-done.29.refs_8_ = f32[512,256]{1,0:T(8,128)S(1)} collective-permute-done((f32[512,256]{1,0:T(8,128)S(1)}, f32[512,256]{1,0:T(8,128)S(1)}, u32[]{:S(2)}, u32[]{:S(2)}) %collective-permute-start.29) | collective-permute-done | bytes 524320 | tf_op jit(solution)/shard_map/ppermute | solution.py:43
  58.9 1.7 %collective-permute-start.10 = (f32[512,256]{1,0:T(8,128)S(1)}, f32[512,256]{1,0:T(8,128)S(1)}, u32[]{:S(2)}, u32[]{:S(2)}) collective-permute-start(f32[512,256]{1,0:T(8,128)S(1)} %get-tuple-element.61), channel_id=1, source_target_pairs={{0,96},{8,104},{16,112},{24,120},{32,0},{40,8},{48,16},{56,24},{64... | collective-permute-start | bytes 1572872 | tf_op jit(solution)/shard_map/ppermute | solution.py:43
  60.6 6.1 %collective-permute-done.6.refs_2_ = f32[512,256]{1,0:T(8,128)S(1)} collective-permute-done((f32[512,256]{1,0:T(8,128)S(1)}, f32[512,256]{1,0:T(8,128)S(1)}, u32[]{:S(2)}, u32[]{:S(2)}) %collective-permute-start.6) | collective-permute-done | bytes 524320 | tf_op jit(solution)/shard_map/ppermute | solution.py:43
  66.7 4.2 %collective-permute-start.11 = (f32[512,256]{1,0:T(8,128)S(1)}, f32[512,256]{1,0:T(8,128)S(1)}, u32[]{:S(2)}, u32[]{:S(2)}) collective-permute-start(f32[512,256]{1,0:T(8,128)S(1)} %get-tuple-element.62), channel_id=1, source_target_pairs={{0,24},{8,0},{16,8},{24,16},{32,56},{40,32},{48,40},{56,48},{64,88... | collective-permute-start | bytes 1572872 | tf_op jit(solution)/shard_map/ppermute | solution.py:47
  71.3 1.1 collective-permute-done.8.refs_8_
  72.3 9.3 %collective-permute-start.30 = (f32[512,256]{1,0:T(8,128)S(1)}, f32[512,256]{1,0:T(8,128)S(1)}, u32[]{:S(2)}, u32[]{:S(2)}) collective-permute-start(f32[512,256]{1,0:T(8,128)S(1)} %get-tuple-element.83), channel_id=1, source_target_pairs={{0,8},{8,16},{16,24},{24,0},{32,40},{40,48},{48,56},{56,32},{64,72... | collective-permute-start | bytes 1572872 | tf_op jit(solution)/shard_map/ppermute | solution.py:47
  82.7 1.3 collective-permute-done.11.refs_11_
  84.0 1.4 collective-permute-start.28
  86.2 1.7 %plan.1.refs_0_.plan_ref = s32[512]{0:T(512)S(1)} custom-call(s32[128]{0:T(128)S(1)} %bitcast.54, s32[128]{0:T(128)S(1)} %bitcast.55, s32[1,1]{1,0:T(1,128)S(6)} %copy.15.refs_2_), custom_call_target="tpu_custom_call" | custom-call | bytes 1048576 | tf_op jit(solution)/shard_map/plan/pallas_call | solution.py:481
  89.5 1.2 listed.5
  90.7 1.8 %collective-permute-done.30.refs_9_ = f32[512,256]{1,0:T(8,128)S(1)} collective-permute-done((f32[512,256]{1,0:T(8,128)S(1)}, f32[512,256]{1,0:T(8,128)S(1)}, u32[]{:S(2)}, u32[]{:S(2)}) %collective-permute-start.30) | collective-permute-done | bytes 524320 | tf_op jit(solution)/shard_map/ppermute | solution.py:47
  93.0 2.4 %collective-permute-done.32.refs_11_ = f32[512,256]{1,0:T(8,128)S(1)} collective-permute-done((f32[512,256]{1,0:T(8,128)S(1)}, f32[512,256]{1,0:T(8,128)S(1)}, u32[]{:S(2)}, u32[]{:S(2)}) %collective-permute-start.32) | collective-permute-done | bytes 524320 | tf_op jit(solution)/shard_map/ppermute | solution.py:47
  96.1 11.1 %collective-permute-done.28.refs_3_ = f32[512,256]{1,0:T(8,128)S(1)} collective-permute-done((f32[512,256]{1,0:T(8,128)S(1)}, f32[512,256]{1,0:T(8,128)S(1)}, u32[]{:S(2)}, u32[]{:S(2)}) %collective-permute-start.28) | collective-permute-done | bytes 524320 | tf_op jit(solution)/shard_map/ppermute | solution.py:47
  108.0 1.2 listed.7
  110.0 1.1 collective-permute-start.17
  111.2 1.4 listed.6
  112.6 1.3 collective-permute-start.18
  113.9 1.4 listed.4
  115.5 3.0 %collective-permute-done.17.from_left_ref = f32[2,128,256]{2,1,0:T(8,128)S(1)} collective-permute-done((f32[2,128,256]{2,1,0:T(8,128)S(1)}, f32[2,128,256]{2,1,0:T(8,128)S(1)}, u32[]{:S(2)}, u32[]{:S(2)}) %collective-permute-start.17) | collective-permute-done | bytes 262176 | tf_op jit(solution)/shard_map/ppermute | solution.py:514
  118.5 3.4 %collective-permute-done.18.from_right_ref = f32[2,128,256]{2,1,0:T(8,128)S(1)} collective-permute-done((f32[2,128,256]{2,1,0:T(8,128)S(1)}, f32[2,128,256]{2,1,0:T(8,128)S(1)}, u32[]{:S(2)}, u32[]{:S(2)}) %collective-permute-start.18) | collective-permute-done | bytes 262176 | tf_op jit(solution)/shard_map/ppermute | solution.py:515
  121.9 2.0 %collective-permute-start.39 = (f32[2,128,256]{2,1,0:T(8,128)S(1)}, f32[2,128,256]{2,1,0:T(8,128)S(1)}, u32[]{:S(2)}, u32[]{:S(2)}) collective-permute-start(f32[2,128,256]{2,1,0:T(8,128)S(1)} %get-tuple-element.96), channel_id=1, source_target_pairs={{0,6},{1,7},{2,0},{3,1},{4,2},{5,3},{6,4},{7,5},{8,14},{9,15},{10,... | collective-permute-start | bytes 786440 | tf_op jit(solution)/shard_map/ppermute | solution.py:515
  124.2 1.3 collective-permute-start.19
  125.6 5.4 %collective-permute-done.38.from_left_ref = f32[2,128,256]{2,1,0:T(8,128)S(1)} collective-permute-done((f32[2,128,256]{2,1,0:T(8,128)S(1)}, f32[2,128,256]{2,1,0:T(8,128)S(1)}, u32[]{:S(2)}, u32[]{:S(2)}) %collective-permute-start.38) | collective-permute-done | bytes 262176 | tf_op jit(solution)/shard_map/ppermute | solution.py:514
  131.2 1.3 collective-permute-start.42
  133.3 3.2 %collective-permute-start.15 = (f32[2,128,256]{2,1,0:T(8,128)S(1)}, f32[2,128,256]{2,1,0:T(8,128)S(1)}, u32[]{:S(2)}, u32[]{:S(2)}) collective-permute-start(f32[2,128,256]{2,1,0:T(8,128)S(1)} %get-tuple-element.69), channel_id=1, source_target_pairs={{0,2},{1,3},{2,4},{3,5},{4,6},{5,7},{6,0},{7,1},{8,10},{9,11},{10,... | collective-permute-start | bytes 786440 | tf_op jit(solution)/shard_map/ppermute | solution.py:534
  136.5 3.0 %collective-permute-done.42 = f32[1,128,256]{2,1,0:T(8,128)S(1)} collective-permute-done((f32[1,128,256]{2,1,0:T(8,128)S(1)}, f32[1,128,256]{2,1,0:T(8,128)S(1)}, u32[]{:S(2)}, u32[]{:S(2)}) %collective-permute-start.42) | collective-permute-done | bytes 131104 | tf_op jit(solution)/shard_map/ppermute | solution.py:548
  139.5 3.2 %collective-permute-start.36 = (f32[2,128,256]{2,1,0:T(8,128)S(1)}, f32[2,128,256]{2,1,0:T(8,128)S(1)}, u32[]{:S(2)}, u32[]{:S(2)}) collective-permute-start(f32[2,128,256]{2,1,0:T(8,128)S(1)} %get-tuple-element.92), channel_id=1, source_target_pairs={{0,2},{1,3},{2,4},{3,5},{4,6},{5,7},{6,0},{7,1},{8,10},{9,11},{10,... | collective-permute-start | bytes 786440 | tf_op jit(solution)/shard_map/ppermute | solution.py:534
  142.9 5.6 %collective-permute-done.14 = f32[2,128,256]{2,1,0:T(8,128)S(1)} collective-permute-done((f32[2,128,256]{2,1,0:T(8,128)S(1)}, f32[2,128,256]{2,1,0:T(8,128)S(1)}, u32[]{:S(2)}, u32[]{:S(2)}) %collective-permute-start.14) | collective-permute-done | bytes 262176 | tf_op jit(solution)/shard_map/ppermute | solution.py:535
  148.5 2.0 %collective-permute-start.41 = (f32[1,128,256]{2,1,0:T(8,128)S(1)}, f32[1,128,256]{2,1,0:T(8,128)S(1)}, u32[]{:S(2)}, u32[]{:S(2)}) collective-permute-start(f32[1,128,256]{2,1,0:T(8,128)S(1)} %get-tuple-element.102), channel_id=1, source_target_pairs={{0,6},{1,7},{2,0},{3,1},{4,2},{5,3},{6,4},{7,5},{8,14},{9,15},{10,... | collective-permute-start | bytes 393224 | tf_op jit(solution)/shard_map/ppermute | solution.py:551
  151.6 2.7 %collective-permute-done.43 = f32[1,128,256]{2,1,0:T(8,128)S(1)} collective-permute-done((f32[1,128,256]{2,1,0:T(8,128)S(1)}, f32[1,128,256]{2,1,0:T(8,128)S(1)}, u32[]{:S(2)}, u32[]{:S(2)}) %collective-permute-start.43) | collective-permute-done | bytes 131104 | tf_op jit(solution)/shard_map/ppermute | solution.py:551
  155.7 1.8 %end.3 = bf16[512,512]{1,0:T(8,128)(2,1)} custom-call(f32[512,512]{1,0:T(8,128)S(1)} %copy-done, bf16[512,2048]{1,0:T(8,128)(2,1)S(1)} %copy-done.1, f32[512,2048]{1,0:T(8,128)S(1)} %begin.1.refs_2_, bf16[2048,512]{1,0:T(8,128)(2,1)S(1)} %copy-done.2, f32[1,512]{1,0:T(1,128)S(1)} %bitcast.52, f32[512,256]{1,0:T(8,128)S(1)} %bitcast.31, ...), custom_call_target="tpu_custom_call" | custom-call | flops 805306368 | bytes 4194304 | tf_op jit(solution)/shard_map/end/pallas_call | solution.py:576
  (83 shorter events, 13.8 us)
Async XLA Ops:
  0.0 88.6 %slice-start = ((s8[8388608]{0:T(1024)(128)(4,1)}), s8[4194304]{0:T(1024)(128)(4,1)S(1)}, s32[]{:S(2)}) async-start(s8[8388608]{0:T(1024)(128)(4,1)} %bitcast.22), calls=%async_computation | async-start | bytes 8388608
  1.3 13.5 %collective-permute-start.23 = (f32[256,256]{1,0:T(8,128)S(1)}, f32[256,256]{1,0:T(8,128)S(1)}, u32[]{:S(2)}, u32[]{:S(2)}) collective-permute-start(f32[256,256]{1,0:T(8,128)S(1)} %get-tuple-element.78.refs_0_), channel_id=1, source_target_pairs={{0,8},{8,16},{16,24},{24,0},{32,40},{40,48},{48,56},{56,32},{64,72... | collective-permute-start | bytes 786440 | tf_op jit(solution)/shard_map/ppermute | solution.py:47
  2.9 15.8 %collective-permute-start.22 = (f32[256,256]{1,0:T(8,128)S(1)}, f32[256,256]{1,0:T(8,128)S(1)}, u32[]{:S(2)}, u32[]{:S(2)}) collective-permute-start(f32[256,256]{1,0:T(8,128)S(1)} %get-tuple-element.78.refs_0_), channel_id=1, source_target_pairs={{0,16},{8,24},{16,0},{24,8},{32,48},{40,56},{48,32},{56,40},{64,80... | collective-permute-start | bytes 786440 | tf_op jit(solution)/shard_map/ppermute | solution.py:47
  5.0 24.2 %collective-permute-start.2 = (f32[264,256]{1,0:T(8,128)S(1)}, f32[264,256]{1,0:T(8,128)S(1)}, u32[]{:S(2)}, u32[]{:S(2)}) collective-permute-start(f32[264,256]{1,0:T(8,128)S(1)} %get-tuple-element.55.refs_0_), channel_id=1, source_target_pairs={{0,8},{8,16},{16,24},{24,0},{32,40},{40,48},{48,56},{56,32},{64,72... | collective-permute-start | bytes 811016 | tf_op jit(solution)/shard_map/ppermute | solution.py:47
  6.1 13.3 %collective-permute-start.21 = (f32[256,256]{1,0:T(8,128)S(1)}, f32[256,256]{1,0:T(8,128)S(1)}, u32[]{:S(2)}, u32[]{:S(2)}) collective-permute-start(f32[256,256]{1,0:T(8,128)S(1)} %get-tuple-element.78.refs_0_), channel_id=1, source_target_pairs={{0,24},{8,0},{16,8},{24,16},{32,56},{40,32},{48,40},{56,48},{64,88... | collective-permute-start | bytes 786440 | tf_op jit(solution)/shard_map/ppermute | solution.py:47
  7.6 11.8 %collective-permute-start.26 = (f32[256,256]{1,0:T(8,128)S(1)}, f32[256,256]{1,0:T(8,128)S(1)}, u32[]{:S(2)}, u32[]{:S(2)}) collective-permute-start(f32[256,256]{1,0:T(8,128)S(1)} %get-tuple-element.79.refs_4_), channel_id=1, source_target_pairs={{0,32},{8,40},{16,48},{24,56},{32,64},{40,72},{48,80},{56,88},{64,... | collective-permute-start | bytes 786440 | tf_op jit(solution)/shard_map/ppermute | solution.py:43
  14.8 9.6 %collective-permute-start.25 = (f32[256,256]{1,0:T(8,128)S(1)}, f32[256,256]{1,0:T(8,128)S(1)}, u32[]{:S(2)}, u32[]{:S(2)}) collective-permute-start(f32[256,256]{1,0:T(8,128)S(1)} %get-tuple-element.79.refs_4_), channel_id=1, source_target_pairs={{0,64},{8,72},{16,80},{24,88},{32,96},{40,104},{48,112},{56,120},{... | collective-permute-start | bytes 786440 | tf_op jit(solution)/shard_map/ppermute | solution.py:43
  18.7 10.6 %collective-permute-start.24 = (f32[256,256]{1,0:T(8,128)S(1)}, f32[256,256]{1,0:T(8,128)S(1)}, u32[]{:S(2)}, u32[]{:S(2)}) collective-permute-start(f32[256,256]{1,0:T(8,128)S(1)} %get-tuple-element.79.refs_4_), channel_id=1, source_target_pairs={{0,96},{8,104},{16,112},{24,120},{32,0},{40,8},{48,16},{56,24},{64... | collective-permute-start | bytes 786440 | tf_op jit(solution)/shard_map/ppermute | solution.py:43
  19.4 13.7 %collective-permute-start.1 = (f32[264,256]{1,0:T(8,128)S(1)}, f32[264,256]{1,0:T(8,128)S(1)}, u32[]{:S(2)}, u32[]{:S(2)}) collective-permute-start(f32[264,256]{1,0:T(8,128)S(1)} %get-tuple-element.55.refs_0_), channel_id=1, source_target_pairs={{0,16},{8,24},{16,0},{24,8},{32,48},{40,56},{48,32},{56,40},{64,80... | collective-permute-start | bytes 811016 | tf_op jit(solution)/shard_map/ppermute | solution.py:47
  19.4 14.1 %collective-permute-start = (f32[264,256]{1,0:T(8,128)S(1)}, f32[264,256]{1,0:T(8,128)S(1)}, u32[]{:S(2)}, u32[]{:S(2)}) collective-permute-start(f32[264,256]{1,0:T(8,128)S(1)} %get-tuple-element.55.refs_0_), channel_id=1, source_target_pairs={{0,24},{8,0},{16,8},{24,16},{32,56},{40,32},{48,40},{56,48},{64,88... | collective-permute-start | bytes 811016 | tf_op jit(solution)/shard_map/ppermute | solution.py:47
  24.4 13.0 %collective-permute-start.5 = (f32[264,256]{1,0:T(8,128)S(1)}, f32[264,256]{1,0:T(8,128)S(1)}, u32[]{:S(2)}, u32[]{:S(2)}) collective-permute-start(f32[264,256]{1,0:T(8,128)S(1)} %get-tuple-element.56.refs_4_), channel_id=1, source_target_pairs={{0,32},{8,40},{16,48},{24,56},{32,64},{40,72},{48,80},{56,88},{64,... | collective-permute-start | bytes 811016 | tf_op jit(solution)/shard_map/ppermute | solution.py:43
  29.3 8.2 %collective-permute-start.4 = (f32[264,256]{1,0:T(8,128)S(1)}, f32[264,256]{1,0:T(8,128)S(1)}, u32[]{:S(2)}, u32[]{:S(2)}) collective-permute-start(f32[264,256]{1,0:T(8,128)S(1)} %get-tuple-element.56.refs_4_), channel_id=1, source_target_pairs={{0,64},{8,72},{16,80},{24,88},{32,96},{40,104},{48,112},{56,120},{... | collective-permute-start | bytes 811016 | tf_op jit(solution)/shard_map/ppermute | solution.py:43
  29.3 13.2 %collective-permute-start.3 = (f32[264,256]{1,0:T(8,128)S(1)}, f32[264,256]{1,0:T(8,128)S(1)}, u32[]{:S(2)}, u32[]{:S(2)}) collective-permute-start(f32[264,256]{1,0:T(8,128)S(1)} %get-tuple-element.56.refs_4_), channel_id=1, source_target_pairs={{0,96},{8,104},{16,112},{24,120},{32,0},{40,8},{48,16},{56,24},{64... | collective-permute-start | bytes 811016 | tf_op jit(solution)/shard_map/ppermute | solution.py:43
  43.7 42.5 %copy-start.6 = (s32[1,1,128]{2,1,0:T(1,128)S(1)}, s32[1,1,128]{2,1,0:T(1,128)}, u32[]{:S(2)}) copy-start(s32[1,1,128]{2,1,0:T(1,128)} %param.12) | copy-start | bytes 1540
  43.7 44.2 %copy-start.3 = (s32[1,1,16,2]{2,3,1,0:T(2,128)S(1)}, s32[1,1,16,2]{2,3,1,0:T(2,128)}, u32[]{:S(2)}) copy-start(s32[1,1,16,2]{2,3,1,0:T(2,128)} %param.15) | copy-start | bytes 388
  43.7 44.9 %slice-start.1 = ((s8[8388608]{0:T(1024)(128)(4,1)}), s8[4194304]{0:T(1024)(128)(4,1)S(1)}, s32[]{:S(2)}) async-start(s8[8388608]{0:T(1024)(128)(4,1)} %bitcast.22), calls=%async_computation.1 | async-start | bytes 8388608
  43.7 15.2 %collective-permute-start.29 = (f32[512,256]{1,0:T(8,128)S(1)}, f32[512,256]{1,0:T(8,128)S(1)}, u32[]{:S(2)}, u32[]{:S(2)}) collective-permute-start(f32[512,256]{1,0:T(8,128)S(1)} %get-tuple-element.82), channel_id=1, source_target_pairs={{0,32},{8,40},{16,48},{24,56},{32,64},{40,72},{48,80},{56,88},{64,... | collective-permute-start | bytes 1572872 | tf_op jit(solution)/shard_map/ppermute | solution.py:43
  45.1 21.7 %collective-permute-start.6 = (f32[512,256]{1,0:T(8,128)S(1)}, f32[512,256]{1,0:T(8,128)S(1)}, u32[]{:S(2)}, u32[]{:S(2)}) collective-permute-start(f32[512,256]{1,0:T(8,128)S(1)} %get-tuple-element.57), channel_id=1, source_target_pairs={{0,64},{8,72},{16,80},{24,88},{32,96},{40,104},{48,112},{56,120},{... | collective-permute-start | bytes 1572872 | tf_op jit(solution)/shard_map/ppermute | solution.py:43
  48.6 22.3 %collective-permute-start.7 = (f32[512,256]{1,0:T(8,128)S(1)}, f32[512,256]{1,0:T(8,128)S(1)}, u32[]{:S(2)}, u32[]{:S(2)}) collective-permute-start(f32[512,256]{1,0:T(8,128)S(1)} %get-tuple-element.58), channel_id=1, source_target_pairs={{0,16},{8,24},{16,0},{24,8},{32,48},{40,56},{48,32},{56,40},{64,80... | collective-permute-start | bytes 1572872 | tf_op jit(solution)/shard_map/ppermute | solution.py:47
  48.9 23.4 %collective-permute-start.8 = (f32[512,256]{1,0:T(8,128)S(1)}, f32[512,256]{1,0:T(8,128)S(1)}, u32[]{:S(2)}, u32[]{:S(2)}) collective-permute-start(f32[512,256]{1,0:T(8,128)S(1)} %get-tuple-element.59), channel_id=1, source_target_pairs={{0,32},{8,40},{16,48},{24,56},{32,64},{40,72},{48,80},{56,88},{64,... | collective-permute-start | bytes 1572872 | tf_op jit(solution)/shard_map/ppermute | solution.py:43
  49.2 32.4 %collective-permute-start.9 = (f32[512,256]{1,0:T(8,128)S(1)}, f32[512,256]{1,0:T(8,128)S(1)}, u32[]{:S(2)}, u32[]{:S(2)}) collective-permute-start(f32[512,256]{1,0:T(8,128)S(1)} %get-tuple-element.60), channel_id=1, source_target_pairs={{0,8},{8,16},{16,24},{24,0},{32,40},{40,48},{48,56},{56,32},{64,72... | collective-permute-start | bytes 1572872 | tf_op jit(solution)/shard_map/ppermute | solution.py:47
  58.9 23.3 %collective-permute-start.10 = (f32[512,256]{1,0:T(8,128)S(1)}, f32[512,256]{1,0:T(8,128)S(1)}, u32[]{:S(2)}, u32[]{:S(2)}) collective-permute-start(f32[512,256]{1,0:T(8,128)S(1)} %get-tuple-element.61), channel_id=1, source_target_pairs={{0,96},{8,104},{16,112},{24,120},{32,0},{40,8},{48,16},{56,24},{64... | collective-permute-start | bytes 1572872 | tf_op jit(solution)/shard_map/ppermute | solution.py:43
  66.7 17.3 %collective-permute-start.11 = (f32[512,256]{1,0:T(8,128)S(1)}, f32[512,256]{1,0:T(8,128)S(1)}, u32[]{:S(2)}, u32[]{:S(2)}) collective-permute-start(f32[512,256]{1,0:T(8,128)S(1)} %get-tuple-element.62), channel_id=1, source_target_pairs={{0,24},{8,0},{16,8},{24,16},{32,56},{40,32},{48,40},{56,48},{64,88... | collective-permute-start | bytes 1572872 | tf_op jit(solution)/shard_map/ppermute | solution.py:47
  70.9 25.2 %collective-permute-start.27 = (f32[512,256]{1,0:T(8,128)S(1)}, f32[512,256]{1,0:T(8,128)S(1)}, u32[]{:S(2)}, u32[]{:S(2)}) collective-permute-start(f32[512,256]{1,0:T(8,128)S(1)} %get-tuple-element.80), channel_id=1, source_target_pairs={{0,64},{8,72},{16,80},{24,88},{32,96},{40,104},{48,112},{56,120},{... | collective-permute-start | bytes 1572872 | tf_op jit(solution)/shard_map/ppermute | solution.py:43
  72.3 20.1 %collective-permute-start.30 = (f32[512,256]{1,0:T(8,128)S(1)}, f32[512,256]{1,0:T(8,128)S(1)}, u32[]{:S(2)}, u32[]{:S(2)}) collective-permute-start(f32[512,256]{1,0:T(8,128)S(1)} %get-tuple-element.83), channel_id=1, source_target_pairs={{0,8},{8,16},{16,24},{24,0},{32,40},{40,48},{48,56},{56,32},{64,72... | collective-permute-start | bytes 1572872 | tf_op jit(solution)/shard_map/ppermute | solution.py:47
  81.6 10.8 %collective-permute-start.31 = (f32[512,256]{1,0:T(8,128)S(1)}, f32[512,256]{1,0:T(8,128)S(1)}, u32[]{:S(2)}, u32[]{:S(2)}) collective-permute-start(f32[512,256]{1,0:T(8,128)S(1)} %get-tuple-element.84), channel_id=1, source_target_pairs={{0,96},{8,104},{16,112},{24,120},{32,0},{40,8},{48,16},{56,24},{64... | collective-permute-start | bytes 1572872 | tf_op jit(solution)/shard_map/ppermute | solution.py:43
  82.2 13.1 %collective-permute-start.32 = (f32[512,256]{1,0:T(8,128)S(1)}, f32[512,256]{1,0:T(8,128)S(1)}, u32[]{:S(2)}, u32[]{:S(2)}) collective-permute-start(f32[512,256]{1,0:T(8,128)S(1)} %get-tuple-element.85), channel_id=1, source_target_pairs={{0,24},{8,0},{16,8},{24,16},{32,56},{40,32},{48,40},{56,48},{64,88... | collective-permute-start | bytes 1572872 | tf_op jit(solution)/shard_map/ppermute | solution.py:47
  84.0 23.1 %collective-permute-start.28 = (f32[512,256]{1,0:T(8,128)S(1)}, f32[512,256]{1,0:T(8,128)S(1)}, u32[]{:S(2)}, u32[]{:S(2)}) collective-permute-start(f32[512,256]{1,0:T(8,128)S(1)} %get-tuple-element.81), channel_id=1, source_target_pairs={{0,16},{8,24},{16,0},{24,8},{32,48},{40,56},{48,32},{56,40},{64,80... | collective-permute-start | bytes 1572872 | tf_op jit(solution)/shard_map/ppermute | solution.py:47
  92.4 17.5 %collective-permute-start.16 = (f32[4,128,256]{2,1,0:T(8,128)S(1)}, f32[4,128,256]{2,1,0:T(8,128)S(1)}, u32[]{:S(2)}, u32[]{:S(2)}) collective-permute-start(f32[4,128,256]{2,1,0:T(8,128)S(1)} %get-tuple-element.71), channel_id=1, source_target_pairs={{0,1},{1,0},{2,3},{3,2},{4,5},{5,4},{6,7},{7,6},{8,9},{9,8},{10,11... | collective-permute-start | bytes 1572872 | tf_op jit(solution)/shard_map/ppermute | solution.py:503
  92.5 29.5 %collective-permute-start.13 = (f32[8,128,256]{2,1,0:T(8,128)S(1)}, f32[8,128,256]{2,1,0:T(8,128)S(1)}, u32[]{:S(2)}, u32[]{:S(2)}) collective-permute-start(f32[8,128,256]{2,1,0:T(8,128)S(1)} %get-tuple-element.67), channel_id=1, source_target_pairs={{0,1},{1,0},{2,3},{3,2},{4,5},{5,4},{6,7},{7,6},{8,9},{9,8},{10,11... | collective-permute-start | bytes 3145736 | tf_op jit(solution)/shard_map/ppermute | solution.py:516
  109.2 15.0 %collective-permute-start.34 = (f32[8,128,256]{2,1,0:T(8,128)S(1)}, f32[8,128,256]{2,1,0:T(8,128)S(1)}, u32[]{:S(2)}, u32[]{:S(2)}) collective-permute-start(f32[8,128,256]{2,1,0:T(8,128)S(1)} %get-tuple-element.90), channel_id=1, source_target_pairs={{0,1},{1,0},{2,3},{3,2},{4,5},{5,4},{6,7},{7,6},{8,9},{9,8},{10,11... | collective-permute-start | bytes 3145736 | tf_op jit(solution)/shard_map/ppermute | solution.py:516
  109.5 5.9 %collective-permute-start.37 = (f32[4,128,256]{2,1,0:T(8,128)S(1)}, f32[4,128,256]{2,1,0:T(8,128)S(1)}, u32[]{:S(2)}, u32[]{:S(2)}) collective-permute-start(f32[4,128,256]{2,1,0:T(8,128)S(1)} %get-tuple-element.94), channel_id=1, source_target_pairs={{0,1},{1,0},{2,3},{3,2},{4,5},{5,4},{6,7},{7,6},{8,9},{9,8},{10,11... | collective-permute-start | bytes 1572872 | tf_op jit(solution)/shard_map/ppermute | solution.py:503
  110.0 8.4 %collective-permute-start.17 = (f32[2,128,256]{2,1,0:T(8,128)S(1)}, f32[2,128,256]{2,1,0:T(8,128)S(1)}, u32[]{:S(2)}, u32[]{:S(2)}) collective-permute-start(f32[2,128,256]{2,1,0:T(8,128)S(1)} %get-tuple-element.72), channel_id=1, source_target_pairs={{0,2},{1,3},{2,4},{3,5},{4,6},{5,7},{6,0},{7,1},{8,10},{9,11},{10,... | collective-permute-start | bytes 786440 | tf_op jit(solution)/shard_map/ppermute | solution.py:514
  112.6 9.3 %collective-permute-start.18 = (f32[2,128,256]{2,1,0:T(8,128)S(1)}, f32[2,128,256]{2,1,0:T(8,128)S(1)}, u32[]{:S(2)}, u32[]{:S(2)}) collective-permute-start(f32[2,128,256]{2,1,0:T(8,128)S(1)} %get-tuple-element.73), channel_id=1, source_target_pairs={{0,6},{1,7},{2,0},{3,1},{4,2},{5,3},{6,4},{7,5},{8,14},{9,15},{10,... | collective-permute-start | bytes 786440 | tf_op jit(solution)/shard_map/ppermute | solution.py:515
  115.4 17.9 %collective-permute-start.33 = (f32[4,128,256]{2,1,0:T(8,128)S(1)}, f32[4,128,256]{2,1,0:T(8,128)S(1)}, u32[]{:S(2)}, u32[]{:S(2)}) collective-permute-start(f32[4,128,256]{2,1,0:T(8,128)S(1)} %get-tuple-element.88), channel_id=1, source_target_pairs={{0,1},{1,0},{2,3},{3,2},{4,5},{5,4},{6,7},{7,6},{8,9},{9,8},{10,11... | collective-permute-start | bytes 1572872 | tf_op jit(solution)/shard_map/ppermute | solution.py:553
  118.4 14.9 %collective-permute-start.12 = (f32[4,128,256]{2,1,0:T(8,128)S(1)}, f32[4,128,256]{2,1,0:T(8,128)S(1)}, u32[]{:S(2)}, u32[]{:S(2)}) collective-permute-start(f32[4,128,256]{2,1,0:T(8,128)S(1)} %get-tuple-element.65), channel_id=1, source_target_pairs={{0,1},{1,0},{2,3},{3,2},{4,5},{5,4},{6,7},{7,6},{8,9},{9,8},{10,11... | collective-permute-start | bytes 1572872 | tf_op jit(solution)/shard_map/ppermute | solution.py:553
  121.9 9.2 %collective-permute-start.38 = (f32[2,128,256]{2,1,0:T(8,128)S(1)}, f32[2,128,256]{2,1,0:T(8,128)S(1)}, u32[]{:S(2)}, u32[]{:S(2)}) collective-permute-start(f32[2,128,256]{2,1,0:T(8,128)S(1)} %get-tuple-element.95), channel_id=1, source_target_pairs={{0,2},{1,3},{2,4},{3,5},{4,6},{5,7},{6,0},{7,1},{8,10},{9,11},{10,... | collective-permute-start | bytes 786440 | tf_op jit(solution)/shard_map/ppermute | solution.py:514
  121.9 9.1 %collective-permute-start.39 = (f32[2,128,256]{2,1,0:T(8,128)S(1)}, f32[2,128,256]{2,1,0:T(8,128)S(1)}, u32[]{:S(2)}, u32[]{:S(2)}) collective-permute-start(f32[2,128,256]{2,1,0:T(8,128)S(1)} %get-tuple-element.96), channel_id=1, source_target_pairs={{0,6},{1,7},{2,0},{3,1},{4,2},{5,3},{6,4},{7,5},{8,14},{9,15},{10,... | collective-permute-start | bytes 786440 | tf_op jit(solution)/shard_map/ppermute | solution.py:515
  124.2 15.3 %collective-permute-start.19 = (f32[2,128,256]{2,1,0:T(8,128)S(1)}, f32[2,128,256]{2,1,0:T(8,128)S(1)}, u32[]{:S(2)}, u32[]{:S(2)}) collective-permute-start(f32[2,128,256]{2,1,0:T(8,128)S(1)} %get-tuple-element.76), channel_id=1, source_target_pairs={{0,2},{1,3},{2,4},{3,5},{4,6},{5,7},{6,0},{7,1},{8,10},{9,11},{10,... | collective-permute-start | bytes 786440 | tf_op jit(solution)/shard_map/ppermute | solution.py:548
  131.2 8.4 %collective-permute-start.42 = (f32[1,128,256]{2,1,0:T(8,128)S(1)}, f32[1,128,256]{2,1,0:T(8,128)S(1)}, u32[]{:S(2)}, u32[]{:S(2)}) collective-permute-start(f32[1,128,256]{2,1,0:T(8,128)S(1)} %get-tuple-element.103), channel_id=1, source_target_pairs={{0,2},{1,3},{2,4},{3,5},{4,6},{5,7},{6,0},{7,1},{8,10},{9,11},{10,... | collective-permute-start | bytes 393224 | tf_op jit(solution)/shard_map/ppermute | solution.py:548
  132.5 10.4 %collective-permute-start.20 = (f32[2,128,256]{2,1,0:T(8,128)S(1)}, f32[2,128,256]{2,1,0:T(8,128)S(1)}, u32[]{:S(2)}, u32[]{:S(2)}) collective-permute-start(f32[2,128,256]{2,1,0:T(8,128)S(1)} %get-tuple-element.77), channel_id=1, source_target_pairs={{0,6},{1,7},{2,0},{3,1},{4,2},{5,3},{6,4},{7,5},{8,14},{9,15},{10,... | collective-permute-start | bytes 786440 | tf_op jit(solution)/shard_map/ppermute | solution.py:551
  133.3 15.2 %collective-permute-start.14 = (f32[2,128,256]{2,1,0:T(8,128)S(1)}, f32[2,128,256]{2,1,0:T(8,128)S(1)}, u32[]{:S(2)}, u32[]{:S(2)}) collective-permute-start(f32[2,128,256]{2,1,0:T(8,128)S(1)} %get-tuple-element.68), channel_id=1, source_target_pairs={{0,6},{1,7},{2,0},{3,1},{4,2},{5,3},{6,4},{7,5},{8,14},{9,15},{10,... | collective-permute-start | bytes 786440 | tf_op jit(solution)/shard_map/ppermute | solution.py:535
  133.3 15.2 %collective-permute-start.15 = (f32[2,128,256]{2,1,0:T(8,128)S(1)}, f32[2,128,256]{2,1,0:T(8,128)S(1)}, u32[]{:S(2)}, u32[]{:S(2)}) collective-permute-start(f32[2,128,256]{2,1,0:T(8,128)S(1)} %get-tuple-element.69), channel_id=1, source_target_pairs={{0,2},{1,3},{2,4},{3,5},{4,6},{5,7},{6,0},{7,1},{8,10},{9,11},{10,... | collective-permute-start | bytes 786440 | tf_op jit(solution)/shard_map/ppermute | solution.py:534
  139.5 14.8 %collective-permute-start.35 = (f32[2,128,256]{2,1,0:T(8,128)S(1)}, f32[2,128,256]{2,1,0:T(8,128)S(1)}, u32[]{:S(2)}, u32[]{:S(2)}) collective-permute-start(f32[2,128,256]{2,1,0:T(8,128)S(1)} %get-tuple-element.91), channel_id=1, source_target_pairs={{0,6},{1,7},{2,0},{3,1},{4,2},{5,3},{6,4},{7,5},{8,14},{9,15},{10,... | collective-permute-start | bytes 786440 | tf_op jit(solution)/shard_map/ppermute | solution.py:535
  139.5 14.7 %collective-permute-start.36 = (f32[2,128,256]{2,1,0:T(8,128)S(1)}, f32[2,128,256]{2,1,0:T(8,128)S(1)}, u32[]{:S(2)}, u32[]{:S(2)}) collective-permute-start(f32[2,128,256]{2,1,0:T(8,128)S(1)} %get-tuple-element.92), channel_id=1, source_target_pairs={{0,2},{1,3},{2,4},{3,5},{4,6},{5,7},{6,0},{7,1},{8,10},{9,11},{10,... | collective-permute-start | bytes 786440 | tf_op jit(solution)/shard_map/ppermute | solution.py:534
  142.9 11.4 %collective-permute-start.43 = (f32[1,128,256]{2,1,0:T(8,128)S(1)}, f32[1,128,256]{2,1,0:T(8,128)S(1)}, u32[]{:S(2)}, u32[]{:S(2)}) collective-permute-start(f32[1,128,256]{2,1,0:T(8,128)S(1)} %get-tuple-element.104), channel_id=1, source_target_pairs={{0,6},{1,7},{2,0},{3,1},{4,2},{5,3},{6,4},{7,5},{8,14},{9,15},{10,... | collective-permute-start | bytes 393224 | tf_op jit(solution)/shard_map/ppermute | solution.py:551
  148.5 6.9 %collective-permute-start.40 = (f32[1,128,256]{2,1,0:T(8,128)S(1)}, f32[1,128,256]{2,1,0:T(8,128)S(1)}, u32[]{:S(2)}, u32[]{:S(2)}) collective-permute-start(f32[1,128,256]{2,1,0:T(8,128)S(1)} %get-tuple-element.101), channel_id=1, source_target_pairs={{0,2},{1,3},{2,4},{3,5},{4,6},{5,7},{6,0},{7,1},{8,10},{9,11},{10,... | collective-permute-start | bytes 393224 | tf_op jit(solution)/shard_map/ppermute | solution.py:548
  148.5 7.2 %collective-permute-start.41 = (f32[1,128,256]{2,1,0:T(8,128)S(1)}, f32[1,128,256]{2,1,0:T(8,128)S(1)}, u32[]{:S(2)}, u32[]{:S(2)}) collective-permute-start(f32[1,128,256]{2,1,0:T(8,128)S(1)} %get-tuple-element.102), channel_id=1, source_target_pairs={{0,6},{1,7},{2,0},{3,1},{4,2},{5,3},{6,4},{7,5},{8,14},{9,15},{10,... | collective-permute-start | bytes 393224 | tf_op jit(solution)/shard_map/ppermute | solution.py:551
  (6 other events, 129.2 us)
